TPU v7x, 128 devices: a whole 4x4x4 slice. The times are simulated.
128 devices in a mesh: ctx: 16 (over y, x_hi, core), tp: 8 (over x_lo, z).
Axes of the slice: x: 4 (x_hi: 2, x_lo: 2; x = x_hi * 2 + x_lo), y: 4, z: 4, core: 2. Of those that a mesh axis runs over, the one named last changes fastest.
Arguments:
- hyena_query: bfloat16 [6144, 8192], P('ctx', 'tp'), may hold values from -6 to 6
- hyena_key: bfloat16 [6144, 8192], P('ctx', 'tp'), may hold values from -6 to 6
- hyena_value: bfloat16 [6144, 8192], P('ctx', 'tp'), may hold values from -6 to 6
- conv_filter: bfloat16 [512, 128], P('tp'), may hold values from -0.5 to 0.5
- skip_gain: float32 [8192], P('tp'), may hold values from -4 to 4
- query_rows: bfloat16 [6144, 8192], P('ctx', 'tp'), may hold values from -80 to 80
- key_rows: bfloat16 [6144, 8192], P('ctx', 'tp'), may hold values from -4 to 4, as said below
- value_rows: bfloat16 [6144, 8192], P('ctx', 'tp'), may hold values from -6 to 6
- out_weight: bfloat16 [8192, 8192], P(None, 'tp'), may hold values from -1 to 1
Outputs:
- hyena_out: bfloat16 [6144, 8192], P('ctx', 'tp')
- attention_out: bfloat16 [8192, 6144], P('tp', 'ctx')
Inputs may be any that keep to these rules, and one draw needn't show every extreme that they name: `key_rows`: keys of order one.
All inputs are finite; a program needn't handle non-finite values.
Results may differ from a plain program's by a relative error of at most 0.014.
Values may be sent and summed in bfloat16 or wider, within the bound.
No kernel may reach another device: no remote copies, remote signals or barrier semaphores. Data moves between devices by JAX's collectives and lax.ppermute only.
A program may use at most 128 MiB of HBM per device.

v0:
```python
import jax
import jax.numpy as jnp
from jax import lax
from jax.experimental import pallas as pl
from jax.experimental.pallas import tpu as pltpu
from jax.sharding import PartitionSpec as P

HEAD_DIM = 128
CHIPS_Y = 4
CHIPS = 8
RING = 4
NEGATIVE = -1e30
EXP_SCALE = HEAD_DIM ** (-0.5) * 1.4426950408889634


VMEM = pltpu.VMEM
SMEM_SPEC = pl.BlockSpec(memory_space=pltpu.SMEM)
VMEM_SPEC = pl.BlockSpec(memory_space=pltpu.VMEM)


def shifted(block, axis, distance):
    devices = range(lax.axis_size(axis))
    route = [(i - distance, i) for i in devices if i - distance in devices]
    return lax.ppermute(block, axis, route)


def toeplitz_pair(filters):
    length = filters.shape[1]
    lag_table = (
        jnp.arange(length, dtype=jnp.int32)[:, None] - jnp.arange(length, dtype=jnp.int32)[None, :]
    )
    taps = jnp.arange(length, dtype=jnp.int32)[:, None, None]
    inner_table = (lag_table[None] == taps).astype(jnp.bfloat16)
    outer_table = (lag_table[None] + length == taps).astype(jnp.bfloat16)
    inner_part = jnp.einsum(
        "gj,jts->gts", filters, inner_table, preferred_element_type=jnp.float32
    ).astype(jnp.bfloat16)
    outer_part = jnp.einsum(
        "gj,jts->gts", filters, outer_table, preferred_element_type=jnp.float32
    ).astype(jnp.bfloat16)
    return (inner_part, outer_part)


def local_conv(current, before, filters):
    blocks, length, feature_width = current.shape
    groups = filters.shape[0]
    split_shape = (blocks, length, groups, feature_width // groups)
    inner_part, outer_part = toeplitz_pair(filters)
    result = jnp.einsum(
        "gts,bsgc->btgc",
        inner_part,
        current.reshape(split_shape),
        preferred_element_type=jnp.float32,
    )
    result = result + jnp.einsum(
        "gts,bsgc->btgc",
        outer_part,
        before.reshape(split_shape),
        preferred_element_type=jnp.float32,
    )
    return result.reshape(blocks * length, feature_width)


def hyena(hyena_query, hyena_key, hyena_value, conv_filter, skip_gain):
    product = (hyena_key.astype(jnp.float32) * hyena_value.astype(jnp.float32)).astype(jnp.bfloat16)
    length = conv_filter.shape[1]
    tokens_here, feature_width = product.shape
    blocks = tokens_here // length
    previous = shifted(product[tokens_here - length :], "ctx", 1)
    widened = product.astype(jnp.float32)
    earlier = jnp.concatenate([previous, product[: tokens_here - length]], axis=0)
    convolved = local_conv(
        product.reshape(blocks, length, feature_width),
        earlier.reshape(blocks, length, feature_width),
        conv_filter,
    )
    return (hyena_query.astype(jnp.float32) * (convolved + skip_gain[None, :] * widened)).astype(
        jnp.bfloat16
    )


def chip_route(step):
    route = []
    for source in range(2 * CHIPS):
        y, x, core = source // 4, source // 2 % 2, source % 2
        target = ((y + step // 2) % CHIPS_Y * 2 + (x + step) % 2) * 2 + core
        route.append((source, target))
    return route


CORE_GROUPS = [list(range(core, 2 * CHIPS, 2)) for core in range(2)]
CORE_ROUTE = [(i, i ^ 1) for i in range(2 * CHIPS)]


def ring_route(step):
    return [(i, i // RING * RING + (i + step) % RING) for i in range(2 * RING)]


PAIR_ROUTE = [(i, (i + RING) % (2 * RING)) for i in range(2 * RING)]


def ahead(y, x, step):
    return ((y + step // 2) & 3) * 2 + ((x + step) & 1)


def behind(y, x, step):
    return ((y - step // 2) & 3) * 2 + ((x - step) & 1)


def split_kernel(q_ref, k_ref, v_ref, out_ref):
    rows = q_ref.shape[0]
    out_ref[0, :rows, :] = k_ref[...]
    out_ref[0, rows : 2 * rows, :] = v_ref[...]
    out_ref[0, 2 * rows :, :] = q_ref[...]


def split_heads(query_rows, key_rows, value_rows):
    rows = query_rows.shape[0]
    spec = pl.BlockSpec((rows, HEAD_DIM), lambda head: (0, head))
    return pl.pallas_call(
        split_kernel,
        grid=(CHIPS,),
        out_shape=jax.ShapeDtypeStruct((CHIPS, 3 * rows, HEAD_DIM), jnp.bfloat16),
        in_specs=[spec] * 3,
        out_specs=pl.BlockSpec((1, 3 * rows, HEAD_DIM), lambda head: (head, 0, 0)),
        name="split_heads",
    )(query_rows, key_rows, value_rows)


def attention_kernel(place, own, other, *refs):
    outs = refs[:CHIPS]
    keys, values, top, total = refs[CHIPS:]
    y, x, core = place[0], place[1], place[2]
    step = pl.program_id(0)
    rows = top.shape[0]

    @pl.when(step == 0)
    def _():
        ones = jnp.ones((2 * rows, HEAD_DIM), jnp.bfloat16)
        for i in range(CHIPS):
            keys[i, :, :rows] = own[i, :rows, :].T
            keys[i, :, rows:] = other[i, :rows, :].T
            values[i, :rows, :HEAD_DIM] = own[i, rows : 2 * rows, :]
            values[i, rows:, :HEAD_DIM] = other[i, rows:, :]
            values[i, :, HEAD_DIM:] = ones

    top[...] = jnp.full_like(top, NEGATIVE)
    total[...] = jnp.zeros_like(total)
    chip = ahead(y, x, step)

    def update(slot, first, width, masked):
        scores = jnp.dot(
            own[chip, 2 * rows :, :],
            keys[slot, :, first : first + width],
            preferred_element_type=jnp.float32,
        )
        if masked:
            row = lax.broadcasted_iota(jnp.int32, scores.shape, 0)
            column = lax.broadcasted_iota(jnp.int32, scores.shape, 1)
            scores = jnp.where(column <= row, scores, NEGATIVE)
        old = top[...]
        new = jnp.maximum(old, jnp.max(scores, axis=1, keepdims=True))
        keep = jnp.exp2((old - new) * EXP_SCALE)
        spread = jnp.concatenate([new] * (width // HEAD_DIM), axis=1)
        weights = jnp.exp2((scores - spread) * EXP_SCALE).astype(jnp.bfloat16)
        total[...] = total[...] * jnp.concatenate([keep, keep], axis=1) + jnp.dot(
            weights, values[slot, first : first + width, :], preferred_element_type=jnp.float32
        )
        top[...] = new

    def full_step(j, unused):
        update(j, 0, 2 * rows, False)
        return unused

    lax.fori_loop(0, chip, full_step, 0)
    update(chip, 0, rows, True)

    @pl.when(core == 1)
    def _():
        update(chip, rows, rows, False)

    result = (total[:, :HEAD_DIM] / total[:, HEAD_DIM:]).astype(jnp.bfloat16)
    for i in range(CHIPS):

        @pl.when(step == i)
        def _(i=i):
            outs[i][...] = result


def attention(place, own, other):
    rows = own.shape[1] // 3
    return pl.pallas_call(
        attention_kernel,
        grid=(CHIPS,),
        out_shape=[jax.ShapeDtypeStruct((rows, HEAD_DIM), jnp.bfloat16)] * CHIPS,
        in_specs=[SMEM_SPEC, VMEM_SPEC, VMEM_SPEC],
        out_specs=[VMEM_SPEC] * CHIPS,
        scratch_shapes=[
            VMEM((CHIPS, HEAD_DIM, 2 * rows), jnp.bfloat16),
            VMEM((CHIPS, 2 * rows, 2 * HEAD_DIM), jnp.bfloat16),
            VMEM((rows, HEAD_DIM), jnp.float32),
            VMEM((rows, 2 * HEAD_DIM), jnp.float32),
        ],
        cost_estimate=pl.CostEstimate(
            flops=12_000_000_000, bytes_accessed=6_000_000, transcendentals=10_000_000
        ),
        name="attention",
    )(place, own, other)


def join_kernel(place, *refs):
    y, x = place[0], place[1]
    joined = refs[CHIPS]
    for step in range(CHIPS):
        column = pl.multiple_of(behind(y, x, step) * HEAD_DIM, HEAD_DIM)
        joined[:, pl.ds(column, HEAD_DIM)] = refs[step][...]


def join_heads(place, pieces):
    rows = pieces[0].shape[0]
    return pl.pallas_call(
        join_kernel,
        out_shape=jax.ShapeDtypeStruct((rows, CHIPS * HEAD_DIM), jnp.bfloat16),
        in_specs=[SMEM_SPEC] + [VMEM_SPEC] * CHIPS,
        out_specs=VMEM_SPEC,
        name="join_heads",
    )(place, *pieces)


def project(place, wanted, out_weight, attended):
    rows, features = attended.shape
    share = out_weight.shape[0] // (4 * RING)

    def weight_block(step, place):
        index = jnp.int32(0)
        for i, (x_off, z_off, half) in enumerate(wanted):
            row = ((((place[3] + x_off) & 1) * RING + ((place[4] + z_off) & 3)) * 2) + half
            index = jnp.where(step == i, row, index)
        return (index, 0)

    def kernel(place, weight_ref, attended_ref, *outs):
        piece = lax.dot_general(
            weight_ref[...],
            attended_ref[...],
            (((1,), (1,)), ((), ())),
            preferred_element_type=jnp.float32,
        ).astype(jnp.bfloat16)
        for i in range(len(wanted)):

            @pl.when(pl.program_id(0) == i)
            def _(i=i):
                outs[i][...] = piece

    count = len(wanted)
    return pl.pallas_call(
        kernel,
        grid_spec=pltpu.PrefetchScalarGridSpec(
            num_scalar_prefetch=1,
            grid=(count,),
            in_specs=[
                pl.BlockSpec((share, features), weight_block),
                pl.BlockSpec((rows, features), lambda step, place: (0, 0)),
            ],
            out_specs=[pl.BlockSpec((share, rows), lambda step, place: (0, 0))] * count,
        ),
        out_shape=[jax.ShapeDtypeStruct((share, rows), jnp.bfloat16)] * count,
        cost_estimate=pl.CostEstimate(
            flops=2 * share * rows * features * count,
            bytes_accessed=share * features * 2 * count,
            transcendentals=0,
        ),
        name="project",
    )(place, out_weight, attended)


def added(*pieces):
    return sum(piece.astype(jnp.float32) for piece in pieces)


def local_step(
    hyena_query,
    hyena_key,
    hyena_value,
    conv_filter,
    skip_gain,
    query_rows,
    key_rows,
    value_rows,
    out_weight,
):
    ctx = lax.axis_index("ctx")
    tp = lax.axis_index("tp")
    place = jnp.stack([ctx // 4, ctx // 2 % 2, ctx % 2, tp // RING, tp % RING]).astype(jnp.int32)

    rows = query_rows.shape[0]
    pieces = split_heads(query_rows, key_rows, value_rows)
    own = lax.all_to_all(pieces, "ctx", 0, 0, axis_index_groups=CORE_GROUPS, tiled=True)
    hyena_out = hyena(hyena_query, hyena_key, hyena_value, conv_filter, skip_gain)
    other = lax.ppermute(own[:, : 2 * rows], "ctx", CORE_ROUTE)
    outs = attention(place, own, other)
    back = [outs[0]] + [
        lax.ppermute(outs[step], "ctx", chip_route(step)) for step in range(1, CHIPS)
    ]
    attended = join_heads(place, back)

    kept = []
    handed = None
    for x_off in (1, 0):

        def sent(block, step):
            return lax.ppermute(block, "tp", ring_route(step))

        far = project(place, [(x_off, 2, 0), (x_off, 2, 1)], out_weight, attended)
        near = project(
            place,
            [
                (x_off, 1, 1),
                (x_off, 3, 0),
                (x_off, 1, 0),
                (x_off, 3, 1),
                (x_off, 0, 0),
                (x_off, 0, 1),
            ],
            out_weight,
            attended,
        )
        from_below = sent(far[0], 1)
        from_above = sent(far[1], -1)
        below_1 = sent(near[0], 1)
        above_0 = sent(near[1], -1)
        up = added(near[2], from_below).astype(jnp.bfloat16)
        down = added(near[3], from_above).astype(jnp.bfloat16)
        below_0 = sent(up, 1)
        above_1 = sent(down, -1)
        first = added(near[4], below_0, above_0)
        second = added(near[5], below_1, above_1)
        if x_off == 1:
            handed = [
                lax.ppermute(part.astype(jnp.bfloat16), "tp", PAIR_ROUTE)
                for part in (first, second)
            ]
        else:
            kept = [first, second]
    attention_out = jnp.concatenate(
        [(kept[i] + handed[i].astype(jnp.float32)).astype(jnp.bfloat16) for i in range(2)], axis=0
    )
    return (hyena_out, attention_out)


def solution(mesh):
    in_specs = (
        P("ctx", "tp"),
        P("ctx", "tp"),
        P("ctx", "tp"),
        P("tp", None),
        P("tp"),
        P("ctx", "tp"),
        P("ctx", "tp"),
        P("ctx", "tp"),
        P(None, "tp"),
    )
    out_specs = (P("ctx", "tp"), P("tp", "ctx"))
    return jax.shard_map(local_step, mesh=mesh, in_specs=in_specs, out_specs=out_specs, check_vma=False)
```

profile of v0, /device:TPU:1, one launch (start us, length us, event | category | flops | bytes accessed | tf_op | source)
XLA Modules:
  0.0 210.7 jit_solution(8675477487515828708)
XLA Ops:
  0.6 6.0 %split_heads.1 = bf16[8,1152,128]{2,1,0:T(8,128)(2,1)} custom-call(bf16[384,1024]{1,0:T(8,128)(2,1)} %q_ref.1, bf16[384,1024]{1,0:T(8,128)(2,1)} %k_ref.1, bf16[384,1024]{1,0:T(8,128)(2,1)} %v_ref.1), custom_call_target="tpu_custom_call" | custom-call | tf_op jit(solution)/shard_map/split_heads/pallas_call | solution.py:120
  6.6 7.6 %all-to-all-start = ((bf16[8,1152,128]{2,1,0:T(8,128)(2,1)}), bf16[8,1152,128]{2,1,0:T(8,128)(2,1)S(1)}, u32[]{:S(2)}, u32[]{:S(2)}) async-start(bf16[8,1152,128]{2,1,0:T(8,128)(2,1)} %split_heads.1), calls=%async_computation | async-start | bytes 4718592 | tf_op jit(solution)/shard_map/all_to_all | solution.py:297
  15.4 2.3 %copy.13 = bf16[384,1024]{0,1:T(8,128)(2,1)} copy(bf16[384,1024]{1,0:T(8,128)(2,1)} %param.10) | data formatting | bytes 1572864 | tf_op args[1]
  19.3 6.0 %collective-permute-start = (bf16[128,1024]{0,1:T(8,128)(2,1)S(1)}, bf16[128,1024]{0,1:T(8,128)(2,1)}, u32[]{:S(2)}, u32[]{:S(2)}) collective-permute-start(bf16[128,1024]{0,1:T(8,128)(2,1)S(1)} %slice.12), channel_id=1, source_target_pairs={{0,8},{8,16},{16,24},{24,32},{32,40},{40,48},{48,56},{56,64},{64,7... | collective-permute-start | bytes 786440 | tf_op jit(solution)/shard_map/ppermute | solution.py:24
  26.4 2.4 %copy.12 = bf16[384,1024]{0,1:T(8,128)(2,1)} copy(bf16[384,1024]{1,0:T(8,128)(2,1)} %param.9) | data formatting | bytes 1572864 | tf_op args[0]
  29.4 2.6 %iota_compare_fusion.1 = pred[128,128,128]{2,1,0:T(32,128)(4,1)} fusion(s32[128,128]{1,0:T(8,128)S(1)} %iota_subtract_fusion), kind=kLoop, calls=%fused_computation.1 | loop fusion | flops 2097152 | bytes 2162688 | tf_op jit(solution)/shard_map/eq | solution.py:33
  32.0 12.7 %all-to-all-done.own = bf16[8,1152,128]{2,1,0:T(8,128)(2,1)S(1)} async-done(((bf16[8,1152,128]{2,1,0:T(8,128)(2,1)}), bf16[8,1152,128]{2,1,0:T(8,128)(2,1)S(1)}, u32[]{:S(2)}, u32[]{:S(2)}) %all-to-all-start) | async-done | bytes 2359328 | tf_op jit(solution)/shard_map/all_to_all | solution.py:297
  44.7 2.1 %collective-permute-start.1 = (bf16[8,768,128]{2,1,0:T(8,128)(2,1)S(1)}, bf16[8,768,128]{2,1,0:T(8,128)(2,1)}, u32[]{:S(2)}, u32[]{:S(2)}) collective-permute-start(bf16[8,768,128]{2,1,0:T(8,128)(2,1)S(1)} %slice.14), channel_id=1, source_target_pairs={{0,8},{8,0},{16,24},{24,16},{32,40},{40,32},{48,56},{56,48},{64,72... | collective-permute-start | bytes 4718600 | tf_op jit(solution)/shard_map/ppermute | solution.py:299
  47.1 3.4 %fusion.2 = bf16[128,128,64]{1,2,0:T(8,128)(2,1)S(1)} fusion(pred[128,128,128]{2,1,0:T(32,128)(4,1)S(1)} %copy-done.7, bf16[64,128]{1,0:T(8,128)(2,1)S(1)} %copy-done), kind=kOutput, calls=%fused_computation.4 | convolution fusion | flops 268435456 | bytes 4210688 | tf_op jit(solution)/shard_map/gj,jts->gts/dot_general | solution.py:35
  51.7 4.7 %fusion = bf16[128,128,64]{1,2,0:T(8,128)(2,1)} fusion(pred[128,128,128]{2,1,0:T(32,128)(4,1)S(1)} %iota_compare_fusion, bf16[64,128]{1,0:T(8,128)(2,1)S(1)} %copy-done), kind=kOutput, calls=%fused_computation.2 | convolution fusion | flops 268435456 | bytes 4210688 | tf_op jit(solution)/shard_map/gj,jts->gts/dot_general | solution.py:38
  56.4 2.3 %fusion.5 = f32[64,3,16,128]{3,2,1,0:T(8,128)S(1)} fusion(bf16[128,128,64]{1,2,0:T(8,128)(2,1)S(1)} %fusion.2, bf16[3,128,64,16]{1,0,3,2:T(4,128)(2,1)S(1)} %copy-done.5), kind=kOutput, calls=%fused_computation.9 | convolution fusion | flops 100663296 | bytes 4456448 | tf_op jit(solution)/shard_map/gts,bsgc->btgc/dot_general | solution.py:49
  58.7 34.1 %attention.1 = (bf16[384,128]{1,0:T(8,128)(2,1)}, bf16[384,128]{1,0:T(8,128)(2,1)}, bf16[384,128]{1,0:T(8,128)(2,1)}, bf16[384,128]{1,0:T(8,128)(2,1)}, bf16[384...) custom-call(s32[5]{0:T(128)} %stack.23.place, ...), custom_call_target="tpu_custom_call" | custom-call | flops 12000000000 | bytes 6000000 | tf_op jit(solution)/shard_map/attention/pallas_call | solution.py:192
  95.3 1.9 pad_maximum_fusion
  97.2 2.4 %reshape_reshape.7 = bf16[3,128,64,16]{1,0,3,2:T(4,128)(2,1)S(1)} reshape(bf16[384,1024]{0,1:T(8,128)(2,1)} %pad_maximum_fusion) | data formatting | bytes 1572864 | tf_op jit(solution)/shard_map/reshape;reshape | solution.py:58
  99.6 2.0 collective-permute-start.4
  101.6 2.4 %collective-permute-start.5 = (bf16[384,128]{1,0:T(8,128)(2,1)}, bf16[384,128]{1,0:T(8,128)(2,1)S(1)}, u32[]{:S(2)}, u32[]{:S(2)}) collective-permute-start(bf16[384,128]{1,0:T(8,128)(2,1)} %get-tuple-element.30), channel_id=1, source_target_pairs={{0,64},{8,72},{16,80},{24,88},{32,96},{40,104},{48,112},{56,120},{... | collective-permute-start | bytes 294920 | tf_op jit(solution)/shard_map/ppermute | solution.py:302
  105.1 2.7 %collective-permute-start.7 = (bf16[384,128]{1,0:T(8,128)(2,1)}, bf16[384,128]{1,0:T(8,128)(2,1)}, u32[]{:S(2)}, u32[]{:S(2)}) collective-permute-start(bf16[384,128]{1,0:T(8,128)(2,1)} %get-tuple-element.32), channel_id=1, source_target_pairs={{0,96},{8,104},{16,112},{24,120},{32,0},{40,8},{48,16},{56,24},{64... | collective-permute-start | bytes 294920 | tf_op jit(solution)/shard_map/ppermute | solution.py:302
  109.6 4.0 %add_bitcast_fusion = f32[3,128,64,16]{1,3,0,2:T(8,128)S(1)} fusion(f32[64,3,16,128]{3,2,1,0:T(8,128)S(1)} %fusion.5, bf16[128,128,64]{1,2,0:T(8,128)(2,1)} %fusion, bf16[3,128,64,16]{1,0,3,2:T(4,128)(2,1)S(1)} %reshape_reshape.7), kind=kOutput, calls=%fused_computation.15 | convolution fusion | flops 101056512 | bytes 6029312 | tf_op jit(solution)/shard_map/gts,bsgc->btgc/dot_general | solution.py:55
  115.2 2.3 %join_heads.1.attended_ref = bf16[384,1024]{1,0:T(8,128)(2,1)} custom-call(s32[5]{0:T(128)} %stack.23.place, bf16[384,128]{1,0:T(8,128)(2,1)} %get-tuple-element.26.refs_0_, bf16[384,128]{1,0:T(8,128)(2,1)} %copy-done.15, bf16[384,128]{1,0:T(8,128)(2,1)} %collective-permute-done.3.refs_2_, bf16[384,128]{1,0:T(8,128)(2,1)} %copy-done.16, ...), custom_call_target="tpu_custom_call" | custom-call | tf_op jit(solution)/shard_map/join_heads/pallas_call | solution.py:221
  117.5 4.6 %project.7 = (bf16[512,384]{1,0:T(8,128)(2,1)}, bf16[512,384]{1,0:T(8,128)(2,1)}) custom-call(s32[5]{0:T(128)} %stack.23.place, bf16[8192,1024]{1,0:T(8,128)(2,1)} %weight_ref.7, bf16[384,1024]{1,0:T(8,128)(2,1)} %join_heads.1.attended_ref), custom_call_target="tpu_custom_call" | custom-call | flops 805306368 | bytes 2097152 | tf_op jit(solution)/shard_map/project/pallas_call | solution.py:255
  122.1 3.8 %collective-permute-start.20 = (bf16[512,384]{1,0:T(8,128)(2,1)}, bf16[512,384]{1,0:T(8,128)(2,1)S(1)}, u32[]{:S(2)}, u32[]{:S(2)}) collective-permute-start(bf16[512,384]{1,0:T(8,128)(2,1)} %get-tuple-element.49), channel_id=1, source_target_pairs={{0,3},{1,0},{2,1},{3,2},{4,7},{5,4},{6,5},{7,6},{8,11},{9,8},{10,9... | collective-permute-start | bytes 1179656 | tf_op jit(solution)/shard_map/ppermute | solution.py:311
  125.9 9.4 %project.6 = (bf16[512,384]{1,0:T(8,128)(2,1)}, bf16[512,384]{1,0:T(8,128)(2,1)}, bf16[512,384]{1,0:T(8,128)(2,1)}, bf16[512,384]{1,0:T(8,128)(2,1)}, bf16[512,3...) custom-call(s32[5]{0:T(128)} %stack.23.place, bf16[8192,1024]{1,0:T(8,128)(2,1)} %weight_ref.7, ...), custom_call_target="tpu_custom_call" | custom-call | flops 2415919104 | bytes 6291456 | tf_op jit(solution)/shard_map/project/pallas_call | solution.py:255
  135.3 4.6 %project.5 = (bf16[512,384]{1,0:T(8,128)(2,1)}, bf16[512,384]{1,0:T(8,128)(2,1)}) custom-call(s32[5]{0:T(128)} %stack.23.place, bf16[8192,1024]{1,0:T(8,128)(2,1)} %weight_ref.7, bf16[384,1024]{1,0:T(8,128)(2,1)} %join_heads.1.attended_ref), custom_call_target="tpu_custom_call" | custom-call | flops 805306368 | bytes 2097152 | tf_op jit(solution)/shard_map/project/pallas_call | solution.py:255
  139.9 2.7 %collective-permute-start.17 = (bf16[512,384]{1,0:T(8,128)(2,1)}, bf16[512,384]{1,0:T(8,128)(2,1)}, u32[]{:S(2)}, u32[]{:S(2)}) collective-permute-start(bf16[512,384]{1,0:T(8,128)(2,1)} %get-tuple-element.45), channel_id=1, source_target_pairs={{0,3},{1,0},{2,1},{3,2},{4,7},{5,4},{6,5},{7,6},{8,11},{9,8},{10,9... | collective-permute-start | bytes 1179656 | tf_op jit(solution)/shard_map/ppermute | solution.py:311
  142.6 9.4 %project.4 = (bf16[512,384]{1,0:T(8,128)(2,1)}, bf16[512,384]{1,0:T(8,128)(2,1)}, bf16[512,384]{1,0:T(8,128)(2,1)}, bf16[512,384]{1,0:T(8,128)(2,1)}, bf16[512,3...) custom-call(s32[5]{0:T(128)} %stack.23.place, bf16[8192,1024]{1,0:T(8,128)(2,1)} %weight_ref.7, ...), custom_call_target="tpu_custom_call" | custom-call | flops 2415919104 | bytes 6291456 | tf_op jit(solution)/shard_map/project/pallas_call | solution.py:255
  152.1 2.7 %collective-permute-start.14 = (bf16[512,384]{1,0:T(8,128)(2,1)}, bf16[512,384]{1,0:T(8,128)(2,1)S(1)}, u32[]{:S(2)}, u32[]{:S(2)}) collective-permute-start(bf16[512,384]{1,0:T(8,128)(2,1)} %get-tuple-element.41), channel_id=1, source_target_pairs={{0,3},{1,0},{2,1},{3,2},{4,7},{5,4},{6,5},{7,6},{8,11},{9,8},{10,9... | collective-permute-start | bytes 1179656 | tf_op jit(solution)/shard_map/ppermute | solution.py:311
  157.2 15.3 %collective-permute-done.12 = bf16[512,384]{1,0:T(8,128)(2,1)S(1)} collective-permute-done((bf16[512,384]{1,0:T(8,128)(2,1)}, bf16[512,384]{1,0:T(8,128)(2,1)S(1)}, u32[]{:S(2)}, u32[]{:S(2)}) %collective-permute-start.12) | collective-permute-done | bytes 393248 | tf_op jit(solution)/shard_map/ppermute | solution.py:311
  172.7 8.3 %collective-permute-done.9 = bf16[512,384]{1,0:T(8,128)(2,1)S(1)} collective-permute-done((bf16[512,384]{1,0:T(8,128)(2,1)}, bf16[512,384]{1,0:T(8,128)(2,1)S(1)}, u32[]{:S(2)}, u32[]{:S(2)}) %collective-permute-start.9) | collective-permute-done | bytes 393248 | tf_op jit(solution)/shard_map/ppermute | solution.py:311
  181.9 2.7 %collective-permute-start.11 = (bf16[512,384]{1,0:T(8,128)(2,1)}, bf16[512,384]{1,0:T(8,128)(2,1)}, u32[]{:S(2)}, u32[]{:S(2)}) collective-permute-start(bf16[512,384]{1,0:T(8,128)(2,1)} %get-tuple-element.37), channel_id=1, source_target_pairs={{0,3},{1,0},{2,1},{3,2},{4,7},{5,4},{6,5},{7,6},{8,11},{9,8},{10,9... | collective-permute-start | bytes 1179656 | tf_op jit(solution)/shard_map/ppermute | solution.py:311
  186.9 5.1 %collective-permute-done.13 = bf16[512,384]{1,0:T(8,128)(2,1)S(1)} collective-permute-done((bf16[512,384]{1,0:T(8,128)(2,1)S(1)}, bf16[512,384]{1,0:T(8,128)(2,1)S(1)}, u32[]{:S(2)}, u32[]{:S(2)}) %collective-permute-start.13) | collective-permute-done | bytes 393248 | tf_op jit(solution)/shard_map/ppermute | solution.py:311
  195.9 4.5 %collective-permute-done.18 = bf16[512,384]{1,0:T(8,128)(2,1)} collective-permute-done((bf16[512,384]{1,0:T(8,128)(2,1)S(1)}, bf16[512,384]{1,0:T(8,128)(2,1)}, u32[]{:S(2)}, u32[]{:S(2)}) %collective-permute-start.18) | collective-permute-done | bytes 393248 | tf_op jit(solution)/shard_map/ppermute | solution.py:311
  202.0 6.2 %collective-permute-done.15 = bf16[512,384]{1,0:T(8,128)(2,1)} collective-permute-done((bf16[512,384]{1,0:T(8,128)(2,1)}, bf16[512,384]{1,0:T(8,128)(2,1)}, u32[]{:S(2)}, u32[]{:S(2)}) %collective-permute-start.15) | collective-permute-done | bytes 393248 | tf_op jit(solution)/shard_map/ppermute | solution.py:339
  (93 shorter events, 26.7 us)
Async XLA Ops:
  0.6 46.2 %copy-start = (bf16[64,128]{1,0:T(8,128)(2,1)S(1)}, bf16[64,128]{1,0:T(8,128)(2,1)}, u32[]{:S(2)}) copy-start(bf16[64,128]{1,0:T(8,128)(2,1)} %param.12) | copy-start | bytes 49156
  6.6 38.0 %all-to-all-start = ((bf16[8,1152,128]{2,1,0:T(8,128)(2,1)}), bf16[8,1152,128]{2,1,0:T(8,128)(2,1)S(1)}, u32[]{:S(2)}, u32[]{:S(2)}) async-start(bf16[8,1152,128]{2,1,0:T(8,128)(2,1)} %split_heads.1), calls=%async_computation | async-start | bytes 4718592 | tf_op jit(solution)/shard_map/all_to_all | solution.py:297
  19.3 76.0 %collective-permute-start = (bf16[128,1024]{0,1:T(8,128)(2,1)S(1)}, bf16[128,1024]{0,1:T(8,128)(2,1)}, u32[]{:S(2)}, u32[]{:S(2)}) collective-permute-start(bf16[128,1024]{0,1:T(8,128)(2,1)S(1)} %slice.12), channel_id=1, source_target_pairs={{0,8},{8,16},{16,24},{24,32},{32,40},{40,48},{48,56},{56,64},{64,7... | collective-permute-start | bytes 786440 | tf_op jit(solution)/shard_map/ppermute | solution.py:24
  44.7 14.0 %collective-permute-start.1 = (bf16[8,768,128]{2,1,0:T(8,128)(2,1)S(1)}, bf16[8,768,128]{2,1,0:T(8,128)(2,1)}, u32[]{:S(2)}, u32[]{:S(2)}) collective-permute-start(bf16[8,768,128]{2,1,0:T(8,128)(2,1)S(1)} %slice.14), channel_id=1, source_target_pairs={{0,8},{8,0},{16,24},{24,16},{32,40},{40,32},{48,56},{56,48},{64,72... | collective-permute-start | bytes 4718600 | tf_op jit(solution)/shard_map/ppermute | solution.py:299
  58.7 36.6 %slice-start = ((bf16[384,1024]{0,1:T(8,128)(2,1)}), bf16[256,1024]{0,1:T(8,128)(2,1)S(1)}, s32[]{:S(2)}) async-start(bf16[384,1024]{0,1:T(8,128)(2,1)} %copy-done.2), calls=%async_computation.1 | async-start | bytes 1048576 | tf_op jit(solution)/shard_map/slice | solution.py:71
  92.8 12.3 %collective-permute-start.2 = (bf16[384,128]{1,0:T(8,128)(2,1)}, bf16[384,128]{1,0:T(8,128)(2,1)S(1)}, u32[]{:S(2)}, u32[]{:S(2)}) collective-permute-start(bf16[384,128]{1,0:T(8,128)(2,1)} %get-tuple-element.27), channel_id=1, source_target_pairs={{0,16},{8,24},{16,0},{24,8},{32,48},{40,56},{48,32},{56,40},{64,80... | collective-permute-start | bytes 294920 | tf_op jit(solution)/shard_map/ppermute | solution.py:302
  93.6 14.2 %collective-permute-start.3 = (bf16[384,128]{1,0:T(8,128)(2,1)}, bf16[384,128]{1,0:T(8,128)(2,1)}, u32[]{:S(2)}, u32[]{:S(2)}) collective-permute-start(bf16[384,128]{1,0:T(8,128)(2,1)} %get-tuple-element.28), channel_id=1, source_target_pairs={{0,32},{8,40},{16,48},{24,56},{32,64},{40,72},{48,80},{56,88},{64,... | collective-permute-start | bytes 294920 | tf_op jit(solution)/shard_map/ppermute | solution.py:302
  99.6 14.9 %collective-permute-start.4 = (bf16[384,128]{1,0:T(8,128)(2,1)}, bf16[384,128]{1,0:T(8,128)(2,1)S(1)}, u32[]{:S(2)}, u32[]{:S(2)}) collective-permute-start(bf16[384,128]{1,0:T(8,128)(2,1)} %get-tuple-element.29), channel_id=1, source_target_pairs={{0,48},{8,56},{16,32},{24,40},{32,80},{40,88},{48,64},{56,72},{64,... | collective-permute-start | bytes 294920 | tf_op jit(solution)/shard_map/ppermute | solution.py:302
  101.6 12.9 %collective-permute-start.5 = (bf16[384,128]{1,0:T(8,128)(2,1)}, bf16[384,128]{1,0:T(8,128)(2,1)S(1)}, u32[]{:S(2)}, u32[]{:S(2)}) collective-permute-start(bf16[384,128]{1,0:T(8,128)(2,1)} %get-tuple-element.30), channel_id=1, source_target_pairs={{0,64},{8,72},{16,80},{24,88},{32,96},{40,104},{48,112},{56,120},{... | collective-permute-start | bytes 294920 | tf_op jit(solution)/shard_map/ppermute | solution.py:302
  104.0 10.6 %collective-permute-start.6 = (bf16[384,128]{1,0:T(8,128)(2,1)}, bf16[384,128]{1,0:T(8,128)(2,1)}, u32[]{:S(2)}, u32[]{:S(2)}) collective-permute-start(bf16[384,128]{1,0:T(8,128)(2,1)} %get-tuple-element.31), channel_id=1, source_target_pairs={{0,80},{8,88},{16,64},{24,72},{32,112},{40,120},{48,96},{56,104},{... | collective-permute-start | bytes 294920 | tf_op jit(solution)/shard_map/ppermute | solution.py:302
  105.1 9.5 %collective-permute-start.7 = (bf16[384,128]{1,0:T(8,128)(2,1)}, bf16[384,128]{1,0:T(8,128)(2,1)}, u32[]{:S(2)}, u32[]{:S(2)}) collective-permute-start(bf16[384,128]{1,0:T(8,128)(2,1)} %get-tuple-element.32), channel_id=1, source_target_pairs={{0,96},{8,104},{16,112},{24,120},{32,0},{40,8},{48,16},{56,24},{64... | collective-permute-start | bytes 294920 | tf_op jit(solution)/shard_map/ppermute | solution.py:302
  107.7 6.8 %collective-permute-start.8 = (bf16[384,128]{1,0:T(8,128)(2,1)}, bf16[384,128]{1,0:T(8,128)(2,1)}, u32[]{:S(2)}, u32[]{:S(2)}) collective-permute-start(bf16[384,128]{1,0:T(8,128)(2,1)} %get-tuple-element.33), channel_id=1, source_target_pairs={{0,112},{8,120},{16,96},{24,104},{32,16},{40,24},{48,0},{56,8},{64... | collective-permute-start | bytes 294920 | tf_op jit(solution)/shard_map/ppermute | solution.py:302
  122.1 32.6 %collective-permute-start.20 = (bf16[512,384]{1,0:T(8,128)(2,1)}, bf16[512,384]{1,0:T(8,128)(2,1)S(1)}, u32[]{:S(2)}, u32[]{:S(2)}) collective-permute-start(bf16[512,384]{1,0:T(8,128)(2,1)} %get-tuple-element.49), channel_id=1, source_target_pairs={{0,3},{1,0},{2,1},{3,2},{4,7},{5,4},{6,5},{7,6},{8,11},{9,8},{10,9... | collective-permute-start | bytes 1179656 | tf_op jit(solution)/shard_map/ppermute | solution.py:311
  135.3 46.6 %collective-permute-start.19 = (bf16[512,384]{1,0:T(8,128)(2,1)}, bf16[512,384]{1,0:T(8,128)(2,1)S(1)}, u32[]{:S(2)}, u32[]{:S(2)}) collective-permute-start(bf16[512,384]{1,0:T(8,128)(2,1)} %get-tuple-element.47), channel_id=1, source_target_pairs={{0,1},{1,2},{2,3},{3,0},{4,5},{5,6},{6,7},{7,4},{8,9},{9,10},{10,1... | collective-permute-start | bytes 1179656 | tf_op jit(solution)/shard_map/ppermute | solution.py:311
  139.9 16.0 %collective-permute-start.17 = (bf16[512,384]{1,0:T(8,128)(2,1)}, bf16[512,384]{1,0:T(8,128)(2,1)}, u32[]{:S(2)}, u32[]{:S(2)}) collective-permute-start(bf16[512,384]{1,0:T(8,128)(2,1)} %get-tuple-element.45), channel_id=1, source_target_pairs={{0,3},{1,0},{2,1},{3,2},{4,7},{5,4},{6,5},{7,6},{8,11},{9,8},{10,9... | collective-permute-start | bytes 1179656 | tf_op jit(solution)/shard_map/ppermute | solution.py:311
  152.0 20.5 %copy-start.11 = (bf16[512,384]{1,0:T(8,128)(2,1)S(1)}, bf16[512,384]{1,0:T(8,128)(2,1)}, u32[]{:S(2)}) copy-start(bf16[512,384]{1,0:T(8,128)(2,1)} %get-tuple-element.39) | copy-start | bytes 1179652
  152.0 29.0 %copy-start.12 = (bf16[512,384]{1,0:T(8,128)(2,1)S(1)}, bf16[512,384]{1,0:T(8,128)(2,1)}, u32[]{:S(2)}) copy-start(bf16[512,384]{1,0:T(8,128)(2,1)} %get-tuple-element.35) | copy-start | bytes 1179652
  152.0 41.1 %collective-permute-start.16 = (bf16[512,384]{1,0:T(8,128)(2,1)}, bf16[512,384]{1,0:T(8,128)(2,1)S(1)}, u32[]{:S(2)}, u32[]{:S(2)}) collective-permute-start(bf16[512,384]{1,0:T(8,128)(2,1)} %get-tuple-element.43), channel_id=1, source_target_pairs={{0,1},{1,2},{2,3},{3,0},{4,5},{5,6},{6,7},{7,4},{8,9},{9,10},{10,1... | collective-permute-start | bytes 1179656 | tf_op jit(solution)/shard_map/ppermute | solution.py:311
  152.1 33.4 %collective-permute-start.14 = (bf16[512,384]{1,0:T(8,128)(2,1)}, bf16[512,384]{1,0:T(8,128)(2,1)S(1)}, u32[]{:S(2)}, u32[]{:S(2)}) collective-permute-start(bf16[512,384]{1,0:T(8,128)(2,1)} %get-tuple-element.41), channel_id=1, source_target_pairs={{0,3},{1,0},{2,1},{3,2},{4,7},{5,4},{6,5},{7,6},{8,11},{9,8},{10,9... | collective-permute-start | bytes 1179656 | tf_op jit(solution)/shard_map/ppermute | solution.py:311
  154.8 17.8 %collective-permute-start.12 = (bf16[512,384]{1,0:T(8,128)(2,1)}, bf16[512,384]{1,0:T(8,128)(2,1)S(1)}, u32[]{:S(2)}, u32[]{:S(2)}) collective-permute-start(bf16[512,384]{1,0:T(8,128)(2,1)} %get-tuple-element.40), channel_id=1, source_target_pairs={{0,1},{1,2},{2,3},{3,0},{4,5},{5,6},{6,7},{7,4},{8,9},{9,10},{10,1... | collective-permute-start | bytes 1179656 | tf_op jit(solution)/shard_map/ppermute | solution.py:311
  154.8 29.8 %copy-start.10 = (bf16[512,384]{1,0:T(8,128)(2,1)S(1)}, bf16[512,384]{1,0:T(8,128)(2,1)}, u32[]{:S(2)}) copy-start(bf16[512,384]{1,0:T(8,128)(2,1)} %get-tuple-element.46) | copy-start | bytes 1179652
  155.9 25.1 %collective-permute-start.9 = (bf16[512,384]{1,0:T(8,128)(2,1)}, bf16[512,384]{1,0:T(8,128)(2,1)S(1)}, u32[]{:S(2)}, u32[]{:S(2)}) collective-permute-start(bf16[512,384]{1,0:T(8,128)(2,1)} %get-tuple-element.36), channel_id=1, source_target_pairs={{0,1},{1,2},{2,3},{3,0},{4,5},{5,6},{6,7},{7,4},{8,9},{9,10},{10,1... | collective-permute-start | bytes 1179656 | tf_op jit(solution)/shard_map/ppermute | solution.py:311
  157.2 35.0 %copy-start.9 = (bf16[512,384]{1,0:T(8,128)(2,1)S(1)}, bf16[512,384]{1,0:T(8,128)(2,1)}, u32[]{:S(2)}) copy-start(bf16[512,384]{1,0:T(8,128)(2,1)} %get-tuple-element.38) | copy-start | bytes 1179652
  172.5 12.0 %collective-permute-start.21 = (bf16[512,384]{1,0:T(8,128)(2,1)S(1)}, bf16[512,384]{1,0:T(8,128)(2,1)S(1)}, u32[]{:S(2)}, u32[]{:S(2)}) collective-permute-start(bf16[512,384]{1,0:T(8,128)(2,1)S(1)} %add_convert_fusion.2), channel_id=1, source_target_pairs={{0,3},{1,0},{2,1},{3,2},{4,7},{5,4},{6,5},{7,6},{8,11},{9,8},{10,9... | collective-permute-start | bytes 1179656 | tf_op jit(solution)/shard_map/ppermute | solution.py:311
  181.0 11.0 %collective-permute-start.13 = (bf16[512,384]{1,0:T(8,128)(2,1)S(1)}, bf16[512,384]{1,0:T(8,128)(2,1)S(1)}, u32[]{:S(2)}, u32[]{:S(2)}) collective-permute-start(bf16[512,384]{1,0:T(8,128)(2,1)S(1)} %add_convert_fusion.6), channel_id=1, source_target_pairs={{0,1},{1,2},{2,3},{3,0},{4,5},{5,6},{6,7},{7,4},{8,9},{9,10},{10,1... | collective-permute-start | bytes 1179656 | tf_op jit(solution)/shard_map/ppermute | solution.py:311
  181.0 13.4 %copy-start.3 = (bf16[384,1024]{0,1:T(8,128)(2,1)S(1)}, bf16[384,1024]{0,1:T(8,128)(2,1)}, u32[]{:S(2)}) copy-start(bf16[384,1024]{0,1:T(8,128)(2,1)} %copy-done.2) | copy-start | bytes 2359300
  181.9 20.2 %collective-permute-start.11 = (bf16[512,384]{1,0:T(8,128)(2,1)}, bf16[512,384]{1,0:T(8,128)(2,1)}, u32[]{:S(2)}, u32[]{:S(2)}) collective-permute-start(bf16[512,384]{1,0:T(8,128)(2,1)} %get-tuple-element.37), channel_id=1, source_target_pairs={{0,3},{1,0},{2,1},{3,2},{4,7},{5,4},{6,5},{7,6},{8,11},{9,8},{10,9... | collective-permute-start | bytes 1179656 | tf_op jit(solution)/shard_map/ppermute | solution.py:311
  184.5 15.9 %collective-permute-start.18 = (bf16[512,384]{1,0:T(8,128)(2,1)S(1)}, bf16[512,384]{1,0:T(8,128)(2,1)}, u32[]{:S(2)}, u32[]{:S(2)}) collective-permute-start(bf16[512,384]{1,0:T(8,128)(2,1)S(1)} %add_convert_fusion.3), channel_id=1, source_target_pairs={{0,3},{1,0},{2,1},{3,2},{4,7},{5,4},{6,5},{7,6},{8,11},{9,8},{10,9... | collective-permute-start | bytes 1179656 | tf_op jit(solution)/shard_map/ppermute | solution.py:311
  185.5 16.5 %collective-permute-start.10 = (bf16[512,384]{1,0:T(8,128)(2,1)}, bf16[512,384]{1,0:T(8,128)(2,1)}, u32[]{:S(2)}, u32[]{:S(2)}) collective-permute-start(bf16[512,384]{1,0:T(8,128)(2,1)} %add_convert_fusion.7), channel_id=1, source_target_pairs={{0,1},{1,2},{2,3},{3,0},{4,5},{5,6},{6,7},{7,4},{8,9},{9,10},{10,1... | collective-permute-start | bytes 1179656 | tf_op jit(solution)/shard_map/ppermute | solution.py:311
  192.0 8.5 %collective-permute-start.22 = (bf16[512,384]{1,0:T(8,128)(2,1)}, bf16[512,384]{1,0:T(8,128)(2,1)}, u32[]{:S(2)}, u32[]{:S(2)}) collective-permute-start(bf16[512,384]{1,0:T(8,128)(2,1)} %add_convert_fusion.1), channel_id=1, source_target_pairs={{0,4},{1,5},{2,6},{3,7},{4,0},{5,1},{6,2},{7,3},{8,12},{9,13},{10,... | collective-permute-start | bytes 1179656 | tf_op jit(solution)/shard_map/ppermute | solution.py:339
  193.2 15.1 %collective-permute-start.15 = (bf16[512,384]{1,0:T(8,128)(2,1)}, bf16[512,384]{1,0:T(8,128)(2,1)}, u32[]{:S(2)}, u32[]{:S(2)}) collective-permute-start(bf16[512,384]{1,0:T(8,128)(2,1)} %add_convert_fusion.5), channel_id=1, source_target_pairs={{0,4},{1,5},{2,6},{3,7},{4,0},{5,1},{6,2},{7,3},{8,12},{9,13},{10,... | collective-permute-start | bytes 1179656 | tf_op jit(solution)/shard_map/ppermute | solution.py:339
  194.7 13.5 %copy-start.13 = (bf16[512,384]{1,0:T(8,128)(2,1)S(1)}, bf16[512,384]{1,0:T(8,128)(2,1)}, u32[]{:S(2)}) copy-start(bf16[512,384]{1,0:T(8,128)(2,1)} %get-tuple-element.34) | copy-start | bytes 1179652
  (12 other events, 78.1 us)
where the time goes:
time: 214 us; the launch traced here: 211 us
  Pallas kernels  70.5 us (33%)
  waiting for transfers between devices  52.2 us (24%)
  starting transfers between devices  43 us (20%)
  other arithmetic  16.8 us (8%)
  matrix products  14.3 us (7%)
  local copies, waits for them, and re-layouts  13 us (6%)
    pallas_call x1, Pallas kernels, attention(): pl.pallas_call(attention_kernel, grid=(CHIPS,), out_shape=[jax.ShapeDtype...  34.1 us
    ppermute x12, waiting for transfers between devices, sent(): return lax.ppermute(block, 'tp', ring_route(step))  33.3 us
    pallas_call x4, Pallas kernels, project(): pl.pallas_call(kernel, grid_spec=pltpu.PrefetchScalarGridSpec(num_scalar_...  28.1 us
    ppermute x12, starting transfers between devices, sent(): return lax.ppermute(block, 'tp', ring_route(step))  13.3 us
    all_to_all x1, waiting for transfers between devices, local_step(): lax.all_to_all(pieces, 'ctx', 0, 0, axis_index_groups=CORE_GROUPS, tiled=...  12.7 us
    ppermute x7, starting transfers between devices, local_step(): lax.ppermute(outs[step], 'ctx', chip_route(step))  12.5 us
    unnamed x42, local copies, waits for them, and re-layouts  7.86 us
    all_to_all x1, starting transfers between devices, local_step(): lax.all_to_all(pieces, 'ctx', 0, 0, axis_index_groups=CORE_GROUPS, tiled=...  7.6 us
  transfers between devices with their start and end apart: 24, of which 6 were waited for; matrix products, arithmetic and copies ran while one was open for 19% of the time, Pallas kernels for 27%

commit v1 on v0

v1 whole, which is shorter than its diff:
```python
import jax
import jax.numpy as jnp
from jax import lax
from jax.experimental import pallas as pl
from jax.experimental.pallas import tpu as pltpu
from jax.sharding import PartitionSpec as P

HEAD_DIM = 128
CHIPS_Y = 4
CHIPS = 8
RING = 4
NEGATIVE = -1e30
EXP_SCALE = HEAD_DIM ** (-0.5) * 1.4426950408889634


VMEM = pltpu.VMEM
SMEM_SPEC = pl.BlockSpec(memory_space=pltpu.SMEM)
VMEM_SPEC = pl.BlockSpec(memory_space=pltpu.VMEM)


def shifted(block, axis, distance):
    devices = range(lax.axis_size(axis))
    route = [(i - distance, i) for i in devices if i - distance in devices]
    return lax.ppermute(block, axis, route)


LANES = 128


def hyena_kernel(query, key, value, before, taps, gain, out, product):
    length = before.shape[0]
    rows = query.shape[0]
    groups = taps.shape[0]
    product[:length, :] = before[...]
    product[length:, :] = (
        key[...].astype(jnp.float32) * value[...].astype(jnp.float32)
    ).astype(jnp.bfloat16)
    tables = []
    for group in range(groups):
        row = jnp.broadcast_to(taps[group : group + 1, :], (length, 2 * length))
        tables.append(pltpu.roll(row, 0, 1, stride=1, stride_axis=0).astype(jnp.bfloat16))
    table = jnp.concatenate(tables, axis=0)
    lane_group = lax.broadcasted_iota(jnp.int32, (length, LANES), 1) // (LANES // groups)
    for first in range(0, rows, length):
        spread = jnp.dot(
            table, product[first : first + 2 * length, :], preferred_element_type=jnp.float32
        )
        convolved = spread[:length]
        for group in range(1, groups):
            convolved = jnp.where(
                lane_group == group, spread[group * length : (group + 1) * length], convolved
            )
        here = slice(first, first + length)
        current = product[first + length : first + 2 * length, :].astype(jnp.float32)
        out[here, :] = (
            query[here, :].astype(jnp.float32) * (convolved + gain[...] * current)
        ).astype(jnp.bfloat16)


def hyena(hyena_query, hyena_key, hyena_value, before, conv_filter, skip_gain):
    rows, width = hyena_query.shape
    groups, length = conv_filter.shape
    share = groups * LANES // width
    taps = jnp.concatenate(
        [
            jnp.zeros((groups, 1), jnp.float32),
            conv_filter[:, ::-1].astype(jnp.float32),
            jnp.zeros((groups, length - 1), jnp.float32),
        ],
        axis=1,
    )

    def columns(height):
        return pl.BlockSpec((height, LANES), lambda i: (0, i))

    return pl.pallas_call(
        hyena_kernel,
        grid=(width // LANES,),
        out_shape=jax.ShapeDtypeStruct((rows, width), jnp.bfloat16),
        in_specs=[
            columns(rows),
            columns(rows),
            columns(rows),
            columns(length),
            pl.BlockSpec((share, 2 * length), lambda i: (i, 0)),
            columns(1),
        ],
        out_specs=columns(rows),
        scratch_shapes=[VMEM((rows + length, LANES), jnp.bfloat16)],
        cost_estimate=pl.CostEstimate(
            flops=3_000_000_000, bytes_accessed=3_000_000, transcendentals=0
        ),
        name="hyena",
    )(hyena_query, hyena_key, hyena_value, before, taps, skip_gain[None, :])


def chip_route(step):
    route = []
    for source in range(2 * CHIPS):
        y, x, core = source // 4, source // 2 % 2, source % 2
        target = ((y + step // 2) % CHIPS_Y * 2 + (x + step) % 2) * 2 + core
        route.append((source, target))
    return route


CORE_GROUPS = [list(range(core, 2 * CHIPS, 2)) for core in range(2)]
CORE_ROUTE = [(i, i ^ 1) for i in range(2 * CHIPS)]


def ring_route(step):
    return [(i, i // RING * RING + (i + step) % RING) for i in range(2 * RING)]


PAIR_ROUTE = [(i, (i + RING) % (2 * RING)) for i in range(2 * RING)]


def ahead(y, x, step):
    return ((y + step // 2) & 3) * 2 + ((x + step) & 1)


def behind(y, x, step):
    return ((y - step // 2) & 3) * 2 + ((x - step) & 1)


def split_kernel(q_ref, k_ref, v_ref, out_ref):
    rows = q_ref.shape[0]
    for head in range(out_ref.shape[0]):
        columns = slice(head * HEAD_DIM, (head + 1) * HEAD_DIM)
        out_ref[head, :rows, :] = k_ref[:, columns]
        out_ref[head, rows : 2 * rows, :] = v_ref[:, columns]
        out_ref[head, 2 * rows :, :] = q_ref[:, columns]


def split_heads(query_rows, key_rows, value_rows):
    rows = query_rows.shape[0]
    at_once = 2
    spec = pl.BlockSpec((rows, at_once * HEAD_DIM), lambda step: (0, step))
    return pl.pallas_call(
        split_kernel,
        grid=(CHIPS // at_once,),
        out_shape=jax.ShapeDtypeStruct((CHIPS, 3 * rows, HEAD_DIM), jnp.bfloat16),
        in_specs=[spec] * 3,
        out_specs=pl.BlockSpec((at_once, 3 * rows, HEAD_DIM), lambda step: (step, 0, 0)),
        name="split_heads",
    )(query_rows, key_rows, value_rows)


def attention_kernel(place, own, other, *refs):
    outs = refs[:CHIPS]
    keys, values, top, total, even, odd = refs[CHIPS:]
    y, x, core = place[0], place[1], place[2]
    step = pl.program_id(0)
    rows = top.shape[0]

    @pl.when(step == 0)
    def _():
        ones = jnp.ones((2 * rows, HEAD_DIM), jnp.bfloat16)
        for i in range(CHIPS):
            keys[i, :, :rows] = own[i, :rows, :].T
            keys[i, :, rows:] = other[i, :rows, :].T
            values[i, :rows, :HEAD_DIM] = own[i, rows : 2 * rows, :]
            values[i, rows:, :HEAD_DIM] = other[i, rows:, :]
            values[i, :, HEAD_DIM:] = ones

    top[...] = jnp.full_like(top, NEGATIVE)
    total[...] = jnp.zeros_like(total)
    chip = ahead(y, x, step)

    def score(held, block):
        held[...] = jnp.dot(
            own[chip, 2 * rows :, :], keys[block], preferred_element_type=jnp.float32
        )

    def weigh(held, block, masked):
        scores = held[...]
        if masked:
            row = lax.broadcasted_iota(jnp.int32, scores.shape, 0)
            column = lax.broadcasted_iota(jnp.int32, scores.shape, 1)
            limit = rows + core * rows
            allowed = (column <= row) | ((column >= rows) & (column < limit))
            scores = jnp.where(allowed, scores, NEGATIVE)
        old = top[...]
        new = jnp.maximum(old, jnp.max(scores, axis=1, keepdims=True))
        keep = jnp.exp2((old - new) * EXP_SCALE)
        spread = jnp.concatenate([new] * (2 * rows // HEAD_DIM), axis=1)
        weights = jnp.exp2((scores - spread) * EXP_SCALE).astype(jnp.bfloat16)
        total[...] = total[...] * jnp.concatenate([keep, keep], axis=1) + jnp.dot(
            weights, values[block], preferred_element_type=jnp.float32
        )
        top[...] = new

    score(even, 0)

    def two_blocks(pair, unused):
        score(odd, 2 * pair + 1)
        weigh(even, 2 * pair, False)
        score(even, 2 * pair + 2)
        weigh(odd, 2 * pair + 1, False)
        return unused

    lax.fori_loop(0, chip >> 1, two_blocks, 0)

    @pl.when((chip & 1) == 0)
    def _():
        weigh(even, chip, True)

    @pl.when((chip & 1) == 1)
    def _():
        score(odd, chip)
        weigh(even, chip - 1, False)
        weigh(odd, chip, True)

    result = (total[:, :HEAD_DIM] / total[:, HEAD_DIM:]).astype(jnp.bfloat16)
    for i in range(CHIPS):

        @pl.when(step == i)
        def _(i=i):
            outs[i][...] = result


def attention(place, own, other):
    rows = own.shape[1] // 3
    return pl.pallas_call(
        attention_kernel,
        grid=(CHIPS,),
        out_shape=[jax.ShapeDtypeStruct((rows, HEAD_DIM), jnp.bfloat16)] * CHIPS,
        in_specs=[SMEM_SPEC, VMEM_SPEC, VMEM_SPEC],
        out_specs=[VMEM_SPEC] * CHIPS,
        scratch_shapes=[
            VMEM((CHIPS, HEAD_DIM, 2 * rows), jnp.bfloat16),
            VMEM((CHIPS, 2 * rows, 2 * HEAD_DIM), jnp.bfloat16),
            VMEM((rows, HEAD_DIM), jnp.float32),
            VMEM((rows, 2 * HEAD_DIM), jnp.float32),
            VMEM((rows, 2 * rows), jnp.float32),
            VMEM((rows, 2 * rows), jnp.float32),
        ],
        cost_estimate=pl.CostEstimate(
            flops=12_000_000_000, bytes_accessed=6_000_000, transcendentals=10_000_000
        ),
        name="attention",
    )(place, own, other)


def join_kernel(place, *refs):
    y, x = place[0], place[1]
    joined = refs[CHIPS]
    for step in range(CHIPS):
        column = pl.multiple_of(behind(y, x, step) * HEAD_DIM, HEAD_DIM)
        joined[:, pl.ds(column, HEAD_DIM)] = refs[step][...]


def join_heads(place, pieces):
    rows = pieces[0].shape[0]
    return pl.pallas_call(
        join_kernel,
        out_shape=jax.ShapeDtypeStruct((rows, CHIPS * HEAD_DIM), jnp.bfloat16),
        in_specs=[SMEM_SPEC] + [VMEM_SPEC] * CHIPS,
        out_specs=VMEM_SPEC,
        name="join_heads",
    )(place, *pieces)


def project(place, wanted, out_weight, attended):
    rows, features = attended.shape
    share = out_weight.shape[0] // (2 * RING)
    count = len(wanted)

    def weight_block(step, place):
        index = jnp.int32(0)
        for i, (x_off, z_off) in enumerate(wanted):
            block = ((place[3] + x_off) & 1) * RING + ((place[4] + z_off) & 3)
            index = jnp.where(step == i, block, index)
        return (index, 0)

    def kernel(place, weight_ref, attended_ref, *outs):
        piece = lax.dot_general(
            attended_ref[...],
            weight_ref[...],
            (((1,), (1,)), ((), ())),
            preferred_element_type=jnp.float32,
        )
        piece = piece.astype(jnp.bfloat16).T
        for i in range(count):

            @pl.when(pl.program_id(0) == i)
            def _(i=i):
                outs[2 * i][...] = piece[: share // 2]
                outs[2 * i + 1][...] = piece[share // 2 :]

    half = pl.BlockSpec((share // 2, rows), lambda step, place: (0, 0))
    return pl.pallas_call(
        kernel,
        grid_spec=pltpu.PrefetchScalarGridSpec(
            num_scalar_prefetch=1,
            grid=(count,),
            in_specs=[
                pl.BlockSpec((share, features), weight_block),
                pl.BlockSpec((rows, features), lambda step, place: (0, 0)),
            ],
            out_specs=[half] * (2 * count),
        ),
        out_shape=[jax.ShapeDtypeStruct((share // 2, rows), jnp.bfloat16)] * (2 * count),
        cost_estimate=pl.CostEstimate(
            flops=2 * share * rows * features * count,
            bytes_accessed=share * features * 2 * count,
            transcendentals=0,
        ),
        name="project",
    )(place, out_weight, attended)


def added(*pieces):
    return sum(piece.astype(jnp.float32) for piece in pieces)


def local_step(
    hyena_query,
    hyena_key,
    hyena_value,
    conv_filter,
    skip_gain,
    query_rows,
    key_rows,
    value_rows,
    out_weight,
):
    ctx = lax.axis_index("ctx")
    tp = lax.axis_index("tp")
    place = jnp.stack([ctx // 4, ctx // 2 % 2, ctx % 2, tp // RING, tp % RING]).astype(jnp.int32)

    rows = query_rows.shape[0]
    length = conv_filter.shape[1]
    tail = (
        hyena_key[rows - length :].astype(jnp.float32)
        * hyena_value[rows - length :].astype(jnp.float32)
    ).astype(jnp.bfloat16)
    before = shifted(tail, "ctx", 1)
    pieces = split_heads(query_rows, key_rows, value_rows)
    own = lax.all_to_all(pieces, "ctx", 0, 0, axis_index_groups=CORE_GROUPS, tiled=True)
    hyena_out = hyena(
        hyena_query, hyena_key, hyena_value, before, conv_filter, skip_gain
    )
    other = lax.ppermute(own[:, : 2 * rows], "ctx", CORE_ROUTE)
    outs = attention(place, own, other)
    back = [outs[0]] + [
        lax.ppermute(outs[step], "ctx", chip_route(step)) for step in range(1, CHIPS)
    ]
    attended = join_heads(place, back)

    kept = []
    handed = None
    for x_off in (1, 0):

        def sent(block, step):
            return lax.ppermute(block, "tp", ring_route(step))

        far = project(place, [(x_off, 2)], out_weight, attended)
        near = project(place, [(x_off, 1), (x_off, 3), (x_off, 0)], out_weight, attended)
        from_below = sent(far[0], 1)
        from_above = sent(far[1], -1)
        below_1 = sent(near[1], 1)
        above_0 = sent(near[2], -1)
        up = added(near[0], from_below).astype(jnp.bfloat16)
        down = added(near[3], from_above).astype(jnp.bfloat16)
        below_0 = sent(up, 1)
        above_1 = sent(down, -1)
        first = added(near[4], below_0, above_0)
        second = added(near[5], below_1, above_1)
        if x_off == 1:
            handed = [
                lax.ppermute(part.astype(jnp.bfloat16), "tp", PAIR_ROUTE)
                for part in (first, second)
            ]
        else:
            kept = [first, second]
    attention_out = jnp.concatenate(
        [(kept[i] + handed[i].astype(jnp.float32)).astype(jnp.bfloat16) for i in range(2)], axis=0
    )
    return (hyena_out, attention_out)


def solution(mesh):
    in_specs = (
        P("ctx", "tp"),
        P("ctx", "tp"),
        P("ctx", "tp"),
        P("tp", None),
        P("tp"),
        P("ctx", "tp"),
        P("ctx", "tp"),
        P("ctx", "tp"),
        P(None, "tp"),
    )
    out_specs = (P("ctx", "tp"), P("tp", "ctx"))
    return jax.shard_map(local_step, mesh=mesh, in_specs=in_specs, out_specs=out_specs, check_vma=False)
```

time: 214 us -> 167 us (0.78)
  blocking collectives: 0 us -> 37.9 us
  waiting for transfers between devices: 52.2 us -> 21.2 us
  matrix products: 14.3 us -> 0 us
  other arithmetic: 16.8 us -> 5.86 us
  Pallas kernels: 70.5 us -> 60.7 us
  local copies, waits for them, and re-layouts: 13 us -> 3.33 us
  starting transfers between devices: 43 us -> 34.5 us
    all_to_all x0 -> x1, blocking collectives: none -> 37.9 us  [local_step(): lax.all_to_all(pieces, 'ctx', 0, 0, axis_index_groups=CORE_GROUPS, tiled=...]
    ppermute x12, waiting for transfers between devices: 33.3 us -> 18.4 us  [sent(): return lax.ppermute(block, 'tp', ring_route(step))]
    dot_general x4 -> x0, matrix products: 14.3 us -> none  [the longest x1 4.72 us: toeplitz_pair(): jnp.einsum('gj,jts->gts', filters, outer_table, preferred_element_type=jn...]
    all_to_all x1 -> x0, waiting for transfers between devices: 12.7 us -> none  [local_step(): lax.all_to_all(pieces, 'ctx', 0, 0, axis_index_groups=CORE_GROUPS, tiled=...]
    pallas_call x1, Pallas kernels: 34.1 us -> 21.6 us  [attention(): pl.pallas_call(attention_kernel, grid=(CHIPS,), out_shape=[jax.ShapeDtype...]
    all_to_all x1 -> x0, starting transfers between devices: 7.6 us -> none  [local_step(): lax.all_to_all(pieces, 'ctx', 0, 0, axis_index_groups=CORE_GROUPS, tiled=...]
    unnamed x42 -> x40, local copies, waits for them, and re-layouts: 7.86 us -> 1.24 us
    pallas_call x1 -> x2, Pallas kernels: 5.98 us -> 12.3 us  [the longest x1 8.23 us: hyena(): pl.pallas_call(hyena_kernel, grid=(width // LANES,), out_shape=jax.ShapeD...]
  transfers between devices with their start and end apart: 24 -> 23, of which waited for: 6 -> 5; matrix products, arithmetic and copies ran while one was open for 19% -> 3% of each run, Pallas kernels for 27% -> 21%
where the time goes in v1:
time: 167 us; the launch traced here: 164 us
  Pallas kernels  60.7 us (36%)
  blocking collectives  37.9 us (23%)
  starting transfers between devices  34.5 us (21%)
  waiting for transfers between devices  21.2 us (13%)
  other arithmetic  5.86 us (4%)
  local copies, waits for them, and re-layouts  3.33 us (2%)
    all_to_all x1, blocking collectives, local_step(): lax.all_to_all(pieces, 'ctx', 0, 0, axis_index_groups=CORE_GROUPS, tiled=...  37.9 us
    pallas_call x4, Pallas kernels, project(): pl.pallas_call(kernel, grid_spec=pltpu.PrefetchScalarGridSpec(num_scalar_...  24.4 us
    pallas_call x1, Pallas kernels, attention(): pl.pallas_call(attention_kernel, grid=(CHIPS,), out_shape=[jax.ShapeDtype...  21.6 us
    ppermute x12, waiting for transfers between devices, sent(): return lax.ppermute(block, 'tp', ring_route(step))  18.4 us
    ppermute x12, starting transfers between devices, sent(): return lax.ppermute(block, 'tp', ring_route(step))  15.1 us
    ppermute x7, starting transfers between devices, local_step(): lax.ppermute(outs[step], 'ctx', chip_route(step))  12.3 us
    pallas_call x1, Pallas kernels, hyena(): pl.pallas_call(hyena_kernel, grid=(width // LANES,), out_shape=jax.ShapeD...  8.23 us
    ppermute x1, starting transfers between devices, shifted(): return lax.ppermute(block, axis, route)  4.69 us
  transfers between devices with their start and end apart: 23, of which 5 were waited for; matrix products, arithmetic and copies ran while one was open for 3% of the time, Pallas kernels for 21%

profile of v1, /device:TPU:1, one launch (start us, length us, event | category | flops | bytes accessed | tf_op | source)
XLA Modules:
  0.0 164.4 jit_solution(10683599207867384100)
XLA Ops:
  0.6 4.1 %split_heads.1 = bf16[8,1152,128]{2,1,0:T(8,128)(2,1)} custom-call(bf16[384,1024]{1,0:T(8,128)(2,1)} %q_ref.1, bf16[384,1024]{1,0:T(8,128)(2,1)} %k_ref.1, bf16[384,1024]{1,0:T(8,128)(2,1)} %v_ref.1), custom_call_target="tpu_custom_call" | custom-call | tf_op jit(solution)/shard_map/split_heads/pallas_call | solution.py:138
  4.7 37.9 %all_to_all.5.own = bf16[8,1152,128]{2,1,0:T(8,128)(2,1)S(1)} all-to-all(bf16[8,1152,128]{2,1,0:T(8,128)(2,1)} %split_heads.1), channel_id=1, replica_groups={{0,16,32,48,64,80,96,112},{8,24,40,56,72,88,104,120},{1,17,33,49,65,81,..., dimensions={0} | all-to-all | bytes 4718592 | tf_op jit(solution)/shard_map/all_to_all | solution.py:339
  42.6 1.4 slice.12
  44.4 1.8 %collective-permute-start.1 = (bf16[8,768,128]{2,1,0:T(8,128)(2,1)}, bf16[8,768,128]{2,1,0:T(8,128)(2,1)}, u32[]{:S(2)}, u32[]{:S(2)}) collective-permute-start(bf16[8,768,128]{2,1,0:T(8,128)(2,1)} %slice.12), channel_id=1, source_target_pairs={{0,8},{8,0},{16,24},{24,16},{32,40},{40,32},{48,56},{56,48},{64,72... | collective-permute-start | bytes 4718600 | tf_op jit(solution)/shard_map/ppermute | solution.py:343
  46.8 2.8 %collective-permute-done.1.other = bf16[8,768,128]{2,1,0:T(8,128)(2,1)} collective-permute-done((bf16[8,768,128]{2,1,0:T(8,128)(2,1)}, bf16[8,768,128]{2,1,0:T(8,128)(2,1)}, u32[]{:S(2)}, u32[]{:S(2)}) %collective-permute-start.1) | collective-permute-done | bytes 1572896 | tf_op jit(solution)/shard_map/ppermute | solution.py:343
  49.6 21.6 %attention.1 = (bf16[384,128]{1,0:T(8,128)(2,1)}, bf16[384,128]{1,0:T(8,128)(2,1)}, bf16[384,128]{1,0:T(8,128)(2,1)}, bf16[384,128]{1,0:T(8,128)(2,1)}, bf16[384...) custom-call(s32[5]{0:T(128)} %stack.23.place, ...), custom_call_target="tpu_custom_call" | custom-call | flops 12000000000 | bytes 6000000 | tf_op jit(solution)/shard_map/attention/pallas_call | solution.py:223
  72.2 1.1 multiply_convert_fusion
  73.4 2.4 %collective-permute-start.4 = (bf16[384,128]{1,0:T(8,128)(2,1)}, bf16[384,128]{1,0:T(8,128)(2,1)S(1)}, u32[]{:S(2)}, u32[]{:S(2)}) collective-permute-start(bf16[384,128]{1,0:T(8,128)(2,1)} %get-tuple-element.29), channel_id=1, source_target_pairs={{0,48},{8,56},{16,32},{24,40},{32,80},{40,88},{48,64},{56,72},{64,... | collective-permute-start | bytes 294920 | tf_op jit(solution)/shard_map/ppermute | solution.py:346
  75.8 3.4 %collective-permute-start.5 = (bf16[384,128]{1,0:T(8,128)(2,1)}, bf16[384,128]{1,0:T(8,128)(2,1)S(1)}, u32[]{:S(2)}, u32[]{:S(2)}) collective-permute-start(bf16[384,128]{1,0:T(8,128)(2,1)} %get-tuple-element.30), channel_id=1, source_target_pairs={{0,64},{8,72},{16,80},{24,88},{32,96},{40,104},{48,112},{56,120},{... | collective-permute-start | bytes 294920 | tf_op jit(solution)/shard_map/ppermute | solution.py:346
  79.5 2.1 %collective-permute-start.7 = (bf16[384,128]{1,0:T(8,128)(2,1)}, bf16[384,128]{1,0:T(8,128)(2,1)S(1)}, u32[]{:S(2)}, u32[]{:S(2)}) collective-permute-start(bf16[384,128]{1,0:T(8,128)(2,1)} %get-tuple-element.32), channel_id=1, source_target_pairs={{0,96},{8,104},{16,112},{24,120},{32,0},{40,8},{48,16},{56,24},{64... | collective-permute-start | bytes 294920 | tf_op jit(solution)/shard_map/ppermute | solution.py:346
  81.6 3.2 %collective-permute-start.8 = (bf16[384,128]{1,0:T(8,128)(2,1)}, bf16[384,128]{1,0:T(8,128)(2,1)S(1)}, u32[]{:S(2)}, u32[]{:S(2)}) collective-permute-start(bf16[384,128]{1,0:T(8,128)(2,1)} %get-tuple-element.33), channel_id=1, source_target_pairs={{0,112},{8,120},{16,96},{24,104},{32,16},{40,24},{48,0},{56,8},{64... | collective-permute-start | bytes 294920 | tf_op jit(solution)/shard_map/ppermute | solution.py:346
  85.5 4.7 %collective-permute-start = (bf16[128,1024]{1,0:T(8,128)(2,1)S(1)}, bf16[128,1024]{1,0:T(8,128)(2,1)}, u32[]{:S(2)}, u32[]{:S(2)}) collective-permute-start(bf16[128,1024]{1,0:T(8,128)(2,1)S(1)} %multiply_convert_fusion), channel_id=1, source_target_pairs={{0,8},{8,16},{16,24},{24,32},{32,40},{40,48},{48,56},{56,64},{64,7... | collective-permute-start | bytes 786440 | tf_op jit(solution)/shard_map/ppermute | solution.py:24
  91.0 2.3 %join_heads.1.attended_ref = bf16[384,1024]{1,0:T(8,128)(2,1)} custom-call(s32[5]{0:T(128)} %stack.23.place, bf16[384,128]{1,0:T(8,128)(2,1)} %get-tuple-element.26.refs_0_, bf16[384,128]{1,0:T(8,128)(2,1)} %copy-done.9, bf16[384,128]{1,0:T(8,128)(2,1)} %copy-done.10, bf16[384,128]{1,0:T(8,128)(2,1)} %copy-done.11, bf16[384,128]{1,0:T(8,128)(2,1)} %copy-done.12, ...), custom_call_target="tpu_custom_call" | custom-call | tf_op jit(solution)/shard_map/join_heads/pallas_call | solution.py:254
  93.4 4.3 %project.7 = (bf16[512,384]{1,0:T(8,128)(2,1)}, bf16[512,384]{1,0:T(8,128)(2,1)}) custom-call(s32[5]{0:T(128)} %stack.23.place, bf16[8192,1024]{1,0:T(8,128)(2,1)} %weight_ref.7, bf16[384,1024]{1,0:T(8,128)(2,1)} %join_heads.1.attended_ref), custom_call_target="tpu_custom_call" | custom-call | flops 805306368 | bytes 2097152 | tf_op jit(solution)/shard_map/project/pallas_call | solution.py:291
  97.7 4.3 %project.5 = (bf16[512,384]{1,0:T(8,128)(2,1)}, bf16[512,384]{1,0:T(8,128)(2,1)}) custom-call(s32[5]{0:T(128)} %stack.23.place, bf16[8192,1024]{1,0:T(8,128)(2,1)} %weight_ref.7, bf16[384,1024]{1,0:T(8,128)(2,1)} %join_heads.1.attended_ref), custom_call_target="tpu_custom_call" | custom-call | flops 805306368 | bytes 2097152 | tf_op jit(solution)/shard_map/project/pallas_call | solution.py:291
  102.0 1.7 %collective-permute-start.12 = (bf16[512,384]{1,0:T(8,128)(2,1)}, bf16[512,384]{1,0:T(8,128)(2,1)S(1)}, u32[]{:S(2)}, u32[]{:S(2)}) collective-permute-start(bf16[512,384]{1,0:T(8,128)(2,1)} %get-tuple-element.40), channel_id=1, source_target_pairs={{0,1},{1,2},{2,3},{3,0},{4,5},{5,6},{6,7},{7,4},{8,9},{9,10},{10,1... | collective-permute-start | bytes 1179656 | tf_op jit(solution)/shard_map/ppermute | solution.py:355
  103.7 2.1 %collective-permute-start.20 = (bf16[512,384]{1,0:T(8,128)(2,1)}, bf16[512,384]{1,0:T(8,128)(2,1)S(1)}, u32[]{:S(2)}, u32[]{:S(2)}) collective-permute-start(bf16[512,384]{1,0:T(8,128)(2,1)} %get-tuple-element.49), channel_id=1, source_target_pairs={{0,3},{1,0},{2,1},{3,2},{4,7},{5,4},{6,5},{7,6},{8,11},{9,8},{10,9... | collective-permute-start | bytes 1179656 | tf_op jit(solution)/shard_map/ppermute | solution.py:355
  105.8 2.7 %collective-permute-start.17 = (bf16[512,384]{1,0:T(8,128)(2,1)}, bf16[512,384]{1,0:T(8,128)(2,1)S(1)}, u32[]{:S(2)}, u32[]{:S(2)}) collective-permute-start(bf16[512,384]{1,0:T(8,128)(2,1)} %get-tuple-element.45), channel_id=1, source_target_pairs={{0,3},{1,0},{2,1},{3,2},{4,7},{5,4},{6,5},{7,6},{8,11},{9,8},{10,9... | collective-permute-start | bytes 1179656 | tf_op jit(solution)/shard_map/ppermute | solution.py:355
  108.5 7.8 %project.6 = (bf16[512,384]{1,0:T(8,128)(2,1)}, bf16[512,384]{1,0:T(8,128)(2,1)}, bf16[512,384]{1,0:T(8,128)(2,1)}, bf16[512,384]{1,0:T(8,128)(2,1)}, bf16[512,3...) custom-call(s32[5]{0:T(128)} %stack.23.place, bf16[8192,1024]{1,0:T(8,128)(2,1)} %weight_ref.7, ...), custom_call_target="tpu_custom_call" | custom-call | flops 2415919104 | bytes 6291456 | tf_op jit(solution)/shard_map/project/pallas_call | solution.py:291
  116.3 7.9 %project.4 = (bf16[512,384]{1,0:T(8,128)(2,1)}, bf16[512,384]{1,0:T(8,128)(2,1)}, bf16[512,384]{1,0:T(8,128)(2,1)}, bf16[512,384]{1,0:T(8,128)(2,1)}, bf16[512,3...) custom-call(s32[5]{0:T(128)} %stack.23.place, bf16[8192,1024]{1,0:T(8,128)(2,1)} %weight_ref.7, ...), custom_call_target="tpu_custom_call" | custom-call | flops 2415919104 | bytes 6291456 | tf_op jit(solution)/shard_map/project/pallas_call | solution.py:291
  124.7 1.3 collective-permute-start.19
  126.3 2.7 %collective-permute-start.21 = (bf16[512,384]{1,0:T(8,128)(2,1)S(1)}, bf16[512,384]{1,0:T(8,128)(2,1)S(1)}, u32[]{:S(2)}, u32[]{:S(2)}) collective-permute-start(bf16[512,384]{1,0:T(8,128)(2,1)S(1)} %add_convert_fusion.2), channel_id=1, source_target_pairs={{0,3},{1,0},{2,1},{3,2},{4,7},{5,4},{6,5},{7,6},{8,11},{9,8},{10,9... | collective-permute-start | bytes 1179656 | tf_op jit(solution)/shard_map/ppermute | solution.py:355
  129.2 4.5 %collective-permute-done.14 = bf16[512,384]{1,0:T(8,128)(2,1)S(1)} collective-permute-done((bf16[512,384]{1,0:T(8,128)(2,1)S(1)}, bf16[512,384]{1,0:T(8,128)(2,1)S(1)}, u32[]{:S(2)}, u32[]{:S(2)}) %collective-permute-start.14) | collective-permute-done | bytes 393248 | tf_op jit(solution)/shard_map/ppermute | solution.py:355
  133.7 1.2 collective-permute-start.11
  134.9 8.3 %collective-permute-done.13 = bf16[512,384]{1,0:T(8,128)(2,1)S(1)} collective-permute-done((bf16[512,384]{1,0:T(8,128)(2,1)S(1)}, bf16[512,384]{1,0:T(8,128)(2,1)S(1)}, u32[]{:S(2)}, u32[]{:S(2)}) %collective-permute-start.13) | collective-permute-done | bytes 393248 | tf_op jit(solution)/shard_map/ppermute | solution.py:355
  144.5 2.5 %collective-permute-start.18 = (bf16[512,384]{1,0:T(8,128)(2,1)S(1)}, bf16[512,384]{1,0:T(8,128)(2,1)S(1)}, u32[]{:S(2)}, u32[]{:S(2)}) collective-permute-start(bf16[512,384]{1,0:T(8,128)(2,1)S(1)} %add_convert_fusion.3), channel_id=1, source_target_pairs={{0,3},{1,0},{2,1},{3,2},{4,7},{5,4},{6,5},{7,6},{8,11},{9,8},{10,9... | collective-permute-start | bytes 1179656 | tf_op jit(solution)/shard_map/ppermute | solution.py:355
  146.9 3.7 %collective-permute-done.11 = bf16[512,384]{1,0:T(8,128)(2,1)S(1)} collective-permute-done((bf16[512,384]{1,0:T(8,128)(2,1)S(1)}, bf16[512,384]{1,0:T(8,128)(2,1)S(1)}, u32[]{:S(2)}, u32[]{:S(2)}) %collective-permute-start.11) | collective-permute-done | bytes 393248 | tf_op jit(solution)/shard_map/ppermute | solution.py:355
  151.0 8.2 %hyena.1 = bf16[384,1024]{1,0:T(8,128)(2,1)} custom-call(bf16[384,1024]{1,0:T(8,128)(2,1)} %query.1, bf16[384,1024]{1,0:T(8,128)(2,1)} %key.1, bf16[384,1024]{1,0:T(8,128)(2,1)} %value.1, bf16[128,1024]{1,0:T(8,128)(2,1)} %collective-permute-done.before, f32[64,256]{1,0:T(8,128)} %maximum_maximum_fusion.taps, f32[1,1024]{1,0:T(1,128)} %bitcast.7), custom_call_target="tpu_custom_call" | custom-call | flops 3000000000 | bytes 3000000 | tf_op jit(solution)/shard_map/hyena/pallas_call | solution.py:76
  159.2 1.8 %collective-permute-done.10 = bf16[512,384]{1,0:T(8,128)(2,1)S(1)} collective-permute-done((bf16[512,384]{1,0:T(8,128)(2,1)S(1)}, bf16[512,384]{1,0:T(8,128)(2,1)S(1)}, u32[]{:S(2)}, u32[]{:S(2)}) %collective-permute-start.10) | collective-permute-done | bytes 393248 | tf_op jit(solution)/shard_map/ppermute | solution.py:355
  161.0 1.2 add_convert_fusion.4
  162.3 1.2 add_convert_fusion
  163.5 1.0 pad_maximum_fusion
  (81 shorter events, 6.3 us)
Async XLA Ops:
  44.4 5.2 %collective-permute-start.1 = (bf16[8,768,128]{2,1,0:T(8,128)(2,1)}, bf16[8,768,128]{2,1,0:T(8,128)(2,1)}, u32[]{:S(2)}, u32[]{:S(2)}) collective-permute-start(bf16[8,768,128]{2,1,0:T(8,128)(2,1)} %slice.12), channel_id=1, source_target_pairs={{0,8},{8,0},{16,24},{24,16},{32,40},{40,32},{48,56},{56,48},{64,72... | collective-permute-start | bytes 4718600 | tf_op jit(solution)/shard_map/ppermute | solution.py:343
  46.8 26.5 %copy-start.16 = (bf16[64,128]{1,0:T(8,128)(2,1)S(1)}, bf16[64,128]{1,0:T(8,128)(2,1)}, u32[]{:S(2)}) copy-start(bf16[64,128]{1,0:T(8,128)(2,1)} %param.12) | copy-start | bytes 49156
  71.2 8.2 %collective-permute-start.2 = (bf16[384,128]{1,0:T(8,128)(2,1)}, bf16[384,128]{1,0:T(8,128)(2,1)S(1)}, u32[]{:S(2)}, u32[]{:S(2)}) collective-permute-start(bf16[384,128]{1,0:T(8,128)(2,1)} %get-tuple-element.27), channel_id=1, source_target_pairs={{0,16},{8,24},{16,0},{24,8},{32,48},{40,56},{48,32},{56,40},{64,80... | collective-permute-start | bytes 294920 | tf_op jit(solution)/shard_map/ppermute | solution.py:346
  71.8 9.7 %collective-permute-start.3 = (bf16[384,128]{1,0:T(8,128)(2,1)}, bf16[384,128]{1,0:T(8,128)(2,1)S(1)}, u32[]{:S(2)}, u32[]{:S(2)}) collective-permute-start(bf16[384,128]{1,0:T(8,128)(2,1)} %get-tuple-element.28), channel_id=1, source_target_pairs={{0,32},{8,40},{16,48},{24,56},{32,64},{40,72},{48,80},{56,88},{64,... | collective-permute-start | bytes 294920 | tf_op jit(solution)/shard_map/ppermute | solution.py:346
  73.4 12.1 %collective-permute-start.4 = (bf16[384,128]{1,0:T(8,128)(2,1)}, bf16[384,128]{1,0:T(8,128)(2,1)S(1)}, u32[]{:S(2)}, u32[]{:S(2)}) collective-permute-start(bf16[384,128]{1,0:T(8,128)(2,1)} %get-tuple-element.29), channel_id=1, source_target_pairs={{0,48},{8,56},{16,32},{24,40},{32,80},{40,88},{48,64},{56,72},{64,... | collective-permute-start | bytes 294920 | tf_op jit(solution)/shard_map/ppermute | solution.py:346
  75.8 14.4 %collective-permute-start.5 = (bf16[384,128]{1,0:T(8,128)(2,1)}, bf16[384,128]{1,0:T(8,128)(2,1)S(1)}, u32[]{:S(2)}, u32[]{:S(2)}) collective-permute-start(bf16[384,128]{1,0:T(8,128)(2,1)} %get-tuple-element.30), channel_id=1, source_target_pairs={{0,64},{8,72},{16,80},{24,88},{32,96},{40,104},{48,112},{56,120},{... | collective-permute-start | bytes 294920 | tf_op jit(solution)/shard_map/ppermute | solution.py:346
  79.2 11.1 %collective-permute-start.6 = (bf16[384,128]{1,0:T(8,128)(2,1)}, bf16[384,128]{1,0:T(8,128)(2,1)S(1)}, u32[]{:S(2)}, u32[]{:S(2)}) collective-permute-start(bf16[384,128]{1,0:T(8,128)(2,1)} %get-tuple-element.31), channel_id=1, source_target_pairs={{0,80},{8,88},{16,64},{24,72},{32,112},{40,120},{48,96},{56,104},{... | collective-permute-start | bytes 294920 | tf_op jit(solution)/shard_map/ppermute | solution.py:346
  79.5 10.9 %copy-start.9 = (bf16[384,128]{1,0:T(8,128)(2,1)}, bf16[384,128]{1,0:T(8,128)(2,1)S(1)}, u32[]{:S(2)}) copy-start(bf16[384,128]{1,0:T(8,128)(2,1)S(1)} %collective-permute-done.2.refs_1_) | copy-start | bytes 294916
  79.5 10.8 %collective-permute-start.7 = (bf16[384,128]{1,0:T(8,128)(2,1)}, bf16[384,128]{1,0:T(8,128)(2,1)S(1)}, u32[]{:S(2)}, u32[]{:S(2)}) collective-permute-start(bf16[384,128]{1,0:T(8,128)(2,1)} %get-tuple-element.32), channel_id=1, source_target_pairs={{0,96},{8,104},{16,112},{24,120},{32,0},{40,8},{48,16},{56,24},{64... | collective-permute-start | bytes 294920 | tf_op jit(solution)/shard_map/ppermute | solution.py:346
  81.6 8.8 %copy-start.10 = (bf16[384,128]{1,0:T(8,128)(2,1)}, bf16[384,128]{1,0:T(8,128)(2,1)S(1)}, u32[]{:S(2)}) copy-start(bf16[384,128]{1,0:T(8,128)(2,1)S(1)} %collective-permute-done.3.refs_2_) | copy-start | bytes 294916
  81.6 8.7 %collective-permute-start.8 = (bf16[384,128]{1,0:T(8,128)(2,1)}, bf16[384,128]{1,0:T(8,128)(2,1)S(1)}, u32[]{:S(2)}, u32[]{:S(2)}) collective-permute-start(bf16[384,128]{1,0:T(8,128)(2,1)} %get-tuple-element.33), channel_id=1, source_target_pairs={{0,112},{8,120},{16,96},{24,104},{32,16},{40,24},{48,0},{56,8},{64... | collective-permute-start | bytes 294920 | tf_op jit(solution)/shard_map/ppermute | solution.py:346
  85.5 58.9 %collective-permute-start = (bf16[128,1024]{1,0:T(8,128)(2,1)S(1)}, bf16[128,1024]{1,0:T(8,128)(2,1)}, u32[]{:S(2)}, u32[]{:S(2)}) collective-permute-start(bf16[128,1024]{1,0:T(8,128)(2,1)S(1)} %multiply_convert_fusion), channel_id=1, source_target_pairs={{0,8},{8,16},{16,24},{24,32},{32,40},{40,48},{48,56},{56,64},{64,7... | collective-permute-start | bytes 786440 | tf_op jit(solution)/shard_map/ppermute | solution.py:24
  102.0 22.7 %collective-permute-start.12 = (bf16[512,384]{1,0:T(8,128)(2,1)}, bf16[512,384]{1,0:T(8,128)(2,1)S(1)}, u32[]{:S(2)}, u32[]{:S(2)}) collective-permute-start(bf16[512,384]{1,0:T(8,128)(2,1)} %get-tuple-element.40), channel_id=1, source_target_pairs={{0,1},{1,2},{2,3},{3,0},{4,5},{5,6},{6,7},{7,4},{8,9},{9,10},{10,1... | collective-permute-start | bytes 1179656 | tf_op jit(solution)/shard_map/ppermute | solution.py:355
  103.7 20.6 %collective-permute-start.20 = (bf16[512,384]{1,0:T(8,128)(2,1)}, bf16[512,384]{1,0:T(8,128)(2,1)S(1)}, u32[]{:S(2)}, u32[]{:S(2)}) collective-permute-start(bf16[512,384]{1,0:T(8,128)(2,1)} %get-tuple-element.49), channel_id=1, source_target_pairs={{0,3},{1,0},{2,1},{3,2},{4,7},{5,4},{6,5},{7,6},{8,11},{9,8},{10,9... | collective-permute-start | bytes 1179656 | tf_op jit(solution)/shard_map/ppermute | solution.py:355
  105.8 20.5 %collective-permute-start.9 = (bf16[512,384]{1,0:T(8,128)(2,1)}, bf16[512,384]{1,0:T(8,128)(2,1)S(1)}, u32[]{:S(2)}, u32[]{:S(2)}) collective-permute-start(bf16[512,384]{1,0:T(8,128)(2,1)} %get-tuple-element.36), channel_id=1, source_target_pairs={{0,1},{1,2},{2,3},{3,0},{4,5},{5,6},{6,7},{7,4},{8,9},{9,10},{10,1... | collective-permute-start | bytes 1179656 | tf_op jit(solution)/shard_map/ppermute | solution.py:355
  105.8 20.3 %collective-permute-start.17 = (bf16[512,384]{1,0:T(8,128)(2,1)}, bf16[512,384]{1,0:T(8,128)(2,1)S(1)}, u32[]{:S(2)}, u32[]{:S(2)}) collective-permute-start(bf16[512,384]{1,0:T(8,128)(2,1)} %get-tuple-element.45), channel_id=1, source_target_pairs={{0,3},{1,0},{2,1},{3,2},{4,7},{5,4},{6,5},{7,6},{8,11},{9,8},{10,9... | collective-permute-start | bytes 1179656 | tf_op jit(solution)/shard_map/ppermute | solution.py:355
  116.3 8.3 %copy-start.6 = (bf16[512,384]{1,0:T(8,128)(2,1)S(1)}, bf16[512,384]{1,0:T(8,128)(2,1)}, u32[]{:S(2)}) copy-start(bf16[512,384]{1,0:T(8,128)(2,1)} %get-tuple-element.48) | copy-start | bytes 1179652
  116.3 8.4 %copy-start.18 = (bf16[512,384]{1,0:T(8,128)(2,1)S(1)}, bf16[512,384]{1,0:T(8,128)(2,1)}, u32[]{:S(2)}) copy-start(bf16[512,384]{1,0:T(8,128)(2,1)} %get-tuple-element.47) | copy-start | bytes 1179652
  116.3 9.7 %copy-start.5 = (bf16[512,384]{1,0:T(8,128)(2,1)S(1)}, bf16[512,384]{1,0:T(8,128)(2,1)}, u32[]{:S(2)}) copy-start(bf16[512,384]{1,0:T(8,128)(2,1)} %get-tuple-element.39) | copy-start | bytes 1179652
  124.2 9.4 %collective-permute-start.14 = (bf16[512,384]{1,0:T(8,128)(2,1)S(1)}, bf16[512,384]{1,0:T(8,128)(2,1)S(1)}, u32[]{:S(2)}, u32[]{:S(2)}) collective-permute-start(bf16[512,384]{1,0:T(8,128)(2,1)S(1)} %copy-done.19), channel_id=1, source_target_pairs={{0,3},{1,0},{2,1},{3,2},{4,7},{5,4},{6,5},{7,6},{8,11},{9,8},{10,9... | collective-permute-start | bytes 1179656 | tf_op jit(solution)/shard_map/ppermute | solution.py:355
  124.7 19.0 %collective-permute-start.19 = (bf16[512,384]{1,0:T(8,128)(2,1)S(1)}, bf16[512,384]{1,0:T(8,128)(2,1)S(1)}, u32[]{:S(2)}, u32[]{:S(2)}) collective-permute-start(bf16[512,384]{1,0:T(8,128)(2,1)S(1)} %copy-done.18), channel_id=1, source_target_pairs={{0,1},{1,2},{2,3},{3,0},{4,5},{5,6},{6,7},{7,4},{8,9},{9,10},{10,1... | collective-permute-start | bytes 1179656 | tf_op jit(solution)/shard_map/ppermute | solution.py:355
  126.0 17.5 %copy-start.2 = (bf16[512,384]{1,0:T(8,128)(2,1)S(1)}, bf16[512,384]{1,0:T(8,128)(2,1)}, u32[]{:S(2)}) copy-start(bf16[512,384]{1,0:T(8,128)(2,1)} %get-tuple-element.38) | copy-start | bytes 1179652
  126.1 17.1 %collective-permute-start.13 = (bf16[512,384]{1,0:T(8,128)(2,1)S(1)}, bf16[512,384]{1,0:T(8,128)(2,1)S(1)}, u32[]{:S(2)}, u32[]{:S(2)}) collective-permute-start(bf16[512,384]{1,0:T(8,128)(2,1)S(1)} %add_convert_fusion.6), channel_id=1, source_target_pairs={{0,1},{1,2},{2,3},{3,0},{4,5},{5,6},{6,7},{7,4},{8,9},{9,10},{10,1... | collective-permute-start | bytes 1179656 | tf_op jit(solution)/shard_map/ppermute | solution.py:355
  126.3 18.0 %copy-start.1 = (bf16[512,384]{1,0:T(8,128)(2,1)S(1)}, bf16[512,384]{1,0:T(8,128)(2,1)}, u32[]{:S(2)}) copy-start(bf16[512,384]{1,0:T(8,128)(2,1)} %get-tuple-element.46) | copy-start | bytes 1179652
  126.3 17.7 %collective-permute-start.21 = (bf16[512,384]{1,0:T(8,128)(2,1)S(1)}, bf16[512,384]{1,0:T(8,128)(2,1)S(1)}, u32[]{:S(2)}, u32[]{:S(2)}) collective-permute-start(bf16[512,384]{1,0:T(8,128)(2,1)S(1)} %add_convert_fusion.2), channel_id=1, source_target_pairs={{0,3},{1,0},{2,1},{3,2},{4,7},{5,4},{6,5},{7,6},{8,11},{9,8},{10,9... | collective-permute-start | bytes 1179656 | tf_op jit(solution)/shard_map/ppermute | solution.py:355
  133.7 17.0 %collective-permute-start.11 = (bf16[512,384]{1,0:T(8,128)(2,1)S(1)}, bf16[512,384]{1,0:T(8,128)(2,1)S(1)}, u32[]{:S(2)}, u32[]{:S(2)}) collective-permute-start(bf16[512,384]{1,0:T(8,128)(2,1)S(1)} %copy-done.17), channel_id=1, source_target_pairs={{0,3},{1,0},{2,1},{3,2},{4,7},{5,4},{6,5},{7,6},{8,11},{9,8},{10,9... | collective-permute-start | bytes 1179656 | tf_op jit(solution)/shard_map/ppermute | solution.py:355
  143.2 19.0 %collective-permute-start.16 = (bf16[512,384]{1,0:T(8,128)(2,1)}, bf16[512,384]{1,0:T(8,128)(2,1)S(1)}, u32[]{:S(2)}, u32[]{:S(2)}) collective-permute-start(bf16[512,384]{1,0:T(8,128)(2,1)} %get-tuple-element.43), channel_id=1, source_target_pairs={{0,1},{1,2},{2,3},{3,0},{4,5},{5,6},{6,7},{7,4},{8,9},{9,10},{10,1... | collective-permute-start | bytes 1179656 | tf_op jit(solution)/shard_map/ppermute | solution.py:355
  143.7 17.4 %collective-permute-start.10 = (bf16[512,384]{1,0:T(8,128)(2,1)S(1)}, bf16[512,384]{1,0:T(8,128)(2,1)S(1)}, u32[]{:S(2)}, u32[]{:S(2)}) collective-permute-start(bf16[512,384]{1,0:T(8,128)(2,1)S(1)} %add_convert_fusion.7), channel_id=1, source_target_pairs={{0,1},{1,2},{2,3},{3,0},{4,5},{5,6},{6,7},{7,4},{8,9},{9,10},{10,1... | collective-permute-start | bytes 1179656 | tf_op jit(solution)/shard_map/ppermute | solution.py:355
  144.0 17.0 %collective-permute-start.15 = (bf16[512,384]{1,0:T(8,128)(2,1)S(1)}, bf16[512,384]{1,0:T(8,128)(2,1)}, u32[]{:S(2)}, u32[]{:S(2)}) collective-permute-start(bf16[512,384]{1,0:T(8,128)(2,1)S(1)} %add_convert_fusion.5), channel_id=1, source_target_pairs={{0,4},{1,5},{2,6},{3,7},{4,0},{5,1},{6,2},{7,3},{8,12},{9,13},{10,... | collective-permute-start | bytes 1179656 | tf_op jit(solution)/shard_map/ppermute | solution.py:371
  144.5 17.7 %collective-permute-start.18 = (bf16[512,384]{1,0:T(8,128)(2,1)S(1)}, bf16[512,384]{1,0:T(8,128)(2,1)S(1)}, u32[]{:S(2)}, u32[]{:S(2)}) collective-permute-start(bf16[512,384]{1,0:T(8,128)(2,1)S(1)} %add_convert_fusion.3), channel_id=1, source_target_pairs={{0,3},{1,0},{2,1},{3,2},{4,7},{5,4},{6,5},{7,6},{8,11},{9,8},{10,9... | collective-permute-start | bytes 1179656 | tf_op jit(solution)/shard_map/ppermute | solution.py:355
  150.6 11.6 %collective-permute-start.22 = (bf16[512,384]{1,0:T(8,128)(2,1)S(1)}, bf16[512,384]{1,0:T(8,128)(2,1)}, u32[]{:S(2)}, u32[]{:S(2)}) collective-permute-start(bf16[512,384]{1,0:T(8,128)(2,1)S(1)} %add_convert_fusion.1), channel_id=1, source_target_pairs={{0,4},{1,5},{2,6},{3,7},{4,0},{5,1},{6,2},{7,3},{8,12},{9,13},{10,... | collective-permute-start | bytes 1179656 | tf_op jit(solution)/shard_map/ppermute | solution.py:371
  151.0 10.1 %copy-start.8 = (bf16[512,384]{1,0:T(8,128)(2,1)S(1)}, bf16[512,384]{1,0:T(8,128)(2,1)}, u32[]{:S(2)}) copy-start(bf16[512,384]{1,0:T(8,128)(2,1)} %get-tuple-element.34) | copy-start | bytes 1179652
  (11 other events, 34.6 us)

commit v2 on v1

--- a/solution.py
+++ b/solution.py
@@ -122,32 +122,65 @@
     return ((y - step // 2) & 3) * 2 + ((x - step) & 1)
 
 
-def split_kernel(q_ref, k_ref, v_ref, out_ref):
-    rows = q_ref.shape[0]
+def split_kernel(*refs):
+    out_ref = refs[-1]
+    rows = refs[0].shape[0]
     for head in range(out_ref.shape[0]):
         columns = slice(head * HEAD_DIM, (head + 1) * HEAD_DIM)
-        out_ref[head, :rows, :] = k_ref[:, columns]
-        out_ref[head, rows : 2 * rows, :] = v_ref[:, columns]
-        out_ref[head, 2 * rows :, :] = q_ref[:, columns]
-
-
-def split_heads(query_rows, key_rows, value_rows):
-    rows = query_rows.shape[0]
-    at_once = 2
+        for i, ref in enumerate(refs[:-1]):
+            out_ref[head, i * rows : (i + 1) * rows, :] = ref[:, columns]
+
+
+def split_heads(*arrays):
+    rows = arrays[0].shape[0]
+    at_once = 4
     spec = pl.BlockSpec((rows, at_once * HEAD_DIM), lambda step: (0, step))
+    tall = len(arrays) * rows
     return pl.pallas_call(
         split_kernel,
         grid=(CHIPS // at_once,),
-        out_shape=jax.ShapeDtypeStruct((CHIPS, 3 * rows, HEAD_DIM), jnp.bfloat16),
-        in_specs=[spec] * 3,
-        out_specs=pl.BlockSpec((at_once, 3 * rows, HEAD_DIM), lambda step: (step, 0, 0)),
+        out_shape=jax.ShapeDtypeStruct((CHIPS, tall, HEAD_DIM), jnp.bfloat16),
+        in_specs=[spec] * len(arrays),
+        out_specs=pl.BlockSpec((at_once, tall, HEAD_DIM), lambda step: (step, 0, 0)),
         name="split_heads",
-    )(query_rows, key_rows, value_rows)
+    )(*arrays)
+
+
+def split_queries_kernel(place, query_ref, *outs):
+    for step in range(CHIPS):
+        column = pl.multiple_of(ahead(place[0], place[1], step) * HEAD_DIM, HEAD_DIM)
+        outs[step][...] = query_ref[:, pl.ds(column, HEAD_DIM)]
+
+
+def split_queries(place, query_rows):
+    rows = query_rows.shape[0]
+    return pl.pallas_call(
+        split_queries_kernel,
+        out_shape=[jax.ShapeDtypeStruct((rows, HEAD_DIM), jnp.bfloat16)] * CHIPS,
+        in_specs=[SMEM_SPEC, VMEM_SPEC],
+        out_specs=[VMEM_SPEC] * CHIPS,
+        name="split_queries",
+    )(place, query_rows)
+
+
+def same_place(place):
+    def kernel(place, out):
+        for i in range(place.shape[0]):
+            out[i] = place[i]
+
+    return pl.pallas_call(
+        kernel,
+        out_shape=jax.ShapeDtypeStruct(place.shape, place.dtype),
+        in_specs=[SMEM_SPEC],
+        out_specs=SMEM_SPEC,
+        name="same_place",
+    )(place)
 
 
 def attention_kernel(place, own, other, *refs):
-    outs = refs[:CHIPS]
-    keys, values, top, total, even, odd = refs[CHIPS:]
+    queries = refs[:CHIPS]
+    outs = refs[CHIPS : 2 * CHIPS]
+    now, keys, values, top, total, even, odd = refs[2 * CHIPS :]
     y, x, core = place[0], place[1], place[2]
     step = pl.program_id(0)
     rows = top.shape[0]
@@ -158,18 +191,22 @@
         for i in range(CHIPS):
             keys[i, :, :rows] = own[i, :rows, :].T
             keys[i, :, rows:] = other[i, :rows, :].T
-            values[i, :rows, :HEAD_DIM] = own[i, rows : 2 * rows, :]
+            values[i, :rows, :HEAD_DIM] = own[i, rows:, :]
             values[i, rows:, :HEAD_DIM] = other[i, rows:, :]
             values[i, :, HEAD_DIM:] = ones
+
+    for i in range(CHIPS):
+
+        @pl.when(step == i)
+        def _(i=i):
+            now[...] = queries[i][...]
 
     top[...] = jnp.full_like(top, NEGATIVE)
     total[...] = jnp.zeros_like(total)
     chip = ahead(y, x, step)
 
     def score(held, block):
-        held[...] = jnp.dot(
-            own[chip, 2 * rows :, :], keys[block], preferred_element_type=jnp.float32
-        )
+        held[...] = jnp.dot(now[...], keys[block], preferred_element_type=jnp.float32)
 
     def weigh(held, block, masked):
         scores = held[...]
@@ -218,15 +255,16 @@
             outs[i][...] = result
 
 
-def attention(place, own, other):
-    rows = own.shape[1] // 3
+def attention(place, queries, own, other):
+    rows = queries[0].shape[0]
     return pl.pallas_call(
         attention_kernel,
         grid=(CHIPS,),
         out_shape=[jax.ShapeDtypeStruct((rows, HEAD_DIM), jnp.bfloat16)] * CHIPS,
-        in_specs=[SMEM_SPEC, VMEM_SPEC, VMEM_SPEC],
+        in_specs=[SMEM_SPEC] + [VMEM_SPEC] * (2 + CHIPS),
         out_specs=[VMEM_SPEC] * CHIPS,
         scratch_shapes=[
+            VMEM((rows, HEAD_DIM), jnp.bfloat16),
             VMEM((CHIPS, HEAD_DIM, 2 * rows), jnp.bfloat16),
             VMEM((CHIPS, 2 * rows, 2 * HEAD_DIM), jnp.bfloat16),
             VMEM((rows, HEAD_DIM), jnp.float32),
@@ -238,26 +276,53 @@
             flops=12_000_000_000, bytes_accessed=6_000_000, transcendentals=10_000_000
         ),
         name="attention",
-    )(place, own, other)
-
-
-def join_kernel(place, *refs):
-    y, x = place[0], place[1]
-    joined = refs[CHIPS]
-    for step in range(CHIPS):
-        column = pl.multiple_of(behind(y, x, step) * HEAD_DIM, HEAD_DIM)
-        joined[:, pl.ds(column, HEAD_DIM)] = refs[step][...]
-
-
-def join_heads(place, pieces):
+    )(place, own, other, *queries)
+
+
+def project_first(place, pieces, out_weight, x_off, z_off):
     rows = pieces[0].shape[0]
-    return pl.pallas_call(
-        join_kernel,
-        out_shape=jax.ShapeDtypeStruct((rows, CHIPS * HEAD_DIM), jnp.bfloat16),
-        in_specs=[SMEM_SPEC] + [VMEM_SPEC] * CHIPS,
-        out_specs=VMEM_SPEC,
-        name="join_heads",
-    )(place, *pieces)
+    share = out_weight.shape[0] // (2 * RING)
+    features = out_weight.shape[1]
+
+    def weight_block(step, place):
+        return (((place[3] + x_off) & 1) * RING + ((place[4] + z_off) & 3), 0)
+
+    def kernel(place, weight_ref, *refs):
+        joined, lower, upper = refs[CHIPS:]
+        for step in range(CHIPS):
+            column = pl.multiple_of(behind(place[0], place[1], step) * HEAD_DIM, HEAD_DIM)
+            joined[:, pl.ds(column, HEAD_DIM)] = refs[step][...]
+        piece = lax.dot_general(
+            joined[...],
+            weight_ref[...],
+            (((1,), (1,)), ((), ())),
+            preferred_element_type=jnp.float32,
+        )
+        piece = piece.astype(jnp.bfloat16).T
+        lower[...] = piece[: share // 2]
+        upper[...] = piece[share // 2 :]
+
+    def whole(height, width):
+        return pl.BlockSpec((height, width), lambda step, place: (0, 0))
+
+    return pl.pallas_call(
+        kernel,
+        grid_spec=pltpu.PrefetchScalarGridSpec(
+            num_scalar_prefetch=1,
+            grid=(1,),
+            in_specs=[pl.BlockSpec((share, features), weight_block)]
+            + [whole(rows, HEAD_DIM)] * CHIPS,
+            out_specs=[whole(rows, features)] + [whole(share // 2, rows)] * 2,
+        ),
+        out_shape=[jax.ShapeDtypeStruct((rows, features), jnp.bfloat16)]
+        + [jax.ShapeDtypeStruct((share // 2, rows), jnp.bfloat16)] * 2,
+        cost_estimate=pl.CostEstimate(
+            flops=2 * share * rows * features,
+            bytes_accessed=share * features * 2,
+            transcendentals=0,
+        ),
+        name="project_first",
+    )(place, out_weight, *pieces)
 
 
 def project(place, wanted, out_weight, attended):
@@ -326,7 +391,8 @@
 ):
     ctx = lax.axis_index("ctx")
     tp = lax.axis_index("tp")
-    place = jnp.stack([ctx // 4, ctx // 2 % 2, ctx % 2, tp // RING, tp % RING]).astype(jnp.int32)
+    place = jnp.stack([ctx // 4, ctx // 2 % 2, ctx % 2, tp // RING, tp % RING])
+    place = place.astype(jnp.int32)
 
     rows = query_rows.shape[0]
     length = conv_filter.shape[1]
@@ -334,19 +400,24 @@
         hyena_key[rows - length :].astype(jnp.float32)
         * hyena_value[rows - length :].astype(jnp.float32)
     ).astype(jnp.bfloat16)
+    pieces = split_heads(key_rows, value_rows)
+    own = lax.all_to_all(pieces, "ctx", 0, 0, axis_index_groups=CORE_GROUPS, tiled=True)
     before = shifted(tail, "ctx", 1)
-    pieces = split_heads(query_rows, key_rows, value_rows)
-    own = lax.all_to_all(pieces, "ctx", 0, 0, axis_index_groups=CORE_GROUPS, tiled=True)
     hyena_out = hyena(
         hyena_query, hyena_key, hyena_value, before, conv_filter, skip_gain
     )
-    other = lax.ppermute(own[:, : 2 * rows], "ctx", CORE_ROUTE)
-    outs = attention(place, own, other)
+    query_rows, hyena_out = lax.optimization_barrier((query_rows, hyena_out))
+    asked = split_queries(place, query_rows)
+    came = [asked[0]] + [
+        lax.ppermute(asked[step], "ctx", chip_route(step)) for step in range(1, CHIPS)
+    ]
+    queries = [came[((-(i // 2)) % CHIPS_Y) * 2 + i % 2] for i in range(CHIPS)]
+    place = same_place(place)
+    other = lax.ppermute(own, "ctx", CORE_ROUTE)
+    outs = attention(place, queries, own, other)
     back = [outs[0]] + [
         lax.ppermute(outs[step], "ctx", chip_route(step)) for step in range(1, CHIPS)
     ]
-    attended = join_heads(place, back)
-
     kept = []
     handed = None
     for x_off in (1, 0):
@@ -354,7 +425,10 @@
         def sent(block, step):
             return lax.ppermute(block, "tp", ring_route(step))
 
-        far = project(place, [(x_off, 2)], out_weight, attended)
+        if x_off == 1:
+            attended, *far = project_first(place, back, out_weight, x_off, 2)
+        else:
+            far = project(place, [(x_off, 2)], out_weight, attended)
         near = project(place, [(x_off, 1), (x_off, 3), (x_off, 0)], out_weight, attended)
         from_below = sent(far[0], 1)
         from_above = sent(far[1], -1)

time: 167 us -> 185 us (1.11)
  the two profiles are of different devices: /device:TPU:1 before, /device:TPU:24 now
where the time goes in v2:
time: 185 us; the launch traced here: 184 us
  Pallas kernels  60.3 us (33%)
  starting transfers between devices  50.2 us (27%)
  waiting for transfers between devices  37.8 us (20%)
  blocking collectives  27.7 us (15%)
  other arithmetic  4.23 us (2%)
  local copies, waits for them, and re-layouts  2.52 us (1%)
    all_to_all x1, blocking collectives, local_step(): lax.all_to_all(pieces, 'ctx', 0, 0, axis_index_groups=CORE_GROUPS, tiled=...  27.7 us
    pallas_call x1, Pallas kernels, attention(): pl.pallas_call(attention_kernel, grid=(CHIPS,), out_shape=[jax.ShapeDtype...  22.1 us
    ppermute x12, waiting for transfers between devices, sent(): return lax.ppermute(block, 'tp', ring_route(step))  20.6 us
    pallas_call x3, Pallas kernels, project(): pl.pallas_call(kernel, grid_spec=pltpu.PrefetchScalarGridSpec(num_scalar_...  19.9 us
    ppermute x12, starting transfers between devices, sent(): return lax.ppermute(block, 'tp', ring_route(step))  17.9 us
    ppermute x7, starting transfers between devices, local_step(): lax.ppermute(asked[step], 'ctx', chip_route(step))  14.2 us
    ppermute x7, starting transfers between devices, local_step(): lax.ppermute(outs[step], 'ctx', chip_route(step))  13.9 us
    ppermute x7, waiting for transfers between devices, local_step(): lax.ppermute(outs[step], 'ctx', chip_route(step))  8.4 us
  transfers between devices with their start and end apart: 30, of which 10 were waited for; matrix products, arithmetic and copies ran while one was open for 2% of the time, Pallas kernels for 17%

profile of v2, /device:TPU:24, one launch (start us, length us, event | category | flops | bytes accessed | tf_op | source)
XLA Modules:
  0.0 183.8 jit_solution(14066787879088491945)
XLA Ops:
  0.6 2.4 %split_heads.1 = bf16[8,768,128]{2,1,0:T(8,128)(2,1)} custom-call(bf16[384,1024]{1,0:T(8,128)(2,1)} %refs_0_.1, bf16[384,1024]{1,0:T(8,128)(2,1)} %refs_1_.1), custom_call_target="tpu_custom_call" | custom-call | tf_op jit(solution)/shard_map/split_heads/pallas_call | solution.py:139
  3.1 27.7 %all_to_all.5.own = bf16[8,768,128]{2,1,0:T(8,128)(2,1)S(1)} all-to-all(bf16[8,768,128]{2,1,0:T(8,128)(2,1)} %split_heads.1), channel_id=1, replica_groups={{0,16,32,48,64,80,96,112},{8,24,40,56,72,88,104,120},{1,17,33,49,65,81,..., dimensions={0} | all-to-all | bytes 3145728 | tf_op jit(solution)/shard_map/all_to_all | solution.py:404
  30.8 1.5 multiply_convert_fusion
  32.2 2.1 %collective-permute-start = (bf16[128,1024]{1,0:T(8,128)(2,1)S(1)}, bf16[128,1024]{1,0:T(8,128)(2,1)}, u32[]{:S(2)}, u32[]{:S(2)}) collective-permute-start(bf16[128,1024]{1,0:T(8,128)(2,1)S(1)} %multiply_convert_fusion), channel_id=1, source_target_pairs={{0,8},{8,16},{16,24},{24,32},{32,40},{40,48},{48,56},{56,64},{64,7... | collective-permute-start | bytes 786440 | tf_op jit(solution)/shard_map/ppermute | solution.py:24
  35.9 6.6 %collective-permute-done.before = bf16[128,1024]{1,0:T(8,128)(2,1)} collective-permute-done((bf16[128,1024]{1,0:T(8,128)(2,1)S(1)}, bf16[128,1024]{1,0:T(8,128)(2,1)}, u32[]{:S(2)}, u32[]{:S(2)}) %collective-permute-start) | collective-permute-done | bytes 262176 | tf_op jit(solution)/shard_map/ppermute | solution.py:24
  42.4 8.2 %hyena.1 = bf16[384,1024]{1,0:T(8,128)(2,1)} custom-call(bf16[384,1024]{1,0:T(8,128)(2,1)} %query.1, bf16[384,1024]{1,0:T(8,128)(2,1)} %key.1, bf16[384,1024]{1,0:T(8,128)(2,1)} %value.1, bf16[128,1024]{1,0:T(8,128)(2,1)} %collective-permute-done.before, f32[64,256]{1,0:T(8,128)} %maximum_maximum_fusion.taps, f32[1,1024]{1,0:T(1,128)} %bitcast.7), custom_call_target="tpu_custom_call" | custom-call | flops 3000000000 | bytes 3000000 | tf_op jit(solution)/shard_map/hyena/pallas_call | solution.py:76
  50.6 2.2 %split_queries.1 = (bf16[384,128]{1,0:T(8,128)(2,1)}, bf16[384,128]{1,0:T(8,128)(2,1)}, bf16[384,128]{1,0:T(8,128)(2,1)}, bf16[384,128]{1,0:T(8,128)(2,1)}, bf16...) custom-call(s32[5]{0:T(128)} %stack.23.place, ...), custom_call_target="tpu_custom_call" | custom-call | tf_op jit(solution)/shard_map/split_queries/pallas_call | solution.py:157
  53.7 4.1 %collective-permute-start.4 = (bf16[384,128]{1,0:T(8,128)(2,1)}, bf16[384,128]{1,0:T(8,128)(2,1)S(1)}, u32[]{:S(2)}, u32[]{:S(2)}) collective-permute-start(bf16[384,128]{1,0:T(8,128)(2,1)} %get-tuple-element.42), channel_id=1, source_target_pairs={{0,112},{8,120},{16,96},{24,104},{32,16},{40,24},{48,0},{56,8},{64... | collective-permute-start | bytes 294920 | tf_op jit(solution)/shard_map/ppermute | solution.py:412
  57.8 2.7 %collective-permute-start.5 = (bf16[384,128]{1,0:T(8,128)(2,1)}, bf16[384,128]{1,0:T(8,128)(2,1)}, u32[]{:S(2)}, u32[]{:S(2)}) collective-permute-start(bf16[384,128]{1,0:T(8,128)(2,1)} %get-tuple-element.43), channel_id=1, source_target_pairs={{0,64},{8,72},{16,80},{24,88},{32,96},{40,104},{48,112},{56,120},{... | collective-permute-start | bytes 294920 | tf_op jit(solution)/shard_map/ppermute | solution.py:412
  62.9 4.1 %collective-permute-start.8 = (bf16[384,128]{1,0:T(8,128)(2,1)}, bf16[384,128]{1,0:T(8,128)(2,1)}, u32[]{:S(2)}, u32[]{:S(2)}) collective-permute-start(bf16[384,128]{1,0:T(8,128)(2,1)} %get-tuple-element.46), channel_id=1, source_target_pairs={{0,48},{8,56},{16,32},{24,40},{32,80},{40,88},{48,64},{56,72},{64,... | collective-permute-start | bytes 294920 | tf_op jit(solution)/shard_map/ppermute | solution.py:412
  71.4 22.1 %attention.1 = (bf16[384,128]{1,0:T(8,128)(2,1)}, bf16[384,128]{1,0:T(8,128)(2,1)}, bf16[384,128]{1,0:T(8,128)(2,1)}, bf16[384,128]{1,0:T(8,128)(2,1)}, bf16[384...) custom-call(s32[5]{0:T(128)} %same_place.1.place, ...), custom_call_target="tpu_custom_call" | custom-call | flops 12000000000 | bytes 6000000 | tf_op jit(solution)/shard_map/attention/pallas_call | solution.py:260
  93.4 3.7 %collective-permute-start.9 = (bf16[384,128]{1,0:T(8,128)(2,1)}, bf16[384,128]{1,0:T(8,128)(2,1)S(1)}, u32[]{:S(2)}, u32[]{:S(2)}) collective-permute-start(bf16[384,128]{1,0:T(8,128)(2,1)} %get-tuple-element.48), channel_id=1, source_target_pairs={{0,16},{8,24},{16,0},{24,8},{32,48},{40,56},{48,32},{56,40},{64,80... | collective-permute-start | bytes 294920 | tf_op jit(solution)/shard_map/ppermute | solution.py:419
  97.2 2.2 %collective-permute-start.10 = (bf16[384,128]{1,0:T(8,128)(2,1)}, bf16[384,128]{1,0:T(8,128)(2,1)S(1)}, u32[]{:S(2)}, u32[]{:S(2)}) collective-permute-start(bf16[384,128]{1,0:T(8,128)(2,1)} %get-tuple-element.49), channel_id=1, source_target_pairs={{0,32},{8,40},{16,48},{24,56},{32,64},{40,72},{48,80},{56,88},{64,... | collective-permute-start | bytes 294920 | tf_op jit(solution)/shard_map/ppermute | solution.py:419
  99.3 1.4 collective-permute-start.12
  100.8 4.5 %collective-permute-start.13 = (bf16[384,128]{1,0:T(8,128)(2,1)}, bf16[384,128]{1,0:T(8,128)(2,1)S(1)}, u32[]{:S(2)}, u32[]{:S(2)}) collective-permute-start(bf16[384,128]{1,0:T(8,128)(2,1)} %get-tuple-element.52), channel_id=1, source_target_pairs={{0,80},{8,88},{16,64},{24,72},{32,112},{40,120},{48,96},{56,104},{... | collective-permute-start | bytes 294920 | tf_op jit(solution)/shard_map/ppermute | solution.py:419
  105.3 2.0 %collective-permute-start.14 = (bf16[384,128]{1,0:T(8,128)(2,1)}, bf16[384,128]{1,0:T(8,128)(2,1)S(1)}, u32[]{:S(2)}, u32[]{:S(2)}) collective-permute-start(bf16[384,128]{1,0:T(8,128)(2,1)} %get-tuple-element.53), channel_id=1, source_target_pairs={{0,96},{8,104},{16,112},{24,120},{32,0},{40,8},{48,16},{56,24},{64... | collective-permute-start | bytes 294920 | tf_op jit(solution)/shard_map/ppermute | solution.py:419
  107.4 2.1 %collective-permute-done.13.refs_5_ = bf16[384,128]{1,0:T(8,128)(2,1)S(1)} collective-permute-done((bf16[384,128]{1,0:T(8,128)(2,1)}, bf16[384,128]{1,0:T(8,128)(2,1)S(1)}, u32[]{:S(2)}, u32[]{:S(2)}) %collective-permute-start.13) | collective-permute-done | bytes 98336 | tf_op jit(solution)/shard_map/ppermute | solution.py:419
  109.5 1.8 collective-permute-done.14.refs_6_
  111.3 4.4 %collective-permute-done.15.refs_7_ = bf16[384,128]{1,0:T(8,128)(2,1)S(1)} collective-permute-done((bf16[384,128]{1,0:T(8,128)(2,1)}, bf16[384,128]{1,0:T(8,128)(2,1)S(1)}, u32[]{:S(2)}, u32[]{:S(2)}) %collective-permute-start.15) | collective-permute-done | bytes 98336 | tf_op jit(solution)/shard_map/ppermute | solution.py:419
  116.4 4.4 %project_first.1 = (bf16[384,1024]{1,0:T(8,128)(2,1)}, bf16[512,384]{1,0:T(8,128)(2,1)}, bf16[512,384]{1,0:T(8,128)(2,1)}) custom-call(s32[5]{0:T(128)} %same_place.1.place, bf16[8192,1024]{1,0:T(8,128)(2,1)} %weight_ref.7, bf16[384,128]{1,0:T(8,128)(2,1)} %get-tuple-element.47.refs_0_, bf16[384,128]{1,0:T(8,128)(2,1)} %copy-done.9, ...), custom_call_target="tpu_custom_call" | custom-call | flops 805306368 | bytes 2097152 | tf_op jit(solution)/shard_map/project_first/pallas_call | solution.py:308
  120.8 1.9 %collective-permute-start.19 = (bf16[512,384]{1,0:T(8,128)(2,1)}, bf16[512,384]{1,0:T(8,128)(2,1)S(1)}, u32[]{:S(2)}, u32[]{:S(2)}) collective-permute-start(bf16[512,384]{1,0:T(8,128)(2,1)} %get-tuple-element.62), channel_id=1, source_target_pairs={{0,1},{1,2},{2,3},{3,0},{4,5},{5,6},{6,7},{7,4},{8,9},{9,10},{10,1... | collective-permute-start | bytes 1179656 | tf_op jit(solution)/shard_map/ppermute | solution.py:426
  122.7 2.1 %collective-permute-start.27 = (bf16[512,384]{1,0:T(8,128)(2,1)}, bf16[512,384]{1,0:T(8,128)(2,1)S(1)}, u32[]{:S(2)}, u32[]{:S(2)}) collective-permute-start(bf16[512,384]{1,0:T(8,128)(2,1)} %get-tuple-element.71), channel_id=1, source_target_pairs={{0,3},{1,0},{2,1},{3,2},{4,7},{5,4},{6,5},{7,6},{8,11},{9,8},{10,9... | collective-permute-start | bytes 1179656 | tf_op jit(solution)/shard_map/ppermute | solution.py:426
  124.8 4.3 %project.4 = (bf16[512,384]{1,0:T(8,128)(2,1)}, bf16[512,384]{1,0:T(8,128)(2,1)}) custom-call(s32[5]{0:T(128)} %same_place.1.place, bf16[8192,1024]{1,0:T(8,128)(2,1)} %weight_ref.7, bf16[384,1024]{1,0:T(8,128)(2,1)} %get-tuple-element.55.attended_ref), custom_call_target="tpu_custom_call" | custom-call | flops 805306368 | bytes 2097152 | tf_op jit(solution)/shard_map/project/pallas_call | solution.py:356
  129.1 3.2 %collective-permute-start.24 = (bf16[512,384]{1,0:T(8,128)(2,1)}, bf16[512,384]{1,0:T(8,128)(2,1)S(1)}, u32[]{:S(2)}, u32[]{:S(2)}) collective-permute-start(bf16[512,384]{1,0:T(8,128)(2,1)} %get-tuple-element.67), channel_id=1, source_target_pairs={{0,3},{1,0},{2,1},{3,2},{4,7},{5,4},{6,5},{7,6},{8,11},{9,8},{10,9... | collective-permute-start | bytes 1179656 | tf_op jit(solution)/shard_map/ppermute | solution.py:426
  132.4 7.8 %project.5 = (bf16[512,384]{1,0:T(8,128)(2,1)}, bf16[512,384]{1,0:T(8,128)(2,1)}, bf16[512,384]{1,0:T(8,128)(2,1)}, bf16[512,384]{1,0:T(8,128)(2,1)}, bf16[512,3...) custom-call(s32[5]{0:T(128)} %same_place.1.place, bf16[8192,1024]{1,0:T(8,128)(2,1)} %weight_ref.7, ...), custom_call_target="tpu_custom_call" | custom-call | flops 2415919104 | bytes 6291456 | tf_op jit(solution)/shard_map/project/pallas_call | solution.py:356
  141.1 7.8 %project.3 = (bf16[512,384]{1,0:T(8,128)(2,1)}, bf16[512,384]{1,0:T(8,128)(2,1)}, bf16[512,384]{1,0:T(8,128)(2,1)}, bf16[512,384]{1,0:T(8,128)(2,1)}, bf16[512,3...) custom-call(s32[5]{0:T(128)} %same_place.1.place, bf16[8192,1024]{1,0:T(8,128)(2,1)} %weight_ref.7, ...), custom_call_target="tpu_custom_call" | custom-call | flops 2415919104 | bytes 6291456 | tf_op jit(solution)/shard_map/project/pallas_call | solution.py:356
  150.5 3.3 %collective-permute-start.18 = (bf16[512,384]{1,0:T(8,128)(2,1)S(1)}, bf16[512,384]{1,0:T(8,128)(2,1)S(1)}, u32[]{:S(2)}, u32[]{:S(2)}) collective-permute-start(bf16[512,384]{1,0:T(8,128)(2,1)S(1)} %copy-done.19), channel_id=1, source_target_pairs={{0,3},{1,0},{2,1},{3,2},{4,7},{5,4},{6,5},{7,6},{8,11},{9,8},{10,9... | collective-permute-start | bytes 1179656 | tf_op jit(solution)/shard_map/ppermute | solution.py:426
  154.8 14.5 %collective-permute-done.20 = bf16[512,384]{1,0:T(8,128)(2,1)S(1)} collective-permute-done((bf16[512,384]{1,0:T(8,128)(2,1)S(1)}, bf16[512,384]{1,0:T(8,128)(2,1)S(1)}, u32[]{:S(2)}, u32[]{:S(2)}) %collective-permute-start.20) | collective-permute-done | bytes 393248 | tf_op jit(solution)/shard_map/ppermute | solution.py:426
  171.4 3.2 %collective-permute-start.25 = (bf16[512,384]{1,0:T(8,128)(2,1)S(1)}, bf16[512,384]{1,0:T(8,128)(2,1)S(1)}, u32[]{:S(2)}, u32[]{:S(2)}) collective-permute-start(bf16[512,384]{1,0:T(8,128)(2,1)S(1)} %add_convert_fusion.3), channel_id=1, source_target_pairs={{0,3},{1,0},{2,1},{3,2},{4,7},{5,4},{6,5},{7,6},{8,11},{9,8},{10,9... | collective-permute-start | bytes 1179656 | tf_op jit(solution)/shard_map/ppermute | solution.py:426
  174.8 1.4 collective-permute-start.29
  176.1 2.1 %collective-permute-done.17 = bf16[512,384]{1,0:T(8,128)(2,1)S(1)} collective-permute-done((bf16[512,384]{1,0:T(8,128)(2,1)S(1)}, bf16[512,384]{1,0:T(8,128)(2,1)S(1)}, u32[]{:S(2)}, u32[]{:S(2)}) %collective-permute-start.17) | collective-permute-done | bytes 393248 | tf_op jit(solution)/shard_map/ppermute | solution.py:426
  178.4 4.0 %collective-permute-done.23 = bf16[512,384]{1,0:T(8,128)(2,1)S(1)} collective-permute-done((bf16[512,384]{1,0:T(8,128)(2,1)S(1)}, bf16[512,384]{1,0:T(8,128)(2,1)S(1)}, u32[]{:S(2)}, u32[]{:S(2)}) %collective-permute-start.23) | collective-permute-done | bytes 393248 | tf_op jit(solution)/shard_map/ppermute | solution.py:426
  (103 shorter events, 16.9 us)
Async XLA Ops:
  3.1 31.4 %copy-start.16 = (bf16[64,128]{1,0:T(8,128)(2,1)S(1)}, bf16[64,128]{1,0:T(8,128)(2,1)}, u32[]{:S(2)}) copy-start(bf16[64,128]{1,0:T(8,128)(2,1)} %param.12) | copy-start | bytes 49156
  30.8 39.4 %collective-permute-start.1 = (bf16[8,768,128]{2,1,0:T(8,128)(2,1)S(1)}, bf16[8,768,128]{2,1,0:T(8,128)(2,1)S(1)}, u32[]{:S(2)}, u32[]{:S(2)}) collective-permute-start(bf16[8,768,128]{2,1,0:T(8,128)(2,1)S(1)} %all_to_all.5.own), channel_id=1, source_target_pairs={{0,8},{8,0},{16,24},{24,16},{32,40},{40,32},{48,56},{56,48},{64,72... | collective-permute-start | bytes 4718600 | tf_op jit(solution)/shard_map/ppermute | solution.py:416
  32.2 10.2 %collective-permute-start = (bf16[128,1024]{1,0:T(8,128)(2,1)S(1)}, bf16[128,1024]{1,0:T(8,128)(2,1)}, u32[]{:S(2)}, u32[]{:S(2)}) collective-permute-start(bf16[128,1024]{1,0:T(8,128)(2,1)S(1)} %multiply_convert_fusion), channel_id=1, source_target_pairs={{0,8},{8,16},{16,24},{24,32},{32,40},{40,48},{48,56},{56,64},{64,7... | collective-permute-start | bytes 786440 | tf_op jit(solution)/shard_map/ppermute | solution.py:24
  52.8 7.7 %collective-permute-start.2 = (bf16[384,128]{1,0:T(8,128)(2,1)}, bf16[384,128]{1,0:T(8,128)(2,1)S(1)}, u32[]{:S(2)}, u32[]{:S(2)}) collective-permute-start(bf16[384,128]{1,0:T(8,128)(2,1)} %get-tuple-element.40), channel_id=1, source_target_pairs={{0,16},{8,24},{16,0},{24,8},{32,48},{40,56},{48,32},{56,40},{64,80... | collective-permute-start | bytes 294920 | tf_op jit(solution)/shard_map/ppermute | solution.py:412
  53.3 8.6 %collective-permute-start.3 = (bf16[384,128]{1,0:T(8,128)(2,1)}, bf16[384,128]{1,0:T(8,128)(2,1)S(1)}, u32[]{:S(2)}, u32[]{:S(2)}) collective-permute-start(bf16[384,128]{1,0:T(8,128)(2,1)} %get-tuple-element.41), channel_id=1, source_target_pairs={{0,96},{8,104},{16,112},{24,120},{32,0},{40,8},{48,16},{56,24},{64... | collective-permute-start | bytes 294920 | tf_op jit(solution)/shard_map/ppermute | solution.py:412
  53.7 9.2 %collective-permute-start.4 = (bf16[384,128]{1,0:T(8,128)(2,1)}, bf16[384,128]{1,0:T(8,128)(2,1)S(1)}, u32[]{:S(2)}, u32[]{:S(2)}) collective-permute-start(bf16[384,128]{1,0:T(8,128)(2,1)} %get-tuple-element.42), channel_id=1, source_target_pairs={{0,112},{8,120},{16,96},{24,104},{32,16},{40,24},{48,0},{56,8},{64... | collective-permute-start | bytes 294920 | tf_op jit(solution)/shard_map/ppermute | solution.py:412
  57.8 10.4 %collective-permute-start.5 = (bf16[384,128]{1,0:T(8,128)(2,1)}, bf16[384,128]{1,0:T(8,128)(2,1)}, u32[]{:S(2)}, u32[]{:S(2)}) collective-permute-start(bf16[384,128]{1,0:T(8,128)(2,1)} %get-tuple-element.43), channel_id=1, source_target_pairs={{0,64},{8,72},{16,80},{24,88},{32,96},{40,104},{48,112},{56,120},{... | collective-permute-start | bytes 294920 | tf_op jit(solution)/shard_map/ppermute | solution.py:412
  60.5 8.8 %collective-permute-start.6 = (bf16[384,128]{1,0:T(8,128)(2,1)}, bf16[384,128]{1,0:T(8,128)(2,1)}, u32[]{:S(2)}, u32[]{:S(2)}) collective-permute-start(bf16[384,128]{1,0:T(8,128)(2,1)} %get-tuple-element.44), channel_id=1, source_target_pairs={{0,80},{8,88},{16,64},{24,72},{32,112},{40,120},{48,96},{56,104},{... | collective-permute-start | bytes 294920 | tf_op jit(solution)/shard_map/ppermute | solution.py:412
  61.8 7.5 %collective-permute-start.7 = (bf16[384,128]{1,0:T(8,128)(2,1)}, bf16[384,128]{1,0:T(8,128)(2,1)}, u32[]{:S(2)}, u32[]{:S(2)}) collective-permute-start(bf16[384,128]{1,0:T(8,128)(2,1)} %get-tuple-element.45), channel_id=1, source_target_pairs={{0,32},{8,40},{16,48},{24,56},{32,64},{40,72},{48,80},{56,88},{64,... | collective-permute-start | bytes 294920 | tf_op jit(solution)/shard_map/ppermute | solution.py:412
  62.9 7.3 %collective-permute-start.8 = (bf16[384,128]{1,0:T(8,128)(2,1)}, bf16[384,128]{1,0:T(8,128)(2,1)}, u32[]{:S(2)}, u32[]{:S(2)}) collective-permute-start(bf16[384,128]{1,0:T(8,128)(2,1)} %get-tuple-element.46), channel_id=1, source_target_pairs={{0,48},{8,56},{16,32},{24,40},{32,80},{40,88},{48,64},{56,72},{64,... | collective-permute-start | bytes 294920 | tf_op jit(solution)/shard_map/ppermute | solution.py:412
  93.4 11.9 %collective-permute-start.9 = (bf16[384,128]{1,0:T(8,128)(2,1)}, bf16[384,128]{1,0:T(8,128)(2,1)S(1)}, u32[]{:S(2)}, u32[]{:S(2)}) collective-permute-start(bf16[384,128]{1,0:T(8,128)(2,1)} %get-tuple-element.48), channel_id=1, source_target_pairs={{0,16},{8,24},{16,0},{24,8},{32,48},{40,56},{48,32},{56,40},{64,80... | collective-permute-start | bytes 294920 | tf_op jit(solution)/shard_map/ppermute | solution.py:419
  97.2 10.2 %collective-permute-start.10 = (bf16[384,128]{1,0:T(8,128)(2,1)}, bf16[384,128]{1,0:T(8,128)(2,1)S(1)}, u32[]{:S(2)}, u32[]{:S(2)}) collective-permute-start(bf16[384,128]{1,0:T(8,128)(2,1)} %get-tuple-element.49), channel_id=1, source_target_pairs={{0,32},{8,40},{16,48},{24,56},{32,64},{40,72},{48,80},{56,88},{64,... | collective-permute-start | bytes 294920 | tf_op jit(solution)/shard_map/ppermute | solution.py:419
  99.3 8.0 %collective-permute-start.11 = (bf16[384,128]{1,0:T(8,128)(2,1)}, bf16[384,128]{1,0:T(8,128)(2,1)S(1)}, u32[]{:S(2)}, u32[]{:S(2)}) collective-permute-start(bf16[384,128]{1,0:T(8,128)(2,1)} %get-tuple-element.50), channel_id=1, source_target_pairs={{0,48},{8,56},{16,32},{24,40},{32,80},{40,88},{48,64},{56,72},{64,... | collective-permute-start | bytes 294920 | tf_op jit(solution)/shard_map/ppermute | solution.py:419
  99.3 8.0 %collective-permute-start.12 = (bf16[384,128]{1,0:T(8,128)(2,1)}, bf16[384,128]{1,0:T(8,128)(2,1)S(1)}, u32[]{:S(2)}, u32[]{:S(2)}) collective-permute-start(bf16[384,128]{1,0:T(8,128)(2,1)} %get-tuple-element.51), channel_id=1, source_target_pairs={{0,64},{8,72},{16,80},{24,88},{32,96},{40,104},{48,112},{56,120},{... | collective-permute-start | bytes 294920 | tf_op jit(solution)/shard_map/ppermute | solution.py:419
  100.8 8.7 %collective-permute-start.13 = (bf16[384,128]{1,0:T(8,128)(2,1)}, bf16[384,128]{1,0:T(8,128)(2,1)S(1)}, u32[]{:S(2)}, u32[]{:S(2)}) collective-permute-start(bf16[384,128]{1,0:T(8,128)(2,1)} %get-tuple-element.52), channel_id=1, source_target_pairs={{0,80},{8,88},{16,64},{24,72},{32,112},{40,120},{48,96},{56,104},{... | collective-permute-start | bytes 294920 | tf_op jit(solution)/shard_map/ppermute | solution.py:419
  105.3 6.0 %collective-permute-start.14 = (bf16[384,128]{1,0:T(8,128)(2,1)}, bf16[384,128]{1,0:T(8,128)(2,1)S(1)}, u32[]{:S(2)}, u32[]{:S(2)}) collective-permute-start(bf16[384,128]{1,0:T(8,128)(2,1)} %get-tuple-element.53), channel_id=1, source_target_pairs={{0,96},{8,104},{16,112},{24,120},{32,0},{40,8},{48,16},{56,24},{64... | collective-permute-start | bytes 294920 | tf_op jit(solution)/shard_map/ppermute | solution.py:419
  107.3 8.4 %collective-permute-start.15 = (bf16[384,128]{1,0:T(8,128)(2,1)}, bf16[384,128]{1,0:T(8,128)(2,1)S(1)}, u32[]{:S(2)}, u32[]{:S(2)}) collective-permute-start(bf16[384,128]{1,0:T(8,128)(2,1)} %get-tuple-element.54), channel_id=1, source_target_pairs={{0,112},{8,120},{16,96},{24,104},{32,16},{40,24},{48,0},{56,8},{64... | collective-permute-start | bytes 294920 | tf_op jit(solution)/shard_map/ppermute | solution.py:419
  120.8 28.1 %collective-permute-start.19 = (bf16[512,384]{1,0:T(8,128)(2,1)}, bf16[512,384]{1,0:T(8,128)(2,1)S(1)}, u32[]{:S(2)}, u32[]{:S(2)}) collective-permute-start(bf16[512,384]{1,0:T(8,128)(2,1)} %get-tuple-element.62), channel_id=1, source_target_pairs={{0,1},{1,2},{2,3},{3,0},{4,5},{5,6},{6,7},{7,4},{8,9},{9,10},{10,1... | collective-permute-start | bytes 1179656 | tf_op jit(solution)/shard_map/ppermute | solution.py:426
  122.7 27.6 %collective-permute-start.27 = (bf16[512,384]{1,0:T(8,128)(2,1)}, bf16[512,384]{1,0:T(8,128)(2,1)S(1)}, u32[]{:S(2)}, u32[]{:S(2)}) collective-permute-start(bf16[512,384]{1,0:T(8,128)(2,1)} %get-tuple-element.71), channel_id=1, source_target_pairs={{0,3},{1,0},{2,1},{3,2},{4,7},{5,4},{6,5},{7,6},{8,11},{9,8},{10,9... | collective-permute-start | bytes 1179656 | tf_op jit(solution)/shard_map/ppermute | solution.py:426
  129.1 21.3 %collective-permute-start.16 = (bf16[512,384]{1,0:T(8,128)(2,1)}, bf16[512,384]{1,0:T(8,128)(2,1)S(1)}, u32[]{:S(2)}, u32[]{:S(2)}) collective-permute-start(bf16[512,384]{1,0:T(8,128)(2,1)} %get-tuple-element.58), channel_id=1, source_target_pairs={{0,1},{1,2},{2,3},{3,0},{4,5},{5,6},{6,7},{7,4},{8,9},{9,10},{10,1... | collective-permute-start | bytes 1179656 | tf_op jit(solution)/shard_map/ppermute | solution.py:426
  129.1 41.2 %collective-permute-start.24 = (bf16[512,384]{1,0:T(8,128)(2,1)}, bf16[512,384]{1,0:T(8,128)(2,1)S(1)}, u32[]{:S(2)}, u32[]{:S(2)}) collective-permute-start(bf16[512,384]{1,0:T(8,128)(2,1)} %get-tuple-element.67), channel_id=1, source_target_pairs={{0,3},{1,0},{2,1},{3,2},{4,7},{5,4},{6,5},{7,6},{8,11},{9,8},{10,9... | collective-permute-start | bytes 1179656 | tf_op jit(solution)/shard_map/ppermute | solution.py:426
  140.2 13.7 %collective-permute-start.21 = (bf16[512,384]{1,0:T(8,128)(2,1)}, bf16[512,384]{1,0:T(8,128)(2,1)S(1)}, u32[]{:S(2)}, u32[]{:S(2)}) collective-permute-start(bf16[512,384]{1,0:T(8,128)(2,1)} %get-tuple-element.63), channel_id=1, source_target_pairs={{0,3},{1,0},{2,1},{3,2},{4,7},{5,4},{6,5},{7,6},{8,11},{9,8},{10,9... | collective-permute-start | bytes 1179656 | tf_op jit(solution)/shard_map/ppermute | solution.py:426
  148.8 22.4 %collective-permute-start.26 = (bf16[512,384]{1,0:T(8,128)(2,1)S(1)}, bf16[512,384]{1,0:T(8,128)(2,1)S(1)}, u32[]{:S(2)}, u32[]{:S(2)}) collective-permute-start(bf16[512,384]{1,0:T(8,128)(2,1)S(1)} %copy-done.20), channel_id=1, source_target_pairs={{0,1},{1,2},{2,3},{3,0},{4,5},{5,6},{6,7},{7,4},{8,9},{9,10},{10,1... | collective-permute-start | bytes 1179656 | tf_op jit(solution)/shard_map/ppermute | solution.py:426
  150.2 19.0 %collective-permute-start.20 = (bf16[512,384]{1,0:T(8,128)(2,1)S(1)}, bf16[512,384]{1,0:T(8,128)(2,1)S(1)}, u32[]{:S(2)}, u32[]{:S(2)}) collective-permute-start(bf16[512,384]{1,0:T(8,128)(2,1)S(1)} %add_convert_fusion.6), channel_id=1, source_target_pairs={{0,1},{1,2},{2,3},{3,0},{4,5},{5,6},{6,7},{7,4},{8,9},{9,10},{10,1... | collective-permute-start | bytes 1179656 | tf_op jit(solution)/shard_map/ppermute | solution.py:426
  150.5 24.3 %collective-permute-start.18 = (bf16[512,384]{1,0:T(8,128)(2,1)S(1)}, bf16[512,384]{1,0:T(8,128)(2,1)S(1)}, u32[]{:S(2)}, u32[]{:S(2)}) collective-permute-start(bf16[512,384]{1,0:T(8,128)(2,1)S(1)} %copy-done.19), channel_id=1, source_target_pairs={{0,3},{1,0},{2,1},{3,2},{4,7},{5,4},{6,5},{7,6},{8,11},{9,8},{10,9... | collective-permute-start | bytes 1179656 | tf_op jit(solution)/shard_map/ppermute | solution.py:426
  153.9 20.7 %copy-start.1 = (bf16[512,384]{1,0:T(8,128)(2,1)S(1)}, bf16[512,384]{1,0:T(8,128)(2,1)}, u32[]{:S(2)}) copy-start(bf16[512,384]{1,0:T(8,128)(2,1)} %get-tuple-element.68) | copy-start | bytes 1179652
  153.9 17.5 %collective-permute-start.28 = (bf16[512,384]{1,0:T(8,128)(2,1)S(1)}, bf16[512,384]{1,0:T(8,128)(2,1)S(1)}, u32[]{:S(2)}, u32[]{:S(2)}) collective-permute-start(bf16[512,384]{1,0:T(8,128)(2,1)S(1)} %add_convert_fusion.2), channel_id=1, source_target_pairs={{0,3},{1,0},{2,1},{3,2},{4,7},{5,4},{6,5},{7,6},{8,11},{9,8},{10,9... | collective-permute-start | bytes 1179656 | tf_op jit(solution)/shard_map/ppermute | solution.py:426
  169.2 9.0 %collective-permute-start.17 = (bf16[512,384]{1,0:T(8,128)(2,1)S(1)}, bf16[512,384]{1,0:T(8,128)(2,1)S(1)}, u32[]{:S(2)}, u32[]{:S(2)}) collective-permute-start(bf16[512,384]{1,0:T(8,128)(2,1)S(1)} %add_convert_fusion.7), channel_id=1, source_target_pairs={{0,1},{1,2},{2,3},{3,0},{4,5},{5,6},{6,7},{7,4},{8,9},{9,10},{10,1... | collective-permute-start | bytes 1179656 | tf_op jit(solution)/shard_map/ppermute | solution.py:426
  170.3 7.9 %collective-permute-start.22 = (bf16[512,384]{1,0:T(8,128)(2,1)S(1)}, bf16[512,384]{1,0:T(8,128)(2,1)S(1)}, u32[]{:S(2)}, u32[]{:S(2)}) collective-permute-start(bf16[512,384]{1,0:T(8,128)(2,1)S(1)} %add_convert_fusion.5), channel_id=1, source_target_pairs={{0,4},{1,5},{2,6},{3,7},{4,0},{5,1},{6,2},{7,3},{8,12},{9,13},{10,... | collective-permute-start | bytes 1179656 | tf_op jit(solution)/shard_map/ppermute | solution.py:445
  171.3 11.2 %collective-permute-start.23 = (bf16[512,384]{1,0:T(8,128)(2,1)S(1)}, bf16[512,384]{1,0:T(8,128)(2,1)S(1)}, u32[]{:S(2)}, u32[]{:S(2)}) collective-permute-start(bf16[512,384]{1,0:T(8,128)(2,1)S(1)} %copy-done.18), channel_id=1, source_target_pairs={{0,1},{1,2},{2,3},{3,0},{4,5},{5,6},{6,7},{7,4},{8,9},{9,10},{10,1... | collective-permute-start | bytes 1179656 | tf_op jit(solution)/shard_map/ppermute | solution.py:426
  171.4 11.1 %collective-permute-start.25 = (bf16[512,384]{1,0:T(8,128)(2,1)S(1)}, bf16[512,384]{1,0:T(8,128)(2,1)S(1)}, u32[]{:S(2)}, u32[]{:S(2)}) collective-permute-start(bf16[512,384]{1,0:T(8,128)(2,1)S(1)} %add_convert_fusion.3), channel_id=1, source_target_pairs={{0,3},{1,0},{2,1},{3,2},{4,7},{5,4},{6,5},{7,6},{8,11},{9,8},{10,9... | collective-permute-start | bytes 1179656 | tf_op jit(solution)/shard_map/ppermute | solution.py:426
  174.8 7.9 %collective-permute-start.29 = (bf16[512,384]{1,0:T(8,128)(2,1)S(1)}, bf16[512,384]{1,0:T(8,128)(2,1)S(1)}, u32[]{:S(2)}, u32[]{:S(2)}) collective-permute-start(bf16[512,384]{1,0:T(8,128)(2,1)S(1)} %add_convert_fusion.1), channel_id=1, source_target_pairs={{0,4},{1,5},{2,6},{3,7},{4,0},{5,1},{6,2},{7,3},{8,12},{9,13},{10,... | collective-permute-start | bytes 1179656 | tf_op jit(solution)/shard_map/ppermute | solution.py:445
  (22 other events, 203.1 us)

commit v3 on v2

--- a/solution.py
+++ b/solution.py
@@ -146,41 +146,9 @@
     )(*arrays)
 
 
-def split_queries_kernel(place, query_ref, *outs):
-    for step in range(CHIPS):
-        column = pl.multiple_of(ahead(place[0], place[1], step) * HEAD_DIM, HEAD_DIM)
-        outs[step][...] = query_ref[:, pl.ds(column, HEAD_DIM)]
-
-
-def split_queries(place, query_rows):
-    rows = query_rows.shape[0]
-    return pl.pallas_call(
-        split_queries_kernel,
-        out_shape=[jax.ShapeDtypeStruct((rows, HEAD_DIM), jnp.bfloat16)] * CHIPS,
-        in_specs=[SMEM_SPEC, VMEM_SPEC],
-        out_specs=[VMEM_SPEC] * CHIPS,
-        name="split_queries",
-    )(place, query_rows)
-
-
-def same_place(place):
-    def kernel(place, out):
-        for i in range(place.shape[0]):
-            out[i] = place[i]
-
-    return pl.pallas_call(
-        kernel,
-        out_shape=jax.ShapeDtypeStruct(place.shape, place.dtype),
-        in_specs=[SMEM_SPEC],
-        out_specs=SMEM_SPEC,
-        name="same_place",
-    )(place)
-
-
 def attention_kernel(place, own, other, *refs):
-    queries = refs[:CHIPS]
-    outs = refs[CHIPS : 2 * CHIPS]
-    now, keys, values, top, total, even, odd = refs[2 * CHIPS :]
+    outs = refs[:CHIPS]
+    keys, values, top, total, even, odd = refs[CHIPS:]
     y, x, core = place[0], place[1], place[2]
     step = pl.program_id(0)
     rows = top.shape[0]
@@ -191,22 +159,18 @@
         for i in range(CHIPS):
             keys[i, :, :rows] = own[i, :rows, :].T
             keys[i, :, rows:] = other[i, :rows, :].T
-            values[i, :rows, :HEAD_DIM] = own[i, rows:, :]
+            values[i, :rows, :HEAD_DIM] = own[i, rows : 2 * rows, :]
             values[i, rows:, :HEAD_DIM] = other[i, rows:, :]
             values[i, :, HEAD_DIM:] = ones
-
-    for i in range(CHIPS):
-
-        @pl.when(step == i)
-        def _(i=i):
-            now[...] = queries[i][...]
 
     top[...] = jnp.full_like(top, NEGATIVE)
     total[...] = jnp.zeros_like(total)
     chip = ahead(y, x, step)
 
     def score(held, block):
-        held[...] = jnp.dot(now[...], keys[block], preferred_element_type=jnp.float32)
+        held[...] = jnp.dot(
+            own[chip, 2 * rows :, :], keys[block], preferred_element_type=jnp.float32
+        )
 
     def weigh(held, block, masked):
         scores = held[...]
@@ -255,16 +219,15 @@
             outs[i][...] = result
 
 
-def attention(place, queries, own, other):
-    rows = queries[0].shape[0]
+def attention(place, own, other):
+    rows = own.shape[1] // 3
     return pl.pallas_call(
         attention_kernel,
         grid=(CHIPS,),
         out_shape=[jax.ShapeDtypeStruct((rows, HEAD_DIM), jnp.bfloat16)] * CHIPS,
-        in_specs=[SMEM_SPEC] + [VMEM_SPEC] * (2 + CHIPS),
+        in_specs=[SMEM_SPEC, VMEM_SPEC, VMEM_SPEC],
         out_specs=[VMEM_SPEC] * CHIPS,
         scratch_shapes=[
-            VMEM((rows, HEAD_DIM), jnp.bfloat16),
             VMEM((CHIPS, HEAD_DIM, 2 * rows), jnp.bfloat16),
             VMEM((CHIPS, 2 * rows, 2 * HEAD_DIM), jnp.bfloat16),
             VMEM((rows, HEAD_DIM), jnp.float32),
@@ -276,7 +239,7 @@
             flops=12_000_000_000, bytes_accessed=6_000_000, transcendentals=10_000_000
         ),
         name="attention",
-    )(place, own, other, *queries)
+    )(place, own, other)
 
 
 def project_first(place, pieces, out_weight, x_off, z_off):
@@ -400,21 +363,14 @@
         hyena_key[rows - length :].astype(jnp.float32)
         * hyena_value[rows - length :].astype(jnp.float32)
     ).astype(jnp.bfloat16)
-    pieces = split_heads(key_rows, value_rows)
+    pieces = split_heads(key_rows, value_rows, query_rows)
     own = lax.all_to_all(pieces, "ctx", 0, 0, axis_index_groups=CORE_GROUPS, tiled=True)
     before = shifted(tail, "ctx", 1)
     hyena_out = hyena(
         hyena_query, hyena_key, hyena_value, before, conv_filter, skip_gain
     )
-    query_rows, hyena_out = lax.optimization_barrier((query_rows, hyena_out))
-    asked = split_queries(place, query_rows)
-    came = [asked[0]] + [
-        lax.ppermute(asked[step], "ctx", chip_route(step)) for step in range(1, CHIPS)
-    ]
-    queries = [came[((-(i // 2)) % CHIPS_Y) * 2 + i % 2] for i in range(CHIPS)]
-    place = same_place(place)
-    other = lax.ppermute(own, "ctx", CORE_ROUTE)
-    outs = attention(place, queries, own, other)
+    other = lax.ppermute(own[:, : 2 * rows], "ctx", CORE_ROUTE)
+    outs = attention(place, own, other)
     back = [outs[0]] + [
         lax.ppermute(outs[step], "ctx", chip_route(step)) for step in range(1, CHIPS)
     ]

time: 185 us -> 164 us (0.89)
  the two profiles are of different devices: /device:TPU:24 before, /device:TPU:1 now
where the time goes in v3:
time: 164 us; the launch traced here: 161 us
  Pallas kernels  57.2 us (35%)
  blocking collectives  37.9 us (23%)
  starting transfers between devices  34.5 us (21%)
  waiting for transfers between devices  21.2 us (13%)
  other arithmetic  5.86 us (4%)
  local copies, waits for them, and re-layouts  3.33 us (2%)
    all_to_all x1, blocking collectives, local_step(): lax.all_to_all(pieces, 'ctx', 0, 0, axis_index_groups=CORE_GROUPS, tiled=...  37.9 us
    pallas_call x1, Pallas kernels, attention(): pl.pallas_call(attention_kernel, grid=(CHIPS,), out_shape=[jax.ShapeDtype...  21.6 us
    pallas_call x3, Pallas kernels, project(): pl.pallas_call(kernel, grid_spec=pltpu.PrefetchScalarGridSpec(num_scalar_...  20.1 us
    ppermute x12, waiting for transfers between devices, sent(): return lax.ppermute(block, 'tp', ring_route(step))  18.4 us
    ppermute x12, starting transfers between devices, sent(): return lax.ppermute(block, 'tp', ring_route(step))  15.1 us
    ppermute x7, starting transfers between devices, local_step(): lax.ppermute(outs[step], 'ctx', chip_route(step))  12.3 us
    pallas_call x1, Pallas kernels, hyena(): pl.pallas_call(hyena_kernel, grid=(width // LANES,), out_shape=jax.ShapeD...  8.23 us
    ppermute x1, starting transfers between devices, shifted(): return lax.ppermute(block, axis, route)  4.7 us
  transfers between devices with their start and end apart: 23, of which 5 were waited for; matrix products, arithmetic and copies ran while one was open for 3% of the time, Pallas kernels for 20%

profile of v3, /device:TPU:1, one launch (start us, length us, event | category | flops | bytes accessed | tf_op | source)
XLA Modules:
  0.0 160.9 jit_solution(311424742066753262)
XLA Ops:
  0.6 2.9 %split_heads.1 = bf16[8,1152,128]{2,1,0:T(8,128)(2,1)} custom-call(bf16[384,1024]{1,0:T(8,128)(2,1)} %refs_0_.1, bf16[384,1024]{1,0:T(8,128)(2,1)} %refs_1_.1, bf16[384,1024]{1,0:T(8,128)(2,1)} %refs_2_.1), custom_call_target="tpu_custom_call" | custom-call | tf_op jit(solution)/shard_map/split_heads/pallas_call | solution.py:139
  3.5 37.9 %all_to_all.5.own = bf16[8,1152,128]{2,1,0:T(8,128)(2,1)S(1)} all-to-all(bf16[8,1152,128]{2,1,0:T(8,128)(2,1)} %split_heads.1), channel_id=1, replica_groups={{0,16,32,48,64,80,96,112},{8,24,40,56,72,88,104,120},{1,17,33,49,65,81,..., dimensions={0} | all-to-all | bytes 4718592 | tf_op jit(solution)/shard_map/all_to_all | solution.py:367
  41.4 1.4 slice.12
  43.2 1.8 %collective-permute-start.1 = (bf16[8,768,128]{2,1,0:T(8,128)(2,1)}, bf16[8,768,128]{2,1,0:T(8,128)(2,1)}, u32[]{:S(2)}, u32[]{:S(2)}) collective-permute-start(bf16[8,768,128]{2,1,0:T(8,128)(2,1)} %slice.12), channel_id=1, source_target_pairs={{0,8},{8,0},{16,24},{24,16},{32,40},{40,32},{48,56},{56,48},{64,72... | collective-permute-start | bytes 4718600 | tf_op jit(solution)/shard_map/ppermute | solution.py:372
  45.6 2.8 %collective-permute-done.1.other = bf16[8,768,128]{2,1,0:T(8,128)(2,1)} collective-permute-done((bf16[8,768,128]{2,1,0:T(8,128)(2,1)}, bf16[8,768,128]{2,1,0:T(8,128)(2,1)}, u32[]{:S(2)}, u32[]{:S(2)}) %collective-permute-start.1) | collective-permute-done | bytes 1572896 | tf_op jit(solution)/shard_map/ppermute | solution.py:372
  48.4 21.6 %attention.1 = (bf16[384,128]{1,0:T(8,128)(2,1)}, bf16[384,128]{1,0:T(8,128)(2,1)}, bf16[384,128]{1,0:T(8,128)(2,1)}, bf16[384,128]{1,0:T(8,128)(2,1)}, bf16[384...) custom-call(s32[5]{0:T(128)} %stack.23.place, ...), custom_call_target="tpu_custom_call" | custom-call | flops 12000000000 | bytes 6000000 | tf_op jit(solution)/shard_map/attention/pallas_call | solution.py:224
  70.9 1.1 multiply_convert_fusion
  72.2 2.4 %collective-permute-start.4 = (bf16[384,128]{1,0:T(8,128)(2,1)}, bf16[384,128]{1,0:T(8,128)(2,1)S(1)}, u32[]{:S(2)}, u32[]{:S(2)}) collective-permute-start(bf16[384,128]{1,0:T(8,128)(2,1)} %get-tuple-element.30), channel_id=1, source_target_pairs={{0,48},{8,56},{16,32},{24,40},{32,80},{40,88},{48,64},{56,72},{64,... | collective-permute-start | bytes 294920 | tf_op jit(solution)/shard_map/ppermute | solution.py:375
  74.6 3.4 %collective-permute-start.5 = (bf16[384,128]{1,0:T(8,128)(2,1)}, bf16[384,128]{1,0:T(8,128)(2,1)S(1)}, u32[]{:S(2)}, u32[]{:S(2)}) collective-permute-start(bf16[384,128]{1,0:T(8,128)(2,1)} %get-tuple-element.31), channel_id=1, source_target_pairs={{0,64},{8,72},{16,80},{24,88},{32,96},{40,104},{48,112},{56,120},{... | collective-permute-start | bytes 294920 | tf_op jit(solution)/shard_map/ppermute | solution.py:375
  78.2 2.1 %collective-permute-start.7 = (bf16[384,128]{1,0:T(8,128)(2,1)}, bf16[384,128]{1,0:T(8,128)(2,1)S(1)}, u32[]{:S(2)}, u32[]{:S(2)}) collective-permute-start(bf16[384,128]{1,0:T(8,128)(2,1)} %get-tuple-element.33), channel_id=1, source_target_pairs={{0,96},{8,104},{16,112},{24,120},{32,0},{40,8},{48,16},{56,24},{64... | collective-permute-start | bytes 294920 | tf_op jit(solution)/shard_map/ppermute | solution.py:375
  80.4 3.2 %collective-permute-start.8 = (bf16[384,128]{1,0:T(8,128)(2,1)}, bf16[384,128]{1,0:T(8,128)(2,1)S(1)}, u32[]{:S(2)}, u32[]{:S(2)}) collective-permute-start(bf16[384,128]{1,0:T(8,128)(2,1)} %get-tuple-element.34), channel_id=1, source_target_pairs={{0,112},{8,120},{16,96},{24,104},{32,16},{40,24},{48,0},{56,8},{64... | collective-permute-start | bytes 294920 | tf_op jit(solution)/shard_map/ppermute | solution.py:375
  83.6 0.7 maximum_maximum_fusion.taps
  84.3 4.7 %collective-permute-start = (bf16[128,1024]{1,0:T(8,128)(2,1)S(1)}, bf16[128,1024]{1,0:T(8,128)(2,1)}, u32[]{:S(2)}, u32[]{:S(2)}) collective-permute-start(bf16[128,1024]{1,0:T(8,128)(2,1)S(1)} %multiply_convert_fusion), channel_id=1, source_target_pairs={{0,8},{8,16},{16,24},{24,32},{32,40},{40,48},{48,56},{56,64},{64,7... | collective-permute-start | bytes 786440 | tf_op jit(solution)/shard_map/ppermute | solution.py:24
  89.8 4.4 %project_first.1 = (bf16[384,1024]{1,0:T(8,128)(2,1)}, bf16[512,384]{1,0:T(8,128)(2,1)}, bf16[512,384]{1,0:T(8,128)(2,1)}) custom-call(s32[5]{0:T(128)} %stack.23.place, bf16[8192,1024]{1,0:T(8,128)(2,1)} %weight_ref.7, bf16[384,128]{1,0:T(8,128)(2,1)} %get-tuple-element.27.refs_0_, bf16[384,128]{1,0:T(8,128)(2,1)} %copy-done.9, ...), custom_call_target="tpu_custom_call" | custom-call | flops 805306368 | bytes 2097152 | tf_op jit(solution)/shard_map/project_first/pallas_call | solution.py:271
  94.2 1.6 %collective-permute-start.12 = (bf16[512,384]{1,0:T(8,128)(2,1)}, bf16[512,384]{1,0:T(8,128)(2,1)S(1)}, u32[]{:S(2)}, u32[]{:S(2)}) collective-permute-start(bf16[512,384]{1,0:T(8,128)(2,1)} %get-tuple-element.42), channel_id=1, source_target_pairs={{0,1},{1,2},{2,3},{3,0},{4,5},{5,6},{6,7},{7,4},{8,9},{9,10},{10,1... | collective-permute-start | bytes 1179656 | tf_op jit(solution)/shard_map/ppermute | solution.py:382
  95.8 2.1 %collective-permute-start.20 = (bf16[512,384]{1,0:T(8,128)(2,1)}, bf16[512,384]{1,0:T(8,128)(2,1)S(1)}, u32[]{:S(2)}, u32[]{:S(2)}) collective-permute-start(bf16[512,384]{1,0:T(8,128)(2,1)} %get-tuple-element.51), channel_id=1, source_target_pairs={{0,3},{1,0},{2,1},{3,2},{4,7},{5,4},{6,5},{7,6},{8,11},{9,8},{10,9... | collective-permute-start | bytes 1179656 | tf_op jit(solution)/shard_map/ppermute | solution.py:382
  97.9 4.3 %project.4 = (bf16[512,384]{1,0:T(8,128)(2,1)}, bf16[512,384]{1,0:T(8,128)(2,1)}) custom-call(s32[5]{0:T(128)} %stack.23.place, bf16[8192,1024]{1,0:T(8,128)(2,1)} %weight_ref.7, bf16[384,1024]{1,0:T(8,128)(2,1)} %get-tuple-element.35.attended_ref), custom_call_target="tpu_custom_call" | custom-call | flops 805306368 | bytes 2097152 | tf_op jit(solution)/shard_map/project/pallas_call | solution.py:319
  102.3 2.7 %collective-permute-start.17 = (bf16[512,384]{1,0:T(8,128)(2,1)}, bf16[512,384]{1,0:T(8,128)(2,1)S(1)}, u32[]{:S(2)}, u32[]{:S(2)}) collective-permute-start(bf16[512,384]{1,0:T(8,128)(2,1)} %get-tuple-element.47), channel_id=1, source_target_pairs={{0,3},{1,0},{2,1},{3,2},{4,7},{5,4},{6,5},{7,6},{8,11},{9,8},{10,9... | collective-permute-start | bytes 1179656 | tf_op jit(solution)/shard_map/ppermute | solution.py:382
  105.0 7.8 %project.5 = (bf16[512,384]{1,0:T(8,128)(2,1)}, bf16[512,384]{1,0:T(8,128)(2,1)}, bf16[512,384]{1,0:T(8,128)(2,1)}, bf16[512,384]{1,0:T(8,128)(2,1)}, bf16[512,3...) custom-call(s32[5]{0:T(128)} %stack.23.place, bf16[8192,1024]{1,0:T(8,128)(2,1)} %weight_ref.7, ...), custom_call_target="tpu_custom_call" | custom-call | flops 2415919104 | bytes 6291456 | tf_op jit(solution)/shard_map/project/pallas_call | solution.py:319
  112.8 7.9 %project.3 = (bf16[512,384]{1,0:T(8,128)(2,1)}, bf16[512,384]{1,0:T(8,128)(2,1)}, bf16[512,384]{1,0:T(8,128)(2,1)}, bf16[512,384]{1,0:T(8,128)(2,1)}, bf16[512,3...) custom-call(s32[5]{0:T(128)} %stack.23.place, bf16[8192,1024]{1,0:T(8,128)(2,1)} %weight_ref.7, ...), custom_call_target="tpu_custom_call" | custom-call | flops 2415919104 | bytes 6291456 | tf_op jit(solution)/shard_map/project/pallas_call | solution.py:319
  121.2 1.3 collective-permute-start.19
  122.8 2.7 %collective-permute-start.21 = (bf16[512,384]{1,0:T(8,128)(2,1)S(1)}, bf16[512,384]{1,0:T(8,128)(2,1)S(1)}, u32[]{:S(2)}, u32[]{:S(2)}) collective-permute-start(bf16[512,384]{1,0:T(8,128)(2,1)S(1)} %add_convert_fusion.2), channel_id=1, source_target_pairs={{0,3},{1,0},{2,1},{3,2},{4,7},{5,4},{6,5},{7,6},{8,11},{9,8},{10,9... | collective-permute-start | bytes 1179656 | tf_op jit(solution)/shard_map/ppermute | solution.py:382
  125.7 4.5 %collective-permute-done.14 = bf16[512,384]{1,0:T(8,128)(2,1)S(1)} collective-permute-done((bf16[512,384]{1,0:T(8,128)(2,1)S(1)}, bf16[512,384]{1,0:T(8,128)(2,1)S(1)}, u32[]{:S(2)}, u32[]{:S(2)}) %collective-permute-start.14) | collective-permute-done | bytes 393248 | tf_op jit(solution)/shard_map/ppermute | solution.py:382
  130.2 1.2 collective-permute-start.11
  131.4 8.3 %collective-permute-done.13 = bf16[512,384]{1,0:T(8,128)(2,1)S(1)} collective-permute-done((bf16[512,384]{1,0:T(8,128)(2,1)S(1)}, bf16[512,384]{1,0:T(8,128)(2,1)S(1)}, u32[]{:S(2)}, u32[]{:S(2)}) %collective-permute-start.13) | collective-permute-done | bytes 393248 | tf_op jit(solution)/shard_map/ppermute | solution.py:382
  141.0 2.5 %collective-permute-start.18 = (bf16[512,384]{1,0:T(8,128)(2,1)S(1)}, bf16[512,384]{1,0:T(8,128)(2,1)S(1)}, u32[]{:S(2)}, u32[]{:S(2)}) collective-permute-start(bf16[512,384]{1,0:T(8,128)(2,1)S(1)} %add_convert_fusion.3), channel_id=1, source_target_pairs={{0,3},{1,0},{2,1},{3,2},{4,7},{5,4},{6,5},{7,6},{8,11},{9,8},{10,9... | collective-permute-start | bytes 1179656 | tf_op jit(solution)/shard_map/ppermute | solution.py:382
  143.4 3.7 %collective-permute-done.11 = bf16[512,384]{1,0:T(8,128)(2,1)S(1)} collective-permute-done((bf16[512,384]{1,0:T(8,128)(2,1)S(1)}, bf16[512,384]{1,0:T(8,128)(2,1)S(1)}, u32[]{:S(2)}, u32[]{:S(2)}) %collective-permute-start.11) | collective-permute-done | bytes 393248 | tf_op jit(solution)/shard_map/ppermute | solution.py:382
  147.4 8.2 %hyena.1 = bf16[384,1024]{1,0:T(8,128)(2,1)} custom-call(bf16[384,1024]{1,0:T(8,128)(2,1)} %query.1, bf16[384,1024]{1,0:T(8,128)(2,1)} %key.1, bf16[384,1024]{1,0:T(8,128)(2,1)} %value.1, bf16[128,1024]{1,0:T(8,128)(2,1)} %collective-permute-done.before, f32[64,256]{1,0:T(8,128)} %maximum_maximum_fusion.taps, f32[1,1024]{1,0:T(1,128)} %bitcast.7), custom_call_target="tpu_custom_call" | custom-call | flops 3000000000 | bytes 3000000 | tf_op jit(solution)/shard_map/hyena/pallas_call | solution.py:76
  155.7 1.8 %collective-permute-done.10 = bf16[512,384]{1,0:T(8,128)(2,1)S(1)} collective-permute-done((bf16[512,384]{1,0:T(8,128)(2,1)S(1)}, bf16[512,384]{1,0:T(8,128)(2,1)S(1)}, u32[]{:S(2)}, u32[]{:S(2)}) %collective-permute-start.10) | collective-permute-done | bytes 393248 | tf_op jit(solution)/shard_map/ppermute | solution.py:382
  157.5 1.2 add_convert_fusion.4
  158.7 1.2 add_convert_fusion
  159.9 1.0 pad_maximum_fusion
  (80 shorter events, 5.6 us)
Async XLA Ops:
  43.2 5.2 %collective-permute-start.1 = (bf16[8,768,128]{2,1,0:T(8,128)(2,1)}, bf16[8,768,128]{2,1,0:T(8,128)(2,1)}, u32[]{:S(2)}, u32[]{:S(2)}) collective-permute-start(bf16[8,768,128]{2,1,0:T(8,128)(2,1)} %slice.12), channel_id=1, source_target_pairs={{0,8},{8,0},{16,24},{24,16},{32,40},{40,32},{48,56},{56,48},{64,72... | collective-permute-start | bytes 4718600 | tf_op jit(solution)/shard_map/ppermute | solution.py:372
  45.6 26.5 %copy-start.16 = (bf16[64,128]{1,0:T(8,128)(2,1)S(1)}, bf16[64,128]{1,0:T(8,128)(2,1)}, u32[]{:S(2)}) copy-start(bf16[64,128]{1,0:T(8,128)(2,1)} %param.12) | copy-start | bytes 49156
  70.0 8.2 %collective-permute-start.2 = (bf16[384,128]{1,0:T(8,128)(2,1)}, bf16[384,128]{1,0:T(8,128)(2,1)S(1)}, u32[]{:S(2)}, u32[]{:S(2)}) collective-permute-start(bf16[384,128]{1,0:T(8,128)(2,1)} %get-tuple-element.28), channel_id=1, source_target_pairs={{0,16},{8,24},{16,0},{24,8},{32,48},{40,56},{48,32},{56,40},{64,80... | collective-permute-start | bytes 294920 | tf_op jit(solution)/shard_map/ppermute | solution.py:375
  70.6 9.7 %collective-permute-start.3 = (bf16[384,128]{1,0:T(8,128)(2,1)}, bf16[384,128]{1,0:T(8,128)(2,1)S(1)}, u32[]{:S(2)}, u32[]{:S(2)}) collective-permute-start(bf16[384,128]{1,0:T(8,128)(2,1)} %get-tuple-element.29), channel_id=1, source_target_pairs={{0,32},{8,40},{16,48},{24,56},{32,64},{40,72},{48,80},{56,88},{64,... | collective-permute-start | bytes 294920 | tf_op jit(solution)/shard_map/ppermute | solution.py:375
  72.2 12.1 %collective-permute-start.4 = (bf16[384,128]{1,0:T(8,128)(2,1)}, bf16[384,128]{1,0:T(8,128)(2,1)S(1)}, u32[]{:S(2)}, u32[]{:S(2)}) collective-permute-start(bf16[384,128]{1,0:T(8,128)(2,1)} %get-tuple-element.30), channel_id=1, source_target_pairs={{0,48},{8,56},{16,32},{24,40},{32,80},{40,88},{48,64},{56,72},{64,... | collective-permute-start | bytes 294920 | tf_op jit(solution)/shard_map/ppermute | solution.py:375
  74.6 14.4 %collective-permute-start.5 = (bf16[384,128]{1,0:T(8,128)(2,1)}, bf16[384,128]{1,0:T(8,128)(2,1)S(1)}, u32[]{:S(2)}, u32[]{:S(2)}) collective-permute-start(bf16[384,128]{1,0:T(8,128)(2,1)} %get-tuple-element.31), channel_id=1, source_target_pairs={{0,64},{8,72},{16,80},{24,88},{32,96},{40,104},{48,112},{56,120},{... | collective-permute-start | bytes 294920 | tf_op jit(solution)/shard_map/ppermute | solution.py:375
  77.9 11.1 %collective-permute-start.6 = (bf16[384,128]{1,0:T(8,128)(2,1)}, bf16[384,128]{1,0:T(8,128)(2,1)S(1)}, u32[]{:S(2)}, u32[]{:S(2)}) collective-permute-start(bf16[384,128]{1,0:T(8,128)(2,1)} %get-tuple-element.32), channel_id=1, source_target_pairs={{0,80},{8,88},{16,64},{24,72},{32,112},{40,120},{48,96},{56,104},{... | collective-permute-start | bytes 294920 | tf_op jit(solution)/shard_map/ppermute | solution.py:375
  78.2 10.9 %copy-start.9 = (bf16[384,128]{1,0:T(8,128)(2,1)}, bf16[384,128]{1,0:T(8,128)(2,1)S(1)}, u32[]{:S(2)}) copy-start(bf16[384,128]{1,0:T(8,128)(2,1)S(1)} %collective-permute-done.2.refs_1_) | copy-start | bytes 294916
  78.2 10.8 %collective-permute-start.7 = (bf16[384,128]{1,0:T(8,128)(2,1)}, bf16[384,128]{1,0:T(8,128)(2,1)S(1)}, u32[]{:S(2)}, u32[]{:S(2)}) collective-permute-start(bf16[384,128]{1,0:T(8,128)(2,1)} %get-tuple-element.33), channel_id=1, source_target_pairs={{0,96},{8,104},{16,112},{24,120},{32,0},{40,8},{48,16},{56,24},{64... | collective-permute-start | bytes 294920 | tf_op jit(solution)/shard_map/ppermute | solution.py:375
  80.4 8.8 %copy-start.10 = (bf16[384,128]{1,0:T(8,128)(2,1)}, bf16[384,128]{1,0:T(8,128)(2,1)S(1)}, u32[]{:S(2)}) copy-start(bf16[384,128]{1,0:T(8,128)(2,1)S(1)} %collective-permute-done.3.refs_2_) | copy-start | bytes 294916
  80.4 8.7 %collective-permute-start.8 = (bf16[384,128]{1,0:T(8,128)(2,1)}, bf16[384,128]{1,0:T(8,128)(2,1)S(1)}, u32[]{:S(2)}, u32[]{:S(2)}) collective-permute-start(bf16[384,128]{1,0:T(8,128)(2,1)} %get-tuple-element.34), channel_id=1, source_target_pairs={{0,112},{8,120},{16,96},{24,104},{32,16},{40,24},{48,0},{56,8},{64... | collective-permute-start | bytes 294920 | tf_op jit(solution)/shard_map/ppermute | solution.py:375
  84.3 56.7 %collective-permute-start = (bf16[128,1024]{1,0:T(8,128)(2,1)S(1)}, bf16[128,1024]{1,0:T(8,128)(2,1)}, u32[]{:S(2)}, u32[]{:S(2)}) collective-permute-start(bf16[128,1024]{1,0:T(8,128)(2,1)S(1)} %multiply_convert_fusion), channel_id=1, source_target_pairs={{0,8},{8,16},{16,24},{24,32},{32,40},{40,48},{48,56},{56,64},{64,7... | collective-permute-start | bytes 786440 | tf_op jit(solution)/shard_map/ppermute | solution.py:24
  94.2 27.0 %collective-permute-start.12 = (bf16[512,384]{1,0:T(8,128)(2,1)}, bf16[512,384]{1,0:T(8,128)(2,1)S(1)}, u32[]{:S(2)}, u32[]{:S(2)}) collective-permute-start(bf16[512,384]{1,0:T(8,128)(2,1)} %get-tuple-element.42), channel_id=1, source_target_pairs={{0,1},{1,2},{2,3},{3,0},{4,5},{5,6},{6,7},{7,4},{8,9},{9,10},{10,1... | collective-permute-start | bytes 1179656 | tf_op jit(solution)/shard_map/ppermute | solution.py:382
  95.8 24.9 %collective-permute-start.20 = (bf16[512,384]{1,0:T(8,128)(2,1)}, bf16[512,384]{1,0:T(8,128)(2,1)S(1)}, u32[]{:S(2)}, u32[]{:S(2)}) collective-permute-start(bf16[512,384]{1,0:T(8,128)(2,1)} %get-tuple-element.51), channel_id=1, source_target_pairs={{0,3},{1,0},{2,1},{3,2},{4,7},{5,4},{6,5},{7,6},{8,11},{9,8},{10,9... | collective-permute-start | bytes 1179656 | tf_op jit(solution)/shard_map/ppermute | solution.py:382
  102.3 20.5 %collective-permute-start.9 = (bf16[512,384]{1,0:T(8,128)(2,1)}, bf16[512,384]{1,0:T(8,128)(2,1)S(1)}, u32[]{:S(2)}, u32[]{:S(2)}) collective-permute-start(bf16[512,384]{1,0:T(8,128)(2,1)} %get-tuple-element.38), channel_id=1, source_target_pairs={{0,1},{1,2},{2,3},{3,0},{4,5},{5,6},{6,7},{7,4},{8,9},{9,10},{10,1... | collective-permute-start | bytes 1179656 | tf_op jit(solution)/shard_map/ppermute | solution.py:382
  102.3 20.3 %collective-permute-start.17 = (bf16[512,384]{1,0:T(8,128)(2,1)}, bf16[512,384]{1,0:T(8,128)(2,1)S(1)}, u32[]{:S(2)}, u32[]{:S(2)}) collective-permute-start(bf16[512,384]{1,0:T(8,128)(2,1)} %get-tuple-element.47), channel_id=1, source_target_pairs={{0,3},{1,0},{2,1},{3,2},{4,7},{5,4},{6,5},{7,6},{8,11},{9,8},{10,9... | collective-permute-start | bytes 1179656 | tf_op jit(solution)/shard_map/ppermute | solution.py:382
  112.8 8.3 %copy-start.6 = (bf16[512,384]{1,0:T(8,128)(2,1)S(1)}, bf16[512,384]{1,0:T(8,128)(2,1)}, u32[]{:S(2)}) copy-start(bf16[512,384]{1,0:T(8,128)(2,1)} %get-tuple-element.50) | copy-start | bytes 1179652
  112.8 8.4 %copy-start.18 = (bf16[512,384]{1,0:T(8,128)(2,1)S(1)}, bf16[512,384]{1,0:T(8,128)(2,1)}, u32[]{:S(2)}) copy-start(bf16[512,384]{1,0:T(8,128)(2,1)} %get-tuple-element.49) | copy-start | bytes 1179652
  112.8 9.7 %copy-start.5 = (bf16[512,384]{1,0:T(8,128)(2,1)S(1)}, bf16[512,384]{1,0:T(8,128)(2,1)}, u32[]{:S(2)}) copy-start(bf16[512,384]{1,0:T(8,128)(2,1)} %get-tuple-element.41) | copy-start | bytes 1179652
  120.7 9.4 %collective-permute-start.14 = (bf16[512,384]{1,0:T(8,128)(2,1)S(1)}, bf16[512,384]{1,0:T(8,128)(2,1)S(1)}, u32[]{:S(2)}, u32[]{:S(2)}) collective-permute-start(bf16[512,384]{1,0:T(8,128)(2,1)S(1)} %copy-done.19), channel_id=1, source_target_pairs={{0,3},{1,0},{2,1},{3,2},{4,7},{5,4},{6,5},{7,6},{8,11},{9,8},{10,9... | collective-permute-start | bytes 1179656 | tf_op jit(solution)/shard_map/ppermute | solution.py:382
  121.2 18.9 %collective-permute-start.19 = (bf16[512,384]{1,0:T(8,128)(2,1)S(1)}, bf16[512,384]{1,0:T(8,128)(2,1)S(1)}, u32[]{:S(2)}, u32[]{:S(2)}) collective-permute-start(bf16[512,384]{1,0:T(8,128)(2,1)S(1)} %copy-done.18), channel_id=1, source_target_pairs={{0,1},{1,2},{2,3},{3,0},{4,5},{5,6},{6,7},{7,4},{8,9},{9,10},{10,1... | collective-permute-start | bytes 1179656 | tf_op jit(solution)/shard_map/ppermute | solution.py:382
  122.5 17.5 %copy-start.2 = (bf16[512,384]{1,0:T(8,128)(2,1)S(1)}, bf16[512,384]{1,0:T(8,128)(2,1)}, u32[]{:S(2)}) copy-start(bf16[512,384]{1,0:T(8,128)(2,1)} %get-tuple-element.40) | copy-start | bytes 1179652
  122.6 17.1 %collective-permute-start.13 = (bf16[512,384]{1,0:T(8,128)(2,1)S(1)}, bf16[512,384]{1,0:T(8,128)(2,1)S(1)}, u32[]{:S(2)}, u32[]{:S(2)}) collective-permute-start(bf16[512,384]{1,0:T(8,128)(2,1)S(1)} %add_convert_fusion.6), channel_id=1, source_target_pairs={{0,1},{1,2},{2,3},{3,0},{4,5},{5,6},{6,7},{7,4},{8,9},{9,10},{10,1... | collective-permute-start | bytes 1179656 | tf_op jit(solution)/shard_map/ppermute | solution.py:382
  122.8 18.0 %copy-start.1 = (bf16[512,384]{1,0:T(8,128)(2,1)S(1)}, bf16[512,384]{1,0:T(8,128)(2,1)}, u32[]{:S(2)}) copy-start(bf16[512,384]{1,0:T(8,128)(2,1)} %get-tuple-element.48) | copy-start | bytes 1179652
  122.8 17.7 %collective-permute-start.21 = (bf16[512,384]{1,0:T(8,128)(2,1)S(1)}, bf16[512,384]{1,0:T(8,128)(2,1)S(1)}, u32[]{:S(2)}, u32[]{:S(2)}) collective-permute-start(bf16[512,384]{1,0:T(8,128)(2,1)S(1)} %add_convert_fusion.2), channel_id=1, source_target_pairs={{0,3},{1,0},{2,1},{3,2},{4,7},{5,4},{6,5},{7,6},{8,11},{9,8},{10,9... | collective-permute-start | bytes 1179656 | tf_op jit(solution)/shard_map/ppermute | solution.py:382
  130.2 17.0 %collective-permute-start.11 = (bf16[512,384]{1,0:T(8,128)(2,1)S(1)}, bf16[512,384]{1,0:T(8,128)(2,1)S(1)}, u32[]{:S(2)}, u32[]{:S(2)}) collective-permute-start(bf16[512,384]{1,0:T(8,128)(2,1)S(1)} %copy-done.17), channel_id=1, source_target_pairs={{0,3},{1,0},{2,1},{3,2},{4,7},{5,4},{6,5},{7,6},{8,11},{9,8},{10,9... | collective-permute-start | bytes 1179656 | tf_op jit(solution)/shard_map/ppermute | solution.py:382
  139.7 19.0 %collective-permute-start.16 = (bf16[512,384]{1,0:T(8,128)(2,1)}, bf16[512,384]{1,0:T(8,128)(2,1)S(1)}, u32[]{:S(2)}, u32[]{:S(2)}) collective-permute-start(bf16[512,384]{1,0:T(8,128)(2,1)} %get-tuple-element.45), channel_id=1, source_target_pairs={{0,1},{1,2},{2,3},{3,0},{4,5},{5,6},{6,7},{7,4},{8,9},{9,10},{10,1... | collective-permute-start | bytes 1179656 | tf_op jit(solution)/shard_map/ppermute | solution.py:382
  140.1 17.3 %collective-permute-start.10 = (bf16[512,384]{1,0:T(8,128)(2,1)S(1)}, bf16[512,384]{1,0:T(8,128)(2,1)S(1)}, u32[]{:S(2)}, u32[]{:S(2)}) collective-permute-start(bf16[512,384]{1,0:T(8,128)(2,1)S(1)} %add_convert_fusion.7), channel_id=1, source_target_pairs={{0,1},{1,2},{2,3},{3,0},{4,5},{5,6},{6,7},{7,4},{8,9},{9,10},{10,1... | collective-permute-start | bytes 1179656 | tf_op jit(solution)/shard_map/ppermute | solution.py:382
  140.5 17.0 %collective-permute-start.15 = (bf16[512,384]{1,0:T(8,128)(2,1)S(1)}, bf16[512,384]{1,0:T(8,128)(2,1)}, u32[]{:S(2)}, u32[]{:S(2)}) collective-permute-start(bf16[512,384]{1,0:T(8,128)(2,1)S(1)} %add_convert_fusion.5), channel_id=1, source_target_pairs={{0,4},{1,5},{2,6},{3,7},{4,0},{5,1},{6,2},{7,3},{8,12},{9,13},{10,... | collective-permute-start | bytes 1179656 | tf_op jit(solution)/shard_map/ppermute | solution.py:401
  141.0 17.7 %collective-permute-start.18 = (bf16[512,384]{1,0:T(8,128)(2,1)S(1)}, bf16[512,384]{1,0:T(8,128)(2,1)S(1)}, u32[]{:S(2)}, u32[]{:S(2)}) collective-permute-start(bf16[512,384]{1,0:T(8,128)(2,1)S(1)} %add_convert_fusion.3), channel_id=1, source_target_pairs={{0,3},{1,0},{2,1},{3,2},{4,7},{5,4},{6,5},{7,6},{8,11},{9,8},{10,9... | collective-permute-start | bytes 1179656 | tf_op jit(solution)/shard_map/ppermute | solution.py:382
  147.1 11.6 %collective-permute-start.22 = (bf16[512,384]{1,0:T(8,128)(2,1)S(1)}, bf16[512,384]{1,0:T(8,128)(2,1)}, u32[]{:S(2)}, u32[]{:S(2)}) collective-permute-start(bf16[512,384]{1,0:T(8,128)(2,1)S(1)} %add_convert_fusion.1), channel_id=1, source_target_pairs={{0,4},{1,5},{2,6},{3,7},{4,0},{5,1},{6,2},{7,3},{8,12},{9,13},{10,... | collective-permute-start | bytes 1179656 | tf_op jit(solution)/shard_map/ppermute | solution.py:401
  147.4 10.1 %copy-start.8 = (bf16[512,384]{1,0:T(8,128)(2,1)S(1)}, bf16[512,384]{1,0:T(8,128)(2,1)}, u32[]{:S(2)}) copy-start(bf16[512,384]{1,0:T(8,128)(2,1)} %get-tuple-element.36) | copy-start | bytes 1179652
  (11 other events, 34.5 us)

commit v4 on v3

--- a/solution.py
+++ b/solution.py
@@ -27,21 +27,16 @@
 LANES = 128
 
 
-def hyena_kernel(query, key, value, before, taps, gain, out, product):
-    length = before.shape[0]
-    rows = query.shape[0]
+def gated_blocks(query, taps, gain, out, product, first_row):
+    length = taps.shape[1] // 2
     groups = taps.shape[0]
-    product[:length, :] = before[...]
-    product[length:, :] = (
-        key[...].astype(jnp.float32) * value[...].astype(jnp.float32)
-    ).astype(jnp.bfloat16)
     tables = []
     for group in range(groups):
         row = jnp.broadcast_to(taps[group : group + 1, :], (length, 2 * length))
         tables.append(pltpu.roll(row, 0, 1, stride=1, stride_axis=0).astype(jnp.bfloat16))
     table = jnp.concatenate(tables, axis=0)
     lane_group = lax.broadcasted_iota(jnp.int32, (length, LANES), 1) // (LANES // groups)
-    for first in range(0, rows, length):
+    for first in range(0, product.shape[0] - length, length):
         spread = jnp.dot(
             table, product[first : first + 2 * length, :], preferred_element_type=jnp.float32
         )
@@ -50,18 +45,34 @@
             convolved = jnp.where(
                 lane_group == group, spread[group * length : (group + 1) * length], convolved
             )
-        here = slice(first, first + length)
+        here = slice(first_row + first, first_row + first + length)
         current = product[first + length : first + 2 * length, :].astype(jnp.float32)
         out[here, :] = (
             query[here, :].astype(jnp.float32) * (convolved + gain[...] * current)
         ).astype(jnp.bfloat16)
 
 
-def hyena(hyena_query, hyena_key, hyena_value, before, conv_filter, skip_gain):
-    rows, width = hyena_query.shape
+def rounded_product(left, right):
+    return (left.astype(jnp.float32) * right.astype(jnp.float32)).astype(jnp.bfloat16)
+
+
+def inner_kernel(query, key, value, taps, gain, out, product):
+    length = taps.shape[1] // 2
+    product[...] = rounded_product(key[...], value[...])
+    out[:length, :] = query[:length, :]
+    gated_blocks(query, taps, gain, out, product, length)
+
+
+def edge_kernel(query, key, value, before, taps, gain, unused, out, product):
+    length = before.shape[0]
+    product[:length, :] = before[...]
+    product[length:, :] = rounded_product(key[...], value[...])
+    gated_blocks(query, taps, gain, out, product, 0)
+
+
+def spread_taps(conv_filter):
     groups, length = conv_filter.shape
-    share = groups * LANES // width
-    taps = jnp.concatenate(
+    return jnp.concatenate(
         [
             jnp.zeros((groups, 1), jnp.float32),
             conv_filter[:, ::-1].astype(jnp.float32),
@@ -70,28 +81,48 @@
         axis=1,
     )
 
-    def columns(height):
-        return pl.BlockSpec((height, LANES), lambda i: (0, i))
-
-    return pl.pallas_call(
-        hyena_kernel,
-        grid=(width // LANES,),
+
+def columns(height):
+    return pl.BlockSpec((height, LANES), lambda i: (0, i))
+
+
+def hyena_inner(hyena_query, hyena_key, hyena_value, taps, gain):
+    rows, width = hyena_query.shape
+    steps = width // LANES
+    tap_spec = pl.BlockSpec((taps.shape[0] // steps, taps.shape[1]), lambda i: (i, 0))
+    return pl.pallas_call(
+        inner_kernel,
+        grid=(steps,),
         out_shape=jax.ShapeDtypeStruct((rows, width), jnp.bfloat16),
-        in_specs=[
-            columns(rows),
-            columns(rows),
-            columns(rows),
-            columns(length),
-            pl.BlockSpec((share, 2 * length), lambda i: (i, 0)),
-            columns(1),
-        ],
+        in_specs=[columns(rows)] * 3 + [tap_spec, columns(1)],
         out_specs=columns(rows),
-        scratch_shapes=[VMEM((rows + length, LANES), jnp.bfloat16)],
+        scratch_shapes=[VMEM((rows, LANES), jnp.bfloat16)],
         cost_estimate=pl.CostEstimate(
             flops=3_000_000_000, bytes_accessed=3_000_000, transcendentals=0
         ),
-        name="hyena",
-    )(hyena_query, hyena_key, hyena_value, before, taps, skip_gain[None, :])
+        name="hyena_inner",
+    )(hyena_query, hyena_key, hyena_value, taps, gain)
+
+
+def hyena_edge(hyena_query, hyena_key, hyena_value, before, taps, gain, inner):
+    rows, width = hyena_query.shape
+    length = before.shape[0]
+    steps = width // LANES
+    tap_spec = pl.BlockSpec((taps.shape[0] // steps, taps.shape[1]), lambda i: (i, 0))
+    return pl.pallas_call(
+        edge_kernel,
+        grid=(steps,),
+        out_shape=jax.ShapeDtypeStruct((rows, width), jnp.bfloat16),
+        in_specs=[columns(length)] * 4
+        + [tap_spec, columns(1), pl.BlockSpec(memory_space=pl.ANY)],
+        out_specs=columns(length),
+        scratch_shapes=[VMEM((2 * length, LANES), jnp.bfloat16)],
+        input_output_aliases={6: 0},
+        cost_estimate=pl.CostEstimate(
+            flops=1_500_000_000, bytes_accessed=1_000_000, transcendentals=0
+        ),
+        name="hyena_edge",
+    )(hyena_query, hyena_key, hyena_value, before, taps, gain, inner)
 
 
 def chip_route(step):
@@ -251,7 +282,7 @@
         return (((place[3] + x_off) & 1) * RING + ((place[4] + z_off) & 3), 0)
 
     def kernel(place, weight_ref, *refs):
-        joined, lower, upper = refs[CHIPS:]
+        joined, block = refs[CHIPS:]
         for step in range(CHIPS):
             column = pl.multiple_of(behind(place[0], place[1], step) * HEAD_DIM, HEAD_DIM)
             joined[:, pl.ds(column, HEAD_DIM)] = refs[step][...]
@@ -261,9 +292,7 @@
             (((1,), (1,)), ((), ())),
             preferred_element_type=jnp.float32,
         )
-        piece = piece.astype(jnp.bfloat16).T
-        lower[...] = piece[: share // 2]
-        upper[...] = piece[share // 2 :]
+        block[...] = piece.astype(jnp.bfloat16).T
 
     def whole(height, width):
         return pl.BlockSpec((height, width), lambda step, place: (0, 0))
@@ -275,10 +304,12 @@
             grid=(1,),
             in_specs=[pl.BlockSpec((share, features), weight_block)]
             + [whole(rows, HEAD_DIM)] * CHIPS,
-            out_specs=[whole(rows, features)] + [whole(share // 2, rows)] * 2,
-        ),
-        out_shape=[jax.ShapeDtypeStruct((rows, features), jnp.bfloat16)]
-        + [jax.ShapeDtypeStruct((share // 2, rows), jnp.bfloat16)] * 2,
+            out_specs=[whole(rows, features), whole(share, rows)],
+        ),
+        out_shape=[
+            jax.ShapeDtypeStruct((rows, features), jnp.bfloat16),
+            jax.ShapeDtypeStruct((share, rows), jnp.bfloat16),
+        ],
         cost_estimate=pl.CostEstimate(
             flops=2 * share * rows * features,
             bytes_accessed=share * features * 2,
@@ -292,10 +323,11 @@
     rows, features = attended.shape
     share = out_weight.shape[0] // (2 * RING)
     count = len(wanted)
+    heights = [share // parts for _, _, parts in wanted for _ in range(parts)]
 
     def weight_block(step, place):
         index = jnp.int32(0)
-        for i, (x_off, z_off) in enumerate(wanted):
+        for i, (x_off, z_off, _) in enumerate(wanted):
             block = ((place[3] + x_off) & 1) * RING + ((place[4] + z_off) & 3)
             index = jnp.where(step == i, block, index)
         return (index, 0)
@@ -308,14 +340,17 @@
             preferred_element_type=jnp.float32,
         )
         piece = piece.astype(jnp.bfloat16).T
-        for i in range(count):
+        at = 0
+        for i, (_, _, parts) in enumerate(wanted):
+            mine = outs[at : at + parts]
+            at += parts
 
             @pl.when(pl.program_id(0) == i)
-            def _(i=i):
-                outs[2 * i][...] = piece[: share // 2]
-                outs[2 * i + 1][...] = piece[share // 2 :]
-
-    half = pl.BlockSpec((share // 2, rows), lambda step, place: (0, 0))
+            def _(mine=mine):
+                height = share // len(mine)
+                for part, out in enumerate(mine):
+                    out[...] = piece[part * height : (part + 1) * height]
+
     return pl.pallas_call(
         kernel,
         grid_spec=pltpu.PrefetchScalarGridSpec(
@@ -325,9 +360,11 @@
                 pl.BlockSpec((share, features), weight_block),
                 pl.BlockSpec((rows, features), lambda step, place: (0, 0)),
             ],
-            out_specs=[half] * (2 * count),
-        ),
-        out_shape=[jax.ShapeDtypeStruct((share // 2, rows), jnp.bfloat16)] * (2 * count),
+            out_specs=[
+                pl.BlockSpec((height, rows), lambda step, place: (0, 0)) for height in heights
+            ],
+        ),
+        out_shape=[jax.ShapeDtypeStruct((height, rows), jnp.bfloat16) for height in heights],
         cost_estimate=pl.CostEstimate(
             flops=2 * share * rows * features * count,
             bytes_accessed=share * features * 2 * count,
@@ -366,45 +403,44 @@
     pieces = split_heads(key_rows, value_rows, query_rows)
     own = lax.all_to_all(pieces, "ctx", 0, 0, axis_index_groups=CORE_GROUPS, tiled=True)
     before = shifted(tail, "ctx", 1)
-    hyena_out = hyena(
-        hyena_query, hyena_key, hyena_value, before, conv_filter, skip_gain
-    )
+    taps = spread_taps(conv_filter)
+    gain = skip_gain[None, :]
+    inner = hyena_inner(hyena_query, hyena_key, hyena_value, taps, gain)
+    hyena_out = hyena_edge(hyena_query, hyena_key, hyena_value, before, taps, gain, inner)
     other = lax.ppermute(own[:, : 2 * rows], "ctx", CORE_ROUTE)
     outs = attention(place, own, other)
     back = [outs[0]] + [
         lax.ppermute(outs[step], "ctx", chip_route(step)) for step in range(1, CHIPS)
     ]
-    kept = []
-    handed = None
-    for x_off in (1, 0):
-
-        def sent(block, step):
-            return lax.ppermute(block, "tp", ring_route(step))
-
-        if x_off == 1:
-            attended, *far = project_first(place, back, out_weight, x_off, 2)
-        else:
-            far = project(place, [(x_off, 2)], out_weight, attended)
-        near = project(place, [(x_off, 1), (x_off, 3), (x_off, 0)], out_weight, attended)
-        from_below = sent(far[0], 1)
-        from_above = sent(far[1], -1)
-        below_1 = sent(near[1], 1)
-        above_0 = sent(near[2], -1)
-        up = added(near[0], from_below).astype(jnp.bfloat16)
-        down = added(near[3], from_above).astype(jnp.bfloat16)
-        below_0 = sent(up, 1)
-        above_1 = sent(down, -1)
-        first = added(near[4], below_0, above_0)
-        second = added(near[5], below_1, above_1)
-        if x_off == 1:
-            handed = [
-                lax.ppermute(part.astype(jnp.bfloat16), "tp", PAIR_ROUTE)
-                for part in (first, second)
-            ]
-        else:
-            kept = [first, second]
+
+    def sent(block, step):
+        return lax.ppermute(block, "tp", ring_route(step))
+
+    attended, far = project_first(place, back, out_weight, 1, 2)
+    crossed = lax.ppermute(far, "tp", PAIR_ROUTE)
+    up, down = project(place, [(1, 1, 1), (1, 3, 1)], out_weight, attended)
+    from_below = sent(up, 1)
+    from_above = sent(down, -1)
+    far_0, far_1, up_0, up_1, down_0, down_1, other_own = project(
+        place, [(0, 2, 2), (0, 1, 2), (0, 3, 2), (1, 0, 1)], out_weight, attended
+    )
+    half = far_0.shape[0]
+    first_below = sent(added(far_0, crossed[:half]).astype(jnp.bfloat16), 1)
+    first_above = sent(added(far_1, crossed[half:]).astype(jnp.bfloat16), -1)
+    below_1 = sent(up_1, 1)
+    above_0 = sent(down_0, -1)
+    handed = lax.ppermute(
+        added(other_own, from_below, from_above).astype(jnp.bfloat16), "tp", PAIR_ROUTE
+    )
+    own_0, own_1 = project(place, [(0, 0, 2)], out_weight, attended)
+    below_0 = sent(added(up_0, first_below).astype(jnp.bfloat16), 1)
+    above_1 = sent(added(down_1, first_above).astype(jnp.bfloat16), -1)
     attention_out = jnp.concatenate(
-        [(kept[i] + handed[i].astype(jnp.float32)).astype(jnp.bfloat16) for i in range(2)], axis=0
+        [
+            added(own_0, below_0, above_0, handed[:half]).astype(jnp.bfloat16),
+            added(own_1, below_1, above_1, handed[half:]).astype(jnp.bfloat16),
+        ],
+        axis=0,
     )
     return (hyena_out, attention_out)
 

time: 164 us -> 171 us (1.043)
  the two profiles are of different devices: /device:TPU:1 before, /device:TPU:6 now
where the time goes in v4:
time: 171 us; the launch traced here: 170 us
  Pallas kernels  62.3 us (36%)
  blocking collectives  36 us (21%)
  waiting for transfers between devices  31.4 us (18%)
  starting transfers between devices  28 us (16%)
  other arithmetic  7.01 us (4%)
  local copies, waits for them, and re-layouts  4.49 us (3%)
    all_to_all x1, blocking collectives, local_step(): lax.all_to_all(pieces, 'ctx', 0, 0, axis_index_groups=CORE_GROUPS, tiled=...  36 us
    pallas_call x1, Pallas kernels, attention(): pl.pallas_call(attention_kernel, grid=(CHIPS,), out_shape=[jax.ShapeDtype...  21.6 us
    ppermute x8, waiting for transfers between devices, sent(): return lax.ppermute(block, 'tp', ring_route(step))  21.2 us
    pallas_call x3, Pallas kernels, project(): pl.pallas_call(kernel, grid_spec=pltpu.PrefetchScalarGridSpec(num_scalar_...  19.6 us
    ppermute x7, starting transfers between devices, local_step(): lax.ppermute(outs[step], 'ctx', chip_route(step))  13.3 us
    ppermute x8, starting transfers between devices, sent(): return lax.ppermute(block, 'tp', ring_route(step))  10.8 us
    pallas_call x1, Pallas kernels, hyena_inner(): pl.pallas_call(inner_kernel, grid=(steps,), out_shape=jax.ShapeDtypeStruc...  7.5 us
    ppermute x7, waiting for transfers between devices, local_step(): lax.ppermute(outs[step], 'ctx', chip_route(step))  7.18 us
  transfers between devices with their start and end apart: 19, of which 8 were waited for; matrix products, arithmetic and copies ran while one was open for 3% of the time, Pallas kernels for 20%

profile of v4, /device:TPU:6, one launch (start us, length us, event | category | flops | bytes accessed | tf_op | source)
XLA Modules:
  0.0 170.1 jit_solution(79770610732962426)
XLA Ops:
  0.6 2.9 %split_heads.1 = bf16[8,1152,128]{2,1,0:T(8,128)(2,1)} custom-call(bf16[384,1024]{1,0:T(8,128)(2,1)} %refs_0_.1, bf16[384,1024]{1,0:T(8,128)(2,1)} %refs_1_.1, bf16[384,1024]{1,0:T(8,128)(2,1)} %refs_2_.1), custom_call_target="tpu_custom_call" | custom-call | tf_op jit(solution)/shard_map/split_heads/pallas_call | solution.py:170
  3.5 36.0 %all_to_all.5.own = bf16[8,1152,128]{2,1,0:T(8,128)(2,1)S(1)} all-to-all(bf16[8,1152,128]{2,1,0:T(8,128)(2,1)} %split_heads.1), channel_id=1, replica_groups={{0,16,32,48,64,80,96,112},{8,24,40,56,72,88,104,120},{1,17,33,49,65,81,..., dimensions={0} | all-to-all | bytes 4718592 | tf_op jit(solution)/shard_map/all_to_all | solution.py:404
  39.5 1.3 slice.28
  42.0 3.0 %collective-permute-done.1.other = bf16[8,768,128]{2,1,0:T(8,128)(2,1)S(1)} collective-permute-done((bf16[8,768,128]{2,1,0:T(8,128)(2,1)}, bf16[8,768,128]{2,1,0:T(8,128)(2,1)S(1)}, u32[]{:S(2)}, u32[]{:S(2)}) %collective-permute-start.1) | collective-permute-done | bytes 1572896 | tf_op jit(solution)/shard_map/ppermute | solution.py:410
  45.1 1.1 copy-done.12
  46.2 21.6 %attention.1 = (bf16[384,128]{1,0:T(8,128)(2,1)}, bf16[384,128]{1,0:T(8,128)(2,1)}, bf16[384,128]{1,0:T(8,128)(2,1)}, bf16[384,128]{1,0:T(8,128)(2,1)}, bf16[384...) custom-call(s32[5]{0:T(128)} %stack.23.place, ...), custom_call_target="tpu_custom_call" | custom-call | flops 12000000000 | bytes 6000000 | tf_op jit(solution)/shard_map/attention/pallas_call | solution.py:255
  67.9 3.0 %collective-permute-start.2 = (bf16[384,128]{1,0:T(8,128)(2,1)}, bf16[384,128]{1,0:T(8,128)(2,1)S(1)}, u32[]{:S(2)}, u32[]{:S(2)}) collective-permute-start(bf16[384,128]{1,0:T(8,128)(2,1)} %get-tuple-element.24), channel_id=1, source_target_pairs={{0,16},{8,24},{16,0},{24,8},{32,48},{40,56},{48,32},{56,40},{64,80... | collective-permute-start | bytes 294920 | tf_op jit(solution)/shard_map/ppermute | solution.py:413
  71.6 3.9 %collective-permute-start.5 = (bf16[384,128]{1,0:T(8,128)(2,1)}, bf16[384,128]{1,0:T(8,128)(2,1)S(1)}, u32[]{:S(2)}, u32[]{:S(2)}) collective-permute-start(bf16[384,128]{1,0:T(8,128)(2,1)} %get-tuple-element.27), channel_id=1, source_target_pairs={{0,64},{8,72},{16,80},{24,88},{32,96},{40,104},{48,112},{56,120},{... | collective-permute-start | bytes 294920 | tf_op jit(solution)/shard_map/ppermute | solution.py:413
  75.5 2.4 %collective-permute-start.6 = (bf16[384,128]{1,0:T(8,128)(2,1)}, bf16[384,128]{1,0:T(8,128)(2,1)S(1)}, u32[]{:S(2)}, u32[]{:S(2)}) collective-permute-start(bf16[384,128]{1,0:T(8,128)(2,1)} %get-tuple-element.28), channel_id=1, source_target_pairs={{0,80},{8,88},{16,64},{24,72},{32,112},{40,120},{48,96},{56,104},{... | collective-permute-start | bytes 294920 | tf_op jit(solution)/shard_map/ppermute | solution.py:413
  77.9 2.2 %collective-permute-start.7 = (bf16[384,128]{1,0:T(8,128)(2,1)}, bf16[384,128]{1,0:T(8,128)(2,1)S(1)}, u32[]{:S(2)}, u32[]{:S(2)}) collective-permute-start(bf16[384,128]{1,0:T(8,128)(2,1)} %get-tuple-element.29), channel_id=1, source_target_pairs={{0,96},{8,104},{16,112},{24,120},{32,0},{40,8},{48,16},{56,24},{64... | collective-permute-start | bytes 294920 | tf_op jit(solution)/shard_map/ppermute | solution.py:413
  82.1 2.5 %collective-permute-done.6.refs_5_ = bf16[384,128]{1,0:T(8,128)(2,1)S(1)} collective-permute-done((bf16[384,128]{1,0:T(8,128)(2,1)}, bf16[384,128]{1,0:T(8,128)(2,1)S(1)}, u32[]{:S(2)}, u32[]{:S(2)}) %collective-permute-start.6) | collective-permute-done | bytes 98336 | tf_op jit(solution)/shard_map/ppermute | solution.py:413
  84.6 3.7 %collective-permute-done.8.refs_7_ = bf16[384,128]{1,0:T(8,128)(2,1)S(1)} collective-permute-done((bf16[384,128]{1,0:T(8,128)(2,1)}, bf16[384,128]{1,0:T(8,128)(2,1)S(1)}, u32[]{:S(2)}, u32[]{:S(2)}) %collective-permute-start.8) | collective-permute-done | bytes 98336 | tf_op jit(solution)/shard_map/ppermute | solution.py:413
  89.0 4.6 %project_first.1 = (bf16[384,1024]{1,0:T(8,128)(2,1)}, bf16[1024,384]{1,0:T(8,128)(2,1)}) custom-call(s32[5]{0:T(128)} %stack.23.place, bf16[8192,1024]{1,0:T(8,128)(2,1)} %weight_ref.7, bf16[384,128]{1,0:T(8,128)(2,1)} %get-tuple-element.23.refs_0_, bf16[384,128]{1,0:T(8,128)(2,1)} %copy-done.4, bf16[384,128]{1,0:T(8,128)(2,1)} %copy-done.5, ...), custom_call_target="tpu_custom_call" | custom-call | flops 805306368 | bytes 2097152 | tf_op jit(solution)/shard_map/project_first/pallas_call | solution.py:300
  94.1 1.8 %multiply_convert_fusion = bf16[128,1024]{1,0:T(8,128)(2,1)} fusion(bf16[384,1024]{1,0:T(8,128)(2,1)} %value.3, bf16[384,1024]{1,0:T(8,128)(2,1)} %key.3), kind=kLoop, calls=%fused_computation.8 | loop fusion | flops 524288 | bytes 786432 | tf_op jit(solution)/shard_map/convert_element_type | solution.py:402
  95.9 1.9 %collective-permute-start = (bf16[128,1024]{1,0:T(8,128)(2,1)}, bf16[128,1024]{1,0:T(8,128)(2,1)}, u32[]{:S(2)}, u32[]{:S(2)}) collective-permute-start(bf16[128,1024]{1,0:T(8,128)(2,1)} %multiply_convert_fusion), channel_id=1, source_target_pairs={{0,8},{8,16},{16,24},{24,32},{32,40},{40,48},{48,56},{56,64},{64,7... | collective-permute-start | bytes 786440 | tf_op jit(solution)/shard_map/ppermute | solution.py:24
  98.0 6.0 %project.5 = (bf16[1024,384]{1,0:T(8,128)(2,1)}, bf16[1024,384]{1,0:T(8,128)(2,1)}) custom-call(s32[5]{0:T(128)} %stack.23.place, bf16[8192,1024]{1,0:T(8,128)(2,1)} %weight_ref.7, bf16[384,1024]{1,0:T(8,128)(2,1)} %get-tuple-element.31.attended_ref), custom_call_target="tpu_custom_call" | custom-call | flops 1610612736 | bytes 4194304 | tf_op jit(solution)/shard_map/project/pallas_call | solution.py:354
  104.0 1.9 %collective-permute-start.13 = (bf16[1024,384]{1,0:T(8,128)(2,1)}, bf16[1024,384]{1,0:T(8,128)(2,1)S(1)}, u32[]{:S(2)}, u32[]{:S(2)}) collective-permute-start(bf16[1024,384]{1,0:T(8,128)(2,1)} %get-tuple-element.38), channel_id=1, source_target_pairs={{0,1},{1,2},{2,3},{3,0},{4,5},{5,6},{6,7},{7,4},{8,9},{9,10},{10,1... | collective-permute-start | bytes 2359304 | tf_op jit(solution)/shard_map/ppermute | solution.py:417
  105.9 2.1 %collective-permute-start.14 = (bf16[1024,384]{1,0:T(8,128)(2,1)}, bf16[1024,384]{1,0:T(8,128)(2,1)S(1)}, u32[]{:S(2)}, u32[]{:S(2)}) collective-permute-start(bf16[1024,384]{1,0:T(8,128)(2,1)} %get-tuple-element.39), channel_id=1, source_target_pairs={{0,3},{1,0},{2,1},{3,2},{4,7},{5,4},{6,5},{7,6},{8,11},{9,8},{10,9... | collective-permute-start | bytes 2359304 | tf_op jit(solution)/shard_map/ppermute | solution.py:417
  108.0 9.3 %project.4 = (bf16[512,384]{1,0:T(8,128)(2,1)}, bf16[512,384]{1,0:T(8,128)(2,1)}, bf16[512,384]{1,0:T(8,128)(2,1)}, bf16[512,384]{1,0:T(8,128)(2,1)}, bf16[512,3...) custom-call(s32[5]{0:T(128)} %stack.23.place, bf16[8192,1024]{1,0:T(8,128)(2,1)} %weight_ref.7, ...), custom_call_target="tpu_custom_call" | custom-call | flops 3221225472 | bytes 8388608 | tf_op jit(solution)/shard_map/project/pallas_call | solution.py:354
  117.4 1.4 add_convert_fusion.6
  118.8 2.1 %collective-permute-start.17 = (bf16[512,384]{1,0:T(8,128)(2,1)S(1)}, bf16[512,384]{1,0:T(8,128)(2,1)S(1)}, u32[]{:S(2)}, u32[]{:S(2)}) collective-permute-start(bf16[512,384]{1,0:T(8,128)(2,1)S(1)} %get-tuple-element.47), channel_id=1, source_target_pairs={{0,3},{1,0},{2,1},{3,2},{4,7},{5,4},{6,5},{7,6},{8,11},{9,8},{10,9... | collective-permute-start | bytes 1179656 | tf_op jit(solution)/shard_map/ppermute | solution.py:417
  122.0 4.2 %collective-permute-done.13 = bf16[1024,384]{1,0:T(8,128)(2,1)S(1)} collective-permute-done((bf16[1024,384]{1,0:T(8,128)(2,1)}, bf16[1024,384]{1,0:T(8,128)(2,1)S(1)}, u32[]{:S(2)}, u32[]{:S(2)}) %collective-permute-start.13) | collective-permute-done | bytes 786464 | tf_op jit(solution)/shard_map/ppermute | solution.py:417
  126.5 2.0 %collective-permute-start.10 = (bf16[512,384]{1,0:T(8,128)(2,1)S(1)}, bf16[512,384]{1,0:T(8,128)(2,1)S(1)}, u32[]{:S(2)}, u32[]{:S(2)}) collective-permute-start(bf16[512,384]{1,0:T(8,128)(2,1)S(1)} %get-tuple-element.46), channel_id=1, source_target_pairs={{0,1},{1,2},{2,3},{3,0},{4,5},{5,6},{6,7},{7,4},{8,9},{9,10},{10,1... | collective-permute-start | bytes 1179656 | tf_op jit(solution)/shard_map/ppermute | solution.py:417
  128.8 6.1 %collective-permute-done.17 = bf16[512,384]{1,0:T(8,128)(2,1)S(1)} collective-permute-done((bf16[512,384]{1,0:T(8,128)(2,1)S(1)}, bf16[512,384]{1,0:T(8,128)(2,1)S(1)}, u32[]{:S(2)}, u32[]{:S(2)}) %collective-permute-start.17) | collective-permute-done | bytes 393248 | tf_op jit(solution)/shard_map/ppermute | solution.py:417
  134.9 1.6 collective-permute-start.15
  136.6 10.7 %collective-permute-done.10 = bf16[512,384]{1,0:T(8,128)(2,1)S(1)} collective-permute-done((bf16[512,384]{1,0:T(8,128)(2,1)S(1)}, bf16[512,384]{1,0:T(8,128)(2,1)S(1)}, u32[]{:S(2)}, u32[]{:S(2)}) %collective-permute-start.10) | collective-permute-done | bytes 393248 | tf_op jit(solution)/shard_map/ppermute | solution.py:417
  147.3 1.1 collective-permute-start.18
  148.6 1.0 collective-permute-start.11
  149.5 7.5 %hyena_inner.1.unused = bf16[384,1024]{1,0:T(8,128)(2,1)} custom-call(bf16[384,1024]{1,0:T(8,128)(2,1)} %query.3, bf16[384,1024]{1,0:T(8,128)(2,1)} %key.3, bf16[384,1024]{1,0:T(8,128)(2,1)} %value.3, f32[64,256]{1,0:T(8,128)} %maximum_maximum_fusion.taps, f32[1,1024]{1,0:T(1,128)} %bitcast.7), custom_call_target="tpu_custom_call" | custom-call | flops 3000000000 | bytes 3000000 | tf_op jit(solution)/shard_map/hyena_inner/pallas_call | solution.py:93
  157.0 6.0 %hyena_edge.1 = bf16[384,1024]{1,0:T(8,128)(2,1)} custom-call(bf16[384,1024]{1,0:T(8,128)(2,1)} %query.3, bf16[384,1024]{1,0:T(8,128)(2,1)} %key.3, bf16[384,1024]{1,0:T(8,128)(2,1)} %value.3, bf16[128,1024]{1,0:T(8,128)(2,1)} %collective-permute-done.before, f32[64,256]{1,0:T(8,128)} %maximum_maximum_fusion.taps, ...), custom_call_target="tpu_custom_call", output_to_operand_aliasing={{}: (6, {})} | custom-call | flops 1500000000 | bytes 1000000 | tf_op jit(solution)/shard_map/hyena_edge/pallas_call | solution.py:112
  163.1 4.4 %project.3 = (bf16[512,384]{1,0:T(8,128)(2,1)}, bf16[512,384]{1,0:T(8,128)(2,1)}) custom-call(s32[5]{0:T(128)} %stack.23.place, bf16[8192,1024]{1,0:T(8,128)(2,1)} %weight_ref.7, bf16[384,1024]{1,0:T(8,128)(2,1)} %get-tuple-element.31.attended_ref), custom_call_target="tpu_custom_call" | custom-call | flops 805306368 | bytes 2097152 | tf_op jit(solution)/shard_map/project/pallas_call | solution.py:354
  167.5 1.6 add_convert_fusion.4
  (56 shorter events, 8.1 us)
Async XLA Ops:
  39.5 1.9 %copy-start = (bf16[8,1152,128]{2,1,0:T(8,128)(2,1)}, bf16[8,1152,128]{2,1,0:T(8,128)(2,1)S(1)}, u32[]{:S(2)}) copy-start(bf16[8,1152,128]{2,1,0:T(8,128)(2,1)S(1)} %all_to_all.5.own) | copy-start | bytes 7077892
  41.5 3.6 %collective-permute-start.1 = (bf16[8,768,128]{2,1,0:T(8,128)(2,1)}, bf16[8,768,128]{2,1,0:T(8,128)(2,1)S(1)}, u32[]{:S(2)}, u32[]{:S(2)}) collective-permute-start(bf16[8,768,128]{2,1,0:T(8,128)(2,1)} %slice.28), channel_id=1, source_target_pairs={{0,8},{8,0},{16,24},{24,16},{32,40},{40,32},{48,56},{56,48},{64,72... | collective-permute-start | bytes 4718600 | tf_op jit(solution)/shard_map/ppermute | solution.py:410
  45.1 1.1 copy-start.12
  67.9 10.1 %collective-permute-start.2 = (bf16[384,128]{1,0:T(8,128)(2,1)}, bf16[384,128]{1,0:T(8,128)(2,1)S(1)}, u32[]{:S(2)}, u32[]{:S(2)}) collective-permute-start(bf16[384,128]{1,0:T(8,128)(2,1)} %get-tuple-element.24), channel_id=1, source_target_pairs={{0,16},{8,24},{16,0},{24,8},{32,48},{40,56},{48,32},{56,40},{64,80... | collective-permute-start | bytes 294920 | tf_op jit(solution)/shard_map/ppermute | solution.py:413
  70.8 10.3 %collective-permute-start.3 = (bf16[384,128]{1,0:T(8,128)(2,1)}, bf16[384,128]{1,0:T(8,128)(2,1)S(1)}, u32[]{:S(2)}, u32[]{:S(2)}) collective-permute-start(bf16[384,128]{1,0:T(8,128)(2,1)} %get-tuple-element.25), channel_id=1, source_target_pairs={{0,32},{8,40},{16,48},{24,56},{32,64},{40,72},{48,80},{56,88},{64,... | collective-permute-start | bytes 294920 | tf_op jit(solution)/shard_map/ppermute | solution.py:413
  71.0 11.0 %collective-permute-start.4 = (bf16[384,128]{1,0:T(8,128)(2,1)}, bf16[384,128]{1,0:T(8,128)(2,1)S(1)}, u32[]{:S(2)}, u32[]{:S(2)}) collective-permute-start(bf16[384,128]{1,0:T(8,128)(2,1)} %get-tuple-element.26), channel_id=1, source_target_pairs={{0,48},{8,56},{16,32},{24,40},{32,80},{40,88},{48,64},{56,72},{64,... | collective-permute-start | bytes 294920 | tf_op jit(solution)/shard_map/ppermute | solution.py:413
  71.6 10.4 %collective-permute-start.5 = (bf16[384,128]{1,0:T(8,128)(2,1)}, bf16[384,128]{1,0:T(8,128)(2,1)S(1)}, u32[]{:S(2)}, u32[]{:S(2)}) collective-permute-start(bf16[384,128]{1,0:T(8,128)(2,1)} %get-tuple-element.27), channel_id=1, source_target_pairs={{0,64},{8,72},{16,80},{24,88},{32,96},{40,104},{48,112},{56,120},{... | collective-permute-start | bytes 294920 | tf_op jit(solution)/shard_map/ppermute | solution.py:413
  75.5 9.0 %collective-permute-start.6 = (bf16[384,128]{1,0:T(8,128)(2,1)}, bf16[384,128]{1,0:T(8,128)(2,1)S(1)}, u32[]{:S(2)}, u32[]{:S(2)}) collective-permute-start(bf16[384,128]{1,0:T(8,128)(2,1)} %get-tuple-element.28), channel_id=1, source_target_pairs={{0,80},{8,88},{16,64},{24,72},{32,112},{40,120},{48,96},{56,104},{... | collective-permute-start | bytes 294920 | tf_op jit(solution)/shard_map/ppermute | solution.py:413
  77.9 10.4 %copy-start.4 = (bf16[384,128]{1,0:T(8,128)(2,1)}, bf16[384,128]{1,0:T(8,128)(2,1)S(1)}, u32[]{:S(2)}) copy-start(bf16[384,128]{1,0:T(8,128)(2,1)S(1)} %collective-permute-done.2.refs_1_) | copy-start | bytes 294916
  77.9 6.6 %collective-permute-start.7 = (bf16[384,128]{1,0:T(8,128)(2,1)}, bf16[384,128]{1,0:T(8,128)(2,1)S(1)}, u32[]{:S(2)}, u32[]{:S(2)}) collective-permute-start(bf16[384,128]{1,0:T(8,128)(2,1)} %get-tuple-element.29), channel_id=1, source_target_pairs={{0,96},{8,104},{16,112},{24,120},{32,0},{40,8},{48,16},{56,24},{64... | collective-permute-start | bytes 294920 | tf_op jit(solution)/shard_map/ppermute | solution.py:413
  81.1 7.2 %copy-start.5 = (bf16[384,128]{1,0:T(8,128)(2,1)}, bf16[384,128]{1,0:T(8,128)(2,1)S(1)}, u32[]{:S(2)}) copy-start(bf16[384,128]{1,0:T(8,128)(2,1)S(1)} %collective-permute-done.3.refs_2_) | copy-start | bytes 294916
  81.1 7.2 %collective-permute-start.8 = (bf16[384,128]{1,0:T(8,128)(2,1)}, bf16[384,128]{1,0:T(8,128)(2,1)S(1)}, u32[]{:S(2)}, u32[]{:S(2)}) collective-permute-start(bf16[384,128]{1,0:T(8,128)(2,1)} %get-tuple-element.30), channel_id=1, source_target_pairs={{0,112},{8,120},{16,96},{24,104},{32,16},{40,24},{48,0},{56,8},{64... | collective-permute-start | bytes 294920 | tf_op jit(solution)/shard_map/ppermute | solution.py:413
  82.0 6.3 %copy-start.6 = (bf16[384,128]{1,0:T(8,128)(2,1)}, bf16[384,128]{1,0:T(8,128)(2,1)S(1)}, u32[]{:S(2)}) copy-start(bf16[384,128]{1,0:T(8,128)(2,1)S(1)} %collective-permute-done.4.refs_3_) | copy-start | bytes 294916
  82.0 6.3 %copy-start.7 = (bf16[384,128]{1,0:T(8,128)(2,1)}, bf16[384,128]{1,0:T(8,128)(2,1)S(1)}, u32[]{:S(2)}) copy-start(bf16[384,128]{1,0:T(8,128)(2,1)S(1)} %collective-permute-done.5.refs_4_) | copy-start | bytes 294916
  84.6 3.8 %copy-start.8 = (bf16[384,128]{1,0:T(8,128)(2,1)}, bf16[384,128]{1,0:T(8,128)(2,1)S(1)}, u32[]{:S(2)}) copy-start(bf16[384,128]{1,0:T(8,128)(2,1)S(1)} %collective-permute-done.6.refs_5_) | copy-start | bytes 294916
  84.6 3.8 %copy-start.9 = (bf16[384,128]{1,0:T(8,128)(2,1)}, bf16[384,128]{1,0:T(8,128)(2,1)S(1)}, u32[]{:S(2)}) copy-start(bf16[384,128]{1,0:T(8,128)(2,1)S(1)} %collective-permute-done.7.refs_6_) | copy-start | bytes 294916
  88.3 0.7 copy-start.10
  89.0 8.9 %copy-start.11 = (bf16[64,128]{1,0:T(8,128)(2,1)S(1)}, bf16[64,128]{1,0:T(8,128)(2,1)}, u32[]{:S(2)}) copy-start(bf16[64,128]{1,0:T(8,128)(2,1)} %param.12) | copy-start | bytes 49156
  93.6 23.8 %collective-permute-start.9 = (bf16[1024,384]{1,0:T(8,128)(2,1)}, bf16[1024,384]{1,0:T(8,128)(2,1)S(1)}, u32[]{:S(2)}, u32[]{:S(2)}) collective-permute-start(bf16[1024,384]{1,0:T(8,128)(2,1)} %get-tuple-element.35), channel_id=1, source_target_pairs={{0,4},{1,5},{2,6},{3,7},{4,0},{5,1},{6,2},{7,3},{8,12},{9,13},{10,... | collective-permute-start | bytes 2359304 | tf_op jit(solution)/shard_map/ppermute | solution.py:420
  95.9 52.6 %collective-permute-start = (bf16[128,1024]{1,0:T(8,128)(2,1)}, bf16[128,1024]{1,0:T(8,128)(2,1)}, u32[]{:S(2)}, u32[]{:S(2)}) collective-permute-start(bf16[128,1024]{1,0:T(8,128)(2,1)} %multiply_convert_fusion), channel_id=1, source_target_pairs={{0,8},{8,16},{16,24},{24,32},{32,40},{40,48},{48,56},{56,64},{64,7... | collective-permute-start | bytes 786440 | tf_op jit(solution)/shard_map/ppermute | solution.py:24
  104.0 22.2 %collective-permute-start.13 = (bf16[1024,384]{1,0:T(8,128)(2,1)}, bf16[1024,384]{1,0:T(8,128)(2,1)S(1)}, u32[]{:S(2)}, u32[]{:S(2)}) collective-permute-start(bf16[1024,384]{1,0:T(8,128)(2,1)} %get-tuple-element.38), channel_id=1, source_target_pairs={{0,1},{1,2},{2,3},{3,0},{4,5},{5,6},{6,7},{7,4},{8,9},{9,10},{10,1... | collective-permute-start | bytes 2359304 | tf_op jit(solution)/shard_map/ppermute | solution.py:417
  105.9 20.6 %collective-permute-start.14 = (bf16[1024,384]{1,0:T(8,128)(2,1)}, bf16[1024,384]{1,0:T(8,128)(2,1)S(1)}, u32[]{:S(2)}, u32[]{:S(2)}) collective-permute-start(bf16[1024,384]{1,0:T(8,128)(2,1)} %get-tuple-element.39), channel_id=1, source_target_pairs={{0,3},{1,0},{2,1},{3,2},{4,7},{5,4},{6,5},{7,6},{8,11},{9,8},{10,9... | collective-permute-start | bytes 2359304 | tf_op jit(solution)/shard_map/ppermute | solution.py:417
  117.4 11.1 %copy-start.1 = (bf16[1024,384]{1,0:T(8,128)(2,1)S(1)}, bf16[1024,384]{1,0:T(8,128)(2,1)}, u32[]{:S(2)}) copy-start(bf16[1024,384]{1,0:T(8,128)(2,1)} %get-tuple-element.37) | copy-start | bytes 2359300
  118.8 16.2 %collective-permute-start.17 = (bf16[512,384]{1,0:T(8,128)(2,1)S(1)}, bf16[512,384]{1,0:T(8,128)(2,1)S(1)}, u32[]{:S(2)}, u32[]{:S(2)}) collective-permute-start(bf16[512,384]{1,0:T(8,128)(2,1)S(1)} %get-tuple-element.47), channel_id=1, source_target_pairs={{0,3},{1,0},{2,1},{3,2},{4,7},{5,4},{6,5},{7,6},{8,11},{9,8},{10,9... | collective-permute-start | bytes 1179656 | tf_op jit(solution)/shard_map/ppermute | solution.py:417
  121.6 45.9 %collective-permute-start.12 = (bf16[512,384]{1,0:T(8,128)(2,1)}, bf16[512,384]{1,0:T(8,128)(2,1)S(1)}, u32[]{:S(2)}, u32[]{:S(2)}) collective-permute-start(bf16[512,384]{1,0:T(8,128)(2,1)} %get-tuple-element.36), channel_id=1, source_target_pairs={{0,3},{1,0},{2,1},{3,2},{4,7},{5,4},{6,5},{7,6},{8,11},{9,8},{10,9... | collective-permute-start | bytes 1179656 | tf_op jit(solution)/shard_map/ppermute | solution.py:417
  126.2 41.2 %collective-permute-start.16 = (bf16[512,384]{1,0:T(8,128)(2,1)}, bf16[512,384]{1,0:T(8,128)(2,1)S(1)}, u32[]{:S(2)}, u32[]{:S(2)}) collective-permute-start(bf16[512,384]{1,0:T(8,128)(2,1)} %get-tuple-element.41), channel_id=1, source_target_pairs={{0,1},{1,2},{2,3},{3,0},{4,5},{5,6},{6,7},{7,4},{8,9},{9,10},{10,1... | collective-permute-start | bytes 1179656 | tf_op jit(solution)/shard_map/ppermute | solution.py:417
  126.5 20.8 %collective-permute-start.10 = (bf16[512,384]{1,0:T(8,128)(2,1)S(1)}, bf16[512,384]{1,0:T(8,128)(2,1)S(1)}, u32[]{:S(2)}, u32[]{:S(2)}) collective-permute-start(bf16[512,384]{1,0:T(8,128)(2,1)S(1)} %get-tuple-element.46), channel_id=1, source_target_pairs={{0,1},{1,2},{2,3},{3,0},{4,5},{5,6},{6,7},{7,4},{8,9},{9,10},{10,1... | collective-permute-start | bytes 1179656 | tf_op jit(solution)/shard_map/ppermute | solution.py:417
  128.5 8.0 %copy-start.3 = (bf16[512,384]{1,0:T(8,128)(2,1)S(1)}, bf16[512,384]{1,0:T(8,128)(2,1)}, u32[]{:S(2)}) copy-start(bf16[512,384]{1,0:T(8,128)(2,1)} %get-tuple-element.42) | copy-start | bytes 1179652
  128.5 20.0 %copy-start.2 = (bf16[512,384]{1,0:T(8,128)(2,1)S(1)}, bf16[512,384]{1,0:T(8,128)(2,1)}, u32[]{:S(2)}) copy-start(bf16[512,384]{1,0:T(8,128)(2,1)} %get-tuple-element.33) | copy-start | bytes 1179652
  134.9 32.5 %collective-permute-start.15 = (bf16[1024,384]{1,0:T(8,128)(2,1)S(1)}, bf16[1024,384]{1,0:T(8,128)(2,1)S(1)}, u32[]{:S(2)}, u32[]{:S(2)}) collective-permute-start(bf16[1024,384]{1,0:T(8,128)(2,1)S(1)} %add_convert_fusion), channel_id=1, source_target_pairs={{0,4},{1,5},{2,6},{3,7},{4,0},{5,1},{6,2},{7,3},{8,12},{9,13},{10,... | collective-permute-start | bytes 2359304 | tf_op jit(solution)/shard_map/ppermute | solution.py:432
  147.3 20.1 %collective-permute-start.18 = (bf16[512,384]{1,0:T(8,128)(2,1)S(1)}, bf16[512,384]{1,0:T(8,128)(2,1)S(1)}, u32[]{:S(2)}, u32[]{:S(2)}) collective-permute-start(bf16[512,384]{1,0:T(8,128)(2,1)S(1)} %add_convert_fusion.2), channel_id=1, source_target_pairs={{0,3},{1,0},{2,1},{3,2},{4,7},{5,4},{6,5},{7,6},{8,11},{9,8},{10,9... | collective-permute-start | bytes 1179656 | tf_op jit(solution)/shard_map/ppermute | solution.py:417
  148.6 18.9 %collective-permute-start.11 = (bf16[512,384]{1,0:T(8,128)(2,1)S(1)}, bf16[512,384]{1,0:T(8,128)(2,1)}, u32[]{:S(2)}, u32[]{:S(2)}) collective-permute-start(bf16[512,384]{1,0:T(8,128)(2,1)S(1)} %add_convert_fusion.5), channel_id=1, source_target_pairs={{0,1},{1,2},{2,3},{3,0},{4,5},{5,6},{6,7},{7,4},{8,9},{9,10},{10,1... | collective-permute-start | bytes 1179656 | tf_op jit(solution)/shard_map/ppermute | solution.py:417

commit v5 on v4

--- a/solution.py
+++ b/solution.py
@@ -273,54 +273,9 @@
     )(place, own, other)
 
 
-def project_first(place, pieces, out_weight, x_off, z_off):
-    rows = pieces[0].shape[0]
-    share = out_weight.shape[0] // (2 * RING)
+def project(place, wanted, out_weight, attended=None, pieces=()):
+    rows = (pieces[0] if pieces else attended).shape[0]
     features = out_weight.shape[1]
-
-    def weight_block(step, place):
-        return (((place[3] + x_off) & 1) * RING + ((place[4] + z_off) & 3), 0)
-
-    def kernel(place, weight_ref, *refs):
-        joined, block = refs[CHIPS:]
-        for step in range(CHIPS):
-            column = pl.multiple_of(behind(place[0], place[1], step) * HEAD_DIM, HEAD_DIM)
-            joined[:, pl.ds(column, HEAD_DIM)] = refs[step][...]
-        piece = lax.dot_general(
-            joined[...],
-            weight_ref[...],
-            (((1,), (1,)), ((), ())),
-            preferred_element_type=jnp.float32,
-        )
-        block[...] = piece.astype(jnp.bfloat16).T
-
-    def whole(height, width):
-        return pl.BlockSpec((height, width), lambda step, place: (0, 0))
-
-    return pl.pallas_call(
-        kernel,
-        grid_spec=pltpu.PrefetchScalarGridSpec(
-            num_scalar_prefetch=1,
-            grid=(1,),
-            in_specs=[pl.BlockSpec((share, features), weight_block)]
-            + [whole(rows, HEAD_DIM)] * CHIPS,
-            out_specs=[whole(rows, features), whole(share, rows)],
-        ),
-        out_shape=[
-            jax.ShapeDtypeStruct((rows, features), jnp.bfloat16),
-            jax.ShapeDtypeStruct((share, rows), jnp.bfloat16),
-        ],
-        cost_estimate=pl.CostEstimate(
-            flops=2 * share * rows * features,
-            bytes_accessed=share * features * 2,
-            transcendentals=0,
-        ),
-        name="project_first",
-    )(place, out_weight, *pieces)
-
-
-def project(place, wanted, out_weight, attended):
-    rows, features = attended.shape
     share = out_weight.shape[0] // (2 * RING)
     count = len(wanted)
     heights = [share // parts for _, _, parts in wanted for _ in range(parts)]
@@ -332,9 +287,21 @@
             index = jnp.where(step == i, block, index)
         return (index, 0)
 
-    def kernel(place, weight_ref, attended_ref, *outs):
+    def kernel(place, weight_ref, *refs):
+        if pieces:
+            joined, *outs = refs[CHIPS:]
+
+            @pl.when(pl.program_id(0) == 0)
+            def _():
+                for step in range(CHIPS):
+                    column = behind(place[0], place[1], step) * HEAD_DIM
+                    column = pl.multiple_of(column, HEAD_DIM)
+                    joined[:, pl.ds(column, HEAD_DIM)] = refs[step][...]
+
+        else:
+            joined, *outs = refs
         piece = lax.dot_general(
-            attended_ref[...],
+            joined[...],
             weight_ref[...],
             (((1,), (1,)), ((), ())),
             preferred_element_type=jnp.float32,
@@ -351,27 +318,28 @@
                 for part, out in enumerate(mine):
                     out[...] = piece[part * height : (part + 1) * height]
 
+    def whole(height, width):
+        return pl.BlockSpec((height, width), lambda step, place: (0, 0))
+
+    outs = [((rows, features) if pieces else None)] + [(height, rows) for height in heights]
+    outs = [shape for shape in outs if shape]
+    inputs = [whole(rows, HEAD_DIM)] * CHIPS if pieces else [whole(rows, features)]
     return pl.pallas_call(
         kernel,
         grid_spec=pltpu.PrefetchScalarGridSpec(
             num_scalar_prefetch=1,
             grid=(count,),
-            in_specs=[
-                pl.BlockSpec((share, features), weight_block),
-                pl.BlockSpec((rows, features), lambda step, place: (0, 0)),
-            ],
-            out_specs=[
-                pl.BlockSpec((height, rows), lambda step, place: (0, 0)) for height in heights
-            ],
+            in_specs=[pl.BlockSpec((share, features), weight_block)] + inputs,
+            out_specs=[whole(*shape) for shape in outs],
         ),
-        out_shape=[jax.ShapeDtypeStruct((height, rows), jnp.bfloat16) for height in heights],
+        out_shape=[jax.ShapeDtypeStruct(shape, jnp.bfloat16) for shape in outs],
         cost_estimate=pl.CostEstimate(
             flops=2 * share * rows * features * count,
             bytes_accessed=share * features * 2 * count,
             transcendentals=0,
         ),
         name="project",
-    )(place, out_weight, attended)
+    )(place, out_weight, *(pieces if pieces else (attended,)))
 
 
 def added(*pieces):
@@ -416,9 +384,10 @@
     def sent(block, step):
         return lax.ppermute(block, "tp", ring_route(step))
 
-    attended, far = project_first(place, back, out_weight, 1, 2)
+    attended, far, up, down = project(
+        place, [(1, 2, 1), (1, 1, 1), (1, 3, 1)], out_weight, pieces=back
+    )
     crossed = lax.ppermute(far, "tp", PAIR_ROUTE)
-    up, down = project(place, [(1, 1, 1), (1, 3, 1)], out_weight, attended)
     from_below = sent(up, 1)
     from_above = sent(down, -1)
     far_0, far_1, up_0, up_1, down_0, down_1, other_own = project(
@@ -432,16 +401,15 @@
     handed = lax.ppermute(
         added(other_own, from_below, from_above).astype(jnp.bfloat16), "tp", PAIR_ROUTE
     )
-    own_0, own_1 = project(place, [(0, 0, 2)], out_weight, attended)
+    (kept,) = project(place, [(0, 0, 1)], out_weight, attended)
     below_0 = sent(added(up_0, first_below).astype(jnp.bfloat16), 1)
     above_1 = sent(added(down_1, first_above).astype(jnp.bfloat16), -1)
-    attention_out = jnp.concatenate(
-        [
-            added(own_0, below_0, above_0, handed[:half]).astype(jnp.bfloat16),
-            added(own_1, below_1, above_1, handed[half:]).astype(jnp.bfloat16),
-        ],
-        axis=0,
-    )
+    partial_out = lax.optimization_barrier(
+        added(kept, jnp.concatenate([above_0, below_1], axis=0), handed)
+    )
+    attention_out = (
+        partial_out + jnp.concatenate([below_0, above_1], axis=0).astype(jnp.float32)
+    ).astype(jnp.bfloat16)
     return (hyena_out, attention_out)
 
 

time: 171 us -> 157 us (0.918)
  the two profiles are of different devices: /device:TPU:6 before, /device:TPU:1 now
where the time goes in v5:
time: 157 us; the launch traced here: 156 us
  Pallas kernels  60.4 us (38%)
  starting transfers between devices  38 us (24%)
  blocking collectives  37.9 us (24%)
  other arithmetic  8.1 us (5%)
  waiting for transfers between devices  7.32 us (5%)
  local copies, waits for them, and re-layouts  3.37 us (2%)
    all_to_all x1, blocking collectives, local_step(): lax.all_to_all(pieces, 'ctx', 0, 0, axis_index_groups=CORE_GROUPS, tiled=...  37.9 us
    pallas_call x3, Pallas kernels, project(): pl.pallas_call(kernel, grid_spec=pltpu.PrefetchScalarGridSpec(num_scalar_...  22.3 us
    pallas_call x1, Pallas kernels, attention(): pl.pallas_call(attention_kernel, grid=(CHIPS,), out_shape=[jax.ShapeDtype...  21.6 us
    ppermute x8, starting transfers between devices, sent(): return lax.ppermute(block, 'tp', ring_route(step))  12.4 us
    ppermute x7, starting transfers between devices, local_step(): lax.ppermute(outs[step], 'ctx', chip_route(step))  12.2 us
    ppermute x1, starting transfers between devices, shifted(): return lax.ppermute(block, axis, route)  9.03 us
    pallas_call x1, Pallas kernels, hyena_inner(): pl.pallas_call(inner_kernel, grid=(steps,), out_shape=jax.ShapeDtypeStruc...  7.58 us
    pallas_call x1, Pallas kernels, hyena_edge(): pl.pallas_call(edge_kernel, grid=(steps,), out_shape=jax.ShapeDtypeStruct...  6.03 us
  transfers between devices with their start and end apart: 19, of which 5 were waited for; matrix products, arithmetic and copies ran while one was open for 5% of the time, Pallas kernels for 18%

profile of v5, /device:TPU:1, one launch (start us, length us, event | category | flops | bytes accessed | tf_op | source)
XLA Modules:
  0.0 155.8 jit_solution(5833700393271558497)
XLA Ops:
  0.6 2.9 %split_heads.1 = bf16[8,1152,128]{2,1,0:T(8,128)(2,1)} custom-call(bf16[384,1024]{1,0:T(8,128)(2,1)} %refs_0_.1, bf16[384,1024]{1,0:T(8,128)(2,1)} %refs_1_.1, bf16[384,1024]{1,0:T(8,128)(2,1)} %refs_2_.1), custom_call_target="tpu_custom_call" | custom-call | tf_op jit(solution)/shard_map/split_heads/pallas_call | solution.py:170
  3.5 37.9 %all_to_all.5.own = bf16[8,1152,128]{2,1,0:T(8,128)(2,1)S(1)} all-to-all(bf16[8,1152,128]{2,1,0:T(8,128)(2,1)} %split_heads.1), channel_id=1, replica_groups={{0,16,32,48,64,80,96,112},{8,24,40,56,72,88,104,120},{1,17,33,49,65,81,..., dimensions={0} | all-to-all | bytes 4718592 | tf_op jit(solution)/shard_map/all_to_all | solution.py:372
  41.4 1.4 slice.20
  43.2 1.8 %collective-permute-start.1 = (bf16[8,768,128]{2,1,0:T(8,128)(2,1)}, bf16[8,768,128]{2,1,0:T(8,128)(2,1)}, u32[]{:S(2)}, u32[]{:S(2)}) collective-permute-start(bf16[8,768,128]{2,1,0:T(8,128)(2,1)} %slice.20), channel_id=1, source_target_pairs={{0,8},{8,0},{16,24},{24,16},{32,40},{40,32},{48,56},{56,48},{64,72... | collective-permute-start | bytes 4718600 | tf_op jit(solution)/shard_map/ppermute | solution.py:378
  45.7 2.7 %collective-permute-done.1.other = bf16[8,768,128]{2,1,0:T(8,128)(2,1)} collective-permute-done((bf16[8,768,128]{2,1,0:T(8,128)(2,1)}, bf16[8,768,128]{2,1,0:T(8,128)(2,1)}, u32[]{:S(2)}, u32[]{:S(2)}) %collective-permute-start.1) | collective-permute-done | bytes 1572896 | tf_op jit(solution)/shard_map/ppermute | solution.py:378
  48.4 21.6 %attention.1 = (bf16[384,128]{1,0:T(8,128)(2,1)}, bf16[384,128]{1,0:T(8,128)(2,1)}, bf16[384,128]{1,0:T(8,128)(2,1)}, bf16[384,128]{1,0:T(8,128)(2,1)}, bf16[384...) custom-call(s32[5]{0:T(128)} %stack.23.place, ...), custom_call_target="tpu_custom_call" | custom-call | flops 12000000000 | bytes 6000000 | tf_op jit(solution)/shard_map/attention/pallas_call | solution.py:255
  71.0 2.3 %collective-permute-start.4 = (bf16[384,128]{1,0:T(8,128)(2,1)}, bf16[384,128]{1,0:T(8,128)(2,1)S(1)}, u32[]{:S(2)}, u32[]{:S(2)}) collective-permute-start(bf16[384,128]{1,0:T(8,128)(2,1)} %get-tuple-element.24), channel_id=1, source_target_pairs={{0,48},{8,56},{16,32},{24,40},{32,80},{40,88},{48,64},{56,72},{64,... | collective-permute-start | bytes 294920 | tf_op jit(solution)/shard_map/ppermute | solution.py:381
  73.3 3.4 %collective-permute-start.5 = (bf16[384,128]{1,0:T(8,128)(2,1)}, bf16[384,128]{1,0:T(8,128)(2,1)S(1)}, u32[]{:S(2)}, u32[]{:S(2)}) collective-permute-start(bf16[384,128]{1,0:T(8,128)(2,1)} %get-tuple-element.25), channel_id=1, source_target_pairs={{0,64},{8,72},{16,80},{24,88},{32,96},{40,104},{48,112},{56,120},{... | collective-permute-start | bytes 294920 | tf_op jit(solution)/shard_map/ppermute | solution.py:381
  76.9 2.1 %collective-permute-start.7 = (bf16[384,128]{1,0:T(8,128)(2,1)}, bf16[384,128]{1,0:T(8,128)(2,1)S(1)}, u32[]{:S(2)}, u32[]{:S(2)}) collective-permute-start(bf16[384,128]{1,0:T(8,128)(2,1)} %get-tuple-element.27), channel_id=1, source_target_pairs={{0,96},{8,104},{16,112},{24,120},{32,0},{40,8},{48,16},{56,24},{64... | collective-permute-start | bytes 294920 | tf_op jit(solution)/shard_map/ppermute | solution.py:381
  79.0 3.2 %collective-permute-start.8 = (bf16[384,128]{1,0:T(8,128)(2,1)}, bf16[384,128]{1,0:T(8,128)(2,1)S(1)}, u32[]{:S(2)}, u32[]{:S(2)}) collective-permute-start(bf16[384,128]{1,0:T(8,128)(2,1)} %get-tuple-element.28), channel_id=1, source_target_pairs={{0,112},{8,120},{16,96},{24,104},{32,16},{40,24},{48,0},{56,8},{64... | collective-permute-start | bytes 294920 | tf_op jit(solution)/shard_map/ppermute | solution.py:381
  82.3 1.9 %collective-permute-done.6.refs_5_ = bf16[384,128]{1,0:T(8,128)(2,1)S(1)} collective-permute-done((bf16[384,128]{1,0:T(8,128)(2,1)}, bf16[384,128]{1,0:T(8,128)(2,1)S(1)}, u32[]{:S(2)}, u32[]{:S(2)}) %collective-permute-start.6) | collective-permute-done | bytes 98336 | tf_op jit(solution)/shard_map/ppermute | solution.py:381
  84.2 1.2 collective-permute-done.8.refs_7_
  86.0 8.4 %project.3 = (bf16[384,1024]{1,0:T(8,128)(2,1)}, bf16[1024,384]{1,0:T(8,128)(2,1)}, bf16[1024,384]{1,0:T(8,128)(2,1)}, bf16[1024,384]{1,0:T(8,128)(2,1)}) custom-call(s32[5]{0:T(128)} %stack.23.place, bf16[8192,1024]{1,0:T(8,128)(2,1)} %weight_ref.5, bf16[384,128]{1,0:T(8,128)(2,1)} %get-tuple-element.21.refs_0_, bf16[384,128]{1,0:T(8,128)(2,1)} %copy-done.4, ...), custom_call_target="tpu_custom_call" | custom-call | flops 2415919104 | bytes 6291456 | tf_op jit(solution)/shard_map/project/pallas_call | solution.py:327
  94.5 1.8 %multiply_convert_fusion = bf16[128,1024]{1,0:T(8,128)(2,1)} fusion(bf16[384,1024]{1,0:T(8,128)(2,1)} %value.3, bf16[384,1024]{1,0:T(8,128)(2,1)} %key.3), kind=kLoop, calls=%fused_computation.7 | loop fusion | flops 524288 | bytes 786432 | tf_op jit(solution)/shard_map/convert_element_type | solution.py:370
  96.3 9.0 %collective-permute-start = (bf16[128,1024]{1,0:T(8,128)(2,1)}, bf16[128,1024]{1,0:T(8,128)(2,1)}, u32[]{:S(2)}, u32[]{:S(2)}) collective-permute-start(bf16[128,1024]{1,0:T(8,128)(2,1)} %multiply_convert_fusion), channel_id=1, source_target_pairs={{0,8},{8,16},{16,24},{24,32},{32,40},{40,48},{48,56},{56,64},{64,7... | collective-permute-start | bytes 786440 | tf_op jit(solution)/shard_map/ppermute | solution.py:24
  105.5 1.7 %collective-permute-start.11 = (bf16[1024,384]{1,0:T(8,128)(2,1)}, bf16[1024,384]{1,0:T(8,128)(2,1)S(1)}, u32[]{:S(2)}, u32[]{:S(2)}) collective-permute-start(bf16[1024,384]{1,0:T(8,128)(2,1)} %get-tuple-element.33), channel_id=1, source_target_pairs={{0,1},{1,2},{2,3},{3,0},{4,5},{5,6},{6,7},{7,4},{8,9},{9,10},{10,1... | collective-permute-start | bytes 2359304 | tf_op jit(solution)/shard_map/ppermute | solution.py:385
  107.2 2.2 %collective-permute-start.12 = (bf16[1024,384]{1,0:T(8,128)(2,1)}, bf16[1024,384]{1,0:T(8,128)(2,1)S(1)}, u32[]{:S(2)}, u32[]{:S(2)}) collective-permute-start(bf16[1024,384]{1,0:T(8,128)(2,1)} %get-tuple-element.34), channel_id=1, source_target_pairs={{0,3},{1,0},{2,1},{3,2},{4,7},{5,4},{6,5},{7,6},{8,11},{9,8},{10,9... | collective-permute-start | bytes 2359304 | tf_op jit(solution)/shard_map/ppermute | solution.py:385
  109.4 0.7 maximum_maximum_fusion.taps
  110.1 9.3 %project.5 = (bf16[512,384]{1,0:T(8,128)(2,1)}, bf16[512,384]{1,0:T(8,128)(2,1)}, bf16[512,384]{1,0:T(8,128)(2,1)}, bf16[512,384]{1,0:T(8,128)(2,1)}, bf16[512,3...) custom-call(s32[5]{0:T(128)} %stack.23.place, bf16[8192,1024]{1,0:T(8,128)(2,1)} %weight_ref.5, ...), custom_call_target="tpu_custom_call" | custom-call | flops 3221225472 | bytes 8388608 | tf_op jit(solution)/shard_map/project/pallas_call | solution.py:327
  119.4 1.4 add_convert_fusion.5
  120.9 2.7 %collective-permute-start.17 = (bf16[512,384]{1,0:T(8,128)(2,1)S(1)}, bf16[512,384]{1,0:T(8,128)(2,1)S(1)}, u32[]{:S(2)}, u32[]{:S(2)}) collective-permute-start(bf16[512,384]{1,0:T(8,128)(2,1)S(1)} %get-tuple-element.41), channel_id=1, source_target_pairs={{0,3},{1,0},{2,1},{3,2},{4,7},{5,4},{6,5},{7,6},{8,11},{9,8},{10,9... | collective-permute-start | bytes 1179656 | tf_op jit(solution)/shard_map/ppermute | solution.py:385
  123.6 1.0 collective-permute-done.11
  124.9 2.5 %collective-permute-start.13 = (bf16[1024,384]{1,0:T(8,128)(2,1)S(1)}, bf16[1024,384]{1,0:T(8,128)(2,1)S(1)}, u32[]{:S(2)}, u32[]{:S(2)}) collective-permute-start(bf16[1024,384]{1,0:T(8,128)(2,1)S(1)} %add_convert_fusion.1), channel_id=1, source_target_pairs={{0,4},{1,5},{2,6},{3,7},{4,0},{5,1},{6,2},{7,3},{8,12},{9,13},{10,... | collective-permute-start | bytes 2359304 | tf_op jit(solution)/shard_map/ppermute | solution.py:401
  127.5 7.6 %hyena_inner.1.unused = bf16[384,1024]{1,0:T(8,128)(2,1)} custom-call(bf16[384,1024]{1,0:T(8,128)(2,1)} %query.3, bf16[384,1024]{1,0:T(8,128)(2,1)} %key.3, bf16[384,1024]{1,0:T(8,128)(2,1)} %value.3, f32[64,256]{1,0:T(8,128)} %maximum_maximum_fusion.taps, f32[1,1024]{1,0:T(1,128)} %bitcast.7), custom_call_target="tpu_custom_call" | custom-call | flops 3000000000 | bytes 3000000 | tf_op jit(solution)/shard_map/hyena_inner/pallas_call | solution.py:93
  135.0 1.4 collective-permute-start.10
  136.5 1.6 collective-permute-start.9
  138.0 1.1 add_convert_fusion.4
  139.4 2.7 %collective-permute-start.18 = (bf16[512,384]{1,0:T(8,128)(2,1)S(1)}, bf16[512,384]{1,0:T(8,128)(2,1)S(1)}, u32[]{:S(2)}, u32[]{:S(2)}) collective-permute-start(bf16[512,384]{1,0:T(8,128)(2,1)S(1)} %add_convert_fusion.2), channel_id=1, source_target_pairs={{0,3},{1,0},{2,1},{3,2},{4,7},{5,4},{6,5},{7,6},{8,11},{9,8},{10,9... | collective-permute-start | bytes 1179656 | tf_op jit(solution)/shard_map/ppermute | solution.py:385
  142.1 6.0 %hyena_edge.1 = bf16[384,1024]{1,0:T(8,128)(2,1)} custom-call(bf16[384,1024]{1,0:T(8,128)(2,1)} %query.3, bf16[384,1024]{1,0:T(8,128)(2,1)} %key.3, bf16[384,1024]{1,0:T(8,128)(2,1)} %value.3, bf16[128,1024]{1,0:T(8,128)(2,1)} %collective-permute-done.before, f32[64,256]{1,0:T(8,128)} %maximum_maximum_fusion.taps, ...), custom_call_target="tpu_custom_call", output_to_operand_aliasing={{}: (6, {})} | custom-call | flops 1500000000 | bytes 1000000 | tf_op jit(solution)/shard_map/hyena_edge/pallas_call | solution.py:112
  148.1 4.5 %project.4 = bf16[1024,384]{1,0:T(8,128)(2,1)} custom-call(s32[5]{0:T(128)} %stack.23.place, bf16[8192,1024]{1,0:T(8,128)(2,1)} %weight_ref.5, bf16[384,1024]{1,0:T(8,128)(2,1)} %get-tuple-element.29.refs_0_), custom_call_target="tpu_custom_call" | custom-call | flops 805306368 | bytes 2097152 | tf_op jit(solution)/shard_map/project/pallas_call | solution.py:327
  152.6 1.6 %convert_add_fusion = f32[1024,384]{1,0:T(8,128)S(1)} fusion(bf16[1024,384]{1,0:T(8,128)(2,1)S(1)} %collective-permute-done.13, bf16[1024,384]{1,0:T(8,128)(2,1)} %project.4, bf16[512,384]{1,0:T(8,128)(2,1)} %collective-permute-done.10, bf16[512,384]{1,0:T(8,128)(2,1)} %collective-permute-done.9), kind=kLoop, calls=%fused_computation.1 | loop fusion | flops 3145728 | bytes 3932160 | tf_op jit(solution)/shard_map/add | solution.py:346
  154.7 1.1 add_convert_fusion
  (53 shorter events, 4.3 us)
Async XLA Ops:
  41.4 1.9 %copy-start = (bf16[8,1152,128]{2,1,0:T(8,128)(2,1)}, bf16[8,1152,128]{2,1,0:T(8,128)(2,1)S(1)}, u32[]{:S(2)}) copy-start(bf16[8,1152,128]{2,1,0:T(8,128)(2,1)S(1)} %all_to_all.5.own) | copy-start | bytes 7077892
  43.2 5.2 %collective-permute-start.1 = (bf16[8,768,128]{2,1,0:T(8,128)(2,1)}, bf16[8,768,128]{2,1,0:T(8,128)(2,1)}, u32[]{:S(2)}, u32[]{:S(2)}) collective-permute-start(bf16[8,768,128]{2,1,0:T(8,128)(2,1)} %slice.20), channel_id=1, source_target_pairs={{0,8},{8,0},{16,24},{24,16},{32,40},{40,32},{48,56},{56,48},{64,72... | collective-permute-start | bytes 4718600 | tf_op jit(solution)/shard_map/ppermute | solution.py:378
  70.1 6.8 %collective-permute-start.2 = (bf16[384,128]{1,0:T(8,128)(2,1)}, bf16[384,128]{1,0:T(8,128)(2,1)S(1)}, u32[]{:S(2)}, u32[]{:S(2)}) collective-permute-start(bf16[384,128]{1,0:T(8,128)(2,1)} %get-tuple-element.22), channel_id=1, source_target_pairs={{0,16},{8,24},{16,0},{24,8},{32,48},{40,56},{48,32},{56,40},{64,80... | collective-permute-start | bytes 294920 | tf_op jit(solution)/shard_map/ppermute | solution.py:381
  70.6 8.4 %collective-permute-start.3 = (bf16[384,128]{1,0:T(8,128)(2,1)}, bf16[384,128]{1,0:T(8,128)(2,1)S(1)}, u32[]{:S(2)}, u32[]{:S(2)}) collective-permute-start(bf16[384,128]{1,0:T(8,128)(2,1)} %get-tuple-element.23), channel_id=1, source_target_pairs={{0,32},{8,40},{16,48},{24,56},{32,64},{40,72},{48,80},{56,88},{64,... | collective-permute-start | bytes 294920 | tf_op jit(solution)/shard_map/ppermute | solution.py:381
  71.0 11.3 %collective-permute-start.4 = (bf16[384,128]{1,0:T(8,128)(2,1)}, bf16[384,128]{1,0:T(8,128)(2,1)S(1)}, u32[]{:S(2)}, u32[]{:S(2)}) collective-permute-start(bf16[384,128]{1,0:T(8,128)(2,1)} %get-tuple-element.24), channel_id=1, source_target_pairs={{0,48},{8,56},{16,32},{24,40},{32,80},{40,88},{48,64},{56,72},{64,... | collective-permute-start | bytes 294920 | tf_op jit(solution)/shard_map/ppermute | solution.py:381
  73.3 9.0 %collective-permute-start.5 = (bf16[384,128]{1,0:T(8,128)(2,1)}, bf16[384,128]{1,0:T(8,128)(2,1)S(1)}, u32[]{:S(2)}, u32[]{:S(2)}) collective-permute-start(bf16[384,128]{1,0:T(8,128)(2,1)} %get-tuple-element.25), channel_id=1, source_target_pairs={{0,64},{8,72},{16,80},{24,88},{32,96},{40,104},{48,112},{56,120},{... | collective-permute-start | bytes 294920 | tf_op jit(solution)/shard_map/ppermute | solution.py:381
  76.6 7.6 %collective-permute-start.6 = (bf16[384,128]{1,0:T(8,128)(2,1)}, bf16[384,128]{1,0:T(8,128)(2,1)S(1)}, u32[]{:S(2)}, u32[]{:S(2)}) collective-permute-start(bf16[384,128]{1,0:T(8,128)(2,1)} %get-tuple-element.26), channel_id=1, source_target_pairs={{0,80},{8,88},{16,64},{24,72},{32,112},{40,120},{48,96},{56,104},{... | collective-permute-start | bytes 294920 | tf_op jit(solution)/shard_map/ppermute | solution.py:381
  76.9 8.5 %copy-start.4 = (bf16[384,128]{1,0:T(8,128)(2,1)}, bf16[384,128]{1,0:T(8,128)(2,1)S(1)}, u32[]{:S(2)}) copy-start(bf16[384,128]{1,0:T(8,128)(2,1)S(1)} %collective-permute-done.2.refs_1_) | copy-start | bytes 294916
  76.9 7.3 %collective-permute-start.7 = (bf16[384,128]{1,0:T(8,128)(2,1)}, bf16[384,128]{1,0:T(8,128)(2,1)S(1)}, u32[]{:S(2)}, u32[]{:S(2)}) collective-permute-start(bf16[384,128]{1,0:T(8,128)(2,1)} %get-tuple-element.27), channel_id=1, source_target_pairs={{0,96},{8,104},{16,112},{24,120},{32,0},{40,8},{48,16},{56,24},{64... | collective-permute-start | bytes 294920 | tf_op jit(solution)/shard_map/ppermute | solution.py:381
  79.0 6.4 %copy-start.5 = (bf16[384,128]{1,0:T(8,128)(2,1)}, bf16[384,128]{1,0:T(8,128)(2,1)S(1)}, u32[]{:S(2)}) copy-start(bf16[384,128]{1,0:T(8,128)(2,1)S(1)} %collective-permute-done.3.refs_2_) | copy-start | bytes 294916
  79.0 6.4 %collective-permute-start.8 = (bf16[384,128]{1,0:T(8,128)(2,1)}, bf16[384,128]{1,0:T(8,128)(2,1)S(1)}, u32[]{:S(2)}, u32[]{:S(2)}) collective-permute-start(bf16[384,128]{1,0:T(8,128)(2,1)} %get-tuple-element.28), channel_id=1, source_target_pairs={{0,112},{8,120},{16,96},{24,104},{32,16},{40,24},{48,0},{56,8},{64... | collective-permute-start | bytes 294920 | tf_op jit(solution)/shard_map/ppermute | solution.py:381
  82.3 3.1 %copy-start.6 = (bf16[384,128]{1,0:T(8,128)(2,1)}, bf16[384,128]{1,0:T(8,128)(2,1)S(1)}, u32[]{:S(2)}) copy-start(bf16[384,128]{1,0:T(8,128)(2,1)S(1)} %collective-permute-done.4.refs_3_) | copy-start | bytes 294916
  82.3 3.1 %copy-start.7 = (bf16[384,128]{1,0:T(8,128)(2,1)}, bf16[384,128]{1,0:T(8,128)(2,1)S(1)}, u32[]{:S(2)}) copy-start(bf16[384,128]{1,0:T(8,128)(2,1)S(1)} %collective-permute-done.5.refs_4_) | copy-start | bytes 294916
  84.2 1.2 copy-start.8
  84.2 1.2 copy-start.9
  85.4 0.6 copy-start.10
  86.0 19.3 %copy-start.11 = (bf16[64,128]{1,0:T(8,128)(2,1)S(1)}, bf16[64,128]{1,0:T(8,128)(2,1)}, u32[]{:S(2)}) copy-start(bf16[64,128]{1,0:T(8,128)(2,1)} %param.12) | copy-start | bytes 49156
  94.5 25.0 %collective-permute-start.14 = (bf16[1024,384]{1,0:T(8,128)(2,1)}, bf16[1024,384]{1,0:T(8,128)(2,1)S(1)}, u32[]{:S(2)}, u32[]{:S(2)}) collective-permute-start(bf16[1024,384]{1,0:T(8,128)(2,1)} %get-tuple-element.37), channel_id=1, source_target_pairs={{0,4},{1,5},{2,6},{3,7},{4,0},{5,1},{6,2},{7,3},{8,12},{9,13},{10,... | collective-permute-start | bytes 2359304 | tf_op jit(solution)/shard_map/ppermute | solution.py:390
  96.3 43.1 %collective-permute-start = (bf16[128,1024]{1,0:T(8,128)(2,1)}, bf16[128,1024]{1,0:T(8,128)(2,1)}, u32[]{:S(2)}, u32[]{:S(2)}) collective-permute-start(bf16[128,1024]{1,0:T(8,128)(2,1)} %multiply_convert_fusion), channel_id=1, source_target_pairs={{0,8},{8,16},{16,24},{24,32},{32,40},{40,48},{48,56},{56,64},{64,7... | collective-permute-start | bytes 786440 | tf_op jit(solution)/shard_map/ppermute | solution.py:24
  105.5 19.1 %collective-permute-start.11 = (bf16[1024,384]{1,0:T(8,128)(2,1)}, bf16[1024,384]{1,0:T(8,128)(2,1)S(1)}, u32[]{:S(2)}, u32[]{:S(2)}) collective-permute-start(bf16[1024,384]{1,0:T(8,128)(2,1)} %get-tuple-element.33), channel_id=1, source_target_pairs={{0,1},{1,2},{2,3},{3,0},{4,5},{5,6},{6,7},{7,4},{8,9},{9,10},{10,1... | collective-permute-start | bytes 2359304 | tf_op jit(solution)/shard_map/ppermute | solution.py:385
  107.2 17.4 %collective-permute-start.12 = (bf16[1024,384]{1,0:T(8,128)(2,1)}, bf16[1024,384]{1,0:T(8,128)(2,1)S(1)}, u32[]{:S(2)}, u32[]{:S(2)}) collective-permute-start(bf16[1024,384]{1,0:T(8,128)(2,1)} %get-tuple-element.34), channel_id=1, source_target_pairs={{0,3},{1,0},{2,1},{3,2},{4,7},{5,4},{6,5},{7,6},{8,11},{9,8},{10,9... | collective-permute-start | bytes 2359304 | tf_op jit(solution)/shard_map/ppermute | solution.py:385
  119.4 5.2 %copy-start.1 = (bf16[1024,384]{1,0:T(8,128)(2,1)S(1)}, bf16[1024,384]{1,0:T(8,128)(2,1)}, u32[]{:S(2)}) copy-start(bf16[1024,384]{1,0:T(8,128)(2,1)} %get-tuple-element.32) | copy-start | bytes 2359300
  120.8 15.7 %collective-permute-start.15 = (bf16[512,384]{1,0:T(8,128)(2,1)S(1)}, bf16[512,384]{1,0:T(8,128)(2,1)}, u32[]{:S(2)}, u32[]{:S(2)}) collective-permute-start(bf16[512,384]{1,0:T(8,128)(2,1)S(1)} %get-tuple-element.40), channel_id=1, source_target_pairs={{0,1},{1,2},{2,3},{3,0},{4,5},{5,6},{6,7},{7,4},{8,9},{9,10},{10,1... | collective-permute-start | bytes 1179656 | tf_op jit(solution)/shard_map/ppermute | solution.py:385
  120.9 18.2 %collective-permute-start.17 = (bf16[512,384]{1,0:T(8,128)(2,1)S(1)}, bf16[512,384]{1,0:T(8,128)(2,1)S(1)}, u32[]{:S(2)}, u32[]{:S(2)}) collective-permute-start(bf16[512,384]{1,0:T(8,128)(2,1)S(1)} %get-tuple-element.41), channel_id=1, source_target_pairs={{0,3},{1,0},{2,1},{3,2},{4,7},{5,4},{6,5},{7,6},{8,11},{9,8},{10,9... | collective-permute-start | bytes 1179656 | tf_op jit(solution)/shard_map/ppermute | solution.py:385
  124.9 27.7 %collective-permute-start.13 = (bf16[1024,384]{1,0:T(8,128)(2,1)S(1)}, bf16[1024,384]{1,0:T(8,128)(2,1)S(1)}, u32[]{:S(2)}, u32[]{:S(2)}) collective-permute-start(bf16[1024,384]{1,0:T(8,128)(2,1)S(1)} %add_convert_fusion.1), channel_id=1, source_target_pairs={{0,4},{1,5},{2,6},{3,7},{4,0},{5,1},{6,2},{7,3},{8,12},{9,13},{10,... | collective-permute-start | bytes 2359304 | tf_op jit(solution)/shard_map/ppermute | solution.py:401
  127.5 10.6 %copy-start.3 = (bf16[512,384]{1,0:T(8,128)(2,1)S(1)}, bf16[512,384]{1,0:T(8,128)(2,1)}, u32[]{:S(2)}) copy-start(bf16[512,384]{1,0:T(8,128)(2,1)} %get-tuple-element.35) | copy-start | bytes 1179652
  127.5 11.8 %copy-start.2 = (bf16[512,384]{1,0:T(8,128)(2,1)S(1)}, bf16[512,384]{1,0:T(8,128)(2,1)}, u32[]{:S(2)}) copy-start(bf16[512,384]{1,0:T(8,128)(2,1)} %get-tuple-element.38) | copy-start | bytes 1179652
  135.0 17.6 %collective-permute-start.10 = (bf16[512,384]{1,0:T(8,128)(2,1)}, bf16[512,384]{1,0:T(8,128)(2,1)}, u32[]{:S(2)}, u32[]{:S(2)}) collective-permute-start(bf16[512,384]{1,0:T(8,128)(2,1)} %get-tuple-element.31), channel_id=1, source_target_pairs={{0,1},{1,2},{2,3},{3,0},{4,5},{5,6},{6,7},{7,4},{8,9},{9,10},{10,1... | collective-permute-start | bytes 1179656 | tf_op jit(solution)/shard_map/ppermute | solution.py:385
  136.5 16.1 %collective-permute-start.9 = (bf16[512,384]{1,0:T(8,128)(2,1)}, bf16[512,384]{1,0:T(8,128)(2,1)}, u32[]{:S(2)}, u32[]{:S(2)}) collective-permute-start(bf16[512,384]{1,0:T(8,128)(2,1)} %get-tuple-element.30), channel_id=1, source_target_pairs={{0,3},{1,0},{2,1},{3,2},{4,7},{5,4},{6,5},{7,6},{8,11},{9,8},{10,9... | collective-permute-start | bytes 1179656 | tf_op jit(solution)/shard_map/ppermute | solution.py:385
  139.1 15.1 %collective-permute-start.16 = (bf16[512,384]{1,0:T(8,128)(2,1)S(1)}, bf16[512,384]{1,0:T(8,128)(2,1)S(1)}, u32[]{:S(2)}, u32[]{:S(2)}) collective-permute-start(bf16[512,384]{1,0:T(8,128)(2,1)S(1)} %add_convert_fusion.4), channel_id=1, source_target_pairs={{0,1},{1,2},{2,3},{3,0},{4,5},{5,6},{6,7},{7,4},{8,9},{9,10},{10,1... | collective-permute-start | bytes 1179656 | tf_op jit(solution)/shard_map/ppermute | solution.py:385
  139.4 15.4 %collective-permute-start.18 = (bf16[512,384]{1,0:T(8,128)(2,1)S(1)}, bf16[512,384]{1,0:T(8,128)(2,1)S(1)}, u32[]{:S(2)}, u32[]{:S(2)}) collective-permute-start(bf16[512,384]{1,0:T(8,128)(2,1)S(1)} %add_convert_fusion.2), channel_id=1, source_target_pairs={{0,3},{1,0},{2,1},{3,2},{4,7},{5,4},{6,5},{7,6},{8,11},{9,8},{10,9... | collective-permute-start | bytes 1179656 | tf_op jit(solution)/shard_map/ppermute | solution.py:385

commit v6 on v5

--- a/solution.py
+++ b/solution.py
@@ -273,12 +273,15 @@
     )(place, own, other)
 
 
+WHOLE, HALVES = (4,), (2, 2)
+
+
 def project(place, wanted, out_weight, attended=None, pieces=()):
     rows = (pieces[0] if pieces else attended).shape[0]
     features = out_weight.shape[1]
     share = out_weight.shape[0] // (2 * RING)
     count = len(wanted)
-    heights = [share // parts for _, _, parts in wanted for _ in range(parts)]
+    heights = [share // 4 * part for _, _, quarters in wanted for part in quarters]
 
     def weight_block(step, place):
         index = jnp.int32(0)
@@ -308,15 +311,16 @@
         )
         piece = piece.astype(jnp.bfloat16).T
         at = 0
-        for i, (_, _, parts) in enumerate(wanted):
-            mine = outs[at : at + parts]
-            at += parts
+        for i, (_, _, quarters) in enumerate(wanted):
+            mine = outs[at : at + len(quarters)]
+            at += len(quarters)
 
             @pl.when(pl.program_id(0) == i)
             def _(mine=mine):
-                height = share // len(mine)
-                for part, out in enumerate(mine):
-                    out[...] = piece[part * height : (part + 1) * height]
+                first = 0
+                for out in mine:
+                    out[...] = piece[first : first + out.shape[0]]
+                    first += out.shape[0]
 
     def whole(height, width):
         return pl.BlockSpec((height, width), lambda step, place: (0, 0))
@@ -385,30 +389,35 @@
         return lax.ppermute(block, "tp", ring_route(step))
 
     attended, far, up, down = project(
-        place, [(1, 2, 1), (1, 1, 1), (1, 3, 1)], out_weight, pieces=back
+        place, [(1, 2, WHOLE), (1, 1, WHOLE), (1, 3, WHOLE)], out_weight, pieces=back
     )
     crossed = lax.ppermute(far, "tp", PAIR_ROUTE)
     from_below = sent(up, 1)
     from_above = sent(down, -1)
-    far_0, far_1, up_0, up_1, down_0, down_1, other_own = project(
-        place, [(0, 2, 2), (0, 1, 2), (0, 3, 2), (1, 0, 1)], out_weight, attended
+    far_0, far_1, up_0, up_1, up_2, down_0, down_1, down_2, other_own = project(
+        place,
+        [(0, 2, HALVES), (0, 1, (2, 1, 1)), (0, 3, (1, 1, 2)), (1, 0, WHOLE)],
+        out_weight,
+        attended,
     )
     half = far_0.shape[0]
+    below_1 = sent(up_1, 1)
+    above_0 = sent(down_0, -1)
     first_below = sent(added(far_0, crossed[:half]).astype(jnp.bfloat16), 1)
     first_above = sent(added(far_1, crossed[half:]).astype(jnp.bfloat16), -1)
-    below_1 = sent(up_1, 1)
-    above_0 = sent(down_0, -1)
+    below_2 = sent(up_2, 1)
+    above_1 = sent(down_1, -1)
     handed = lax.ppermute(
         added(other_own, from_below, from_above).astype(jnp.bfloat16), "tp", PAIR_ROUTE
     )
-    (kept,) = project(place, [(0, 0, 1)], out_weight, attended)
+    (kept,) = project(place, [(0, 0, WHOLE)], out_weight, attended)
     below_0 = sent(added(up_0, first_below).astype(jnp.bfloat16), 1)
-    above_1 = sent(added(down_1, first_above).astype(jnp.bfloat16), -1)
+    above_2 = sent(added(down_2, first_above).astype(jnp.bfloat16), -1)
     partial_out = lax.optimization_barrier(
-        added(kept, jnp.concatenate([above_0, below_1], axis=0), handed)
+        added(kept, jnp.concatenate([above_0, above_1, below_1, below_2], axis=0), handed)
     )
     attention_out = (
-        partial_out + jnp.concatenate([below_0, above_1], axis=0).astype(jnp.float32)
+        partial_out + jnp.concatenate([below_0, above_2], axis=0).astype(jnp.float32)
     ).astype(jnp.bfloat16)
     return (hyena_out, attention_out)
 

time: 157 us -> 162 us (1.032)
  waiting for transfers between devices: 7.32 us -> 10.6 us
    ppermute x8 -> x10, waiting for transfers between devices: 1.51 us -> 4.74 us  [sent(): return lax.ppermute(block, 'tp', ring_route(step))]
    ppermute x8 -> x10, starting transfers between devices: 12.4 us -> 12.5 us  [sent(): return lax.ppermute(block, 'tp', ring_route(step))]
  transfers between devices with their start and end apart: 19 -> 21, of which waited for: 5 -> 5; matrix products, arithmetic and copies ran while one was open for 5% -> 5% of each run, Pallas kernels for 18% -> 17%
where the time goes in v6:
time: 162 us; the launch traced here: 160 us
  Pallas kernels  60.5 us (37%)
  starting transfers between devices  38.1 us (24%)
  blocking collectives  37.9 us (23%)
  waiting for transfers between devices  10.6 us (7%)
  other arithmetic  7.98 us (5%)
  local copies, waits for them, and re-layouts  4.49 us (3%)
    all_to_all x1, blocking collectives, local_step(): lax.all_to_all(pieces, 'ctx', 0, 0, axis_index_groups=CORE_GROUPS, tiled=...  37.9 us
    pallas_call x3, Pallas kernels, project(): pl.pallas_call(kernel, grid_spec=pltpu.PrefetchScalarGridSpec(num_scalar_...  22.4 us
    pallas_call x1, Pallas kernels, attention(): pl.pallas_call(attention_kernel, grid=(CHIPS,), out_shape=[jax.ShapeDtype...  21.6 us
    ppermute x10, starting transfers between devices, sent(): return lax.ppermute(block, 'tp', ring_route(step))  12.5 us
    ppermute x7, starting transfers between devices, local_step(): lax.ppermute(outs[step], 'ctx', chip_route(step))  12.2 us
    ppermute x1, starting transfers between devices, shifted(): return lax.ppermute(block, axis, route)  9.03 us
    pallas_call x1, Pallas kernels, hyena_inner(): pl.pallas_call(inner_kernel, grid=(steps,), out_shape=jax.ShapeDtypeStruc...  7.58 us
    pallas_call x1, Pallas kernels, hyena_edge(): pl.pallas_call(edge_kernel, grid=(steps,), out_shape=jax.ShapeDtypeStruct...  6.08 us
  transfers between devices with their start and end apart: 21, of which 5 were waited for; matrix products, arithmetic and copies ran while one was open for 5% of the time, Pallas kernels for 17%

profile of v6, /device:TPU:1, one launch (start us, length us, event | category | flops | bytes accessed | tf_op | source)
XLA Modules:
  0.0 160.4 jit_solution(3111995144760962863)
XLA Ops:
  0.6 2.9 %split_heads.1 = bf16[8,1152,128]{2,1,0:T(8,128)(2,1)} custom-call(bf16[384,1024]{1,0:T(8,128)(2,1)} %refs_0_.1, bf16[384,1024]{1,0:T(8,128)(2,1)} %refs_1_.1, bf16[384,1024]{1,0:T(8,128)(2,1)} %refs_2_.1), custom_call_target="tpu_custom_call" | custom-call | tf_op jit(solution)/shard_map/split_heads/pallas_call | solution.py:170
  3.5 37.9 %all_to_all.5.own = bf16[8,1152,128]{2,1,0:T(8,128)(2,1)S(1)} all-to-all(bf16[8,1152,128]{2,1,0:T(8,128)(2,1)} %split_heads.1), channel_id=1, replica_groups={{0,16,32,48,64,80,96,112},{8,24,40,56,72,88,104,120},{1,17,33,49,65,81,..., dimensions={0} | all-to-all | bytes 4718592 | tf_op jit(solution)/shard_map/all_to_all | solution.py:376
  41.4 1.4 slice.20
  43.3 1.8 %collective-permute-start.1 = (bf16[8,768,128]{2,1,0:T(8,128)(2,1)}, bf16[8,768,128]{2,1,0:T(8,128)(2,1)}, u32[]{:S(2)}, u32[]{:S(2)}) collective-permute-start(bf16[8,768,128]{2,1,0:T(8,128)(2,1)} %slice.20), channel_id=1, source_target_pairs={{0,8},{8,0},{16,24},{24,16},{32,40},{40,32},{48,56},{56,48},{64,72... | collective-permute-start | bytes 4718600 | tf_op jit(solution)/shard_map/ppermute | solution.py:382
  45.7 2.8 %collective-permute-done.1.other = bf16[8,768,128]{2,1,0:T(8,128)(2,1)} collective-permute-done((bf16[8,768,128]{2,1,0:T(8,128)(2,1)}, bf16[8,768,128]{2,1,0:T(8,128)(2,1)}, u32[]{:S(2)}, u32[]{:S(2)}) %collective-permute-start.1) | collective-permute-done | bytes 1572896 | tf_op jit(solution)/shard_map/ppermute | solution.py:382
  48.4 21.6 %attention.1 = (bf16[384,128]{1,0:T(8,128)(2,1)}, bf16[384,128]{1,0:T(8,128)(2,1)}, bf16[384,128]{1,0:T(8,128)(2,1)}, bf16[384,128]{1,0:T(8,128)(2,1)}, bf16[384...) custom-call(s32[5]{0:T(128)} %stack.23.place, ...), custom_call_target="tpu_custom_call" | custom-call | flops 12000000000 | bytes 6000000 | tf_op jit(solution)/shard_map/attention/pallas_call | solution.py:255
  71.0 2.3 %collective-permute-start.4 = (bf16[384,128]{1,0:T(8,128)(2,1)}, bf16[384,128]{1,0:T(8,128)(2,1)S(1)}, u32[]{:S(2)}, u32[]{:S(2)}) collective-permute-start(bf16[384,128]{1,0:T(8,128)(2,1)} %get-tuple-element.26), channel_id=1, source_target_pairs={{0,48},{8,56},{16,32},{24,40},{32,80},{40,88},{48,64},{56,72},{64,... | collective-permute-start | bytes 294920 | tf_op jit(solution)/shard_map/ppermute | solution.py:385
  73.3 3.3 %collective-permute-start.5 = (bf16[384,128]{1,0:T(8,128)(2,1)}, bf16[384,128]{1,0:T(8,128)(2,1)S(1)}, u32[]{:S(2)}, u32[]{:S(2)}) collective-permute-start(bf16[384,128]{1,0:T(8,128)(2,1)} %get-tuple-element.27), channel_id=1, source_target_pairs={{0,64},{8,72},{16,80},{24,88},{32,96},{40,104},{48,112},{56,120},{... | collective-permute-start | bytes 294920 | tf_op jit(solution)/shard_map/ppermute | solution.py:385
  76.9 2.1 %collective-permute-start.7 = (bf16[384,128]{1,0:T(8,128)(2,1)}, bf16[384,128]{1,0:T(8,128)(2,1)S(1)}, u32[]{:S(2)}, u32[]{:S(2)}) collective-permute-start(bf16[384,128]{1,0:T(8,128)(2,1)} %get-tuple-element.29), channel_id=1, source_target_pairs={{0,96},{8,104},{16,112},{24,120},{32,0},{40,8},{48,16},{56,24},{64... | collective-permute-start | bytes 294920 | tf_op jit(solution)/shard_map/ppermute | solution.py:385
  79.0 3.2 %collective-permute-start.8 = (bf16[384,128]{1,0:T(8,128)(2,1)}, bf16[384,128]{1,0:T(8,128)(2,1)S(1)}, u32[]{:S(2)}, u32[]{:S(2)}) collective-permute-start(bf16[384,128]{1,0:T(8,128)(2,1)} %get-tuple-element.30), channel_id=1, source_target_pairs={{0,112},{8,120},{16,96},{24,104},{32,16},{40,24},{48,0},{56,8},{64... | collective-permute-start | bytes 294920 | tf_op jit(solution)/shard_map/ppermute | solution.py:385
  82.3 1.9 %collective-permute-done.6.refs_5_ = bf16[384,128]{1,0:T(8,128)(2,1)S(1)} collective-permute-done((bf16[384,128]{1,0:T(8,128)(2,1)}, bf16[384,128]{1,0:T(8,128)(2,1)S(1)}, u32[]{:S(2)}, u32[]{:S(2)}) %collective-permute-start.6) | collective-permute-done | bytes 98336 | tf_op jit(solution)/shard_map/ppermute | solution.py:385
  84.2 1.2 collective-permute-done.8.refs_7_
  86.1 8.4 %project.3 = (bf16[384,1024]{1,0:T(8,128)(2,1)}, bf16[1024,384]{1,0:T(8,128)(2,1)}, bf16[1024,384]{1,0:T(8,128)(2,1)}, bf16[1024,384]{1,0:T(8,128)(2,1)}) custom-call(s32[5]{0:T(128)} %stack.23.place, bf16[8192,1024]{1,0:T(8,128)(2,1)} %weight_ref.5, bf16[384,128]{1,0:T(8,128)(2,1)} %get-tuple-element.23.refs_0_, bf16[384,128]{1,0:T(8,128)(2,1)} %copy-done.8, ...), custom_call_target="tpu_custom_call" | custom-call | flops 2415919104 | bytes 6291456 | tf_op jit(solution)/shard_map/project/pallas_call | solution.py:331
  94.5 1.8 %multiply_convert_fusion = bf16[128,1024]{1,0:T(8,128)(2,1)} fusion(bf16[384,1024]{1,0:T(8,128)(2,1)} %value.3, bf16[384,1024]{1,0:T(8,128)(2,1)} %key.3), kind=kLoop, calls=%fused_computation.7 | loop fusion | flops 524288 | bytes 786432 | tf_op jit(solution)/shard_map/convert_element_type | solution.py:374
  96.3 9.0 %collective-permute-start = (bf16[128,1024]{1,0:T(8,128)(2,1)}, bf16[128,1024]{1,0:T(8,128)(2,1)}, u32[]{:S(2)}, u32[]{:S(2)}) collective-permute-start(bf16[128,1024]{1,0:T(8,128)(2,1)} %multiply_convert_fusion), channel_id=1, source_target_pairs={{0,8},{8,16},{16,24},{24,32},{32,40},{40,48},{48,56},{56,64},{64,7... | collective-permute-start | bytes 786440 | tf_op jit(solution)/shard_map/ppermute | solution.py:24
  105.5 1.7 %collective-permute-start.13 = (bf16[1024,384]{1,0:T(8,128)(2,1)}, bf16[1024,384]{1,0:T(8,128)(2,1)S(1)}, u32[]{:S(2)}, u32[]{:S(2)}) collective-permute-start(bf16[1024,384]{1,0:T(8,128)(2,1)} %get-tuple-element.37), channel_id=1, source_target_pairs={{0,1},{1,2},{2,3},{3,0},{4,5},{5,6},{6,7},{7,4},{8,9},{9,10},{10,1... | collective-permute-start | bytes 2359304 | tf_op jit(solution)/shard_map/ppermute | solution.py:389
  107.2 2.2 %collective-permute-start.14 = (bf16[1024,384]{1,0:T(8,128)(2,1)}, bf16[1024,384]{1,0:T(8,128)(2,1)S(1)}, u32[]{:S(2)}, u32[]{:S(2)}) collective-permute-start(bf16[1024,384]{1,0:T(8,128)(2,1)} %get-tuple-element.38), channel_id=1, source_target_pairs={{0,3},{1,0},{2,1},{3,2},{4,7},{5,4},{6,5},{7,6},{8,11},{9,8},{10,9... | collective-permute-start | bytes 2359304 | tf_op jit(solution)/shard_map/ppermute | solution.py:389
  109.4 0.7 maximum_maximum_fusion.taps
  110.1 9.3 %project.5 = (bf16[512,384]{1,0:T(8,128)(2,1)}, bf16[512,384]{1,0:T(8,128)(2,1)}, bf16[512,384]{1,0:T(8,128)(2,1)}, bf16[256,384]{1,0:T(8,128)(2,1)}, bf16[256,3...) custom-call(s32[5]{0:T(128)} %stack.23.place, ...), custom_call_target="tpu_custom_call" | custom-call | flops 3221225472 | bytes 8388608 | tf_op jit(solution)/shard_map/project/pallas_call | solution.py:331
  119.4 1.4 add_convert_fusion.5
  120.9 2.7 %collective-permute-start.19 = (bf16[512,384]{1,0:T(8,128)(2,1)S(1)}, bf16[512,384]{1,0:T(8,128)(2,1)S(1)}, u32[]{:S(2)}, u32[]{:S(2)}) collective-permute-start(bf16[512,384]{1,0:T(8,128)(2,1)S(1)} %get-tuple-element.45), channel_id=1, source_target_pairs={{0,3},{1,0},{2,1},{3,2},{4,7},{5,4},{6,5},{7,6},{8,11},{9,8},{10,9... | collective-permute-start | bytes 1179656 | tf_op jit(solution)/shard_map/ppermute | solution.py:389
  123.6 1.0 collective-permute-done.13
  124.9 2.5 %collective-permute-start.15 = (bf16[1024,384]{1,0:T(8,128)(2,1)S(1)}, bf16[1024,384]{1,0:T(8,128)(2,1)S(1)}, u32[]{:S(2)}, u32[]{:S(2)}) collective-permute-start(bf16[1024,384]{1,0:T(8,128)(2,1)S(1)} %add_convert_fusion.1), channel_id=1, source_target_pairs={{0,4},{1,5},{2,6},{3,7},{4,0},{5,1},{6,2},{7,3},{8,12},{9,13},{10,... | collective-permute-start | bytes 2359304 | tf_op jit(solution)/shard_map/ppermute | solution.py:410
  127.4 7.6 %hyena_inner.1.unused = bf16[384,1024]{1,0:T(8,128)(2,1)} custom-call(bf16[384,1024]{1,0:T(8,128)(2,1)} %query.3, bf16[384,1024]{1,0:T(8,128)(2,1)} %key.3, bf16[384,1024]{1,0:T(8,128)(2,1)} %value.3, f32[64,256]{1,0:T(8,128)} %maximum_maximum_fusion.taps, f32[1,1024]{1,0:T(1,128)} %bitcast.7), custom_call_target="tpu_custom_call" | custom-call | flops 3000000000 | bytes 3000000 | tf_op jit(solution)/shard_map/hyena_inner/pallas_call | solution.py:93
  135.0 2.9 %collective-permute-start.10 = (bf16[256,384]{1,0:T(8,128)(2,1)}, bf16[256,384]{1,0:T(8,128)(2,1)S(1)}, u32[]{:S(2)}, u32[]{:S(2)}) collective-permute-start(bf16[256,384]{1,0:T(8,128)(2,1)} %get-tuple-element.33), channel_id=1, source_target_pairs={{0,3},{1,0},{2,1},{3,2},{4,7},{5,4},{6,5},{7,6},{8,11},{9,8},{10,9... | collective-permute-start | bytes 589832 | tf_op jit(solution)/shard_map/ppermute | solution.py:389
  138.0 1.1 add_convert_fusion.4
  139.3 2.7 %collective-permute-start.9 = (bf16[256,384]{1,0:T(8,128)(2,1)}, bf16[256,384]{1,0:T(8,128)(2,1)}, u32[]{:S(2)}, u32[]{:S(2)}) collective-permute-start(bf16[256,384]{1,0:T(8,128)(2,1)} %get-tuple-element.32), channel_id=1, source_target_pairs={{0,3},{1,0},{2,1},{3,2},{4,7},{5,4},{6,5},{7,6},{8,11},{9,8},{10,9... | collective-permute-start | bytes 589832 | tf_op jit(solution)/shard_map/ppermute | solution.py:389
  142.7 3.7 %collective-permute-done.11 = bf16[256,384]{1,0:T(8,128)(2,1)S(1)} collective-permute-done((bf16[256,384]{1,0:T(8,128)(2,1)}, bf16[256,384]{1,0:T(8,128)(2,1)S(1)}, u32[]{:S(2)}, u32[]{:S(2)}) %collective-permute-start.11) | collective-permute-done | bytes 196640 | tf_op jit(solution)/shard_map/ppermute | solution.py:389
  147.1 6.1 %hyena_edge.1 = bf16[384,1024]{1,0:T(8,128)(2,1)} custom-call(bf16[384,1024]{1,0:T(8,128)(2,1)} %query.3, bf16[384,1024]{1,0:T(8,128)(2,1)} %key.3, bf16[384,1024]{1,0:T(8,128)(2,1)} %value.3, bf16[128,1024]{1,0:T(8,128)(2,1)} %collective-permute-done.before, f32[64,256]{1,0:T(8,128)} %maximum_maximum_fusion.taps, ...), custom_call_target="tpu_custom_call", output_to_operand_aliasing={{}: (6, {})} | custom-call | flops 1500000000 | bytes 1000000 | tf_op jit(solution)/shard_map/hyena_edge/pallas_call | solution.py:112
  153.1 4.6 %project.4 = bf16[1024,384]{1,0:T(8,128)(2,1)} custom-call(s32[5]{0:T(128)} %stack.23.place, bf16[8192,1024]{1,0:T(8,128)(2,1)} %weight_ref.5, bf16[384,1024]{1,0:T(8,128)(2,1)} %get-tuple-element.31.refs_0_), custom_call_target="tpu_custom_call" | custom-call | flops 805306368 | bytes 2097152 | tf_op jit(solution)/shard_map/project/pallas_call | solution.py:331
  157.8 1.5 convert_add_fusion
  159.3 1.1 add_convert_fusion
  (65 shorter events, 5.1 us)
Async XLA Ops:
  41.4 1.9 %copy-start = (bf16[8,1152,128]{2,1,0:T(8,128)(2,1)}, bf16[8,1152,128]{2,1,0:T(8,128)(2,1)S(1)}, u32[]{:S(2)}) copy-start(bf16[8,1152,128]{2,1,0:T(8,128)(2,1)S(1)} %all_to_all.5.own) | copy-start | bytes 7077892
  43.3 5.2 %collective-permute-start.1 = (bf16[8,768,128]{2,1,0:T(8,128)(2,1)}, bf16[8,768,128]{2,1,0:T(8,128)(2,1)}, u32[]{:S(2)}, u32[]{:S(2)}) collective-permute-start(bf16[8,768,128]{2,1,0:T(8,128)(2,1)} %slice.20), channel_id=1, source_target_pairs={{0,8},{8,0},{16,24},{24,16},{32,40},{40,32},{48,56},{56,48},{64,72... | collective-permute-start | bytes 4718600 | tf_op jit(solution)/shard_map/ppermute | solution.py:382
  70.1 6.9 %collective-permute-start.2 = (bf16[384,128]{1,0:T(8,128)(2,1)}, bf16[384,128]{1,0:T(8,128)(2,1)S(1)}, u32[]{:S(2)}, u32[]{:S(2)}) collective-permute-start(bf16[384,128]{1,0:T(8,128)(2,1)} %get-tuple-element.24), channel_id=1, source_target_pairs={{0,16},{8,24},{16,0},{24,8},{32,48},{40,56},{48,32},{56,40},{64,80... | collective-permute-start | bytes 294920 | tf_op jit(solution)/shard_map/ppermute | solution.py:385
  70.7 8.4 %collective-permute-start.3 = (bf16[384,128]{1,0:T(8,128)(2,1)}, bf16[384,128]{1,0:T(8,128)(2,1)S(1)}, u32[]{:S(2)}, u32[]{:S(2)}) collective-permute-start(bf16[384,128]{1,0:T(8,128)(2,1)} %get-tuple-element.25), channel_id=1, source_target_pairs={{0,32},{8,40},{16,48},{24,56},{32,64},{40,72},{48,80},{56,88},{64,... | collective-permute-start | bytes 294920 | tf_op jit(solution)/shard_map/ppermute | solution.py:385
  71.0 11.3 %collective-permute-start.4 = (bf16[384,128]{1,0:T(8,128)(2,1)}, bf16[384,128]{1,0:T(8,128)(2,1)S(1)}, u32[]{:S(2)}, u32[]{:S(2)}) collective-permute-start(bf16[384,128]{1,0:T(8,128)(2,1)} %get-tuple-element.26), channel_id=1, source_target_pairs={{0,48},{8,56},{16,32},{24,40},{32,80},{40,88},{48,64},{56,72},{64,... | collective-permute-start | bytes 294920 | tf_op jit(solution)/shard_map/ppermute | solution.py:385
  73.3 9.0 %collective-permute-start.5 = (bf16[384,128]{1,0:T(8,128)(2,1)}, bf16[384,128]{1,0:T(8,128)(2,1)S(1)}, u32[]{:S(2)}, u32[]{:S(2)}) collective-permute-start(bf16[384,128]{1,0:T(8,128)(2,1)} %get-tuple-element.27), channel_id=1, source_target_pairs={{0,64},{8,72},{16,80},{24,88},{32,96},{40,104},{48,112},{56,120},{... | collective-permute-start | bytes 294920 | tf_op jit(solution)/shard_map/ppermute | solution.py:385
  76.6 7.6 %collective-permute-start.6 = (bf16[384,128]{1,0:T(8,128)(2,1)}, bf16[384,128]{1,0:T(8,128)(2,1)S(1)}, u32[]{:S(2)}, u32[]{:S(2)}) collective-permute-start(bf16[384,128]{1,0:T(8,128)(2,1)} %get-tuple-element.28), channel_id=1, source_target_pairs={{0,80},{8,88},{16,64},{24,72},{32,112},{40,120},{48,96},{56,104},{... | collective-permute-start | bytes 294920 | tf_op jit(solution)/shard_map/ppermute | solution.py:385
  76.9 8.5 %copy-start.8 = (bf16[384,128]{1,0:T(8,128)(2,1)}, bf16[384,128]{1,0:T(8,128)(2,1)S(1)}, u32[]{:S(2)}) copy-start(bf16[384,128]{1,0:T(8,128)(2,1)S(1)} %collective-permute-done.2.refs_1_) | copy-start | bytes 294916
  76.9 7.3 %collective-permute-start.7 = (bf16[384,128]{1,0:T(8,128)(2,1)}, bf16[384,128]{1,0:T(8,128)(2,1)S(1)}, u32[]{:S(2)}, u32[]{:S(2)}) collective-permute-start(bf16[384,128]{1,0:T(8,128)(2,1)} %get-tuple-element.29), channel_id=1, source_target_pairs={{0,96},{8,104},{16,112},{24,120},{32,0},{40,8},{48,16},{56,24},{64... | collective-permute-start | bytes 294920 | tf_op jit(solution)/shard_map/ppermute | solution.py:385
  79.0 6.4 %copy-start.9 = (bf16[384,128]{1,0:T(8,128)(2,1)}, bf16[384,128]{1,0:T(8,128)(2,1)S(1)}, u32[]{:S(2)}) copy-start(bf16[384,128]{1,0:T(8,128)(2,1)S(1)} %collective-permute-done.3.refs_2_) | copy-start | bytes 294916
  79.0 6.4 %collective-permute-start.8 = (bf16[384,128]{1,0:T(8,128)(2,1)}, bf16[384,128]{1,0:T(8,128)(2,1)S(1)}, u32[]{:S(2)}, u32[]{:S(2)}) collective-permute-start(bf16[384,128]{1,0:T(8,128)(2,1)} %get-tuple-element.30), channel_id=1, source_target_pairs={{0,112},{8,120},{16,96},{24,104},{32,16},{40,24},{48,0},{56,8},{64... | collective-permute-start | bytes 294920 | tf_op jit(solution)/shard_map/ppermute | solution.py:385
  82.3 3.1 %copy-start.10 = (bf16[384,128]{1,0:T(8,128)(2,1)}, bf16[384,128]{1,0:T(8,128)(2,1)S(1)}, u32[]{:S(2)}) copy-start(bf16[384,128]{1,0:T(8,128)(2,1)S(1)} %collective-permute-done.4.refs_3_) | copy-start | bytes 294916
  82.3 3.1 %copy-start.11 = (bf16[384,128]{1,0:T(8,128)(2,1)}, bf16[384,128]{1,0:T(8,128)(2,1)S(1)}, u32[]{:S(2)}) copy-start(bf16[384,128]{1,0:T(8,128)(2,1)S(1)} %collective-permute-done.5.refs_4_) | copy-start | bytes 294916
  86.1 19.3 %copy-start.15 = (bf16[64,128]{1,0:T(8,128)(2,1)S(1)}, bf16[64,128]{1,0:T(8,128)(2,1)}, u32[]{:S(2)}) copy-start(bf16[64,128]{1,0:T(8,128)(2,1)} %param.12) | copy-start | bytes 49156
  94.5 25.0 %collective-permute-start.16 = (bf16[1024,384]{1,0:T(8,128)(2,1)}, bf16[1024,384]{1,0:T(8,128)(2,1)S(1)}, u32[]{:S(2)}, u32[]{:S(2)}) collective-permute-start(bf16[1024,384]{1,0:T(8,128)(2,1)} %get-tuple-element.41), channel_id=1, source_target_pairs={{0,4},{1,5},{2,6},{3,7},{4,0},{5,1},{6,2},{7,3},{8,12},{9,13},{10,... | collective-permute-start | bytes 2359304 | tf_op jit(solution)/shard_map/ppermute | solution.py:394
  96.3 43.0 %collective-permute-start = (bf16[128,1024]{1,0:T(8,128)(2,1)}, bf16[128,1024]{1,0:T(8,128)(2,1)}, u32[]{:S(2)}, u32[]{:S(2)}) collective-permute-start(bf16[128,1024]{1,0:T(8,128)(2,1)} %multiply_convert_fusion), channel_id=1, source_target_pairs={{0,8},{8,16},{16,24},{24,32},{32,40},{40,48},{48,56},{56,64},{64,7... | collective-permute-start | bytes 786440 | tf_op jit(solution)/shard_map/ppermute | solution.py:24
  105.5 19.1 %collective-permute-start.13 = (bf16[1024,384]{1,0:T(8,128)(2,1)}, bf16[1024,384]{1,0:T(8,128)(2,1)S(1)}, u32[]{:S(2)}, u32[]{:S(2)}) collective-permute-start(bf16[1024,384]{1,0:T(8,128)(2,1)} %get-tuple-element.37), channel_id=1, source_target_pairs={{0,1},{1,2},{2,3},{3,0},{4,5},{5,6},{6,7},{7,4},{8,9},{9,10},{10,1... | collective-permute-start | bytes 2359304 | tf_op jit(solution)/shard_map/ppermute | solution.py:389
  107.2 17.4 %collective-permute-start.14 = (bf16[1024,384]{1,0:T(8,128)(2,1)}, bf16[1024,384]{1,0:T(8,128)(2,1)S(1)}, u32[]{:S(2)}, u32[]{:S(2)}) collective-permute-start(bf16[1024,384]{1,0:T(8,128)(2,1)} %get-tuple-element.38), channel_id=1, source_target_pairs={{0,3},{1,0},{2,1},{3,2},{4,7},{5,4},{6,5},{7,6},{8,11},{9,8},{10,9... | collective-permute-start | bytes 2359304 | tf_op jit(solution)/shard_map/ppermute | solution.py:389
  119.4 5.2 %copy-start.1 = (bf16[1024,384]{1,0:T(8,128)(2,1)S(1)}, bf16[1024,384]{1,0:T(8,128)(2,1)}, u32[]{:S(2)}) copy-start(bf16[1024,384]{1,0:T(8,128)(2,1)} %get-tuple-element.36) | copy-start | bytes 2359300
  120.8 17.1 %collective-permute-start.17 = (bf16[512,384]{1,0:T(8,128)(2,1)S(1)}, bf16[512,384]{1,0:T(8,128)(2,1)}, u32[]{:S(2)}, u32[]{:S(2)}) collective-permute-start(bf16[512,384]{1,0:T(8,128)(2,1)S(1)} %get-tuple-element.44), channel_id=1, source_target_pairs={{0,1},{1,2},{2,3},{3,0},{4,5},{5,6},{6,7},{7,4},{8,9},{9,10},{10,1... | collective-permute-start | bytes 1179656 | tf_op jit(solution)/shard_map/ppermute | solution.py:389
  120.9 18.1 %collective-permute-start.19 = (bf16[512,384]{1,0:T(8,128)(2,1)S(1)}, bf16[512,384]{1,0:T(8,128)(2,1)S(1)}, u32[]{:S(2)}, u32[]{:S(2)}) collective-permute-start(bf16[512,384]{1,0:T(8,128)(2,1)S(1)} %get-tuple-element.45), channel_id=1, source_target_pairs={{0,3},{1,0},{2,1},{3,2},{4,7},{5,4},{6,5},{7,6},{8,11},{9,8},{10,9... | collective-permute-start | bytes 1179656 | tf_op jit(solution)/shard_map/ppermute | solution.py:389
  124.9 32.9 %collective-permute-start.15 = (bf16[1024,384]{1,0:T(8,128)(2,1)S(1)}, bf16[1024,384]{1,0:T(8,128)(2,1)S(1)}, u32[]{:S(2)}, u32[]{:S(2)}) collective-permute-start(bf16[1024,384]{1,0:T(8,128)(2,1)S(1)} %add_convert_fusion.1), channel_id=1, source_target_pairs={{0,4},{1,5},{2,6},{3,7},{4,0},{5,1},{6,2},{7,3},{8,12},{9,13},{10,... | collective-permute-start | bytes 2359304 | tf_op jit(solution)/shard_map/ppermute | solution.py:410
  127.4 10.5 %copy-start.3 = (bf16[512,384]{1,0:T(8,128)(2,1)S(1)}, bf16[512,384]{1,0:T(8,128)(2,1)}, u32[]{:S(2)}) copy-start(bf16[512,384]{1,0:T(8,128)(2,1)} %get-tuple-element.39) | copy-start | bytes 1179652
  127.4 11.7 %copy-start.2 = (bf16[512,384]{1,0:T(8,128)(2,1)S(1)}, bf16[512,384]{1,0:T(8,128)(2,1)}, u32[]{:S(2)}) copy-start(bf16[512,384]{1,0:T(8,128)(2,1)} %get-tuple-element.42) | copy-start | bytes 1179652
  135.0 7.0 %collective-permute-start.10 = (bf16[256,384]{1,0:T(8,128)(2,1)}, bf16[256,384]{1,0:T(8,128)(2,1)S(1)}, u32[]{:S(2)}, u32[]{:S(2)}) collective-permute-start(bf16[256,384]{1,0:T(8,128)(2,1)} %get-tuple-element.33), channel_id=1, source_target_pairs={{0,3},{1,0},{2,1},{3,2},{4,7},{5,4},{6,5},{7,6},{8,11},{9,8},{10,9... | collective-permute-start | bytes 589832 | tf_op jit(solution)/shard_map/ppermute | solution.py:389
  137.9 8.4 %collective-permute-start.11 = (bf16[256,384]{1,0:T(8,128)(2,1)}, bf16[256,384]{1,0:T(8,128)(2,1)S(1)}, u32[]{:S(2)}, u32[]{:S(2)}) collective-permute-start(bf16[256,384]{1,0:T(8,128)(2,1)} %get-tuple-element.34), channel_id=1, source_target_pairs={{0,1},{1,2},{2,3},{3,0},{4,5},{5,6},{6,7},{7,4},{8,9},{9,10},{10,1... | collective-permute-start | bytes 589832 | tf_op jit(solution)/shard_map/ppermute | solution.py:389
  139.1 18.7 %collective-permute-start.12 = (bf16[256,384]{1,0:T(8,128)(2,1)}, bf16[256,384]{1,0:T(8,128)(2,1)}, u32[]{:S(2)}, u32[]{:S(2)}) collective-permute-start(bf16[256,384]{1,0:T(8,128)(2,1)} %get-tuple-element.35), channel_id=1, source_target_pairs={{0,1},{1,2},{2,3},{3,0},{4,5},{5,6},{6,7},{7,4},{8,9},{9,10},{10,1... | collective-permute-start | bytes 589832 | tf_op jit(solution)/shard_map/ppermute | solution.py:389
  139.3 18.5 %collective-permute-start.9 = (bf16[256,384]{1,0:T(8,128)(2,1)}, bf16[256,384]{1,0:T(8,128)(2,1)}, u32[]{:S(2)}, u32[]{:S(2)}) collective-permute-start(bf16[256,384]{1,0:T(8,128)(2,1)} %get-tuple-element.32), channel_id=1, source_target_pairs={{0,3},{1,0},{2,1},{3,2},{4,7},{5,4},{6,5},{7,6},{8,11},{9,8},{10,9... | collective-permute-start | bytes 589832 | tf_op jit(solution)/shard_map/ppermute | solution.py:389
  142.0 17.3 %collective-permute-start.18 = (bf16[512,384]{1,0:T(8,128)(2,1)S(1)}, bf16[512,384]{1,0:T(8,128)(2,1)S(1)}, u32[]{:S(2)}, u32[]{:S(2)}) collective-permute-start(bf16[512,384]{1,0:T(8,128)(2,1)S(1)} %add_convert_fusion.4), channel_id=1, source_target_pairs={{0,1},{1,2},{2,3},{3,0},{4,5},{5,6},{6,7},{7,4},{8,9},{9,10},{10,1... | collective-permute-start | bytes 1179656 | tf_op jit(solution)/shard_map/ppermute | solution.py:389
  147.1 12.2 %collective-permute-start.20 = (bf16[512,384]{1,0:T(8,128)(2,1)S(1)}, bf16[512,384]{1,0:T(8,128)(2,1)S(1)}, u32[]{:S(2)}, u32[]{:S(2)}) collective-permute-start(bf16[512,384]{1,0:T(8,128)(2,1)S(1)} %add_convert_fusion.2), channel_id=1, source_target_pairs={{0,3},{1,0},{2,1},{3,2},{4,7},{5,4},{6,5},{7,6},{8,11},{9,8},{10,9... | collective-permute-start | bytes 1179656 | tf_op jit(solution)/shard_map/ppermute | solution.py:389
  153.1 4.6 %copy-start.5 = (bf16[256,384]{1,0:T(8,128)(2,1)S(1)}, bf16[256,384]{1,0:T(8,128)(2,1)}, u32[]{:S(2)}) copy-start(bf16[256,384]{1,0:T(8,128)(2,1)} %copy-done.4) | copy-start | bytes 589828
  153.1 4.6 %copy-start.7 = (bf16[256,384]{1,0:T(8,128)(2,1)S(1)}, bf16[256,384]{1,0:T(8,128)(2,1)}, u32[]{:S(2)}) copy-start(bf16[256,384]{1,0:T(8,128)(2,1)} %copy-done.6) | copy-start | bytes 589828
  (5 other events, 4.5 us)

commit v7 on v5

--- a/solution.py
+++ b/solution.py
@@ -134,7 +134,6 @@
     return route
 
 
-CORE_GROUPS = [list(range(core, 2 * CHIPS, 2)) for core in range(2)]
 CORE_ROUTE = [(i, i ^ 1) for i in range(2 * CHIPS)]
 
 
@@ -153,33 +152,32 @@
     return ((y - step // 2) & 3) * 2 + ((x - step) & 1)
 
 
-def split_kernel(*refs):
-    out_ref = refs[-1]
-    rows = refs[0].shape[0]
-    for head in range(out_ref.shape[0]):
-        columns = slice(head * HEAD_DIM, (head + 1) * HEAD_DIM)
-        for i, ref in enumerate(refs[:-1]):
-            out_ref[head, i * rows : (i + 1) * rows, :] = ref[:, columns]
-
-
-def split_heads(*arrays):
-    rows = arrays[0].shape[0]
-    at_once = 4
-    spec = pl.BlockSpec((rows, at_once * HEAD_DIM), lambda step: (0, step))
-    tall = len(arrays) * rows
+def split_kernel(k_ref, v_ref, q_ref, *outs):
+    ctx = lax.axis_index("ctx")
+    y, x = ctx // 4, ctx // 2 % 2
+    rows = k_ref.shape[0]
+    for step in range(CHIPS):
+        column = pl.multiple_of(ahead(y, x, step) * HEAD_DIM, HEAD_DIM)
+        for i, ref in enumerate((k_ref, v_ref, q_ref)):
+            outs[step][i * rows : (i + 1) * rows, :] = ref[:, pl.ds(column, HEAD_DIM)]
+
+
+def split_heads(key_rows, value_rows, query_rows):
+    rows = key_rows.shape[0]
     return pl.pallas_call(
         split_kernel,
-        grid=(CHIPS // at_once,),
-        out_shape=jax.ShapeDtypeStruct((CHIPS, tall, HEAD_DIM), jnp.bfloat16),
-        in_specs=[spec] * len(arrays),
-        out_specs=pl.BlockSpec((at_once, tall, HEAD_DIM), lambda step: (step, 0, 0)),
+        out_shape=[jax.ShapeDtypeStruct((3 * rows, HEAD_DIM), jnp.bfloat16)] * CHIPS,
+        in_specs=[VMEM_SPEC] * 3,
+        out_specs=[VMEM_SPEC] * CHIPS,
         name="split_heads",
-    )(*arrays)
-
-
-def attention_kernel(place, own, other, *refs):
-    outs = refs[:CHIPS]
-    keys, values, top, total, even, odd = refs[CHIPS:]
+    )(key_rows, value_rows, query_rows)
+
+
+def attention_kernel(place, *refs):
+    own = refs[:CHIPS]
+    other = refs[CHIPS : 2 * CHIPS]
+    outs = refs[2 * CHIPS : 3 * CHIPS]
+    queries, keys, values, top, total, even, odd = refs[3 * CHIPS :]
     y, x, core = place[0], place[1], place[2]
     step = pl.program_id(0)
     rows = top.shape[0]
@@ -188,11 +186,13 @@
     def _():
         ones = jnp.ones((2 * rows, HEAD_DIM), jnp.bfloat16)
         for i in range(CHIPS):
-            keys[i, :, :rows] = own[i, :rows, :].T
-            keys[i, :, rows:] = other[i, :rows, :].T
-            values[i, :rows, :HEAD_DIM] = own[i, rows : 2 * rows, :]
-            values[i, rows:, :HEAD_DIM] = other[i, rows:, :]
-            values[i, :, HEAD_DIM:] = ones
+            chip = behind(y, x, i)
+            queries[chip] = own[i][2 * rows :, :]
+            keys[chip, :, :rows] = own[i][:rows, :].T
+            keys[chip, :, rows:] = other[i][:rows, :].T
+            values[chip, :rows, :HEAD_DIM] = own[i][rows : 2 * rows, :]
+            values[chip, rows:, :HEAD_DIM] = other[i][rows : 2 * rows, :]
+            values[chip, :, HEAD_DIM:] = ones
 
     top[...] = jnp.full_like(top, NEGATIVE)
     total[...] = jnp.zeros_like(total)
@@ -200,7 +200,7 @@
 
     def score(held, block):
         held[...] = jnp.dot(
-            own[chip, 2 * rows :, :], keys[block], preferred_element_type=jnp.float32
+            queries[chip], keys[block], preferred_element_type=jnp.float32
         )
 
     def weigh(held, block, masked):
@@ -251,14 +251,15 @@
 
 
 def attention(place, own, other):
-    rows = own.shape[1] // 3
+    rows = own[0].shape[0] // 3
     return pl.pallas_call(
         attention_kernel,
         grid=(CHIPS,),
         out_shape=[jax.ShapeDtypeStruct((rows, HEAD_DIM), jnp.bfloat16)] * CHIPS,
-        in_specs=[SMEM_SPEC, VMEM_SPEC, VMEM_SPEC],
+        in_specs=[SMEM_SPEC] + [VMEM_SPEC] * (2 * CHIPS),
         out_specs=[VMEM_SPEC] * CHIPS,
         scratch_shapes=[
+            VMEM((CHIPS, rows, HEAD_DIM), jnp.bfloat16),
             VMEM((CHIPS, HEAD_DIM, 2 * rows), jnp.bfloat16),
             VMEM((CHIPS, 2 * rows, 2 * HEAD_DIM), jnp.bfloat16),
             VMEM((rows, HEAD_DIM), jnp.float32),
@@ -270,7 +271,7 @@
             flops=12_000_000_000, bytes_accessed=6_000_000, transcendentals=10_000_000
         ),
         name="attention",
-    )(place, own, other)
+    )(place, *own, *other)
 
 
 def project(place, wanted, out_weight, attended=None, pieces=()):
@@ -364,22 +365,23 @@
 
     rows = query_rows.shape[0]
     length = conv_filter.shape[1]
-    tail = (
-        hyena_key[rows - length :].astype(jnp.float32)
-        * hyena_value[rows - length :].astype(jnp.float32)
-    ).astype(jnp.bfloat16)
     pieces = split_heads(key_rows, value_rows, query_rows)
-    own = lax.all_to_all(pieces, "ctx", 0, 0, axis_index_groups=CORE_GROUPS, tiled=True)
-    before = shifted(tail, "ctx", 1)
+    own = [pieces[0]] + [
+        lax.ppermute(pieces[step], "ctx", chip_route(step)) for step in range(1, CHIPS)
+    ]
     taps = spread_taps(conv_filter)
     gain = skip_gain[None, :]
     inner = hyena_inner(hyena_query, hyena_key, hyena_value, taps, gain)
-    hyena_out = hyena_edge(hyena_query, hyena_key, hyena_value, before, taps, gain, inner)
-    other = lax.ppermute(own[:, : 2 * rows], "ctx", CORE_ROUTE)
+    other = [lax.ppermute(block, "ctx", CORE_ROUTE) for block in own]
     outs = attention(place, own, other)
     back = [outs[0]] + [
         lax.ppermute(outs[step], "ctx", chip_route(step)) for step in range(1, CHIPS)
     ]
+    tail_key, tail_value, _ = lax.optimization_barrier(
+        (hyena_key[rows - length :], hyena_value[rows - length :], outs[0])
+    )
+    before = shifted(rounded_product(tail_key, tail_value), "ctx", 1)
+    hyena_out = hyena_edge(hyena_query, hyena_key, hyena_value, before, taps, gain, inner)
 
     def sent(block, step):
         return lax.ppermute(block, "tp", ring_route(step))

time: 157 us -> 154 us (0.981)
  blocking collectives: 37.9 us -> 0 us
  starting transfers between devices: 38 us -> 58.4 us
  waiting for transfers between devices: 7.32 us -> 21.2 us
  local copies, waits for them, and re-layouts: 3.37 us -> 1.51 us
    all_to_all x1 -> x0, blocking collectives: 37.9 us -> none  [local_step(): lax.all_to_all(pieces, 'ctx', 0, 0, axis_index_groups=CORE_GROUPS, tiled=...]
    ppermute x1 -> x15, starting transfers between devices: 1.81 us -> 24.5 us  [the longest x7 16.7 us: local_step(): lax.ppermute(pieces[step], 'ctx', chip_route(step))]
    ppermute x1 -> x15, waiting for transfers between devices: 2.7 us -> 15.7 us  [the longest x7 14.4 us: local_step(): lax.ppermute(pieces[step], 'ctx', chip_route(step))]
    ppermute x8, waiting for transfers between devices: 1.51 us -> 3.5 us  [sent(): return lax.ppermute(block, 'tp', ring_route(step))]
    ppermute x1, starting transfers between devices: 2.54 us -> 0.69 us  [local_step(): lax.ppermute(added(other_own, from_below, from_above).astype(jnp.bfloat16...]
    convert_element_type x1, other arithmetic: 0.1 us -> 1.84 us  [local_step(): above_1 = sent(added(down_1, first_above).astype(jnp.bfloat16), -1)]
    ppermute x8, starting transfers between devices: 12.4 us -> 10.6 us  [sent(): return lax.ppermute(block, 'tp', ring_route(step))]
    convert_element_type x1, other arithmetic: 1.8 us -> 0.07 us  [rounded_product(): (left.astype(jnp.float32) * right.astype(jnp.float32)).astype(jnp.bfloat16)]
  transfers between devices with their start and end apart: 19 -> 33, of which waited for: 5 -> 9; matrix products, arithmetic and copies ran while one was open for 5% -> 6% of each run, Pallas kernels for 18% -> 18%
where the time goes in v7:
time: 154 us; the launch traced here: 153 us
  Pallas kernels  61.3 us (40%)
  starting transfers between devices  58.4 us (38%)
  waiting for transfers between devices  21.2 us (14%)
  other arithmetic  9.37 us (6%)
    pallas_call x1, Pallas kernels, attention(): pl.pallas_call(attention_kernel, grid=(CHIPS,), out_shape=[jax.ShapeDtype...  22.1 us
    pallas_call x3, Pallas kernels, project(): pl.pallas_call(kernel, grid_spec=pltpu.PrefetchScalarGridSpec(num_scalar_...  22.1 us
    ppermute x7, starting transfers between devices, local_step(): lax.ppermute(pieces[step], 'ctx', chip_route(step))  16.7 us
    ppermute x7, waiting for transfers between devices, local_step(): lax.ppermute(pieces[step], 'ctx', chip_route(step))  14.4 us
    ppermute x7, starting transfers between devices, local_step(): lax.ppermute(outs[step], 'ctx', chip_route(step))  12.3 us
    ppermute x8, starting transfers between devices, sent(): return lax.ppermute(block, 'tp', ring_route(step))  10.6 us
    ppermute x1, starting transfers between devices, shifted(): return lax.ppermute(block, axis, route)  9.47 us
    ppermute x8, starting transfers between devices, local_step(): other = [lax.ppermute(block, 'ctx', CORE_ROUTE) for block in own]  7.79 us
  transfers between devices with their start and end apart: 33, of which 9 were waited for; matrix products, arithmetic and copies ran while one was open for 6% of the time, Pallas kernels for 18%

profile of v7, /device:TPU:1, one launch (start us, length us, event | category | flops | bytes accessed | tf_op | source)
XLA Modules:
  0.0 152.8 jit_solution(11369363436001416764)
XLA Ops:
  0.6 3.6 %split_heads.1 = (bf16[1152,128]{1,0:T(8,128)(2,1)}, bf16[1152,128]{1,0:T(8,128)(2,1)}, bf16[1152,128]{1,0:T(8,128)(2,1)}, bf16[1152,128]{1,0:T(8,128)(2,1)}, bf...) custom-call(bf16[384,1024]{1,0:T(8,128)(2,1)} %k_ref.1, ...), custom_call_target="tpu_custom_call" | custom-call | tf_op jit(solution)/shard_map/split_heads/pallas_call | solution.py:167
  4.2 4.6 %collective-permute-start.2 = (bf16[1152,128]{1,0:T(8,128)(2,1)}, bf16[1152,128]{1,0:T(8,128)(2,1)S(1)}, u32[]{:S(2)}, u32[]{:S(2)}) collective-permute-start(bf16[1152,128]{1,0:T(8,128)(2,1)} %get-tuple-element.34), channel_id=1, source_target_pairs={{0,48},{8,56},{16,32},{24,40},{32,80},{40,88},{48,64},{56,72},{64,... | collective-permute-start | bytes 884744 | tf_op jit(solution)/shard_map/ppermute | solution.py:370
  8.8 2.6 %collective-permute-start.3 = (bf16[1152,128]{1,0:T(8,128)(2,1)}, bf16[1152,128]{1,0:T(8,128)(2,1)S(1)}, u32[]{:S(2)}, u32[]{:S(2)}) collective-permute-start(bf16[1152,128]{1,0:T(8,128)(2,1)} %get-tuple-element.35), channel_id=1, source_target_pairs={{0,64},{8,72},{16,80},{24,88},{32,96},{40,104},{48,112},{56,120},{... | collective-permute-start | bytes 884744 | tf_op jit(solution)/shard_map/ppermute | solution.py:370
  11.7 1.5 collective-permute-start.5
  13.2 3.9 %collective-permute-start.6 = (bf16[1152,128]{1,0:T(8,128)(2,1)}, bf16[1152,128]{1,0:T(8,128)(2,1)S(1)}, u32[]{:S(2)}, u32[]{:S(2)}) collective-permute-start(bf16[1152,128]{1,0:T(8,128)(2,1)} %get-tuple-element.38), channel_id=1, source_target_pairs={{0,112},{8,120},{16,96},{24,104},{32,16},{40,24},{48,0},{56,8},{64... | collective-permute-start | bytes 884744 | tf_op jit(solution)/shard_map/ppermute | solution.py:370
  17.1 3.5 %collective-permute-start = (bf16[1152,128]{1,0:T(8,128)(2,1)}, bf16[1152,128]{1,0:T(8,128)(2,1)S(1)}, u32[]{:S(2)}, u32[]{:S(2)}) collective-permute-start(bf16[1152,128]{1,0:T(8,128)(2,1)} %get-tuple-element.32), channel_id=1, source_target_pairs={{0,16},{8,24},{16,0},{24,8},{32,48},{40,56},{48,32},{56,40},{64,80... | collective-permute-start | bytes 884744 | tf_op jit(solution)/shard_map/ppermute | solution.py:370
  20.6 11.1 %collective-permute-done.3.refs_4_ = bf16[1152,128]{1,0:T(8,128)(2,1)S(1)} collective-permute-done((bf16[1152,128]{1,0:T(8,128)(2,1)}, bf16[1152,128]{1,0:T(8,128)(2,1)S(1)}, u32[]{:S(2)}, u32[]{:S(2)}) %collective-permute-start.3) | collective-permute-done | bytes 294944 | tf_op jit(solution)/shard_map/ppermute | solution.py:370
  32.0 3.6 %collective-permute-start.7 = (bf16[1152,128]{1,0:T(8,128)(2,1)}, bf16[1152,128]{1,0:T(8,128)(2,1)S(1)}, u32[]{:S(2)}, u32[]{:S(2)}) collective-permute-start(bf16[1152,128]{1,0:T(8,128)(2,1)} %get-tuple-element.31.refs_0_), channel_id=1, source_target_pairs={{0,8},{8,0},{16,24},{24,16},{32,40},{40,32},{48,56},{56,48},{64,72... | collective-permute-start | bytes 884744 | tf_op jit(solution)/shard_map/ppermute | solution.py:375
  36.5 1.4 collective-permute-start.10
  38.5 2.4 %collective-permute-done.1.refs_2_ = bf16[1152,128]{1,0:T(8,128)(2,1)S(1)} collective-permute-done((bf16[1152,128]{1,0:T(8,128)(2,1)}, bf16[1152,128]{1,0:T(8,128)(2,1)S(1)}, u32[]{:S(2)}, u32[]{:S(2)}) %collective-permute-start.1) | collective-permute-done | bytes 294944 | tf_op jit(solution)/shard_map/ppermute | solution.py:370
  40.9 1.6 %collective-permute-start.13 = (bf16[1152,128]{1,0:T(8,128)(2,1)S(1)}, bf16[1152,128]{1,0:T(8,128)(2,1)S(1)}, u32[]{:S(2)}, u32[]{:S(2)}) collective-permute-start(bf16[1152,128]{1,0:T(8,128)(2,1)S(1)} %collective-permute-done.5.refs_6_), channel_id=1, source_target_pairs={{0,8},{8,0},{16,24},{24,16},{32,40},{40,32},{48,56},{56,48},{64,72... | collective-permute-start | bytes 884744 | tf_op jit(solution)/shard_map/ppermute | solution.py:375
  45.2 22.1 %attention.1 = (bf16[384,128]{1,0:T(8,128)(2,1)}, bf16[384,128]{1,0:T(8,128)(2,1)}, bf16[384,128]{1,0:T(8,128)(2,1)}, bf16[384,128]{1,0:T(8,128)(2,1)}, bf16[384...) custom-call(s32[5]{0:T(128)} %stack.23.place, ...), custom_call_target="tpu_custom_call" | custom-call | flops 12000000000 | bytes 6000000 | tf_op jit(solution)/shard_map/attention/pallas_call | solution.py:255
  67.5 2.3 %collective-permute-start.18 = (bf16[384,128]{1,0:T(8,128)(2,1)}, bf16[384,128]{1,0:T(8,128)(2,1)S(1)}, u32[]{:S(2)}, u32[]{:S(2)}) collective-permute-start(bf16[384,128]{1,0:T(8,128)(2,1)} %get-tuple-element.44), channel_id=1, source_target_pairs={{0,48},{8,56},{16,32},{24,40},{32,80},{40,88},{48,64},{56,72},{64,... | collective-permute-start | bytes 294920 | tf_op jit(solution)/shard_map/ppermute | solution.py:378
  69.8 4.1 %collective-permute-start.19 = (bf16[384,128]{1,0:T(8,128)(2,1)}, bf16[384,128]{1,0:T(8,128)(2,1)S(1)}, u32[]{:S(2)}, u32[]{:S(2)}) collective-permute-start(bf16[384,128]{1,0:T(8,128)(2,1)} %get-tuple-element.45), channel_id=1, source_target_pairs={{0,64},{8,72},{16,80},{24,88},{32,96},{40,104},{48,112},{56,120},{... | collective-permute-start | bytes 294920 | tf_op jit(solution)/shard_map/ppermute | solution.py:378
  74.4 1.4 collective-permute-start.21
  75.8 3.9 %collective-permute-start.22 = (bf16[384,128]{1,0:T(8,128)(2,1)}, bf16[384,128]{1,0:T(8,128)(2,1)S(1)}, u32[]{:S(2)}, u32[]{:S(2)}) collective-permute-start(bf16[384,128]{1,0:T(8,128)(2,1)} %get-tuple-element.48), channel_id=1, source_target_pairs={{0,112},{8,120},{16,96},{24,104},{32,16},{40,24},{48,0},{56,8},{64... | collective-permute-start | bytes 294920 | tf_op jit(solution)/shard_map/ppermute | solution.py:378
  79.9 1.7 %collective-permute-done.20.refs_5_ = bf16[384,128]{1,0:T(8,128)(2,1)S(1)} collective-permute-done((bf16[384,128]{1,0:T(8,128)(2,1)}, bf16[384,128]{1,0:T(8,128)(2,1)S(1)}, u32[]{:S(2)}, u32[]{:S(2)}) %collective-permute-start.20) | collective-permute-done | bytes 98336 | tf_op jit(solution)/shard_map/ppermute | solution.py:378
  82.5 8.3 %project.3 = (bf16[384,1024]{1,0:T(8,128)(2,1)}, bf16[1024,384]{1,0:T(8,128)(2,1)}, bf16[1024,384]{1,0:T(8,128)(2,1)}, bf16[1024,384]{1,0:T(8,128)(2,1)}) custom-call(s32[5]{0:T(128)} %stack.23.place, bf16[8192,1024]{1,0:T(8,128)(2,1)} %weight_ref.5, bf16[384,128]{1,0:T(8,128)(2,1)} %get-tuple-element.39.refs_0_, bf16[384,128]{1,0:T(8,128)(2,1)} %copy-done.4, ...), custom_call_target="tpu_custom_call" | custom-call | flops 2415919104 | bytes 6291456 | tf_op jit(solution)/shard_map/project/pallas_call | solution.py:328
  92.3 1.6 %collective-permute-start.25 = (bf16[1024,384]{1,0:T(8,128)(2,1)}, bf16[1024,384]{1,0:T(8,128)(2,1)S(1)}, u32[]{:S(2)}, u32[]{:S(2)}) collective-permute-start(bf16[1024,384]{1,0:T(8,128)(2,1)} %get-tuple-element.53), channel_id=1, source_target_pairs={{0,1},{1,2},{2,3},{3,0},{4,5},{5,6},{6,7},{7,4},{8,9},{9,10},{10,1... | collective-permute-start | bytes 2359304 | tf_op jit(solution)/shard_map/ppermute | solution.py:387
  93.9 2.1 %collective-permute-start.26 = (bf16[1024,384]{1,0:T(8,128)(2,1)}, bf16[1024,384]{1,0:T(8,128)(2,1)S(1)}, u32[]{:S(2)}, u32[]{:S(2)}) collective-permute-start(bf16[1024,384]{1,0:T(8,128)(2,1)} %get-tuple-element.54), channel_id=1, source_target_pairs={{0,3},{1,0},{2,1},{3,2},{4,7},{5,4},{6,5},{7,6},{8,11},{9,8},{10,9... | collective-permute-start | bytes 2359304 | tf_op jit(solution)/shard_map/ppermute | solution.py:387
  96.1 7.5 %hyena_inner.1.unused = bf16[384,1024]{1,0:T(8,128)(2,1)} custom-call(bf16[384,1024]{1,0:T(8,128)(2,1)} %query.3, bf16[384,1024]{1,0:T(8,128)(2,1)} %key.3, bf16[384,1024]{1,0:T(8,128)(2,1)} %value.3, f32[64,256]{1,0:T(8,128)} %maximum_maximum_fusion.taps, f32[1,1024]{1,0:T(1,128)} %bitcast.7), custom_call_target="tpu_custom_call" | custom-call | flops 3000000000 | bytes 3000000 | tf_op jit(solution)/shard_map/hyena_inner/pallas_call | solution.py:93
  103.6 9.3 %project.5 = (bf16[512,384]{1,0:T(8,128)(2,1)}, bf16[512,384]{1,0:T(8,128)(2,1)}, bf16[512,384]{1,0:T(8,128)(2,1)}, bf16[512,384]{1,0:T(8,128)(2,1)}, bf16[512,3...) custom-call(s32[5]{0:T(128)} %stack.23.place, bf16[8192,1024]{1,0:T(8,128)(2,1)} %weight_ref.5, ...), custom_call_target="tpu_custom_call" | custom-call | flops 3221225472 | bytes 8388608 | tf_op jit(solution)/shard_map/project/pallas_call | solution.py:328
  112.9 2.1 %add_convert_fusion.5 = (bf16[512,384]{1,0:T(8,128)(2,1)}, bf16[512,384]{1,0:T(8,128)(2,1)S(1)}) fusion(bf16[512,384]{1,0:T(8,128)(2,1)} %get-tuple-element.56, bf16[1024,384]{1,0:T(8,128)(2,1)S(1)} %collective-permute-done.28, bf16[512,384]{1,0:T(8,128)(2,1)} %get-tuple-element.59), kind=kLoop, calls=%fused_computation.6 | loop fusion | flops 1572864 | bytes 2359296 | tf_op jit(solution)/shard_map/convert_element_type | solution.py:399
  115.1 2.7 %collective-permute-start.31 = (bf16[512,384]{1,0:T(8,128)(2,1)S(1)}, bf16[512,384]{1,0:T(8,128)(2,1)}, u32[]{:S(2)}, u32[]{:S(2)}) collective-permute-start(bf16[512,384]{1,0:T(8,128)(2,1)S(1)} %get-tuple-element.61), channel_id=1, source_target_pairs={{0,3},{1,0},{2,1},{3,2},{4,7},{5,4},{6,5},{7,6},{8,11},{9,8},{10,9... | collective-permute-start | bytes 1179656 | tf_op jit(solution)/shard_map/ppermute | solution.py:387
  118.9 9.5 %collective-permute-start.15 = (bf16[128,1024]{1,0:T(8,128)(2,1)S(1)}, bf16[128,1024]{1,0:T(8,128)(2,1)}, u32[]{:S(2)}, u32[]{:S(2)}) collective-permute-start(bf16[128,1024]{1,0:T(8,128)(2,1)S(1)} %multiply_convert_fusion), channel_id=1, source_target_pairs={{0,8},{8,16},{16,24},{24,32},{32,40},{40,48},{48,56},{56,64},{64,7... | collective-permute-start | bytes 786440 | tf_op jit(solution)/shard_map/ppermute | solution.py:24
  129.0 4.5 %project.4 = bf16[1024,384]{1,0:T(8,128)(2,1)} custom-call(s32[5]{0:T(128)} %stack.23.place, bf16[8192,1024]{1,0:T(8,128)(2,1)} %weight_ref.5, bf16[384,1024]{1,0:T(8,128)(2,1)} %get-tuple-element.49.refs_0_), custom_call_target="tpu_custom_call" | custom-call | flops 805306368 | bytes 2097152 | tf_op jit(solution)/shard_map/project/pallas_call | solution.py:328
  134.4 1.8 %add_convert_fusion.4 = bf16[512,384]{1,0:T(8,128)(2,1)} fusion(bf16[512,384]{1,0:T(8,128)(2,1)} %collective-permute-done.29, bf16[512,384]{1,0:T(8,128)(2,1)S(1)} %copy-done.3), kind=kLoop, calls=%fused_computation.5 | loop fusion | flops 786432 | bytes 1179648 | tf_op jit(solution)/shard_map/convert_element_type | solution.py:407
  136.2 1.8 %add_convert_fusion.2 = bf16[512,384]{1,0:T(8,128)(2,1)} fusion(bf16[512,384]{1,0:T(8,128)(2,1)} %collective-permute-done.31, bf16[512,384]{1,0:T(8,128)(2,1)S(1)} %copy-done.2), kind=kLoop, calls=%fused_computation.3 | loop fusion | flops 786432 | bytes 1179648 | tf_op jit(solution)/shard_map/convert_element_type | solution.py:408
  138.1 2.7 %collective-permute-start.32 = (bf16[512,384]{1,0:T(8,128)(2,1)}, bf16[512,384]{1,0:T(8,128)(2,1)S(1)}, u32[]{:S(2)}, u32[]{:S(2)}) collective-permute-start(bf16[512,384]{1,0:T(8,128)(2,1)} %add_convert_fusion.2), channel_id=1, source_target_pairs={{0,3},{1,0},{2,1},{3,2},{4,7},{5,4},{6,5},{7,6},{8,11},{9,8},{10,9... | collective-permute-start | bytes 1179656 | tf_op jit(solution)/shard_map/ppermute | solution.py:387
  140.8 6.0 %hyena_edge.1 = bf16[384,1024]{1,0:T(8,128)(2,1)} custom-call(bf16[384,1024]{1,0:T(8,128)(2,1)} %query.3, bf16[384,1024]{1,0:T(8,128)(2,1)} %key.3, bf16[384,1024]{1,0:T(8,128)(2,1)} %value.3, bf16[128,1024]{1,0:T(8,128)(2,1)} %collective-permute-done.15.before, f32[64,256]{1,0:T(8,128)} %maximum_maximum_fusion.taps, ...), custom_call_target="tpu_custom_call", output_to_operand_aliasing={{}: (6, {})} | custom-call | flops 1500000000 | bytes 1000000 | tf_op jit(solution)/shard_map/hyena_edge/pallas_call | solution.py:112
  146.8 1.4 convert_add_fusion
  148.2 3.5 %collective-permute-done.30 = bf16[512,384]{1,0:T(8,128)(2,1)S(1)} collective-permute-done((bf16[512,384]{1,0:T(8,128)(2,1)}, bf16[512,384]{1,0:T(8,128)(2,1)S(1)}, u32[]{:S(2)}, u32[]{:S(2)}) %collective-permute-start.30) | collective-permute-done | bytes 393248 | tf_op jit(solution)/shard_map/ppermute | solution.py:387
  (107 shorter events, 11.7 us)
Async XLA Ops:
  4.2 12.9 %collective-permute-start.2 = (bf16[1152,128]{1,0:T(8,128)(2,1)}, bf16[1152,128]{1,0:T(8,128)(2,1)S(1)}, u32[]{:S(2)}, u32[]{:S(2)}) collective-permute-start(bf16[1152,128]{1,0:T(8,128)(2,1)} %get-tuple-element.34), channel_id=1, source_target_pairs={{0,48},{8,56},{16,32},{24,40},{32,80},{40,88},{48,64},{56,72},{64,... | collective-permute-start | bytes 884744 | tf_op jit(solution)/shard_map/ppermute | solution.py:370
  8.8 22.9 %collective-permute-start.3 = (bf16[1152,128]{1,0:T(8,128)(2,1)}, bf16[1152,128]{1,0:T(8,128)(2,1)S(1)}, u32[]{:S(2)}, u32[]{:S(2)}) collective-permute-start(bf16[1152,128]{1,0:T(8,128)(2,1)} %get-tuple-element.35), channel_id=1, source_target_pairs={{0,64},{8,72},{16,80},{24,88},{32,96},{40,104},{48,112},{56,120},{... | collective-permute-start | bytes 884744 | tf_op jit(solution)/shard_map/ppermute | solution.py:370
  11.4 20.6 %collective-permute-start.4 = (bf16[1152,128]{1,0:T(8,128)(2,1)}, bf16[1152,128]{1,0:T(8,128)(2,1)S(1)}, u32[]{:S(2)}, u32[]{:S(2)}) collective-permute-start(bf16[1152,128]{1,0:T(8,128)(2,1)} %get-tuple-element.36), channel_id=1, source_target_pairs={{0,80},{8,88},{16,64},{24,72},{32,112},{40,120},{48,96},{56,104},{... | collective-permute-start | bytes 884744 | tf_op jit(solution)/shard_map/ppermute | solution.py:370
  11.7 24.8 %collective-permute-start.5 = (bf16[1152,128]{1,0:T(8,128)(2,1)}, bf16[1152,128]{1,0:T(8,128)(2,1)S(1)}, u32[]{:S(2)}, u32[]{:S(2)}) collective-permute-start(bf16[1152,128]{1,0:T(8,128)(2,1)} %get-tuple-element.37), channel_id=1, source_target_pairs={{0,96},{8,104},{16,112},{24,120},{32,0},{40,8},{48,16},{56,24},{64... | collective-permute-start | bytes 884744 | tf_op jit(solution)/shard_map/ppermute | solution.py:370
  13.2 24.7 %collective-permute-start.6 = (bf16[1152,128]{1,0:T(8,128)(2,1)}, bf16[1152,128]{1,0:T(8,128)(2,1)S(1)}, u32[]{:S(2)}, u32[]{:S(2)}) collective-permute-start(bf16[1152,128]{1,0:T(8,128)(2,1)} %get-tuple-element.38), channel_id=1, source_target_pairs={{0,112},{8,120},{16,96},{24,104},{32,16},{40,24},{48,0},{56,8},{64... | collective-permute-start | bytes 884744 | tf_op jit(solution)/shard_map/ppermute | solution.py:370
  17.1 20.9 %collective-permute-start = (bf16[1152,128]{1,0:T(8,128)(2,1)}, bf16[1152,128]{1,0:T(8,128)(2,1)S(1)}, u32[]{:S(2)}, u32[]{:S(2)}) collective-permute-start(bf16[1152,128]{1,0:T(8,128)(2,1)} %get-tuple-element.32), channel_id=1, source_target_pairs={{0,16},{8,24},{16,0},{24,8},{32,48},{40,56},{48,32},{56,40},{64,80... | collective-permute-start | bytes 884744 | tf_op jit(solution)/shard_map/ppermute | solution.py:370
  31.7 9.2 %collective-permute-start.1 = (bf16[1152,128]{1,0:T(8,128)(2,1)}, bf16[1152,128]{1,0:T(8,128)(2,1)S(1)}, u32[]{:S(2)}, u32[]{:S(2)}) collective-permute-start(bf16[1152,128]{1,0:T(8,128)(2,1)} %get-tuple-element.33), channel_id=1, source_target_pairs={{0,32},{8,40},{16,48},{24,56},{32,64},{40,72},{48,80},{56,88},{64,... | collective-permute-start | bytes 884744 | tf_op jit(solution)/shard_map/ppermute | solution.py:370
  32.0 10.5 %collective-permute-start.7 = (bf16[1152,128]{1,0:T(8,128)(2,1)}, bf16[1152,128]{1,0:T(8,128)(2,1)S(1)}, u32[]{:S(2)}, u32[]{:S(2)}) collective-permute-start(bf16[1152,128]{1,0:T(8,128)(2,1)} %get-tuple-element.31.refs_0_), channel_id=1, source_target_pairs={{0,8},{8,0},{16,24},{24,16},{32,40},{40,32},{48,56},{56,48},{64,72... | collective-permute-start | bytes 884744 | tf_op jit(solution)/shard_map/ppermute | solution.py:375
  36.5 6.1 %collective-permute-start.10 = (bf16[1152,128]{1,0:T(8,128)(2,1)S(1)}, bf16[1152,128]{1,0:T(8,128)(2,1)S(1)}, u32[]{:S(2)}, u32[]{:S(2)}) collective-permute-start(bf16[1152,128]{1,0:T(8,128)(2,1)S(1)} %collective-permute-done.2.refs_3_), channel_id=1, source_target_pairs={{0,8},{8,0},{16,24},{24,16},{32,40},{40,32},{48,56},{56,48},{64,72... | collective-permute-start | bytes 884744 | tf_op jit(solution)/shard_map/ppermute | solution.py:375
  37.9 5.1 %collective-permute-start.11 = (bf16[1152,128]{1,0:T(8,128)(2,1)S(1)}, bf16[1152,128]{1,0:T(8,128)(2,1)S(1)}, u32[]{:S(2)}, u32[]{:S(2)}) collective-permute-start(bf16[1152,128]{1,0:T(8,128)(2,1)S(1)} %collective-permute-done.3.refs_4_), channel_id=1, source_target_pairs={{0,8},{8,0},{16,24},{24,16},{32,40},{40,32},{48,56},{56,48},{64,72... | collective-permute-start | bytes 884744 | tf_op jit(solution)/shard_map/ppermute | solution.py:375
  38.0 5.8 %collective-permute-start.12 = (bf16[1152,128]{1,0:T(8,128)(2,1)S(1)}, bf16[1152,128]{1,0:T(8,128)(2,1)S(1)}, u32[]{:S(2)}, u32[]{:S(2)}) collective-permute-start(bf16[1152,128]{1,0:T(8,128)(2,1)S(1)} %collective-permute-done.4.refs_5_), channel_id=1, source_target_pairs={{0,8},{8,0},{16,24},{24,16},{32,40},{40,32},{48,56},{56,48},{64,72... | collective-permute-start | bytes 884744 | tf_op jit(solution)/shard_map/ppermute | solution.py:375
  40.9 2.9 %collective-permute-start.13 = (bf16[1152,128]{1,0:T(8,128)(2,1)S(1)}, bf16[1152,128]{1,0:T(8,128)(2,1)S(1)}, u32[]{:S(2)}, u32[]{:S(2)}) collective-permute-start(bf16[1152,128]{1,0:T(8,128)(2,1)S(1)} %collective-permute-done.5.refs_6_), channel_id=1, source_target_pairs={{0,8},{8,0},{16,24},{24,16},{32,40},{40,32},{48,56},{56,48},{64,72... | collective-permute-start | bytes 884744 | tf_op jit(solution)/shard_map/ppermute | solution.py:375
  42.6 2.1 %collective-permute-start.8 = (bf16[1152,128]{1,0:T(8,128)(2,1)S(1)}, bf16[1152,128]{1,0:T(8,128)(2,1)}, u32[]{:S(2)}, u32[]{:S(2)}) collective-permute-start(bf16[1152,128]{1,0:T(8,128)(2,1)S(1)} %collective-permute-done.refs_1_), channel_id=1, source_target_pairs={{0,8},{8,0},{16,24},{24,16},{32,40},{40,32},{48,56},{56,48},{64,72... | collective-permute-start | bytes 884744 | tf_op jit(solution)/shard_map/ppermute | solution.py:375
  43.1 2.1 %collective-permute-start.9 = (bf16[1152,128]{1,0:T(8,128)(2,1)S(1)}, bf16[1152,128]{1,0:T(8,128)(2,1)}, u32[]{:S(2)}, u32[]{:S(2)}) collective-permute-start(bf16[1152,128]{1,0:T(8,128)(2,1)S(1)} %collective-permute-done.1.refs_2_), channel_id=1, source_target_pairs={{0,8},{8,0},{16,24},{24,16},{32,40},{40,32},{48,56},{56,48},{64,72... | collective-permute-start | bytes 884744 | tf_op jit(solution)/shard_map/ppermute | solution.py:375
  67.4 7.1 %collective-permute-start.16 = (bf16[384,128]{1,0:T(8,128)(2,1)}, bf16[384,128]{1,0:T(8,128)(2,1)S(1)}, u32[]{:S(2)}, u32[]{:S(2)}) collective-permute-start(bf16[384,128]{1,0:T(8,128)(2,1)} %get-tuple-element.42), channel_id=1, source_target_pairs={{0,16},{8,24},{16,0},{24,8},{32,48},{40,56},{48,32},{56,40},{64,80... | collective-permute-start | bytes 294920 | tf_op jit(solution)/shard_map/ppermute | solution.py:378
  67.4 8.3 %collective-permute-start.17 = (bf16[384,128]{1,0:T(8,128)(2,1)}, bf16[384,128]{1,0:T(8,128)(2,1)S(1)}, u32[]{:S(2)}, u32[]{:S(2)}) collective-permute-start(bf16[384,128]{1,0:T(8,128)(2,1)} %get-tuple-element.43), channel_id=1, source_target_pairs={{0,32},{8,40},{16,48},{24,56},{32,64},{40,72},{48,80},{56,88},{64,... | collective-permute-start | bytes 294920 | tf_op jit(solution)/shard_map/ppermute | solution.py:378
  67.5 12.3 %collective-permute-start.18 = (bf16[384,128]{1,0:T(8,128)(2,1)}, bf16[384,128]{1,0:T(8,128)(2,1)S(1)}, u32[]{:S(2)}, u32[]{:S(2)}) collective-permute-start(bf16[384,128]{1,0:T(8,128)(2,1)} %get-tuple-element.44), channel_id=1, source_target_pairs={{0,48},{8,56},{16,32},{24,40},{32,80},{40,88},{48,64},{56,72},{64,... | collective-permute-start | bytes 294920 | tf_op jit(solution)/shard_map/ppermute | solution.py:378
  69.8 10.0 %collective-permute-start.19 = (bf16[384,128]{1,0:T(8,128)(2,1)}, bf16[384,128]{1,0:T(8,128)(2,1)S(1)}, u32[]{:S(2)}, u32[]{:S(2)}) collective-permute-start(bf16[384,128]{1,0:T(8,128)(2,1)} %get-tuple-element.45), channel_id=1, source_target_pairs={{0,64},{8,72},{16,80},{24,88},{32,96},{40,104},{48,112},{56,120},{... | collective-permute-start | bytes 294920 | tf_op jit(solution)/shard_map/ppermute | solution.py:378
  74.0 7.6 %collective-permute-start.20 = (bf16[384,128]{1,0:T(8,128)(2,1)}, bf16[384,128]{1,0:T(8,128)(2,1)S(1)}, u32[]{:S(2)}, u32[]{:S(2)}) collective-permute-start(bf16[384,128]{1,0:T(8,128)(2,1)} %get-tuple-element.46), channel_id=1, source_target_pairs={{0,80},{8,88},{16,64},{24,72},{32,112},{40,120},{48,96},{56,104},{... | collective-permute-start | bytes 294920 | tf_op jit(solution)/shard_map/ppermute | solution.py:378
  74.4 7.1 %collective-permute-start.21 = (bf16[384,128]{1,0:T(8,128)(2,1)}, bf16[384,128]{1,0:T(8,128)(2,1)S(1)}, u32[]{:S(2)}, u32[]{:S(2)}) collective-permute-start(bf16[384,128]{1,0:T(8,128)(2,1)} %get-tuple-element.47), channel_id=1, source_target_pairs={{0,96},{8,104},{16,112},{24,120},{32,0},{40,8},{48,16},{56,24},{64... | collective-permute-start | bytes 294920 | tf_op jit(solution)/shard_map/ppermute | solution.py:378
  75.8 6.1 %collective-permute-start.22 = (bf16[384,128]{1,0:T(8,128)(2,1)}, bf16[384,128]{1,0:T(8,128)(2,1)S(1)}, u32[]{:S(2)}, u32[]{:S(2)}) collective-permute-start(bf16[384,128]{1,0:T(8,128)(2,1)} %get-tuple-element.48), channel_id=1, source_target_pairs={{0,112},{8,120},{16,96},{24,104},{32,16},{40,24},{48,0},{56,8},{64... | collective-permute-start | bytes 294920 | tf_op jit(solution)/shard_map/ppermute | solution.py:378
  90.8 22.2 %collective-permute-start.28 = (bf16[1024,384]{1,0:T(8,128)(2,1)}, bf16[1024,384]{1,0:T(8,128)(2,1)S(1)}, u32[]{:S(2)}, u32[]{:S(2)}) collective-permute-start(bf16[1024,384]{1,0:T(8,128)(2,1)} %get-tuple-element.57), channel_id=1, source_target_pairs={{0,4},{1,5},{2,6},{3,7},{4,0},{5,1},{6,2},{7,3},{8,12},{9,13},{10,... | collective-permute-start | bytes 2359304 | tf_op jit(solution)/shard_map/ppermute | solution.py:392
  92.3 25.4 %collective-permute-start.25 = (bf16[1024,384]{1,0:T(8,128)(2,1)}, bf16[1024,384]{1,0:T(8,128)(2,1)S(1)}, u32[]{:S(2)}, u32[]{:S(2)}) collective-permute-start(bf16[1024,384]{1,0:T(8,128)(2,1)} %get-tuple-element.53), channel_id=1, source_target_pairs={{0,1},{1,2},{2,3},{3,0},{4,5},{5,6},{6,7},{7,4},{8,9},{9,10},{10,1... | collective-permute-start | bytes 2359304 | tf_op jit(solution)/shard_map/ppermute | solution.py:387
  93.9 23.8 %collective-permute-start.26 = (bf16[1024,384]{1,0:T(8,128)(2,1)}, bf16[1024,384]{1,0:T(8,128)(2,1)S(1)}, u32[]{:S(2)}, u32[]{:S(2)}) collective-permute-start(bf16[1024,384]{1,0:T(8,128)(2,1)} %get-tuple-element.54), channel_id=1, source_target_pairs={{0,3},{1,0},{2,1},{3,2},{4,7},{5,4},{6,5},{7,6},{8,11},{9,8},{10,9... | collective-permute-start | bytes 2359304 | tf_op jit(solution)/shard_map/ppermute | solution.py:387
  115.1 18.4 %collective-permute-start.29 = (bf16[512,384]{1,0:T(8,128)(2,1)}, bf16[512,384]{1,0:T(8,128)(2,1)}, u32[]{:S(2)}, u32[]{:S(2)}) collective-permute-start(bf16[512,384]{1,0:T(8,128)(2,1)} %get-tuple-element.60), channel_id=1, source_target_pairs={{0,1},{1,2},{2,3},{3,0},{4,5},{5,6},{6,7},{7,4},{8,9},{9,10},{10,1... | collective-permute-start | bytes 1179656 | tf_op jit(solution)/shard_map/ppermute | solution.py:387
  115.1 21.2 %collective-permute-start.31 = (bf16[512,384]{1,0:T(8,128)(2,1)S(1)}, bf16[512,384]{1,0:T(8,128)(2,1)}, u32[]{:S(2)}, u32[]{:S(2)}) collective-permute-start(bf16[512,384]{1,0:T(8,128)(2,1)S(1)} %get-tuple-element.61), channel_id=1, source_target_pairs={{0,3},{1,0},{2,1},{3,2},{4,7},{5,4},{6,5},{7,6},{8,11},{9,8},{10,9... | collective-permute-start | bytes 1179656 | tf_op jit(solution)/shard_map/ppermute | solution.py:387
  118.1 28.7 %collective-permute-start.27 = (bf16[1024,384]{1,0:T(8,128)(2,1)S(1)}, bf16[1024,384]{1,0:T(8,128)(2,1)S(1)}, u32[]{:S(2)}, u32[]{:S(2)}) collective-permute-start(bf16[1024,384]{1,0:T(8,128)(2,1)S(1)} %add_convert_fusion.1), channel_id=1, source_target_pairs={{0,4},{1,5},{2,6},{3,7},{4,0},{5,1},{6,2},{7,3},{8,12},{9,13},{10,... | collective-permute-start | bytes 2359304 | tf_op jit(solution)/shard_map/ppermute | solution.py:403
  118.9 19.2 %collective-permute-start.15 = (bf16[128,1024]{1,0:T(8,128)(2,1)S(1)}, bf16[128,1024]{1,0:T(8,128)(2,1)}, u32[]{:S(2)}, u32[]{:S(2)}) collective-permute-start(bf16[128,1024]{1,0:T(8,128)(2,1)S(1)} %multiply_convert_fusion), channel_id=1, source_target_pairs={{0,8},{8,16},{16,24},{24,32},{32,40},{40,48},{48,56},{56,64},{64,7... | collective-permute-start | bytes 786440 | tf_op jit(solution)/shard_map/ppermute | solution.py:24
  128.4 18.4 %collective-permute-start.23 = (bf16[512,384]{1,0:T(8,128)(2,1)}, bf16[512,384]{1,0:T(8,128)(2,1)}, u32[]{:S(2)}, u32[]{:S(2)}) collective-permute-start(bf16[512,384]{1,0:T(8,128)(2,1)} %get-tuple-element.50), channel_id=1, source_target_pairs={{0,3},{1,0},{2,1},{3,2},{4,7},{5,4},{6,5},{7,6},{8,11},{9,8},{10,9... | collective-permute-start | bytes 1179656 | tf_op jit(solution)/shard_map/ppermute | solution.py:387
  133.5 13.3 %collective-permute-start.24 = (bf16[512,384]{1,0:T(8,128)(2,1)}, bf16[512,384]{1,0:T(8,128)(2,1)}, u32[]{:S(2)}, u32[]{:S(2)}) collective-permute-start(bf16[512,384]{1,0:T(8,128)(2,1)} %get-tuple-element.51), channel_id=1, source_target_pairs={{0,1},{1,2},{2,3},{3,0},{4,5},{5,6},{6,7},{7,4},{8,9},{9,10},{10,1... | collective-permute-start | bytes 1179656 | tf_op jit(solution)/shard_map/ppermute | solution.py:387
  136.2 15.4 %collective-permute-start.30 = (bf16[512,384]{1,0:T(8,128)(2,1)}, bf16[512,384]{1,0:T(8,128)(2,1)S(1)}, u32[]{:S(2)}, u32[]{:S(2)}) collective-permute-start(bf16[512,384]{1,0:T(8,128)(2,1)} %add_convert_fusion.4), channel_id=1, source_target_pairs={{0,1},{1,2},{2,3},{3,0},{4,5},{5,6},{6,7},{7,4},{8,9},{9,10},{10,1... | collective-permute-start | bytes 1179656 | tf_op jit(solution)/shard_map/ppermute | solution.py:387
  138.1 13.6 %collective-permute-start.32 = (bf16[512,384]{1,0:T(8,128)(2,1)}, bf16[512,384]{1,0:T(8,128)(2,1)S(1)}, u32[]{:S(2)}, u32[]{:S(2)}) collective-permute-start(bf16[512,384]{1,0:T(8,128)(2,1)} %add_convert_fusion.2), channel_id=1, source_target_pairs={{0,3},{1,0},{2,1},{3,2},{4,7},{5,4},{6,5},{7,6},{8,11},{9,8},{10,9... | collective-permute-start | bytes 1179656 | tf_op jit(solution)/shard_map/ppermute | solution.py:387
  (27 other events, 178.9 us)

commit v8 on v7

--- a/solution.py
+++ b/solution.py
@@ -163,12 +163,15 @@
 
 
 def split_heads(key_rows, value_rows, query_rows):
-    rows = key_rows.shape[0]
+    rows, width = key_rows.shape
+    half = pl.BlockSpec((rows // 2, width), lambda part: (part, 0))
+    out = pl.BlockSpec((3 * rows // 2, HEAD_DIM), lambda part: (part, 0))
     return pl.pallas_call(
         split_kernel,
+        grid=(2,),
         out_shape=[jax.ShapeDtypeStruct((3 * rows, HEAD_DIM), jnp.bfloat16)] * CHIPS,
-        in_specs=[VMEM_SPEC] * 3,
-        out_specs=[VMEM_SPEC] * CHIPS,
+        in_specs=[half] * 3,
+        out_specs=[out] * CHIPS,
         name="split_heads",
     )(key_rows, value_rows, query_rows)
 
@@ -181,17 +184,23 @@
     y, x, core = place[0], place[1], place[2]
     step = pl.program_id(0)
     rows = top.shape[0]
+    half = rows // 2
 
     @pl.when(step == 0)
     def _():
         ones = jnp.ones((2 * rows, HEAD_DIM), jnp.bfloat16)
         for i in range(CHIPS):
             chip = behind(y, x, i)
-            queries[chip] = own[i][2 * rows :, :]
-            keys[chip, :, :rows] = own[i][:rows, :].T
-            keys[chip, :, rows:] = other[i][:rows, :].T
-            values[chip, :rows, :HEAD_DIM] = own[i][rows : 2 * rows, :]
-            values[chip, rows:, :HEAD_DIM] = other[i][rows : 2 * rows, :]
+            for part in range(2):
+                first = part * 3 * half
+                here = slice(part * half, (part + 1) * half)
+                there = slice(rows + part * half, rows + (part + 1) * half)
+                queries[chip, here, :] = own[i][first + 2 * half : first + 3 * half, :]
+                for ref, place_of in ((own[i], here), (other[i], there)):
+                    values[chip, place_of, :HEAD_DIM] = ref[first + half : first + 2 * half, :]
+            for ref, first in ((own[i], 0), (other[i], rows)):
+                joined = jnp.concatenate([ref[:half, :], ref[3 * half : 4 * half, :]], axis=0)
+                keys[chip, :, first : first + rows] = joined.T
             values[chip, :, HEAD_DIM:] = ones
 
     top[...] = jnp.full_like(top, NEGATIVE)
@@ -365,18 +374,20 @@
 
     rows = query_rows.shape[0]
     length = conv_filter.shape[1]
+
+    def brought(block, step):
+        return lax.ppermute(block, "ctx", chip_route(step))
+
     pieces = split_heads(key_rows, value_rows, query_rows)
-    own = [pieces[0]] + [
-        lax.ppermute(pieces[step], "ctx", chip_route(step)) for step in range(1, CHIPS)
-    ]
+    own = [pieces[0]] + [brought(pieces[step], step) for step in range(1, CHIPS)]
     taps = spread_taps(conv_filter)
     gain = skip_gain[None, :]
     inner = hyena_inner(hyena_query, hyena_key, hyena_value, taps, gain)
-    other = [lax.ppermute(block, "ctx", CORE_ROUTE) for block in own]
+    other = []
+    for block in own:
+        other.append(lax.ppermute(block, "ctx", CORE_ROUTE))
     outs = attention(place, own, other)
-    back = [outs[0]] + [
-        lax.ppermute(outs[step], "ctx", chip_route(step)) for step in range(1, CHIPS)
-    ]
+    back = [outs[0]] + [brought(outs[step], step) for step in range(1, CHIPS)]
     tail_key, tail_value, _ = lax.optimization_barrier(
         (hyena_key[rows - length :], hyena_value[rows - length :], outs[0])
     )

time: 154 us -> 153 us (level)
  no operation moved by 1% of the time
where the time goes in v8:
time: 153 us; the launch traced here: 152 us
  Pallas kernels  60.7 us (40%)
  starting transfers between devices  58.4 us (38%)
  waiting for transfers between devices  21.3 us (14%)
  other arithmetic  9.37 us (6%)
  local copies, waits for them, and re-layouts  1.53 us (1%)
    ppermute x14, starting transfers between devices, brought(): return lax.ppermute(block, 'ctx', chip_route(step))  29 us
    pallas_call x1, Pallas kernels, attention(): pl.pallas_call(attention_kernel, grid=(CHIPS,), out_shape=[jax.ShapeDtype...  22.1 us
    pallas_call x3, Pallas kernels, project(): pl.pallas_call(kernel, grid_spec=pltpu.PrefetchScalarGridSpec(num_scalar_...  22.1 us
    ppermute x14, waiting for transfers between devices, brought(): return lax.ppermute(block, 'ctx', chip_route(step))  16.4 us
    ppermute x8, starting transfers between devices, sent(): return lax.ppermute(block, 'tp', ring_route(step))  10.7 us
    ppermute x1, starting transfers between devices, shifted(): return lax.ppermute(block, axis, route)  9.44 us
    ppermute x8, starting transfers between devices, local_step(): other.append(lax.ppermute(block, 'ctx', CORE_ROUTE))  7.79 us
    pallas_call x1, Pallas kernels, hyena_inner(): pl.pallas_call(inner_kernel, grid=(steps,), out_shape=jax.ShapeDtypeStruc...  7.5 us
  transfers between devices with their start and end apart: 33, of which 9 were waited for; matrix products, arithmetic and copies ran while one was open for 6% of the time, Pallas kernels for 18%

profile of v8, /device:TPU:1, one launch (start us, length us, event | category | flops | bytes accessed | tf_op | source)
XLA Modules:
  0.0 152.2 jit_solution(9038613375126654053)
XLA Ops:
  0.6 2.9 %split_heads.1 = (bf16[1152,128]{1,0:T(8,128)(2,1)}, bf16[1152,128]{1,0:T(8,128)(2,1)}, bf16[1152,128]{1,0:T(8,128)(2,1)}, bf16[1152,128]{1,0:T(8,128)(2,1)}, bf...) custom-call(bf16[384,1024]{1,0:T(8,128)(2,1)} %k_ref.1, ...), custom_call_target="tpu_custom_call" | custom-call | tf_op jit(solution)/shard_map/split_heads/pallas_call | solution.py:169
  3.6 4.6 %collective-permute-start.2 = (bf16[1152,128]{1,0:T(8,128)(2,1)}, bf16[1152,128]{1,0:T(8,128)(2,1)S(1)}, u32[]{:S(2)}, u32[]{:S(2)}) collective-permute-start(bf16[1152,128]{1,0:T(8,128)(2,1)} %get-tuple-element.34), channel_id=1, source_target_pairs={{0,48},{8,56},{16,32},{24,40},{32,80},{40,88},{48,64},{56,72},{64,... | collective-permute-start | bytes 884744 | tf_op jit(solution)/shard_map/ppermute | solution.py:379
  8.2 2.6 %collective-permute-start.3 = (bf16[1152,128]{1,0:T(8,128)(2,1)}, bf16[1152,128]{1,0:T(8,128)(2,1)S(1)}, u32[]{:S(2)}, u32[]{:S(2)}) collective-permute-start(bf16[1152,128]{1,0:T(8,128)(2,1)} %get-tuple-element.35), channel_id=1, source_target_pairs={{0,64},{8,72},{16,80},{24,88},{32,96},{40,104},{48,112},{56,120},{... | collective-permute-start | bytes 884744 | tf_op jit(solution)/shard_map/ppermute | solution.py:379
  11.1 1.6 %collective-permute-start.5 = (bf16[1152,128]{1,0:T(8,128)(2,1)}, bf16[1152,128]{1,0:T(8,128)(2,1)S(1)}, u32[]{:S(2)}, u32[]{:S(2)}) collective-permute-start(bf16[1152,128]{1,0:T(8,128)(2,1)} %get-tuple-element.37), channel_id=1, source_target_pairs={{0,96},{8,104},{16,112},{24,120},{32,0},{40,8},{48,16},{56,24},{64... | collective-permute-start | bytes 884744 | tf_op jit(solution)/shard_map/ppermute | solution.py:379
  12.7 3.8 %collective-permute-start.6 = (bf16[1152,128]{1,0:T(8,128)(2,1)}, bf16[1152,128]{1,0:T(8,128)(2,1)S(1)}, u32[]{:S(2)}, u32[]{:S(2)}) collective-permute-start(bf16[1152,128]{1,0:T(8,128)(2,1)} %get-tuple-element.38), channel_id=1, source_target_pairs={{0,112},{8,120},{16,96},{24,104},{32,16},{40,24},{48,0},{56,8},{64... | collective-permute-start | bytes 884744 | tf_op jit(solution)/shard_map/ppermute | solution.py:379
  16.5 3.5 %collective-permute-start = (bf16[1152,128]{1,0:T(8,128)(2,1)}, bf16[1152,128]{1,0:T(8,128)(2,1)S(1)}, u32[]{:S(2)}, u32[]{:S(2)}) collective-permute-start(bf16[1152,128]{1,0:T(8,128)(2,1)} %get-tuple-element.32), channel_id=1, source_target_pairs={{0,16},{8,24},{16,0},{24,8},{32,48},{40,56},{48,32},{56,40},{64,80... | collective-permute-start | bytes 884744 | tf_op jit(solution)/shard_map/ppermute | solution.py:379
  20.0 11.1 %collective-permute-done.3.refs_4_ = bf16[1152,128]{1,0:T(8,128)(2,1)S(1)} collective-permute-done((bf16[1152,128]{1,0:T(8,128)(2,1)}, bf16[1152,128]{1,0:T(8,128)(2,1)S(1)}, u32[]{:S(2)}, u32[]{:S(2)}) %collective-permute-start.3) | collective-permute-done | bytes 294944 | tf_op jit(solution)/shard_map/ppermute | solution.py:379
  31.4 3.6 %collective-permute-start.7 = (bf16[1152,128]{1,0:T(8,128)(2,1)}, bf16[1152,128]{1,0:T(8,128)(2,1)S(1)}, u32[]{:S(2)}, u32[]{:S(2)}) collective-permute-start(bf16[1152,128]{1,0:T(8,128)(2,1)} %get-tuple-element.31.refs_0_), channel_id=1, source_target_pairs={{0,8},{8,0},{16,24},{24,16},{32,40},{40,32},{48,56},{56,48},{64,72... | collective-permute-start | bytes 884744 | tf_op jit(solution)/shard_map/ppermute | solution.py:388
  35.9 1.4 collective-permute-start.10
  37.9 2.4 %collective-permute-done.1.refs_2_ = bf16[1152,128]{1,0:T(8,128)(2,1)S(1)} collective-permute-done((bf16[1152,128]{1,0:T(8,128)(2,1)}, bf16[1152,128]{1,0:T(8,128)(2,1)S(1)}, u32[]{:S(2)}, u32[]{:S(2)}) %collective-permute-start.1) | collective-permute-done | bytes 294944 | tf_op jit(solution)/shard_map/ppermute | solution.py:379
  40.3 1.6 %collective-permute-start.13 = (bf16[1152,128]{1,0:T(8,128)(2,1)S(1)}, bf16[1152,128]{1,0:T(8,128)(2,1)S(1)}, u32[]{:S(2)}, u32[]{:S(2)}) collective-permute-start(bf16[1152,128]{1,0:T(8,128)(2,1)S(1)} %collective-permute-done.5.refs_6_), channel_id=1, source_target_pairs={{0,8},{8,0},{16,24},{24,16},{32,40},{40,32},{48,56},{56,48},{64,72... | collective-permute-start | bytes 884744 | tf_op jit(solution)/shard_map/ppermute | solution.py:388
  44.6 22.1 %attention.1 = (bf16[384,128]{1,0:T(8,128)(2,1)}, bf16[384,128]{1,0:T(8,128)(2,1)}, bf16[384,128]{1,0:T(8,128)(2,1)}, bf16[384,128]{1,0:T(8,128)(2,1)}, bf16[384...) custom-call(s32[5]{0:T(128)} %stack.23.place, ...), custom_call_target="tpu_custom_call" | custom-call | flops 12000000000 | bytes 6000000 | tf_op jit(solution)/shard_map/attention/pallas_call | solution.py:264
  66.9 2.3 %collective-permute-start.18 = (bf16[384,128]{1,0:T(8,128)(2,1)}, bf16[384,128]{1,0:T(8,128)(2,1)S(1)}, u32[]{:S(2)}, u32[]{:S(2)}) collective-permute-start(bf16[384,128]{1,0:T(8,128)(2,1)} %get-tuple-element.44), channel_id=1, source_target_pairs={{0,48},{8,56},{16,32},{24,40},{32,80},{40,88},{48,64},{56,72},{64,... | collective-permute-start | bytes 294920 | tf_op jit(solution)/shard_map/ppermute | solution.py:379
  69.2 4.1 %collective-permute-start.19 = (bf16[384,128]{1,0:T(8,128)(2,1)}, bf16[384,128]{1,0:T(8,128)(2,1)S(1)}, u32[]{:S(2)}, u32[]{:S(2)}) collective-permute-start(bf16[384,128]{1,0:T(8,128)(2,1)} %get-tuple-element.45), channel_id=1, source_target_pairs={{0,64},{8,72},{16,80},{24,88},{32,96},{40,104},{48,112},{56,120},{... | collective-permute-start | bytes 294920 | tf_op jit(solution)/shard_map/ppermute | solution.py:379
  73.8 1.4 collective-permute-start.21
  75.2 3.9 %collective-permute-start.22 = (bf16[384,128]{1,0:T(8,128)(2,1)}, bf16[384,128]{1,0:T(8,128)(2,1)S(1)}, u32[]{:S(2)}, u32[]{:S(2)}) collective-permute-start(bf16[384,128]{1,0:T(8,128)(2,1)} %get-tuple-element.48), channel_id=1, source_target_pairs={{0,112},{8,120},{16,96},{24,104},{32,16},{40,24},{48,0},{56,8},{64... | collective-permute-start | bytes 294920 | tf_op jit(solution)/shard_map/ppermute | solution.py:379
  79.2 1.7 %collective-permute-done.20.refs_5_ = bf16[384,128]{1,0:T(8,128)(2,1)S(1)} collective-permute-done((bf16[384,128]{1,0:T(8,128)(2,1)}, bf16[384,128]{1,0:T(8,128)(2,1)S(1)}, u32[]{:S(2)}, u32[]{:S(2)}) %collective-permute-start.20) | collective-permute-done | bytes 98336 | tf_op jit(solution)/shard_map/ppermute | solution.py:379
  81.9 8.3 %project.3 = (bf16[384,1024]{1,0:T(8,128)(2,1)}, bf16[1024,384]{1,0:T(8,128)(2,1)}, bf16[1024,384]{1,0:T(8,128)(2,1)}, bf16[1024,384]{1,0:T(8,128)(2,1)}) custom-call(s32[5]{0:T(128)} %stack.23.place, bf16[8192,1024]{1,0:T(8,128)(2,1)} %weight_ref.5, bf16[384,128]{1,0:T(8,128)(2,1)} %get-tuple-element.39.refs_0_, bf16[384,128]{1,0:T(8,128)(2,1)} %copy-done.4, ...), custom_call_target="tpu_custom_call" | custom-call | flops 2415919104 | bytes 6291456 | tf_op jit(solution)/shard_map/project/pallas_call | solution.py:337
  91.7 1.6 %collective-permute-start.25 = (bf16[1024,384]{1,0:T(8,128)(2,1)}, bf16[1024,384]{1,0:T(8,128)(2,1)S(1)}, u32[]{:S(2)}, u32[]{:S(2)}) collective-permute-start(bf16[1024,384]{1,0:T(8,128)(2,1)} %get-tuple-element.53), channel_id=1, source_target_pairs={{0,1},{1,2},{2,3},{3,0},{4,5},{5,6},{6,7},{7,4},{8,9},{9,10},{10,1... | collective-permute-start | bytes 2359304 | tf_op jit(solution)/shard_map/ppermute | solution.py:398
  93.3 2.1 %collective-permute-start.26 = (bf16[1024,384]{1,0:T(8,128)(2,1)}, bf16[1024,384]{1,0:T(8,128)(2,1)S(1)}, u32[]{:S(2)}, u32[]{:S(2)}) collective-permute-start(bf16[1024,384]{1,0:T(8,128)(2,1)} %get-tuple-element.54), channel_id=1, source_target_pairs={{0,3},{1,0},{2,1},{3,2},{4,7},{5,4},{6,5},{7,6},{8,11},{9,8},{10,9... | collective-permute-start | bytes 2359304 | tf_op jit(solution)/shard_map/ppermute | solution.py:398
  95.5 7.5 %hyena_inner.1.unused = bf16[384,1024]{1,0:T(8,128)(2,1)} custom-call(bf16[384,1024]{1,0:T(8,128)(2,1)} %query.3, bf16[384,1024]{1,0:T(8,128)(2,1)} %key.3, bf16[384,1024]{1,0:T(8,128)(2,1)} %value.3, f32[64,256]{1,0:T(8,128)} %maximum_maximum_fusion.taps, f32[1,1024]{1,0:T(1,128)} %bitcast.7), custom_call_target="tpu_custom_call" | custom-call | flops 3000000000 | bytes 3000000 | tf_op jit(solution)/shard_map/hyena_inner/pallas_call | solution.py:93
  103.0 9.3 %project.5 = (bf16[512,384]{1,0:T(8,128)(2,1)}, bf16[512,384]{1,0:T(8,128)(2,1)}, bf16[512,384]{1,0:T(8,128)(2,1)}, bf16[512,384]{1,0:T(8,128)(2,1)}, bf16[512,3...) custom-call(s32[5]{0:T(128)} %stack.23.place, bf16[8192,1024]{1,0:T(8,128)(2,1)} %weight_ref.5, ...), custom_call_target="tpu_custom_call" | custom-call | flops 3221225472 | bytes 8388608 | tf_op jit(solution)/shard_map/project/pallas_call | solution.py:337
  112.3 2.1 %add_convert_fusion.5 = (bf16[512,384]{1,0:T(8,128)(2,1)}, bf16[512,384]{1,0:T(8,128)(2,1)S(1)}) fusion(bf16[512,384]{1,0:T(8,128)(2,1)} %get-tuple-element.56, bf16[1024,384]{1,0:T(8,128)(2,1)S(1)} %collective-permute-done.28, bf16[512,384]{1,0:T(8,128)(2,1)} %get-tuple-element.59), kind=kLoop, calls=%fused_computation.6 | loop fusion | flops 1572864 | bytes 2359296 | tf_op jit(solution)/shard_map/convert_element_type | solution.py:410
  114.5 2.7 %collective-permute-start.31 = (bf16[512,384]{1,0:T(8,128)(2,1)S(1)}, bf16[512,384]{1,0:T(8,128)(2,1)}, u32[]{:S(2)}, u32[]{:S(2)}) collective-permute-start(bf16[512,384]{1,0:T(8,128)(2,1)S(1)} %get-tuple-element.61), channel_id=1, source_target_pairs={{0,3},{1,0},{2,1},{3,2},{4,7},{5,4},{6,5},{7,6},{8,11},{9,8},{10,9... | collective-permute-start | bytes 1179656 | tf_op jit(solution)/shard_map/ppermute | solution.py:398
  118.3 9.4 %collective-permute-start.15 = (bf16[128,1024]{1,0:T(8,128)(2,1)S(1)}, bf16[128,1024]{1,0:T(8,128)(2,1)}, u32[]{:S(2)}, u32[]{:S(2)}) collective-permute-start(bf16[128,1024]{1,0:T(8,128)(2,1)S(1)} %multiply_convert_fusion), channel_id=1, source_target_pairs={{0,8},{8,16},{16,24},{24,32},{32,40},{40,48},{48,56},{56,64},{64,7... | collective-permute-start | bytes 786440 | tf_op jit(solution)/shard_map/ppermute | solution.py:24
  128.3 4.5 %project.4 = bf16[1024,384]{1,0:T(8,128)(2,1)} custom-call(s32[5]{0:T(128)} %stack.23.place, bf16[8192,1024]{1,0:T(8,128)(2,1)} %weight_ref.5, bf16[384,1024]{1,0:T(8,128)(2,1)} %get-tuple-element.49.refs_0_), custom_call_target="tpu_custom_call" | custom-call | flops 805306368 | bytes 2097152 | tf_op jit(solution)/shard_map/project/pallas_call | solution.py:337
  133.8 1.8 %add_convert_fusion.4 = bf16[512,384]{1,0:T(8,128)(2,1)} fusion(bf16[512,384]{1,0:T(8,128)(2,1)} %collective-permute-done.29, bf16[512,384]{1,0:T(8,128)(2,1)S(1)} %copy-done.3), kind=kLoop, calls=%fused_computation.5 | loop fusion | flops 786432 | bytes 1179648 | tf_op jit(solution)/shard_map/convert_element_type | solution.py:418
  135.6 1.8 %add_convert_fusion.2 = bf16[512,384]{1,0:T(8,128)(2,1)} fusion(bf16[512,384]{1,0:T(8,128)(2,1)} %collective-permute-done.31, bf16[512,384]{1,0:T(8,128)(2,1)S(1)} %copy-done.2), kind=kLoop, calls=%fused_computation.3 | loop fusion | flops 786432 | bytes 1179648 | tf_op jit(solution)/shard_map/convert_element_type | solution.py:419
  137.5 2.7 %collective-permute-start.32 = (bf16[512,384]{1,0:T(8,128)(2,1)}, bf16[512,384]{1,0:T(8,128)(2,1)S(1)}, u32[]{:S(2)}, u32[]{:S(2)}) collective-permute-start(bf16[512,384]{1,0:T(8,128)(2,1)} %add_convert_fusion.2), channel_id=1, source_target_pairs={{0,3},{1,0},{2,1},{3,2},{4,7},{5,4},{6,5},{7,6},{8,11},{9,8},{10,9... | collective-permute-start | bytes 1179656 | tf_op jit(solution)/shard_map/ppermute | solution.py:398
  140.1 6.0 %hyena_edge.1 = bf16[384,1024]{1,0:T(8,128)(2,1)} custom-call(bf16[384,1024]{1,0:T(8,128)(2,1)} %query.3, bf16[384,1024]{1,0:T(8,128)(2,1)} %key.3, bf16[384,1024]{1,0:T(8,128)(2,1)} %value.3, bf16[128,1024]{1,0:T(8,128)(2,1)} %collective-permute-done.15.before, f32[64,256]{1,0:T(8,128)} %maximum_maximum_fusion.taps, ...), custom_call_target="tpu_custom_call", output_to_operand_aliasing={{}: (6, {})} | custom-call | flops 1500000000 | bytes 1000000 | tf_op jit(solution)/shard_map/hyena_edge/pallas_call | solution.py:112
  146.2 1.4 convert_add_fusion
  147.6 3.5 %collective-permute-done.30 = bf16[512,384]{1,0:T(8,128)(2,1)S(1)} collective-permute-done((bf16[512,384]{1,0:T(8,128)(2,1)}, bf16[512,384]{1,0:T(8,128)(2,1)S(1)}, u32[]{:S(2)}, u32[]{:S(2)}) %collective-permute-start.30) | collective-permute-done | bytes 393248 | tf_op jit(solution)/shard_map/ppermute | solution.py:398
  (107 shorter events, 11.7 us)
Async XLA Ops:
  3.6 12.9 %collective-permute-start.2 = (bf16[1152,128]{1,0:T(8,128)(2,1)}, bf16[1152,128]{1,0:T(8,128)(2,1)S(1)}, u32[]{:S(2)}, u32[]{:S(2)}) collective-permute-start(bf16[1152,128]{1,0:T(8,128)(2,1)} %get-tuple-element.34), channel_id=1, source_target_pairs={{0,48},{8,56},{16,32},{24,40},{32,80},{40,88},{48,64},{56,72},{64,... | collective-permute-start | bytes 884744 | tf_op jit(solution)/shard_map/ppermute | solution.py:379
  8.2 22.9 %collective-permute-start.3 = (bf16[1152,128]{1,0:T(8,128)(2,1)}, bf16[1152,128]{1,0:T(8,128)(2,1)S(1)}, u32[]{:S(2)}, u32[]{:S(2)}) collective-permute-start(bf16[1152,128]{1,0:T(8,128)(2,1)} %get-tuple-element.35), channel_id=1, source_target_pairs={{0,64},{8,72},{16,80},{24,88},{32,96},{40,104},{48,112},{56,120},{... | collective-permute-start | bytes 884744 | tf_op jit(solution)/shard_map/ppermute | solution.py:379
  10.8 20.6 %collective-permute-start.4 = (bf16[1152,128]{1,0:T(8,128)(2,1)}, bf16[1152,128]{1,0:T(8,128)(2,1)S(1)}, u32[]{:S(2)}, u32[]{:S(2)}) collective-permute-start(bf16[1152,128]{1,0:T(8,128)(2,1)} %get-tuple-element.36), channel_id=1, source_target_pairs={{0,80},{8,88},{16,64},{24,72},{32,112},{40,120},{48,96},{56,104},{... | collective-permute-start | bytes 884744 | tf_op jit(solution)/shard_map/ppermute | solution.py:379
  11.1 24.8 %collective-permute-start.5 = (bf16[1152,128]{1,0:T(8,128)(2,1)}, bf16[1152,128]{1,0:T(8,128)(2,1)S(1)}, u32[]{:S(2)}, u32[]{:S(2)}) collective-permute-start(bf16[1152,128]{1,0:T(8,128)(2,1)} %get-tuple-element.37), channel_id=1, source_target_pairs={{0,96},{8,104},{16,112},{24,120},{32,0},{40,8},{48,16},{56,24},{64... | collective-permute-start | bytes 884744 | tf_op jit(solution)/shard_map/ppermute | solution.py:379
  12.7 24.6 %collective-permute-start.6 = (bf16[1152,128]{1,0:T(8,128)(2,1)}, bf16[1152,128]{1,0:T(8,128)(2,1)S(1)}, u32[]{:S(2)}, u32[]{:S(2)}) collective-permute-start(bf16[1152,128]{1,0:T(8,128)(2,1)} %get-tuple-element.38), channel_id=1, source_target_pairs={{0,112},{8,120},{16,96},{24,104},{32,16},{40,24},{48,0},{56,8},{64... | collective-permute-start | bytes 884744 | tf_op jit(solution)/shard_map/ppermute | solution.py:379
  16.5 20.9 %collective-permute-start = (bf16[1152,128]{1,0:T(8,128)(2,1)}, bf16[1152,128]{1,0:T(8,128)(2,1)S(1)}, u32[]{:S(2)}, u32[]{:S(2)}) collective-permute-start(bf16[1152,128]{1,0:T(8,128)(2,1)} %get-tuple-element.32), channel_id=1, source_target_pairs={{0,16},{8,24},{16,0},{24,8},{32,48},{40,56},{48,32},{56,40},{64,80... | collective-permute-start | bytes 884744 | tf_op jit(solution)/shard_map/ppermute | solution.py:379
  31.1 9.2 %collective-permute-start.1 = (bf16[1152,128]{1,0:T(8,128)(2,1)}, bf16[1152,128]{1,0:T(8,128)(2,1)S(1)}, u32[]{:S(2)}, u32[]{:S(2)}) collective-permute-start(bf16[1152,128]{1,0:T(8,128)(2,1)} %get-tuple-element.33), channel_id=1, source_target_pairs={{0,32},{8,40},{16,48},{24,56},{32,64},{40,72},{48,80},{56,88},{64,... | collective-permute-start | bytes 884744 | tf_op jit(solution)/shard_map/ppermute | solution.py:379
  31.4 10.5 %collective-permute-start.7 = (bf16[1152,128]{1,0:T(8,128)(2,1)}, bf16[1152,128]{1,0:T(8,128)(2,1)S(1)}, u32[]{:S(2)}, u32[]{:S(2)}) collective-permute-start(bf16[1152,128]{1,0:T(8,128)(2,1)} %get-tuple-element.31.refs_0_), channel_id=1, source_target_pairs={{0,8},{8,0},{16,24},{24,16},{32,40},{40,32},{48,56},{56,48},{64,72... | collective-permute-start | bytes 884744 | tf_op jit(solution)/shard_map/ppermute | solution.py:388
  35.9 6.1 %collective-permute-start.10 = (bf16[1152,128]{1,0:T(8,128)(2,1)S(1)}, bf16[1152,128]{1,0:T(8,128)(2,1)S(1)}, u32[]{:S(2)}, u32[]{:S(2)}) collective-permute-start(bf16[1152,128]{1,0:T(8,128)(2,1)S(1)} %collective-permute-done.2.refs_3_), channel_id=1, source_target_pairs={{0,8},{8,0},{16,24},{24,16},{32,40},{40,32},{48,56},{56,48},{64,72... | collective-permute-start | bytes 884744 | tf_op jit(solution)/shard_map/ppermute | solution.py:388
  37.3 5.1 %collective-permute-start.11 = (bf16[1152,128]{1,0:T(8,128)(2,1)S(1)}, bf16[1152,128]{1,0:T(8,128)(2,1)S(1)}, u32[]{:S(2)}, u32[]{:S(2)}) collective-permute-start(bf16[1152,128]{1,0:T(8,128)(2,1)S(1)} %collective-permute-done.3.refs_4_), channel_id=1, source_target_pairs={{0,8},{8,0},{16,24},{24,16},{32,40},{40,32},{48,56},{56,48},{64,72... | collective-permute-start | bytes 884744 | tf_op jit(solution)/shard_map/ppermute | solution.py:388
  37.4 5.7 %collective-permute-start.12 = (bf16[1152,128]{1,0:T(8,128)(2,1)S(1)}, bf16[1152,128]{1,0:T(8,128)(2,1)S(1)}, u32[]{:S(2)}, u32[]{:S(2)}) collective-permute-start(bf16[1152,128]{1,0:T(8,128)(2,1)S(1)} %collective-permute-done.4.refs_5_), channel_id=1, source_target_pairs={{0,8},{8,0},{16,24},{24,16},{32,40},{40,32},{48,56},{56,48},{64,72... | collective-permute-start | bytes 884744 | tf_op jit(solution)/shard_map/ppermute | solution.py:388
  40.3 2.9 %collective-permute-start.13 = (bf16[1152,128]{1,0:T(8,128)(2,1)S(1)}, bf16[1152,128]{1,0:T(8,128)(2,1)S(1)}, u32[]{:S(2)}, u32[]{:S(2)}) collective-permute-start(bf16[1152,128]{1,0:T(8,128)(2,1)S(1)} %collective-permute-done.5.refs_6_), channel_id=1, source_target_pairs={{0,8},{8,0},{16,24},{24,16},{32,40},{40,32},{48,56},{56,48},{64,72... | collective-permute-start | bytes 884744 | tf_op jit(solution)/shard_map/ppermute | solution.py:388
  42.0 2.1 %collective-permute-start.8 = (bf16[1152,128]{1,0:T(8,128)(2,1)S(1)}, bf16[1152,128]{1,0:T(8,128)(2,1)}, u32[]{:S(2)}, u32[]{:S(2)}) collective-permute-start(bf16[1152,128]{1,0:T(8,128)(2,1)S(1)} %collective-permute-done.refs_1_), channel_id=1, source_target_pairs={{0,8},{8,0},{16,24},{24,16},{32,40},{40,32},{48,56},{56,48},{64,72... | collective-permute-start | bytes 884744 | tf_op jit(solution)/shard_map/ppermute | solution.py:388
  42.5 2.1 %collective-permute-start.9 = (bf16[1152,128]{1,0:T(8,128)(2,1)S(1)}, bf16[1152,128]{1,0:T(8,128)(2,1)}, u32[]{:S(2)}, u32[]{:S(2)}) collective-permute-start(bf16[1152,128]{1,0:T(8,128)(2,1)S(1)} %collective-permute-done.1.refs_2_), channel_id=1, source_target_pairs={{0,8},{8,0},{16,24},{24,16},{32,40},{40,32},{48,56},{56,48},{64,72... | collective-permute-start | bytes 884744 | tf_op jit(solution)/shard_map/ppermute | solution.py:388
  66.7 7.1 %collective-permute-start.16 = (bf16[384,128]{1,0:T(8,128)(2,1)}, bf16[384,128]{1,0:T(8,128)(2,1)S(1)}, u32[]{:S(2)}, u32[]{:S(2)}) collective-permute-start(bf16[384,128]{1,0:T(8,128)(2,1)} %get-tuple-element.42), channel_id=1, source_target_pairs={{0,16},{8,24},{16,0},{24,8},{32,48},{40,56},{48,32},{56,40},{64,80... | collective-permute-start | bytes 294920 | tf_op jit(solution)/shard_map/ppermute | solution.py:379
  66.8 8.3 %collective-permute-start.17 = (bf16[384,128]{1,0:T(8,128)(2,1)}, bf16[384,128]{1,0:T(8,128)(2,1)S(1)}, u32[]{:S(2)}, u32[]{:S(2)}) collective-permute-start(bf16[384,128]{1,0:T(8,128)(2,1)} %get-tuple-element.43), channel_id=1, source_target_pairs={{0,32},{8,40},{16,48},{24,56},{32,64},{40,72},{48,80},{56,88},{64,... | collective-permute-start | bytes 294920 | tf_op jit(solution)/shard_map/ppermute | solution.py:379
  66.9 12.3 %collective-permute-start.18 = (bf16[384,128]{1,0:T(8,128)(2,1)}, bf16[384,128]{1,0:T(8,128)(2,1)S(1)}, u32[]{:S(2)}, u32[]{:S(2)}) collective-permute-start(bf16[384,128]{1,0:T(8,128)(2,1)} %get-tuple-element.44), channel_id=1, source_target_pairs={{0,48},{8,56},{16,32},{24,40},{32,80},{40,88},{48,64},{56,72},{64,... | collective-permute-start | bytes 294920 | tf_op jit(solution)/shard_map/ppermute | solution.py:379
  69.2 10.0 %collective-permute-start.19 = (bf16[384,128]{1,0:T(8,128)(2,1)}, bf16[384,128]{1,0:T(8,128)(2,1)S(1)}, u32[]{:S(2)}, u32[]{:S(2)}) collective-permute-start(bf16[384,128]{1,0:T(8,128)(2,1)} %get-tuple-element.45), channel_id=1, source_target_pairs={{0,64},{8,72},{16,80},{24,88},{32,96},{40,104},{48,112},{56,120},{... | collective-permute-start | bytes 294920 | tf_op jit(solution)/shard_map/ppermute | solution.py:379
  73.4 7.6 %collective-permute-start.20 = (bf16[384,128]{1,0:T(8,128)(2,1)}, bf16[384,128]{1,0:T(8,128)(2,1)S(1)}, u32[]{:S(2)}, u32[]{:S(2)}) collective-permute-start(bf16[384,128]{1,0:T(8,128)(2,1)} %get-tuple-element.46), channel_id=1, source_target_pairs={{0,80},{8,88},{16,64},{24,72},{32,112},{40,120},{48,96},{56,104},{... | collective-permute-start | bytes 294920 | tf_op jit(solution)/shard_map/ppermute | solution.py:379
  73.8 7.1 %collective-permute-start.21 = (bf16[384,128]{1,0:T(8,128)(2,1)}, bf16[384,128]{1,0:T(8,128)(2,1)S(1)}, u32[]{:S(2)}, u32[]{:S(2)}) collective-permute-start(bf16[384,128]{1,0:T(8,128)(2,1)} %get-tuple-element.47), channel_id=1, source_target_pairs={{0,96},{8,104},{16,112},{24,120},{32,0},{40,8},{48,16},{56,24},{64... | collective-permute-start | bytes 294920 | tf_op jit(solution)/shard_map/ppermute | solution.py:379
  75.2 6.1 %collective-permute-start.22 = (bf16[384,128]{1,0:T(8,128)(2,1)}, bf16[384,128]{1,0:T(8,128)(2,1)S(1)}, u32[]{:S(2)}, u32[]{:S(2)}) collective-permute-start(bf16[384,128]{1,0:T(8,128)(2,1)} %get-tuple-element.48), channel_id=1, source_target_pairs={{0,112},{8,120},{16,96},{24,104},{32,16},{40,24},{48,0},{56,8},{64... | collective-permute-start | bytes 294920 | tf_op jit(solution)/shard_map/ppermute | solution.py:379
  90.1 22.2 %collective-permute-start.28 = (bf16[1024,384]{1,0:T(8,128)(2,1)}, bf16[1024,384]{1,0:T(8,128)(2,1)S(1)}, u32[]{:S(2)}, u32[]{:S(2)}) collective-permute-start(bf16[1024,384]{1,0:T(8,128)(2,1)} %get-tuple-element.57), channel_id=1, source_target_pairs={{0,4},{1,5},{2,6},{3,7},{4,0},{5,1},{6,2},{7,3},{8,12},{9,13},{10,... | collective-permute-start | bytes 2359304 | tf_op jit(solution)/shard_map/ppermute | solution.py:403
  91.7 25.5 %collective-permute-start.25 = (bf16[1024,384]{1,0:T(8,128)(2,1)}, bf16[1024,384]{1,0:T(8,128)(2,1)S(1)}, u32[]{:S(2)}, u32[]{:S(2)}) collective-permute-start(bf16[1024,384]{1,0:T(8,128)(2,1)} %get-tuple-element.53), channel_id=1, source_target_pairs={{0,1},{1,2},{2,3},{3,0},{4,5},{5,6},{6,7},{7,4},{8,9},{9,10},{10,1... | collective-permute-start | bytes 2359304 | tf_op jit(solution)/shard_map/ppermute | solution.py:398
  93.3 23.8 %collective-permute-start.26 = (bf16[1024,384]{1,0:T(8,128)(2,1)}, bf16[1024,384]{1,0:T(8,128)(2,1)S(1)}, u32[]{:S(2)}, u32[]{:S(2)}) collective-permute-start(bf16[1024,384]{1,0:T(8,128)(2,1)} %get-tuple-element.54), channel_id=1, source_target_pairs={{0,3},{1,0},{2,1},{3,2},{4,7},{5,4},{6,5},{7,6},{8,11},{9,8},{10,9... | collective-permute-start | bytes 2359304 | tf_op jit(solution)/shard_map/ppermute | solution.py:398
  114.5 18.4 %collective-permute-start.29 = (bf16[512,384]{1,0:T(8,128)(2,1)}, bf16[512,384]{1,0:T(8,128)(2,1)}, u32[]{:S(2)}, u32[]{:S(2)}) collective-permute-start(bf16[512,384]{1,0:T(8,128)(2,1)} %get-tuple-element.60), channel_id=1, source_target_pairs={{0,1},{1,2},{2,3},{3,0},{4,5},{5,6},{6,7},{7,4},{8,9},{9,10},{10,1... | collective-permute-start | bytes 1179656 | tf_op jit(solution)/shard_map/ppermute | solution.py:398
  114.5 21.1 %collective-permute-start.31 = (bf16[512,384]{1,0:T(8,128)(2,1)S(1)}, bf16[512,384]{1,0:T(8,128)(2,1)}, u32[]{:S(2)}, u32[]{:S(2)}) collective-permute-start(bf16[512,384]{1,0:T(8,128)(2,1)S(1)} %get-tuple-element.61), channel_id=1, source_target_pairs={{0,3},{1,0},{2,1},{3,2},{4,7},{5,4},{6,5},{7,6},{8,11},{9,8},{10,9... | collective-permute-start | bytes 1179656 | tf_op jit(solution)/shard_map/ppermute | solution.py:398
  117.5 28.7 %collective-permute-start.27 = (bf16[1024,384]{1,0:T(8,128)(2,1)S(1)}, bf16[1024,384]{1,0:T(8,128)(2,1)S(1)}, u32[]{:S(2)}, u32[]{:S(2)}) collective-permute-start(bf16[1024,384]{1,0:T(8,128)(2,1)S(1)} %add_convert_fusion.1), channel_id=1, source_target_pairs={{0,4},{1,5},{2,6},{3,7},{4,0},{5,1},{6,2},{7,3},{8,12},{9,13},{10,... | collective-permute-start | bytes 2359304 | tf_op jit(solution)/shard_map/ppermute | solution.py:414
  118.3 19.2 %collective-permute-start.15 = (bf16[128,1024]{1,0:T(8,128)(2,1)S(1)}, bf16[128,1024]{1,0:T(8,128)(2,1)}, u32[]{:S(2)}, u32[]{:S(2)}) collective-permute-start(bf16[128,1024]{1,0:T(8,128)(2,1)S(1)} %multiply_convert_fusion), channel_id=1, source_target_pairs={{0,8},{8,16},{16,24},{24,32},{32,40},{40,48},{48,56},{56,64},{64,7... | collective-permute-start | bytes 786440 | tf_op jit(solution)/shard_map/ppermute | solution.py:24
  127.7 18.4 %collective-permute-start.23 = (bf16[512,384]{1,0:T(8,128)(2,1)}, bf16[512,384]{1,0:T(8,128)(2,1)}, u32[]{:S(2)}, u32[]{:S(2)}) collective-permute-start(bf16[512,384]{1,0:T(8,128)(2,1)} %get-tuple-element.50), channel_id=1, source_target_pairs={{0,3},{1,0},{2,1},{3,2},{4,7},{5,4},{6,5},{7,6},{8,11},{9,8},{10,9... | collective-permute-start | bytes 1179656 | tf_op jit(solution)/shard_map/ppermute | solution.py:398
  132.8 13.3 %collective-permute-start.24 = (bf16[512,384]{1,0:T(8,128)(2,1)}, bf16[512,384]{1,0:T(8,128)(2,1)}, u32[]{:S(2)}, u32[]{:S(2)}) collective-permute-start(bf16[512,384]{1,0:T(8,128)(2,1)} %get-tuple-element.51), channel_id=1, source_target_pairs={{0,1},{1,2},{2,3},{3,0},{4,5},{5,6},{6,7},{7,4},{8,9},{9,10},{10,1... | collective-permute-start | bytes 1179656 | tf_op jit(solution)/shard_map/ppermute | solution.py:398
  135.6 15.5 %collective-permute-start.30 = (bf16[512,384]{1,0:T(8,128)(2,1)}, bf16[512,384]{1,0:T(8,128)(2,1)S(1)}, u32[]{:S(2)}, u32[]{:S(2)}) collective-permute-start(bf16[512,384]{1,0:T(8,128)(2,1)} %add_convert_fusion.4), channel_id=1, source_target_pairs={{0,1},{1,2},{2,3},{3,0},{4,5},{5,6},{6,7},{7,4},{8,9},{9,10},{10,1... | collective-permute-start | bytes 1179656 | tf_op jit(solution)/shard_map/ppermute | solution.py:398
  137.5 13.6 %collective-permute-start.32 = (bf16[512,384]{1,0:T(8,128)(2,1)}, bf16[512,384]{1,0:T(8,128)(2,1)S(1)}, u32[]{:S(2)}, u32[]{:S(2)}) collective-permute-start(bf16[512,384]{1,0:T(8,128)(2,1)} %add_convert_fusion.2), channel_id=1, source_target_pairs={{0,3},{1,0},{2,1},{3,2},{4,7},{5,4},{6,5},{7,6},{8,11},{9,8},{10,9... | collective-permute-start | bytes 1179656 | tf_op jit(solution)/shard_map/ppermute | solution.py:398
  (27 other events, 178.8 us)

commit v9 on v8

--- a/solution.py
+++ b/solution.py
@@ -403,8 +403,11 @@
     crossed = lax.ppermute(far, "tp", PAIR_ROUTE)
     from_below = sent(up, 1)
     from_above = sent(down, -1)
-    far_0, far_1, up_0, up_1, down_0, down_1, other_own = project(
-        place, [(0, 2, 2), (0, 1, 2), (0, 3, 2), (1, 0, 1)], out_weight, attended
+    far_0, far_1, up_0, up_1, down_0, down_1, other_own, kept = project(
+        place,
+        [(0, 2, 2), (0, 1, 2), (0, 3, 2), (1, 0, 1), (0, 0, 1)],
+        out_weight,
+        attended,
     )
     half = far_0.shape[0]
     first_below = sent(added(far_0, crossed[:half]).astype(jnp.bfloat16), 1)
@@ -414,7 +417,6 @@
     handed = lax.ppermute(
         added(other_own, from_below, from_above).astype(jnp.bfloat16), "tp", PAIR_ROUTE
     )
-    (kept,) = project(place, [(0, 0, 1)], out_weight, attended)
     below_0 = sent(added(up_0, first_below).astype(jnp.bfloat16), 1)
     above_1 = sent(added(down_1, first_above).astype(jnp.bfloat16), -1)
     partial_out = lax.optimization_barrier(

time: 153 us -> 152 us (level)
  waiting for transfers between devices: 21.3 us -> 27 us
  other arithmetic: 9.37 us -> 6.64 us
  Pallas kernels: 60.7 us -> 58 us
  starting transfers between devices: 58.4 us -> 55.9 us
    ppermute x1, waiting for transfers between devices: 0.01 us -> 5.65 us  [shifted(): return lax.ppermute(block, axis, route)]
    pallas_call x3 -> x2, Pallas kernels: 22.1 us -> 19.4 us  [project(): pl.pallas_call(kernel, grid_spec=pltpu.PrefetchScalarGridSpec(num_scalar_...]
    ppermute x8, starting transfers between devices: 10.7 us -> 8.04 us  [sent(): return lax.ppermute(block, 'tp', ring_route(step))]
  transfers between devices with their start and end apart: 33 -> 33, of which waited for: 9 -> 11; matrix products, arithmetic and copies ran while one was open for 6% -> 4% of each run, Pallas kernels for 18% -> 16%
where the time goes in v9:
time: 152 us; the launch traced here: 151 us
  Pallas kernels  58 us (38%)
  starting transfers between devices  55.9 us (37%)
  waiting for transfers between devices  27 us (18%)
  other arithmetic  6.64 us (4%)
  local copies, waits for them, and re-layouts  2.17 us (1%)
    ppermute x14, starting transfers between devices, brought(): return lax.ppermute(block, 'ctx', chip_route(step))  29 us
    pallas_call x1, Pallas kernels, attention(): pl.pallas_call(attention_kernel, grid=(CHIPS,), out_shape=[jax.ShapeDtype...  22.1 us
    pallas_call x2, Pallas kernels, project(): pl.pallas_call(kernel, grid_spec=pltpu.PrefetchScalarGridSpec(num_scalar_...  19.4 us
    ppermute x14, waiting for transfers between devices, brought(): return lax.ppermute(block, 'ctx', chip_route(step))  16.4 us
    ppermute x1, starting transfers between devices, shifted(): return lax.ppermute(block, axis, route)  9.46 us
    ppermute x8, starting transfers between devices, sent(): return lax.ppermute(block, 'tp', ring_route(step))  8.04 us
    ppermute x8, starting transfers between devices, local_step(): other.append(lax.ppermute(block, 'ctx', CORE_ROUTE))  7.79 us
    pallas_call x1, Pallas kernels, hyena_inner(): pl.pallas_call(inner_kernel, grid=(steps,), out_shape=jax.ShapeDtypeStruc...  7.5 us
  transfers between devices with their start and end apart: 33, of which 11 were waited for; matrix products, arithmetic and copies ran while one was open for 4% of the time, Pallas kernels for 16%

profile of v9, /device:TPU:1, one launch (start us, length us, event | category | flops | bytes accessed | tf_op | source)
XLA Modules:
  0.0 150.5 jit_solution(11840066248642899795)
XLA Ops:
  0.6 2.9 %split_heads.1 = (bf16[1152,128]{1,0:T(8,128)(2,1)}, bf16[1152,128]{1,0:T(8,128)(2,1)}, bf16[1152,128]{1,0:T(8,128)(2,1)}, bf16[1152,128]{1,0:T(8,128)(2,1)}, bf...) custom-call(bf16[384,1024]{1,0:T(8,128)(2,1)} %k_ref.1, ...), custom_call_target="tpu_custom_call" | custom-call | tf_op jit(solution)/shard_map/split_heads/pallas_call | solution.py:169
  3.6 4.6 %collective-permute-start.2 = (bf16[1152,128]{1,0:T(8,128)(2,1)}, bf16[1152,128]{1,0:T(8,128)(2,1)S(1)}, u32[]{:S(2)}, u32[]{:S(2)}) collective-permute-start(bf16[1152,128]{1,0:T(8,128)(2,1)} %get-tuple-element.35), channel_id=1, source_target_pairs={{0,48},{8,56},{16,32},{24,40},{32,80},{40,88},{48,64},{56,72},{64,... | collective-permute-start | bytes 884744 | tf_op jit(solution)/shard_map/ppermute | solution.py:379
  8.2 2.6 %collective-permute-start.3 = (bf16[1152,128]{1,0:T(8,128)(2,1)}, bf16[1152,128]{1,0:T(8,128)(2,1)S(1)}, u32[]{:S(2)}, u32[]{:S(2)}) collective-permute-start(bf16[1152,128]{1,0:T(8,128)(2,1)} %get-tuple-element.36), channel_id=1, source_target_pairs={{0,64},{8,72},{16,80},{24,88},{32,96},{40,104},{48,112},{56,120},{... | collective-permute-start | bytes 884744 | tf_op jit(solution)/shard_map/ppermute | solution.py:379
  11.1 1.6 %collective-permute-start.5 = (bf16[1152,128]{1,0:T(8,128)(2,1)}, bf16[1152,128]{1,0:T(8,128)(2,1)S(1)}, u32[]{:S(2)}, u32[]{:S(2)}) collective-permute-start(bf16[1152,128]{1,0:T(8,128)(2,1)} %get-tuple-element.38), channel_id=1, source_target_pairs={{0,96},{8,104},{16,112},{24,120},{32,0},{40,8},{48,16},{56,24},{64... | collective-permute-start | bytes 884744 | tf_op jit(solution)/shard_map/ppermute | solution.py:379
  12.7 3.8 %collective-permute-start.6 = (bf16[1152,128]{1,0:T(8,128)(2,1)}, bf16[1152,128]{1,0:T(8,128)(2,1)S(1)}, u32[]{:S(2)}, u32[]{:S(2)}) collective-permute-start(bf16[1152,128]{1,0:T(8,128)(2,1)} %get-tuple-element.39), channel_id=1, source_target_pairs={{0,112},{8,120},{16,96},{24,104},{32,16},{40,24},{48,0},{56,8},{64... | collective-permute-start | bytes 884744 | tf_op jit(solution)/shard_map/ppermute | solution.py:379
  16.5 3.5 %collective-permute-start = (bf16[1152,128]{1,0:T(8,128)(2,1)}, bf16[1152,128]{1,0:T(8,128)(2,1)S(1)}, u32[]{:S(2)}, u32[]{:S(2)}) collective-permute-start(bf16[1152,128]{1,0:T(8,128)(2,1)} %get-tuple-element.33), channel_id=1, source_target_pairs={{0,16},{8,24},{16,0},{24,8},{32,48},{40,56},{48,32},{56,40},{64,80... | collective-permute-start | bytes 884744 | tf_op jit(solution)/shard_map/ppermute | solution.py:379
  20.0 11.1 %collective-permute-done.3.refs_4_ = bf16[1152,128]{1,0:T(8,128)(2,1)S(1)} collective-permute-done((bf16[1152,128]{1,0:T(8,128)(2,1)}, bf16[1152,128]{1,0:T(8,128)(2,1)S(1)}, u32[]{:S(2)}, u32[]{:S(2)}) %collective-permute-start.3) | collective-permute-done | bytes 294944 | tf_op jit(solution)/shard_map/ppermute | solution.py:379
  31.4 3.6 %collective-permute-start.7 = (bf16[1152,128]{1,0:T(8,128)(2,1)}, bf16[1152,128]{1,0:T(8,128)(2,1)S(1)}, u32[]{:S(2)}, u32[]{:S(2)}) collective-permute-start(bf16[1152,128]{1,0:T(8,128)(2,1)} %get-tuple-element.32.refs_0_), channel_id=1, source_target_pairs={{0,8},{8,0},{16,24},{24,16},{32,40},{40,32},{48,56},{56,48},{64,72... | collective-permute-start | bytes 884744 | tf_op jit(solution)/shard_map/ppermute | solution.py:388
  35.0 0.9 collective-permute-done.5.refs_6_
  35.9 1.4 collective-permute-start.10
  37.9 2.4 %collective-permute-done.1.refs_2_ = bf16[1152,128]{1,0:T(8,128)(2,1)S(1)} collective-permute-done((bf16[1152,128]{1,0:T(8,128)(2,1)}, bf16[1152,128]{1,0:T(8,128)(2,1)S(1)}, u32[]{:S(2)}, u32[]{:S(2)}) %collective-permute-start.1) | collective-permute-done | bytes 294944 | tf_op jit(solution)/shard_map/ppermute | solution.py:379
  40.3 1.6 %collective-permute-start.13 = (bf16[1152,128]{1,0:T(8,128)(2,1)S(1)}, bf16[1152,128]{1,0:T(8,128)(2,1)}, u32[]{:S(2)}, u32[]{:S(2)}) collective-permute-start(bf16[1152,128]{1,0:T(8,128)(2,1)S(1)} %collective-permute-done.5.refs_6_), channel_id=1, source_target_pairs={{0,8},{8,0},{16,24},{24,16},{32,40},{40,32},{48,56},{56,48},{64,72... | collective-permute-start | bytes 884744 | tf_op jit(solution)/shard_map/ppermute | solution.py:388
  44.6 22.1 %attention.1 = (bf16[384,128]{1,0:T(8,128)(2,1)}, bf16[384,128]{1,0:T(8,128)(2,1)}, bf16[384,128]{1,0:T(8,128)(2,1)}, bf16[384,128]{1,0:T(8,128)(2,1)}, bf16[384...) custom-call(s32[5]{0:T(128)} %stack.23.place, ...), custom_call_target="tpu_custom_call" | custom-call | flops 12000000000 | bytes 6000000 | tf_op jit(solution)/shard_map/attention/pallas_call | solution.py:264
  66.9 2.3 %collective-permute-start.18 = (bf16[384,128]{1,0:T(8,128)(2,1)}, bf16[384,128]{1,0:T(8,128)(2,1)S(1)}, u32[]{:S(2)}, u32[]{:S(2)}) collective-permute-start(bf16[384,128]{1,0:T(8,128)(2,1)} %get-tuple-element.45), channel_id=1, source_target_pairs={{0,48},{8,56},{16,32},{24,40},{32,80},{40,88},{48,64},{56,72},{64,... | collective-permute-start | bytes 294920 | tf_op jit(solution)/shard_map/ppermute | solution.py:379
  69.2 4.1 %collective-permute-start.19 = (bf16[384,128]{1,0:T(8,128)(2,1)}, bf16[384,128]{1,0:T(8,128)(2,1)S(1)}, u32[]{:S(2)}, u32[]{:S(2)}) collective-permute-start(bf16[384,128]{1,0:T(8,128)(2,1)} %get-tuple-element.46), channel_id=1, source_target_pairs={{0,64},{8,72},{16,80},{24,88},{32,96},{40,104},{48,112},{56,120},{... | collective-permute-start | bytes 294920 | tf_op jit(solution)/shard_map/ppermute | solution.py:379
  73.8 1.4 collective-permute-start.21
  75.1 3.9 %collective-permute-start.22 = (bf16[384,128]{1,0:T(8,128)(2,1)}, bf16[384,128]{1,0:T(8,128)(2,1)S(1)}, u32[]{:S(2)}, u32[]{:S(2)}) collective-permute-start(bf16[384,128]{1,0:T(8,128)(2,1)} %get-tuple-element.49), channel_id=1, source_target_pairs={{0,112},{8,120},{16,96},{24,104},{32,16},{40,24},{48,0},{56,8},{64... | collective-permute-start | bytes 294920 | tf_op jit(solution)/shard_map/ppermute | solution.py:379
  79.2 1.7 %collective-permute-done.20.refs_5_ = bf16[384,128]{1,0:T(8,128)(2,1)S(1)} collective-permute-done((bf16[384,128]{1,0:T(8,128)(2,1)}, bf16[384,128]{1,0:T(8,128)(2,1)S(1)}, u32[]{:S(2)}, u32[]{:S(2)}) %collective-permute-start.20) | collective-permute-done | bytes 98336 | tf_op jit(solution)/shard_map/ppermute | solution.py:379
  81.8 8.3 %project.2 = (bf16[384,1024]{1,0:T(8,128)(2,1)}, bf16[1024,384]{1,0:T(8,128)(2,1)}, bf16[1024,384]{1,0:T(8,128)(2,1)}, bf16[1024,384]{1,0:T(8,128)(2,1)}) custom-call(s32[5]{0:T(128)} %stack.23.place, bf16[8192,1024]{1,0:T(8,128)(2,1)} %weight_ref.3, bf16[384,128]{1,0:T(8,128)(2,1)} %get-tuple-element.40.refs_0_, bf16[384,128]{1,0:T(8,128)(2,1)} %copy-done.4, ...), custom_call_target="tpu_custom_call" | custom-call | flops 2415919104 | bytes 6291456 | tf_op jit(solution)/shard_map/project/pallas_call | solution.py:337
  91.6 1.6 %collective-permute-start.25 = (bf16[1024,384]{1,0:T(8,128)(2,1)}, bf16[1024,384]{1,0:T(8,128)(2,1)S(1)}, u32[]{:S(2)}, u32[]{:S(2)}) collective-permute-start(bf16[1024,384]{1,0:T(8,128)(2,1)} %get-tuple-element.55), channel_id=1, source_target_pairs={{0,1},{1,2},{2,3},{3,0},{4,5},{5,6},{6,7},{7,4},{8,9},{9,10},{10,1... | collective-permute-start | bytes 2359304 | tf_op jit(solution)/shard_map/ppermute | solution.py:398
  93.3 2.1 %collective-permute-start.26 = (bf16[1024,384]{1,0:T(8,128)(2,1)}, bf16[1024,384]{1,0:T(8,128)(2,1)S(1)}, u32[]{:S(2)}, u32[]{:S(2)}) collective-permute-start(bf16[1024,384]{1,0:T(8,128)(2,1)} %get-tuple-element.56), channel_id=1, source_target_pairs={{0,3},{1,0},{2,1},{3,2},{4,7},{5,4},{6,5},{7,6},{8,11},{9,8},{10,9... | collective-permute-start | bytes 2359304 | tf_op jit(solution)/shard_map/ppermute | solution.py:398
  95.4 7.5 %hyena_inner.1.unused = bf16[384,1024]{1,0:T(8,128)(2,1)} custom-call(bf16[384,1024]{1,0:T(8,128)(2,1)} %query.3, bf16[384,1024]{1,0:T(8,128)(2,1)} %key.3, bf16[384,1024]{1,0:T(8,128)(2,1)} %value.3, f32[64,256]{1,0:T(8,128)} %maximum_maximum_fusion.taps, f32[1,1024]{1,0:T(1,128)} %bitcast.7), custom_call_target="tpu_custom_call" | custom-call | flops 3000000000 | bytes 3000000 | tf_op jit(solution)/shard_map/hyena_inner/pallas_call | solution.py:93
  102.9 11.2 %project.3 = (bf16[512,384]{1,0:T(8,128)(2,1)}, bf16[512,384]{1,0:T(8,128)(2,1)}, bf16[512,384]{1,0:T(8,128)(2,1)}, bf16[512,384]{1,0:T(8,128)(2,1)}, bf16[512,3...) custom-call(s32[5]{0:T(128)} %stack.23.place, ...), custom_call_target="tpu_custom_call" | custom-call | flops 4026531840 | bytes 10485760 | tf_op jit(solution)/shard_map/project/pallas_call | solution.py:337
  114.1 1.4 add_convert_fusion.5
  115.6 2.7 %collective-permute-start.31 = (bf16[512,384]{1,0:T(8,128)(2,1)S(1)}, bf16[512,384]{1,0:T(8,128)(2,1)S(1)}, u32[]{:S(2)}, u32[]{:S(2)}) collective-permute-start(bf16[512,384]{1,0:T(8,128)(2,1)S(1)} %get-tuple-element.63), channel_id=1, source_target_pairs={{0,3},{1,0},{2,1},{3,2},{4,7},{5,4},{6,5},{7,6},{8,11},{9,8},{10,9... | collective-permute-start | bytes 1179656 | tf_op jit(solution)/shard_map/ppermute | solution.py:398
  119.4 9.5 %collective-permute-start.15 = (bf16[128,1024]{1,0:T(8,128)(2,1)S(1)}, bf16[128,1024]{1,0:T(8,128)(2,1)S(1)}, u32[]{:S(2)}, u32[]{:S(2)}) collective-permute-start(bf16[128,1024]{1,0:T(8,128)(2,1)S(1)} %multiply_convert_fusion), channel_id=1, source_target_pairs={{0,8},{8,16},{16,24},{24,32},{32,40},{40,48},{48,56},{56,64},{64,7... | collective-permute-start | bytes 786440 | tf_op jit(solution)/shard_map/ppermute | solution.py:24
  129.4 0.9 collective-permute-start.24
  132.1 5.7 %collective-permute-done.15.before = bf16[128,1024]{1,0:T(8,128)(2,1)S(1)} collective-permute-done((bf16[128,1024]{1,0:T(8,128)(2,1)S(1)}, bf16[128,1024]{1,0:T(8,128)(2,1)S(1)}, u32[]{:S(2)}, u32[]{:S(2)}) %collective-permute-start.15) | collective-permute-done | bytes 262176 | tf_op jit(solution)/shard_map/ppermute | solution.py:24
  138.5 6.0 %hyena_edge.1 = bf16[384,1024]{1,0:T(8,128)(2,1)} custom-call(bf16[384,1024]{1,0:T(8,128)(2,1)} %query.3, bf16[384,1024]{1,0:T(8,128)(2,1)} %key.3, bf16[384,1024]{1,0:T(8,128)(2,1)} %value.3, bf16[128,1024]{1,0:T(8,128)(2,1)} %copy-done.23, f32[64,256]{1,0:T(8,128)} %maximum_maximum_fusion.taps, f32[1,1024]{1,0:T(1,128)} %bitcast.8, ...), custom_call_target="tpu_custom_call", output_to_operand_aliasing={{}: (6, {})} | custom-call | flops 1500000000 | bytes 1000000 | tf_op jit(solution)/shard_map/hyena_edge/pallas_call | solution.py:112
  144.5 1.4 convert_add_fusion
  145.9 3.5 %collective-permute-done.30 = bf16[512,384]{1,0:T(8,128)(2,1)S(1)} collective-permute-done((bf16[512,384]{1,0:T(8,128)(2,1)}, bf16[512,384]{1,0:T(8,128)(2,1)S(1)}, u32[]{:S(2)}, u32[]{:S(2)}) %collective-permute-start.30) | collective-permute-done | bytes 393248 | tf_op jit(solution)/shard_map/ppermute | solution.py:398
  149.4 1.1 add_convert_fusion
  (106 shorter events, 11.3 us)
Async XLA Ops:
  3.6 12.9 %collective-permute-start.2 = (bf16[1152,128]{1,0:T(8,128)(2,1)}, bf16[1152,128]{1,0:T(8,128)(2,1)S(1)}, u32[]{:S(2)}, u32[]{:S(2)}) collective-permute-start(bf16[1152,128]{1,0:T(8,128)(2,1)} %get-tuple-element.35), channel_id=1, source_target_pairs={{0,48},{8,56},{16,32},{24,40},{32,80},{40,88},{48,64},{56,72},{64,... | collective-permute-start | bytes 884744 | tf_op jit(solution)/shard_map/ppermute | solution.py:379
  8.2 22.9 %collective-permute-start.3 = (bf16[1152,128]{1,0:T(8,128)(2,1)}, bf16[1152,128]{1,0:T(8,128)(2,1)S(1)}, u32[]{:S(2)}, u32[]{:S(2)}) collective-permute-start(bf16[1152,128]{1,0:T(8,128)(2,1)} %get-tuple-element.36), channel_id=1, source_target_pairs={{0,64},{8,72},{16,80},{24,88},{32,96},{40,104},{48,112},{56,120},{... | collective-permute-start | bytes 884744 | tf_op jit(solution)/shard_map/ppermute | solution.py:379
  10.8 20.6 %collective-permute-start.4 = (bf16[1152,128]{1,0:T(8,128)(2,1)}, bf16[1152,128]{1,0:T(8,128)(2,1)S(1)}, u32[]{:S(2)}, u32[]{:S(2)}) collective-permute-start(bf16[1152,128]{1,0:T(8,128)(2,1)} %get-tuple-element.37), channel_id=1, source_target_pairs={{0,80},{8,88},{16,64},{24,72},{32,112},{40,120},{48,96},{56,104},{... | collective-permute-start | bytes 884744 | tf_op jit(solution)/shard_map/ppermute | solution.py:379
  11.1 24.8 %collective-permute-start.5 = (bf16[1152,128]{1,0:T(8,128)(2,1)}, bf16[1152,128]{1,0:T(8,128)(2,1)S(1)}, u32[]{:S(2)}, u32[]{:S(2)}) collective-permute-start(bf16[1152,128]{1,0:T(8,128)(2,1)} %get-tuple-element.38), channel_id=1, source_target_pairs={{0,96},{8,104},{16,112},{24,120},{32,0},{40,8},{48,16},{56,24},{64... | collective-permute-start | bytes 884744 | tf_op jit(solution)/shard_map/ppermute | solution.py:379
  12.7 24.6 %collective-permute-start.6 = (bf16[1152,128]{1,0:T(8,128)(2,1)}, bf16[1152,128]{1,0:T(8,128)(2,1)S(1)}, u32[]{:S(2)}, u32[]{:S(2)}) collective-permute-start(bf16[1152,128]{1,0:T(8,128)(2,1)} %get-tuple-element.39), channel_id=1, source_target_pairs={{0,112},{8,120},{16,96},{24,104},{32,16},{40,24},{48,0},{56,8},{64... | collective-permute-start | bytes 884744 | tf_op jit(solution)/shard_map/ppermute | solution.py:379
  16.5 20.9 %collective-permute-start = (bf16[1152,128]{1,0:T(8,128)(2,1)}, bf16[1152,128]{1,0:T(8,128)(2,1)S(1)}, u32[]{:S(2)}, u32[]{:S(2)}) collective-permute-start(bf16[1152,128]{1,0:T(8,128)(2,1)} %get-tuple-element.33), channel_id=1, source_target_pairs={{0,16},{8,24},{16,0},{24,8},{32,48},{40,56},{48,32},{56,40},{64,80... | collective-permute-start | bytes 884744 | tf_op jit(solution)/shard_map/ppermute | solution.py:379
  31.1 9.2 %collective-permute-start.1 = (bf16[1152,128]{1,0:T(8,128)(2,1)}, bf16[1152,128]{1,0:T(8,128)(2,1)S(1)}, u32[]{:S(2)}, u32[]{:S(2)}) collective-permute-start(bf16[1152,128]{1,0:T(8,128)(2,1)} %get-tuple-element.34), channel_id=1, source_target_pairs={{0,32},{8,40},{16,48},{24,56},{32,64},{40,72},{48,80},{56,88},{64,... | collective-permute-start | bytes 884744 | tf_op jit(solution)/shard_map/ppermute | solution.py:379
  31.4 10.5 %collective-permute-start.7 = (bf16[1152,128]{1,0:T(8,128)(2,1)}, bf16[1152,128]{1,0:T(8,128)(2,1)S(1)}, u32[]{:S(2)}, u32[]{:S(2)}) collective-permute-start(bf16[1152,128]{1,0:T(8,128)(2,1)} %get-tuple-element.32.refs_0_), channel_id=1, source_target_pairs={{0,8},{8,0},{16,24},{24,16},{32,40},{40,32},{48,56},{56,48},{64,72... | collective-permute-start | bytes 884744 | tf_op jit(solution)/shard_map/ppermute | solution.py:388
  35.9 6.1 %collective-permute-start.10 = (bf16[1152,128]{1,0:T(8,128)(2,1)S(1)}, bf16[1152,128]{1,0:T(8,128)(2,1)S(1)}, u32[]{:S(2)}, u32[]{:S(2)}) collective-permute-start(bf16[1152,128]{1,0:T(8,128)(2,1)S(1)} %collective-permute-done.2.refs_3_), channel_id=1, source_target_pairs={{0,8},{8,0},{16,24},{24,16},{32,40},{40,32},{48,56},{56,48},{64,72... | collective-permute-start | bytes 884744 | tf_op jit(solution)/shard_map/ppermute | solution.py:388
  37.3 5.1 %collective-permute-start.11 = (bf16[1152,128]{1,0:T(8,128)(2,1)S(1)}, bf16[1152,128]{1,0:T(8,128)(2,1)S(1)}, u32[]{:S(2)}, u32[]{:S(2)}) collective-permute-start(bf16[1152,128]{1,0:T(8,128)(2,1)S(1)} %collective-permute-done.3.refs_4_), channel_id=1, source_target_pairs={{0,8},{8,0},{16,24},{24,16},{32,40},{40,32},{48,56},{56,48},{64,72... | collective-permute-start | bytes 884744 | tf_op jit(solution)/shard_map/ppermute | solution.py:388
  37.4 5.7 %collective-permute-start.12 = (bf16[1152,128]{1,0:T(8,128)(2,1)S(1)}, bf16[1152,128]{1,0:T(8,128)(2,1)S(1)}, u32[]{:S(2)}, u32[]{:S(2)}) collective-permute-start(bf16[1152,128]{1,0:T(8,128)(2,1)S(1)} %collective-permute-done.4.refs_5_), channel_id=1, source_target_pairs={{0,8},{8,0},{16,24},{24,16},{32,40},{40,32},{48,56},{56,48},{64,72... | collective-permute-start | bytes 884744 | tf_op jit(solution)/shard_map/ppermute | solution.py:388
  40.3 3.0 %collective-permute-start.13 = (bf16[1152,128]{1,0:T(8,128)(2,1)S(1)}, bf16[1152,128]{1,0:T(8,128)(2,1)}, u32[]{:S(2)}, u32[]{:S(2)}) collective-permute-start(bf16[1152,128]{1,0:T(8,128)(2,1)S(1)} %collective-permute-done.5.refs_6_), channel_id=1, source_target_pairs={{0,8},{8,0},{16,24},{24,16},{32,40},{40,32},{48,56},{56,48},{64,72... | collective-permute-start | bytes 884744 | tf_op jit(solution)/shard_map/ppermute | solution.py:388
  42.0 2.1 %collective-permute-start.8 = (bf16[1152,128]{1,0:T(8,128)(2,1)S(1)}, bf16[1152,128]{1,0:T(8,128)(2,1)}, u32[]{:S(2)}, u32[]{:S(2)}) collective-permute-start(bf16[1152,128]{1,0:T(8,128)(2,1)S(1)} %collective-permute-done.refs_1_), channel_id=1, source_target_pairs={{0,8},{8,0},{16,24},{24,16},{32,40},{40,32},{48,56},{56,48},{64,72... | collective-permute-start | bytes 884744 | tf_op jit(solution)/shard_map/ppermute | solution.py:388
  42.5 2.1 %collective-permute-start.9 = (bf16[1152,128]{1,0:T(8,128)(2,1)S(1)}, bf16[1152,128]{1,0:T(8,128)(2,1)}, u32[]{:S(2)}, u32[]{:S(2)}) collective-permute-start(bf16[1152,128]{1,0:T(8,128)(2,1)S(1)} %collective-permute-done.1.refs_2_), channel_id=1, source_target_pairs={{0,8},{8,0},{16,24},{24,16},{32,40},{40,32},{48,56},{56,48},{64,72... | collective-permute-start | bytes 884744 | tf_op jit(solution)/shard_map/ppermute | solution.py:388
  66.7 7.1 %collective-permute-start.16 = (bf16[384,128]{1,0:T(8,128)(2,1)}, bf16[384,128]{1,0:T(8,128)(2,1)S(1)}, u32[]{:S(2)}, u32[]{:S(2)}) collective-permute-start(bf16[384,128]{1,0:T(8,128)(2,1)} %get-tuple-element.43), channel_id=1, source_target_pairs={{0,16},{8,24},{16,0},{24,8},{32,48},{40,56},{48,32},{56,40},{64,80... | collective-permute-start | bytes 294920 | tf_op jit(solution)/shard_map/ppermute | solution.py:379
  66.8 8.3 %collective-permute-start.17 = (bf16[384,128]{1,0:T(8,128)(2,1)}, bf16[384,128]{1,0:T(8,128)(2,1)S(1)}, u32[]{:S(2)}, u32[]{:S(2)}) collective-permute-start(bf16[384,128]{1,0:T(8,128)(2,1)} %get-tuple-element.44), channel_id=1, source_target_pairs={{0,32},{8,40},{16,48},{24,56},{32,64},{40,72},{48,80},{56,88},{64,... | collective-permute-start | bytes 294920 | tf_op jit(solution)/shard_map/ppermute | solution.py:379
  66.9 12.3 %collective-permute-start.18 = (bf16[384,128]{1,0:T(8,128)(2,1)}, bf16[384,128]{1,0:T(8,128)(2,1)S(1)}, u32[]{:S(2)}, u32[]{:S(2)}) collective-permute-start(bf16[384,128]{1,0:T(8,128)(2,1)} %get-tuple-element.45), channel_id=1, source_target_pairs={{0,48},{8,56},{16,32},{24,40},{32,80},{40,88},{48,64},{56,72},{64,... | collective-permute-start | bytes 294920 | tf_op jit(solution)/shard_map/ppermute | solution.py:379
  69.2 10.0 %collective-permute-start.19 = (bf16[384,128]{1,0:T(8,128)(2,1)}, bf16[384,128]{1,0:T(8,128)(2,1)S(1)}, u32[]{:S(2)}, u32[]{:S(2)}) collective-permute-start(bf16[384,128]{1,0:T(8,128)(2,1)} %get-tuple-element.46), channel_id=1, source_target_pairs={{0,64},{8,72},{16,80},{24,88},{32,96},{40,104},{48,112},{56,120},{... | collective-permute-start | bytes 294920 | tf_op jit(solution)/shard_map/ppermute | solution.py:379
  73.3 7.6 %collective-permute-start.20 = (bf16[384,128]{1,0:T(8,128)(2,1)}, bf16[384,128]{1,0:T(8,128)(2,1)S(1)}, u32[]{:S(2)}, u32[]{:S(2)}) collective-permute-start(bf16[384,128]{1,0:T(8,128)(2,1)} %get-tuple-element.47), channel_id=1, source_target_pairs={{0,80},{8,88},{16,64},{24,72},{32,112},{40,120},{48,96},{56,104},{... | collective-permute-start | bytes 294920 | tf_op jit(solution)/shard_map/ppermute | solution.py:379
  73.8 7.1 %collective-permute-start.21 = (bf16[384,128]{1,0:T(8,128)(2,1)}, bf16[384,128]{1,0:T(8,128)(2,1)S(1)}, u32[]{:S(2)}, u32[]{:S(2)}) collective-permute-start(bf16[384,128]{1,0:T(8,128)(2,1)} %get-tuple-element.48), channel_id=1, source_target_pairs={{0,96},{8,104},{16,112},{24,120},{32,0},{40,8},{48,16},{56,24},{64... | collective-permute-start | bytes 294920 | tf_op jit(solution)/shard_map/ppermute | solution.py:379
  75.1 6.1 %collective-permute-start.22 = (bf16[384,128]{1,0:T(8,128)(2,1)}, bf16[384,128]{1,0:T(8,128)(2,1)S(1)}, u32[]{:S(2)}, u32[]{:S(2)}) collective-permute-start(bf16[384,128]{1,0:T(8,128)(2,1)} %get-tuple-element.49), channel_id=1, source_target_pairs={{0,112},{8,120},{16,96},{24,104},{32,16},{40,24},{48,0},{56,8},{64... | collective-permute-start | bytes 294920 | tf_op jit(solution)/shard_map/ppermute | solution.py:379
  90.1 24.0 %collective-permute-start.28 = (bf16[1024,384]{1,0:T(8,128)(2,1)}, bf16[1024,384]{1,0:T(8,128)(2,1)S(1)}, u32[]{:S(2)}, u32[]{:S(2)}) collective-permute-start(bf16[1024,384]{1,0:T(8,128)(2,1)} %get-tuple-element.59), channel_id=1, source_target_pairs={{0,4},{1,5},{2,6},{3,7},{4,0},{5,1},{6,2},{7,3},{8,12},{9,13},{10,... | collective-permute-start | bytes 2359304 | tf_op jit(solution)/shard_map/ppermute | solution.py:403
  91.6 26.6 %collective-permute-start.25 = (bf16[1024,384]{1,0:T(8,128)(2,1)}, bf16[1024,384]{1,0:T(8,128)(2,1)S(1)}, u32[]{:S(2)}, u32[]{:S(2)}) collective-permute-start(bf16[1024,384]{1,0:T(8,128)(2,1)} %get-tuple-element.55), channel_id=1, source_target_pairs={{0,1},{1,2},{2,3},{3,0},{4,5},{5,6},{6,7},{7,4},{8,9},{9,10},{10,1... | collective-permute-start | bytes 2359304 | tf_op jit(solution)/shard_map/ppermute | solution.py:398
  93.3 24.9 %collective-permute-start.26 = (bf16[1024,384]{1,0:T(8,128)(2,1)}, bf16[1024,384]{1,0:T(8,128)(2,1)S(1)}, u32[]{:S(2)}, u32[]{:S(2)}) collective-permute-start(bf16[1024,384]{1,0:T(8,128)(2,1)} %get-tuple-element.56), channel_id=1, source_target_pairs={{0,3},{1,0},{2,1},{3,2},{4,7},{5,4},{6,5},{7,6},{8,11},{9,8},{10,9... | collective-permute-start | bytes 2359304 | tf_op jit(solution)/shard_map/ppermute | solution.py:398
  115.5 14.0 %collective-permute-start.29 = (bf16[512,384]{1,0:T(8,128)(2,1)S(1)}, bf16[512,384]{1,0:T(8,128)(2,1)S(1)}, u32[]{:S(2)}, u32[]{:S(2)}) collective-permute-start(bf16[512,384]{1,0:T(8,128)(2,1)S(1)} %get-tuple-element.62), channel_id=1, source_target_pairs={{0,1},{1,2},{2,3},{3,0},{4,5},{5,6},{6,7},{7,4},{8,9},{9,10},{10,1... | collective-permute-start | bytes 1179656 | tf_op jit(solution)/shard_map/ppermute | solution.py:398
  115.6 15.7 %collective-permute-start.31 = (bf16[512,384]{1,0:T(8,128)(2,1)S(1)}, bf16[512,384]{1,0:T(8,128)(2,1)S(1)}, u32[]{:S(2)}, u32[]{:S(2)}) collective-permute-start(bf16[512,384]{1,0:T(8,128)(2,1)S(1)} %get-tuple-element.63), channel_id=1, source_target_pairs={{0,3},{1,0},{2,1},{3,2},{4,7},{5,4},{6,5},{7,6},{8,11},{9,8},{10,9... | collective-permute-start | bytes 1179656 | tf_op jit(solution)/shard_map/ppermute | solution.py:398
  118.6 25.9 %collective-permute-start.27 = (bf16[1024,384]{1,0:T(8,128)(2,1)S(1)}, bf16[1024,384]{1,0:T(8,128)(2,1)S(1)}, u32[]{:S(2)}, u32[]{:S(2)}) collective-permute-start(bf16[1024,384]{1,0:T(8,128)(2,1)S(1)} %add_convert_fusion.1), channel_id=1, source_target_pairs={{0,4},{1,5},{2,6},{3,7},{4,0},{5,1},{6,2},{7,3},{8,12},{9,13},{10,... | collective-permute-start | bytes 2359304 | tf_op jit(solution)/shard_map/ppermute | solution.py:417
  119.4 18.4 %collective-permute-start.15 = (bf16[128,1024]{1,0:T(8,128)(2,1)S(1)}, bf16[128,1024]{1,0:T(8,128)(2,1)S(1)}, u32[]{:S(2)}, u32[]{:S(2)}) collective-permute-start(bf16[128,1024]{1,0:T(8,128)(2,1)S(1)} %multiply_convert_fusion), channel_id=1, source_target_pairs={{0,8},{8,16},{16,24},{24,32},{32,40},{40,48},{48,56},{56,64},{64,7... | collective-permute-start | bytes 786440 | tf_op jit(solution)/shard_map/ppermute | solution.py:24
  128.8 15.6 %collective-permute-start.23 = (bf16[512,384]{1,0:T(8,128)(2,1)}, bf16[512,384]{1,0:T(8,128)(2,1)}, u32[]{:S(2)}, u32[]{:S(2)}) collective-permute-start(bf16[512,384]{1,0:T(8,128)(2,1)} %get-tuple-element.52), channel_id=1, source_target_pairs={{0,3},{1,0},{2,1},{3,2},{4,7},{5,4},{6,5},{7,6},{8,11},{9,8},{10,9... | collective-permute-start | bytes 1179656 | tf_op jit(solution)/shard_map/ppermute | solution.py:398
  129.4 15.0 %collective-permute-start.24 = (bf16[512,384]{1,0:T(8,128)(2,1)}, bf16[512,384]{1,0:T(8,128)(2,1)}, u32[]{:S(2)}, u32[]{:S(2)}) collective-permute-start(bf16[512,384]{1,0:T(8,128)(2,1)} %get-tuple-element.53), channel_id=1, source_target_pairs={{0,1},{1,2},{2,3},{3,0},{4,5},{5,6},{6,7},{7,4},{8,9},{9,10},{10,1... | collective-permute-start | bytes 1179656 | tf_op jit(solution)/shard_map/ppermute | solution.py:398
  131.2 18.2 %collective-permute-start.30 = (bf16[512,384]{1,0:T(8,128)(2,1)}, bf16[512,384]{1,0:T(8,128)(2,1)S(1)}, u32[]{:S(2)}, u32[]{:S(2)}) collective-permute-start(bf16[512,384]{1,0:T(8,128)(2,1)} %add_convert_fusion.4), channel_id=1, source_target_pairs={{0,1},{1,2},{2,3},{3,0},{4,5},{5,6},{6,7},{7,4},{8,9},{9,10},{10,1... | collective-permute-start | bytes 1179656 | tf_op jit(solution)/shard_map/ppermute | solution.py:398
  137.8 11.7 %collective-permute-start.32 = (bf16[512,384]{1,0:T(8,128)(2,1)}, bf16[512,384]{1,0:T(8,128)(2,1)S(1)}, u32[]{:S(2)}, u32[]{:S(2)}) collective-permute-start(bf16[512,384]{1,0:T(8,128)(2,1)} %add_convert_fusion.2), channel_id=1, source_target_pairs={{0,3},{1,0},{2,1},{3,2},{4,7},{5,4},{6,5},{7,6},{8,11},{9,8},{10,9... | collective-permute-start | bytes 1179656 | tf_op jit(solution)/shard_map/ppermute | solution.py:398
  (27 other events, 191.9 us)
